TPU v7x, 32 devices: a whole 2x2x4 slice. The times are simulated.
32 devices in a mesh: dom: 32 (over z, y, x, core).
Axes of the slice: x: 2, y: 2, z: 4, core: 2. Of those that a mesh axis runs over, the one named last changes fastest.
Arguments:
- features: bfloat16 [64, 262144], P(None, 'dom'), may hold values from -6 to 6
- cheb_weight: bfloat16 [4, 64, 64], replicated, may hold values from -0.375 to 0.375
- lap_tiles: bfloat16 [2048, 3, 128, 128], P('dom'), may hold values from -0.25 to 0.25
- col_index: int32 [2048, 3], P('dom'), may hold values from 0 to 63
- cross_tiles: bfloat16 [32, 5, 2, 128, 128], P('dom'), may hold values from -0.25 to 0.25
- send_index: int32 [32, 5, 2], P('dom'), may hold values from 0 to 63
- row_index: int32 [32, 5, 2], P('dom'), may hold values from 0 to 63
- pair_on: int32 [32, 5], P('dom'), may hold values 0 or 1
- blk_live: int32 [32], P('dom'), may hold values from 1 to 64, 1536 in all
- cotangent: bfloat16 [64, 262144], P(None, 'dom'), may hold values from -6 to 6
Outputs:
- conv_out: bfloat16 [64, 262144], P(None, 'dom')
- grad_x: bfloat16 [64, 262144], P(None, 'dom')
- grad_w: float32 [4, 64, 64], replicated
Inputs may be any that keep to these rules, and one draw needn't show every extreme that they name: `blk_live`: the counts sum to 1536 and the largest is exactly 64.
All inputs are finite; a program needn't handle non-finite values. No bound on the sum of `pair_on` or of `blk_live` on one device may be relied on, other than what follows from the above.
Results may differ from a plain program's by a relative error of at most 0.0059.
Values may be sent and summed in bfloat16 or wider, within the bound.
No kernel may reach another device: no remote copies, remote signals or barrier semaphores. Data moves between devices by JAX's collectives and lax.ppermute only.
A program may use at most 128 MiB of HBM per device.

v0:
```python
import jax
import jax.numpy as jnp
from jax import lax
from jax.sharding import PartitionSpec as P


def from_partner(block, axis, bit):
    count = lax.axis_size(axis)
    route = []
    for low in range(count):
        high = low | 1 << bit
        if high != low and high < count:
            route += [(low, high), (high, low)]
    return lax.ppermute(block, axis, route)


def local(
    features,
    cheb_weight,
    lap_tiles,
    col_index,
    cross_tiles,
    send_index,
    row_index,
    pair_on,
    blk_live,
    cotangent,
):
    channels = features.shape[0]
    block_count = lap_tiles.shape[0]
    block_size = lap_tiles.shape[2]
    rounds = cross_tiles.shape[1]
    live_blocks = blk_live[0]
    mask_half = (jnp.arange(block_count) < live_blocks).astype(jnp.bfloat16)[None, :, None]
    mask_full = mask_half.astype(jnp.float32)
    send_rows = send_index[0] % live_blocks
    recv_rows = row_index[0] % live_blocks
    switch = pair_on[0].astype(jnp.float32)
    coupling = cross_tiles[0]

    def apply_forward(values):
        gathered = jnp.take(values, col_index, axis=1)
        summed = jnp.einsum(
            "inab,finb->fia", lap_tiles, gathered, preferred_element_type=jnp.float32
        )
        for level in range(rounds):
            outgoing = jnp.take(values, send_rows[level], axis=1)
            incoming = from_partner(outgoing, "dom", level)
            product = jnp.einsum(
                "hab,fhb->fha", coupling[level], incoming, preferred_element_type=jnp.float32
            )
            summed = summed.at[:, recv_rows[level]].add(switch[level] * product)
        return summed

    def local_adjoint(values):
        terms = jnp.einsum("inab,fia->finb", lap_tiles, values, preferred_element_type=jnp.float32)
        return (
            jnp.zeros((channels, block_count, block_size), jnp.float32).at[:, col_index].add(terms)
        )

    flagged = coupling * pair_on[0].astype(jnp.bfloat16)[:, None, None, None]
    copies = [from_partner(flagged[level], "dom", level) for level in range(rounds)]

    def apply_adjoint(values):
        summed = local_adjoint(values)
        for level in range(rounds):
            slices = jnp.take(values, recv_rows[level], axis=1)
            incoming = from_partner(slices, "dom", level)
            contrib = jnp.einsum(
                "hab,fha->fhb", copies[level], incoming, preferred_element_type=jnp.float32
            )
            summed = summed.at[:, send_rows[level]].add(contrib)
        return summed

    zeroth = features.reshape(channels, block_count, block_size) * mask_half
    first = (apply_forward(zeroth) * mask_full).astype(jnp.bfloat16)
    second = ((2.0 * apply_forward(first) - zeroth.astype(jnp.float32)) * mask_full).astype(
        jnp.bfloat16
    )
    third = ((2.0 * apply_forward(second) - first.astype(jnp.float32)) * mask_full).astype(
        jnp.bfloat16
    )
    orders = jnp.stack([zeroth, first, second, third])
    output = (
        jnp.einsum("kfg,kfib->gib", cheb_weight, orders, preferred_element_type=jnp.float32)
        * mask_full
    )
    conv_out = output.astype(jnp.bfloat16).reshape(channels, block_count * block_size)
    upstream = cotangent.reshape(channels, block_count, block_size) * mask_half
    weight_terms = jnp.einsum("kfib,gib->kfg", orders, upstream, preferred_element_type=jnp.float32)
    grad_w = lax.psum(weight_terms, "dom")
    lifted = jnp.einsum("kfg,gib->kfib", cheb_weight, upstream, preferred_element_type=jnp.float32)
    back_third = (lifted[3] * mask_full).astype(jnp.bfloat16)
    adjoint_two = lifted[2] + 2.0 * apply_adjoint(back_third)
    back_second = (adjoint_two * mask_full).astype(jnp.bfloat16)
    adjoint_one = lifted[1] + 2.0 * apply_adjoint(back_second) - back_third.astype(jnp.float32)
    back_first = (adjoint_one * mask_full).astype(jnp.bfloat16)
    adjoint_zero = lifted[0] + apply_adjoint(back_first) - back_second.astype(jnp.float32)
    grad_x = (
        (adjoint_zero * mask_full).astype(jnp.bfloat16).reshape(channels, block_count * block_size)
    )
    return (conv_out, grad_x, grad_w)


def solution(mesh):
    in_specs = (
        P(None, "dom"),
        P(),
        P("dom", None, None, None),
        P("dom", None),
        P("dom", None, None, None, None),
        P("dom", None, None),
        P("dom", None, None),
        P("dom", None),
        P("dom"),
        P(None, "dom"),
    )
    out_specs = (P(None, "dom"), P(None, "dom"), P())
    return jax.shard_map(local, mesh=mesh, in_specs=in_specs, out_specs=out_specs, check_vma=False)
```

profile of v0, /device:TPU:0, one launch (start us, length us, event | category | flops | bytes accessed | tf_op | source)
XLA Modules:
  0.0 540.2 jit_solution(13784177287233342524)
XLA Ops:
  10.1 2.1 convolution_bitcast_fusion
  12.2 3.2 copy-done.3
  20.1 3.0 collective-permute-start.17
  57.3 3.2 slice_bitcast_fusion.3
  62.1 6.7 %fusion.42 = f32[64,64,3,128]{3,1,2,0:T(8,128)} fusion(bf16[64,3,128,128]{3,2,1,0:T(8,128)(2,1)} %param.16, bf16[64,64,128]{2,0,1:T(8,128)(2,1)S(1)} %fusion.13), kind=kOutput, calls=%fused_computation.133 | convolution fusion | flops 402653184 | bytes 13631488 | tf_op jit(solution)/shard_map/inab,fia->finb/dot_general | solution.py:56
  73.0 2.7 gather_fusion
  86.8 2.6 copy_multiply_fusion
  91.5 7.0 %fusion.22 = f32[64,64,128]{2,0,1:T(8,128)} fusion(bf16[64,3,128,128]{3,2,1,0:T(8,128)(2,1)} %param.16, bf16[64,3,64,128]{3,2,1,0:T(8,128)(2,1)S(1)} %bitcast.374, pred[64,3]{1,0:T(8,128)(4,1)S(1)} %copy.20), kind=kOutput, calls=%fused_computation.99 | convolution fusion | flops 404226048 | bytes 11534528 | tf_op jit(solution)/shard_map/inab,finb->fia/dot_general | solution.py:43
  102.2 20.1 %scatter_fusion.15 = f32[64,64,128]{2,0,1:T(8,128)S(1)} fusion(f32[64,64,128]{2,0,1:T(8,128)S(1)} %broadcast.220.clone, s32[192]{0:T(256)S(1)} %reshape.935, f32[192,64,128]{2,1,0:T(8,128)} %bitcast.367), kind=kCustom, calls=%fused_computation.48 | custom fusion | flops 1572864 | bytes 18875136 | tf_op jit(solution)/shard_map/scatter-add | solution.py:58
  124.4 2.2 convolution_multiply_fusion.14
  134.9 2.9 collective-permute-start.4
  143.2 2.2 scatter_fusion
  145.4 2.2 scatter_fusion.1
  147.6 2.2 scatter_fusion.2
  149.8 2.2 scatter_fusion.3
  152.0 2.2 scatter_fusion.4
  157.9 2.9 collective-permute-start.23
  177.7 6.7 %fusion.40 = f32[64,64,3,128]{3,1,2,0:T(8,128)} fusion(bf16[64,3,128,128]{3,2,1,0:T(8,128)(2,1)} %param.16, bf16[64,64,128]{2,0,1:T(8,128)(2,1)S(1)} %fusion.16), kind=kOutput, calls=%fused_computation.131 | convolution fusion | flops 402653184 | bytes 13631488 | tf_op jit(solution)/shard_map/inab,fia->finb/dot_general | solution.py:56
  202.4 2.9 collective-permute-start.29
  205.5 19.9 %scatter_fusion.21 = f32[64,64,128]{2,0,1:T(8,128)S(1)} fusion(f32[64,64,128]{2,0,1:T(8,128)S(1)} %broadcast.220, s32[192]{0:T(256)S(1)} %reshape.935, f32[192,64,128]{2,1,0:T(8,128)} %bitcast.368), kind=kCustom, calls=%fused_computation.54 | custom fusion | flops 1572864 | bytes 18875136 | tf_op jit(solution)/shard_map/scatter-add | solution.py:58
  233.4 2.2 scatter_fusion.22
  235.6 2.2 scatter_fusion.23
  237.8 2.2 scatter_fusion.24
  240.0 2.2 scatter_fusion.25
  243.8 2.2 scatter_fusion.26
  246.0 5.7 %fusion.20 = (bf16[64,64,128]{2,0,1:T(8,128)(2,1)S(1)}, bf16[64,64,128]{2,0,1:T(8,128)(2,1)}) fusion(f32[4,64,64,128]{3,1,2,0:T(8,128)} %copy-done.3, f32[64,64,128]{2,0,1:T(8,128)} %scatter_fusion.26, f32[64]{0:T(128)} %copy-done.32, f32[64,64,128]{2,0,1:T(8,128)} %scatter_fusion.4), kind=kLoop, calls=%fused_computation.91 | loop fusion | flops 5242880 | bytes 10486016 | tf_op jit(solution)/shard_map/convert_element_type | solution.py:97
  252.7 3.9 fusion.38
  266.2 4.0 gather_fusion.6
  270.1 2.5 gather_fusion.7
  272.6 2.5 gather_fusion.8
  275.1 2.5 gather_fusion.9
  277.6 2.5 gather_fusion.10
  280.1 2.5 gather_fusion.11
  287.3 8.1 %fusion.25 = f32[64,64,128]{2,0,1:T(8,128)} fusion(bf16[64,3,128,128]{3,2,1,0:T(8,128)(2,1)} %param.16, bf16[64,3,64,128]{3,2,1,0:T(8,128)(2,1)} %bitcast.373, pred[64,3]{1,0:T(8,128)(4,1)S(1)} %copy.20), kind=kOutput, calls=%fused_computation.100 | convolution fusion | flops 404226048 | bytes 11534528 | tf_op jit(solution)/shard_map/inab,finb->fia/dot_general | solution.py:43
  298.8 19.9 %scatter_fusion.27 = f32[64,64,128]{2,0,1:T(8,128)S(1)} fusion(f32[64,64,128]{2,0,1:T(8,128)S(1)} %copy-done.1, s32[192]{0:T(256)S(1)} %reshape.935, f32[192,64,128]{2,1,0:T(8,128)} %bitcast.366), kind=kCustom, calls=%fused_computation.60 | custom fusion | flops 1572864 | bytes 18875136 | tf_op jit(solution)/shard_map/scatter-add | solution.py:58
  329.6 2.9 collective-permute-start.9
  346.6 2.2 scatter_fusion.5
  348.8 2.2 scatter_fusion.6
  351.0 2.2 scatter_fusion.7
  353.2 2.2 scatter_fusion.8
  356.9 2.1 scatter_fusion.9
  359.0 4.2 fusion.36
  363.2 4.0 gather_fusion.12
  372.0 8.1 %fusion.28 = f32[64,64,128]{2,0,1:T(8,128)} fusion(bf16[64,3,128,128]{3,2,1,0:T(8,128)(2,1)} %param.16, bf16[64,3,64,128]{3,2,1,0:T(8,128)(2,1)} %bitcast.375, pred[64,3]{1,0:T(8,128)(4,1)S(1)} %copy.20), kind=kOutput, calls=%fused_computation.101 | convolution fusion | flops 404226048 | bytes 11534528 | tf_op jit(solution)/shard_map/inab,finb->fia/dot_general | solution.py:43
  392.4 2.2 scatter_fusion.12
  394.6 2.2 scatter_fusion.13
  405.3 2.6 fusion.34
  409.1 122.7 %all-reduce.2.cloned.1.call-done = f32[4,64,64]{2,1,0:T(8,128)} async-done(((f32[4,64,64]{2,1,0:T(8,128)}), f32[4,64,64]{2,1,0:T(8,128)}) %all-reduce.2.cloned.1.call-update) | async-done | bytes 65552 | tf_op jit(solution)/shard_map/psum | solution.py:91
  (400 shorter events, 200.6 us)
Async XLA Ops:
  7.2 524.7 %all-reduce.2.cloned.1.call-start = ((), (), s32[]{:S(2)}) async-start(), calls=%async_computation | async-start | bytes 262144 | tf_op jit(solution)/shard_map/psum | solution.py:91
  15.7 21.3 %copy-start.37 = (s32[64,3]{0,1:T(4,128)S(1)}, s32[64,3]{0,1:T(4,128)}, u32[]{:S(2)}) copy-start(s32[64,3]{0,1:T(4,128)} %param.17) | copy-start | bytes 2308
  17.0 137.2 %collective-permute-start.15 = (bf16[64,2,128]{2,0,1:T(8,128)(2,1)}, bf16[64,2,128]{2,0,1:T(8,128)(2,1)}, u32[]{:S(2)}, u32[]{:S(2)}) collective-permute-start(bf16[64,2,128]{2,0,1:T(8,128)(2,1)} %select_bitcast_fusion.14), channel_id=1, source_target_pairs={{0,1},{1,0},{2,3},{3,2},{4,5},{5,4},{6,7},{7,6},{8,9},{9,8},{10,11... | collective-permute-start | bytes 98312 | tf_op jit(solution)/shard_map/ppermute | solution.py:14
  18.8 135.5 %collective-permute-start.16 = (bf16[2,128,128]{2,1,0:T(8,128)(2,1)}, bf16[2,128,128]{2,1,0:T(8,128)(2,1)S(1)}, u32[]{:S(2)}, u32[]{:S(2)}) collective-permute-start(bf16[2,128,128]{2,1,0:T(8,128)(2,1)} %get-tuple-element.19), channel_id=1, source_target_pairs={{0,1},{1,0},{2,3},{3,2},{4,5},{5,4},{6,7},{7,6},{8,9},{9,8},{10,11... | collective-permute-start | bytes 196616 | tf_op jit(solution)/shard_map/ppermute | solution.py:14
  20.1 137.6 %collective-permute-start.17 = (bf16[64,2,128]{2,0,1:T(8,128)(2,1)}, bf16[64,2,128]{2,0,1:T(8,128)(2,1)}, u32[]{:S(2)}, u32[]{:S(2)}) collective-permute-start(bf16[64,2,128]{2,0,1:T(8,128)(2,1)} %select_bitcast_fusion.13), channel_id=1, source_target_pairs={{0,2},{2,0},{1,3},{3,1},{4,6},{6,4},{5,7},{7,5},{8,10},{10,8},{9,1... | collective-permute-start | bytes 98312 | tf_op jit(solution)/shard_map/ppermute | solution.py:14
  23.1 134.8 %collective-permute-start.18 = (bf16[2,128,128]{2,1,0:T(8,128)(2,1)}, bf16[2,128,128]{2,1,0:T(8,128)(2,1)}, u32[]{:S(2)}, u32[]{:S(2)}) collective-permute-start(bf16[2,128,128]{2,1,0:T(8,128)(2,1)} %get-tuple-element.18), channel_id=1, source_target_pairs={{0,2},{2,0},{1,3},{3,1},{4,6},{6,4},{5,7},{7,5},{8,10},{10,8},{9,1... | collective-permute-start | bytes 196616 | tf_op jit(solution)/shard_map/ppermute | solution.py:14
  24.5 36.0 %copy-start.47 = (pred[2]{0:T(512)(128)(4,1)}, pred[2]{0:T(512)(128)(4,1)S(1)}, u32[]{:S(2)}) copy-start(pred[2]{0:T(512)(128)(4,1)S(1)} %compare_and_fusion.9) | copy-start | bytes 10
  28.6 93.7 %collective-permute-start = (bf16[64,2,128]{2,0,1:T(8,128)(2,1)}, bf16[64,2,128]{2,0,1:T(8,128)(2,1)}, u32[]{:S(2)}, u32[]{:S(2)}) collective-permute-start(bf16[64,2,128]{2,0,1:T(8,128)(2,1)} %select_bitcast_fusion.29), channel_id=1, source_target_pairs={{0,1},{1,0},{2,3},{3,2},{4,5},{5,4},{6,7},{7,6},{8,9},{9,8},{10,11... | collective-permute-start | bytes 98312 | tf_op jit(solution)/shard_map/ppermute | solution.py:14
  122.3 4.3 collective-permute-start.1
  126.7 4.1 collective-permute-start.2
  130.8 4.1 collective-permute-start.3
  134.9 5.0 collective-permute-start.4
  139.9 22.5 %collective-permute-start.19 = (bf16[64,2,128]{2,0,1:T(8,128)(2,1)}, bf16[64,2,128]{2,0,1:T(8,128)(2,1)}, u32[]{:S(2)}, u32[]{:S(2)}) collective-permute-start(bf16[64,2,128]{2,0,1:T(8,128)(2,1)} %select_bitcast_fusion.12), channel_id=1, source_target_pairs={{0,4},{4,0},{1,5},{5,1},{2,6},{6,2},{3,7},{7,3},{8,12},{12,8},{9,1... | collective-permute-start | bytes 98312 | tf_op jit(solution)/shard_map/ppermute | solution.py:14
  154.2 8.3 %collective-permute-start.20 = (bf16[2,128,128]{2,1,0:T(8,128)(2,1)}, bf16[2,128,128]{2,1,0:T(8,128)(2,1)S(1)}, u32[]{:S(2)}, u32[]{:S(2)}) collective-permute-start(bf16[2,128,128]{2,1,0:T(8,128)(2,1)} %get-tuple-element.17), channel_id=1, source_target_pairs={{0,4},{4,0},{1,5},{5,1},{2,6},{6,2},{3,7},{7,3},{8,12},{12,8},{9,1... | collective-permute-start | bytes 196616 | tf_op jit(solution)/shard_map/ppermute | solution.py:14
  154.3 9.7 %collective-permute-start.21 = (bf16[64,2,128]{2,0,1:T(8,128)(2,1)}, bf16[64,2,128]{2,0,1:T(8,128)(2,1)S(1)}, u32[]{:S(2)}, u32[]{:S(2)}) collective-permute-start(bf16[64,2,128]{2,0,1:T(8,128)(2,1)} %select_bitcast_fusion.11), channel_id=1, source_target_pairs={{0,8},{8,0},{1,9},{9,1},{2,10},{10,2},{3,11},{11,3},{4,12},{12,4},... | collective-permute-start | bytes 98312 | tf_op jit(solution)/shard_map/ppermute | solution.py:14
  157.8 6.2 %collective-permute-start.22 = (bf16[2,128,128]{2,1,0:T(8,128)(2,1)}, bf16[2,128,128]{2,1,0:T(8,128)(2,1)S(1)}, u32[]{:S(2)}, u32[]{:S(2)}) collective-permute-start(bf16[2,128,128]{2,1,0:T(8,128)(2,1)} %get-tuple-element.16), channel_id=1, source_target_pairs={{0,8},{8,0},{1,9},{9,1},{2,10},{10,2},{3,11},{11,3},{4,12},{12,4},... | collective-permute-start | bytes 196616 | tf_op jit(solution)/shard_map/ppermute | solution.py:14
  157.9 13.8 %collective-permute-start.23 = (bf16[64,2,128]{2,0,1:T(8,128)(2,1)}, bf16[64,2,128]{2,0,1:T(8,128)(2,1)}, u32[]{:S(2)}, u32[]{:S(2)}) collective-permute-start(bf16[64,2,128]{2,0,1:T(8,128)(2,1)} %select_bitcast_fusion.10), channel_id=1, source_target_pairs={{0,16},{16,0},{1,17},{17,1},{2,18},{18,2},{3,19},{19,3},{4,20},{20... | collective-permute-start | bytes 98312 | tf_op jit(solution)/shard_map/ppermute | solution.py:14
  162.4 9.2 %collective-permute-start.24 = (bf16[2,128,128]{2,1,0:T(8,128)(2,1)}, bf16[2,128,128]{2,1,0:T(8,128)(2,1)}, u32[]{:S(2)}, u32[]{:S(2)}) collective-permute-start(bf16[2,128,128]{2,1,0:T(8,128)(2,1)} %get-tuple-element.15), channel_id=1, source_target_pairs={{0,16},{16,0},{1,17},{17,1},{2,18},{18,2},{3,19},{19,3},{4,20},{20... | collective-permute-start | bytes 196616 | tf_op jit(solution)/shard_map/ppermute | solution.py:14
  177.7 19.6 %copy-start.75 = (pred[2]{0:T(512)(128)(4,1)S(1)}, pred[2]{0:T(512)(128)(4,1)}, u32[]{:S(2)}) copy-start(pred[2]{0:T(512)(128)(4,1)} %compare_and_fusion.2) | copy-start | bytes 10
  177.7 21.7 %copy-start.72 = (pred[2]{0:T(512)(128)(4,1)S(1)}, pred[2]{0:T(512)(128)(4,1)}, u32[]{:S(2)}) copy-start(pred[2]{0:T(512)(128)(4,1)} %compare_and_fusion.1) | copy-start | bytes 10
  177.7 24.0 %copy-start.69 = (pred[2]{0:T(512)(128)(4,1)S(1)}, pred[2]{0:T(512)(128)(4,1)}, u32[]{:S(2)}) copy-start(pred[2]{0:T(512)(128)(4,1)} %compare_and_fusion) | copy-start | bytes 10
  194.7 32.2 %collective-permute-start.25 = (bf16[64,2,128]{2,0,1:T(8,128)(2,1)}, bf16[64,2,128]{2,0,1:T(8,128)(2,1)}, u32[]{:S(2)}, u32[]{:S(2)}) collective-permute-start(bf16[64,2,128]{2,0,1:T(8,128)(2,1)} %select_bitcast_fusion.9), channel_id=1, source_target_pairs={{0,1},{1,0},{2,3},{3,2},{4,5},{5,4},{6,7},{7,6},{8,9},{9,8},{10,11... | collective-permute-start | bytes 98312 | tf_op jit(solution)/shard_map/ppermute | solution.py:14
  195.4 33.2 %collective-permute-start.26 = (bf16[64,2,128]{2,0,1:T(8,128)(2,1)}, bf16[64,2,128]{2,0,1:T(8,128)(2,1)}, u32[]{:S(2)}, u32[]{:S(2)}) collective-permute-start(bf16[64,2,128]{2,0,1:T(8,128)(2,1)} %select_bitcast_fusion.8), channel_id=1, source_target_pairs={{0,2},{2,0},{1,3},{3,1},{4,6},{6,4},{5,7},{7,5},{8,10},{10,8},{9,1... | collective-permute-start | bytes 98312 | tf_op jit(solution)/shard_map/ppermute | solution.py:14
  197.9 32.2 %collective-permute-start.27 = (bf16[64,2,128]{2,0,1:T(8,128)(2,1)}, bf16[64,2,128]{2,0,1:T(8,128)(2,1)}, u32[]{:S(2)}, u32[]{:S(2)}) collective-permute-start(bf16[64,2,128]{2,0,1:T(8,128)(2,1)} %select_bitcast_fusion.7), channel_id=1, source_target_pairs={{0,4},{4,0},{1,5},{5,1},{2,6},{6,2},{3,7},{7,3},{8,12},{12,8},{9,1... | collective-permute-start | bytes 98312 | tf_op jit(solution)/shard_map/ppermute | solution.py:14
  200.1 31.7 %collective-permute-start.28 = (bf16[64,2,128]{2,0,1:T(8,128)(2,1)}, bf16[64,2,128]{2,0,1:T(8,128)(2,1)}, u32[]{:S(2)}, u32[]{:S(2)}) collective-permute-start(bf16[64,2,128]{2,0,1:T(8,128)(2,1)} %select_bitcast_fusion.6), channel_id=1, source_target_pairs={{0,8},{8,0},{1,9},{9,1},{2,10},{10,2},{3,11},{11,3},{4,12},{12,4},... | collective-permute-start | bytes 98312 | tf_op jit(solution)/shard_map/ppermute | solution.py:14
  202.4 39.8 %collective-permute-start.29 = (bf16[64,2,128]{2,0,1:T(8,128)(2,1)}, bf16[64,2,128]{2,0,1:T(8,128)(2,1)}, u32[]{:S(2)}, u32[]{:S(2)}) collective-permute-start(bf16[64,2,128]{2,0,1:T(8,128)(2,1)} %select_bitcast_fusion.5), channel_id=1, source_target_pairs={{0,16},{16,0},{1,17},{17,1},{2,18},{18,2},{3,19},{19,3},{4,20},{20... | collective-permute-start | bytes 98312 | tf_op jit(solution)/shard_map/ppermute | solution.py:14
  226.9 25.8 %slice-start = ((s8[6291456]{0:T(1024)(128)(4,1)}), s8[2097152]{0:T(1024)(128)(4,1)S(1)}, s32[]{:S(2)}) async-start(s8[6291456]{0:T(1024)(128)(4,1)} %bitcast.364), calls=%async_computation.1 | async-start | bytes 4194304
  266.1 18.3 %copy-start.76 = (pred[2]{0:T(512)(128)(4,1)S(1)}, pred[2]{0:T(512)(128)(4,1)}, u32[]{:S(2)}) copy-start(pred[2]{0:T(512)(128)(4,1)} %compare_and_fusion.2) | copy-start | bytes 10
  266.1 19.5 %copy-start.73 = (pred[2]{0:T(512)(128)(4,1)S(1)}, pred[2]{0:T(512)(128)(4,1)}, u32[]{:S(2)}) copy-start(pred[2]{0:T(512)(128)(4,1)} %compare_and_fusion.1) | copy-start | bytes 10
  266.2 20.4 %copy-start.70 = (pred[2]{0:T(512)(128)(4,1)S(1)}, pred[2]{0:T(512)(128)(4,1)}, u32[]{:S(2)}) copy-start(pred[2]{0:T(512)(128)(4,1)} %compare_and_fusion) | copy-start | bytes 10
  283.3 35.4 %collective-permute-start.30 = (bf16[64,2,128]{2,0,1:T(8,128)(2,1)}, bf16[64,2,128]{2,0,1:T(8,128)(2,1)}, u32[]{:S(2)}, u32[]{:S(2)}) collective-permute-start(bf16[64,2,128]{2,0,1:T(8,128)(2,1)} %select_bitcast_fusion.4), channel_id=1, source_target_pairs={{0,1},{1,0},{2,3},{3,2},{4,5},{5,4},{6,7},{7,6},{8,9},{9,8},{10,11... | collective-permute-start | bytes 98312 | tf_op jit(solution)/shard_map/ppermute | solution.py:14
  284.0 36.4 %collective-permute-start.31 = (bf16[64,2,128]{2,0,1:T(8,128)(2,1)}, bf16[64,2,128]{2,0,1:T(8,128)(2,1)}, u32[]{:S(2)}, u32[]{:S(2)}) collective-permute-start(bf16[64,2,128]{2,0,1:T(8,128)(2,1)} %select_bitcast_fusion.3), channel_id=1, source_target_pairs={{0,2},{2,0},{1,3},{3,1},{4,6},{6,4},{5,7},{7,5},{8,10},{10,8},{9,1... | collective-permute-start | bytes 98312 | tf_op jit(solution)/shard_map/ppermute | solution.py:14
  285.1 38.1 %collective-permute-start.32 = (bf16[64,2,128]{2,0,1:T(8,128)(2,1)}, bf16[64,2,128]{2,0,1:T(8,128)(2,1)}, u32[]{:S(2)}, u32[]{:S(2)}) collective-permute-start(bf16[64,2,128]{2,0,1:T(8,128)(2,1)} %select_bitcast_fusion.2), channel_id=1, source_target_pairs={{0,4},{4,0},{1,5},{5,1},{2,6},{6,2},{3,7},{7,3},{8,12},{12,8},{9,1... | collective-permute-start | bytes 98312 | tf_op jit(solution)/shard_map/ppermute | solution.py:14
  286.3 40.1 %collective-permute-start.33 = (bf16[64,2,128]{2,0,1:T(8,128)(2,1)}, bf16[64,2,128]{2,0,1:T(8,128)(2,1)}, u32[]{:S(2)}, u32[]{:S(2)}) collective-permute-start(bf16[64,2,128]{2,0,1:T(8,128)(2,1)} %select_bitcast_fusion.1), channel_id=1, source_target_pairs={{0,8},{8,0},{1,9},{9,1},{2,10},{10,2},{3,11},{11,3},{4,12},{12,4},... | collective-permute-start | bytes 98312 | tf_op jit(solution)/shard_map/ppermute | solution.py:14
  287.2 42.4 %collective-permute-start.34 = (bf16[64,2,128]{2,0,1:T(8,128)(2,1)}, bf16[64,2,128]{2,0,1:T(8,128)(2,1)}, u32[]{:S(2)}, u32[]{:S(2)}) collective-permute-start(bf16[64,2,128]{2,0,1:T(8,128)(2,1)} %select_bitcast_fusion), channel_id=1, source_target_pairs={{0,16},{16,0},{1,17},{17,1},{2,18},{18,2},{3,19},{19,3},{4,20},{20... | collective-permute-start | bytes 98312 | tf_op jit(solution)/shard_map/ppermute | solution.py:14
  318.8 40.3 %copy-start.33 = (f32[64]{0:T(128)S(1)}, f32[64]{0:T(128)}, u32[]{:S(2)}) copy-start(f32[64]{0:T(128)} %copy-done.32) | copy-start | bytes 772
  318.8 15.4 %collective-permute-start.5 = (bf16[64,2,128]{2,0,1:T(8,128)(2,1)}, bf16[64,2,128]{2,0,1:T(8,128)(2,1)S(1)}, u32[]{:S(2)}, u32[]{:S(2)}) collective-permute-start(bf16[64,2,128]{2,0,1:T(8,128)(2,1)} %select_bitcast_fusion.24), channel_id=1, source_target_pairs={{0,1},{1,0},{2,3},{3,2},{4,5},{5,4},{6,7},{7,6},{8,9},{9,8},{10,11... | collective-permute-start | bytes 98312 | tf_op jit(solution)/shard_map/ppermute | solution.py:14
  320.4 15.2 %collective-permute-start.6 = (bf16[64,2,128]{2,0,1:T(8,128)(2,1)}, bf16[64,2,128]{2,0,1:T(8,128)(2,1)S(1)}, u32[]{:S(2)}, u32[]{:S(2)}) collective-permute-start(bf16[64,2,128]{2,0,1:T(8,128)(2,1)} %select_bitcast_fusion.23), channel_id=1, source_target_pairs={{0,2},{2,0},{1,3},{3,1},{4,6},{6,4},{5,7},{7,5},{8,10},{10,8},{9,1... | collective-permute-start | bytes 98312 | tf_op jit(solution)/shard_map/ppermute | solution.py:14
  323.3 13.7 %collective-permute-start.7 = (bf16[64,2,128]{2,0,1:T(8,128)(2,1)}, bf16[64,2,128]{2,0,1:T(8,128)(2,1)S(1)}, u32[]{:S(2)}, u32[]{:S(2)}) collective-permute-start(bf16[64,2,128]{2,0,1:T(8,128)(2,1)} %select_bitcast_fusion.22), channel_id=1, source_target_pairs={{0,4},{4,0},{1,5},{5,1},{2,6},{6,2},{3,7},{7,3},{8,12},{12,8},{9,1... | collective-permute-start | bytes 98312 | tf_op jit(solution)/shard_map/ppermute | solution.py:14
  326.4 11.9 %collective-permute-start.8 = (bf16[64,2,128]{2,0,1:T(8,128)(2,1)}, bf16[64,2,128]{2,0,1:T(8,128)(2,1)S(1)}, u32[]{:S(2)}, u32[]{:S(2)}) collective-permute-start(bf16[64,2,128]{2,0,1:T(8,128)(2,1)} %select_bitcast_fusion.21), channel_id=1, source_target_pairs={{0,8},{8,0},{1,9},{9,1},{2,10},{10,2},{3,11},{11,3},{4,12},{12,4},... | collective-permute-start | bytes 98312 | tf_op jit(solution)/shard_map/ppermute | solution.py:14
  329.6 25.8 %collective-permute-start.9 = (bf16[64,2,128]{2,0,1:T(8,128)(2,1)}, bf16[64,2,128]{2,0,1:T(8,128)(2,1)}, u32[]{:S(2)}, u32[]{:S(2)}) collective-permute-start(bf16[64,2,128]{2,0,1:T(8,128)(2,1)} %select_bitcast_fusion.20), channel_id=1, source_target_pairs={{0,16},{16,0},{1,17},{17,1},{2,18},{18,2},{3,19},{19,3},{4,20},{20... | collective-permute-start | bytes 98312 | tf_op jit(solution)/shard_map/ppermute | solution.py:14
  380.0 18.3 %copy-start.44 = (s32[2]{0:T(128)S(1)}, s32[2]{0:T(128)}, u32[]{:S(2)}) copy-start(s32[2]{0:T(128)} %fusion.84) | copy-start | bytes 28
  380.1 20.2 %copy-start.4 = (bf16[64,64,128]{2,0,1:T(8,128)(2,1)S(1)}, bf16[64,64,128]{2,0,1:T(8,128)(2,1)}, u32[]{:S(2)}) copy-start(bf16[64,64,128]{2,0,1:T(8,128)(2,1)} %get-tuple-element.23) | copy-start | bytes 3145732
  380.1 3.3 collective-permute-start.10
  380.3 4.0 collective-permute-start.11
  380.8 4.9 collective-permute-start.12
  381.4 5.7 %collective-permute-start.13 = (bf16[64,2,128]{2,0,1:T(8,128)(2,1)S(1)}, bf16[64,2,128]{2,0,1:T(8,128)(2,1)S(1)}, u32[]{:S(2)}, u32[]{:S(2)}) collective-permute-start(bf16[64,2,128]{2,0,1:T(8,128)(2,1)S(1)} %select_bitcast_fusion.16), channel_id=1, source_target_pairs={{0,8},{8,0},{1,9},{9,1},{2,10},{10,2},{3,11},{11,3},{4,12},{12,4},... | collective-permute-start | bytes 98312 | tf_op jit(solution)/shard_map/ppermute | solution.py:14
  382.3 14.5 %collective-permute-start.14 = (bf16[64,2,128]{2,0,1:T(8,128)(2,1)}, bf16[64,2,128]{2,0,1:T(8,128)(2,1)}, u32[]{:S(2)}, u32[]{:S(2)}) collective-permute-start(bf16[64,2,128]{2,0,1:T(8,128)(2,1)} %select_bitcast_fusion.15), channel_id=1, source_target_pairs={{0,16},{16,0},{1,17},{17,1},{2,18},{18,2},{3,19},{19,3},{4,20},{20... | collective-permute-start | bytes 98312 | tf_op jit(solution)/shard_map/ppermute | solution.py:14
  (73 other events, 498.6 us)
Sparse Core Ops, SparseCore 0:
  405.4 126.3 all-reduce.1
where the time goes:
time: 546 us; the launch traced here: 540 us
  other arithmetic  190 us (35%)
  waiting for transfers between devices  125 us (23%)
  matrix products  91 us (17%)
  local copies, waits for them, and re-layouts  80.2 us (15%)
  starting transfers between devices  37.6 us (7%)
  between operations  15.7 us (3%)
    psum x1, waiting for transfers between devices, local(): grad_w = lax.psum(weight_terms, 'dom')  123 us
    scatter-add x3, other arithmetic, local_adjoint(): jnp.zeros((channels, block_count, block_size), jnp.float32).at[:, col_index]  60 us
    ppermute x35, starting transfers between devices, from_partner(): return lax.ppermute(block, axis, route)  37.5 us
    scatter-add x15, other arithmetic, apply_forward(): summed = summed.at[:, recv_rows[level]].add(switch[level] * product)  32.2 us
    scatter-add x15, other arithmetic, apply_adjoint(): summed = summed.at[:, send_rows[level]].add(contrib)  25.6 us
    gather x15, local copies, waits for them, and re-layouts, apply_adjoint(): slices = jnp.take(values, recv_rows[level], axis=1)  23.7 us
    gather x15, local copies, waits for them, and re-layouts, apply_forward(): outgoing = jnp.take(values, send_rows[level], axis=1)  23.4 us
    dot_general x3, matrix products, apply_forward(): jnp.einsum('inab,finb->fia', lap_tiles, gathered, preferred_element_type=...  23.2 us
  transfers between devices with their start and end apart: 36, of which 5 were waited for; matrix products, arithmetic and copies ran while one was open for 46% of the time, Pallas kernels for 0%

commit v1 on v0

v1 whole, which is shorter than its diff:
```python
import functools

import jax
import jax.numpy as jnp
from jax import lax
from jax.experimental import pallas as pl
from jax.experimental.pallas import tpu as pltpu
from jax.sharding import PartitionSpec as P

F32 = jnp.float32
BF16 = jnp.bfloat16
SUB = 8
LANES = 128
UNROLL = 4

VMEM = pl.BlockSpec(memory_space=pltpu.VMEM)
SMEM = pl.BlockSpec(memory_space=pltpu.SMEM)
ANY = pl.BlockSpec(memory_space=pl.ANY)


def shape(dims, dtype):
    return jax.ShapeDtypeStruct(dims, dtype)


def nt(a, b):
    return lax.dot_general(a, b, (((1,), (1,)), ((), ())), preferred_element_type=F32)


def nn(a, b):
    return lax.dot_general(a, b, (((1,), (0,)), ((), ())), preferred_element_type=F32)


class Sizes:
    def __init__(self, features, lap_tiles, cross_tiles):
        self.chan = features.shape[0]
        self.blocks, self.nz, self.blk = lap_tiles.shape[:3]
        self.rounds, self.hb = cross_tiles.shape[1:3]
        self.pairs = self.rounds * self.hb
        self.rows = 0
        self.sends = self.pairs
        self.first_row = 2 * self.pairs
        self.first_send = 3 * self.pairs
        self.flags = 4 * self.pairs
        self.live = self.flags + self.rounds
        self.meta = self.live + 1
        self.half = self.hb * self.chan

    def couplings(self):
        return [(r, h, r * self.hb + h) for r in range(self.rounds) for h in range(self.hb)]


def call(kernel, in_specs, out_specs, out_shape, scratch, flops, moved, limit, name):
    return pl.pallas_call(
        kernel,
        in_specs=in_specs,
        out_specs=out_specs,
        out_shape=out_shape,
        scratch_shapes=scratch,
        compiler_params=pltpu.CompilerParams(vmem_limit_bytes=limit << 20),
        cost_estimate=pl.CostEstimate(flops=flops, bytes_accessed=moved, transcendentals=0),
        name=name,
    )


def pack_kernel(sz, *refs):
    x4, u4, cross, send, row, pair, live = refs[:7]
    xb, ub, meta = refs[7:10]
    pays = refs[10 : 10 + sz.rounds]
    sem_x, sem_u, sem_t = refs[10 + sz.rounds :]
    copies = []
    for t in range(sz.chan // SUB):
        rows = pl.ds(t * SUB, SUB)
        copies.append(pltpu.make_async_copy(x4.at[t], xb.at[:, rows, :], sem_x.at[t]))
        copies.append(pltpu.make_async_copy(u4.at[t], ub.at[:, rows, :], sem_u.at[t]))
    tiles = []
    for r, h, j in sz.couplings():
        spot = pays[r].at[pl.ds(2 * sz.half + h * sz.blk, sz.blk), :]
        tiles.append(pltpu.make_async_copy(cross.at[0, r, h], spot, sem_t.at[j]))
    for copy in copies + tiles:
        copy.start()
    count = live[0]
    rows = [lax.rem(row[0, r, h], count) for r, h, _ in sz.couplings()]
    sends = [lax.rem(send[0, r, h], count) for r, h, _ in sz.couplings()]
    for values, spot, first in (
        (rows, sz.rows, sz.first_row),
        (sends, sz.sends, sz.first_send),
    ):
        for j, value in enumerate(values):
            earliest = jnp.int32(j)
            for q in reversed(range(j)):
                earliest = jnp.where(values[q] == value, q, earliest)
            meta[spot + j] = value
            meta[first + j] = earliest
    for r in range(sz.rounds):
        meta[sz.flags + r] = pair[0, r]
    meta[sz.live] = count
    for copy in copies:
        copy.wait()

    def clear(i, carry):
        xb[i] = jnp.zeros(xb.shape[1:], BF16)
        ub[i] = jnp.zeros(ub.shape[1:], BF16)
        return carry

    lax.fori_loop(count, sz.blocks, clear, 0)
    for r, h, j in sz.couplings():
        pays[r][pl.ds(h * sz.chan, sz.chan), :] = xb[sends[j]]
        pays[r][pl.ds(sz.half + h * sz.chan, sz.chan), :] = ub[rows[j]]
    for r, h, j in sz.couplings():
        tiles[j].wait()

        @pl.when(pair[0, r] == 0)
        def _():
            spot = pl.ds(2 * sz.half + h * sz.blk, sz.blk)
            pays[r][spot, :] = jnp.zeros((sz.blk, sz.blk), BF16)


def pack(sz, x4, u4, cross, send, row, pair, live):
    field = shape((sz.blocks, sz.chan, sz.blk), BF16)
    pay = shape((2 * sz.half + sz.hb * sz.blk, sz.blk), BF16)
    outs = [field, field, shape((sz.meta,), jnp.int32)] + [pay] * sz.rounds
    groups = sz.chan // SUB
    return call(
        functools.partial(pack_kernel, sz),
        [ANY, ANY, ANY, SMEM, SMEM, SMEM, SMEM],
        [VMEM, VMEM, SMEM] + [VMEM] * sz.rounds,
        outs,
        [
            pltpu.SemaphoreType.DMA((groups,)),
            pltpu.SemaphoreType.DMA((groups,)),
            pltpu.SemaphoreType.DMA((sz.pairs,)),
        ],
        1000,
        4 << 20,
        8,
        "pack",
    )(x4, u4, cross, send, row, pair, live)


def local_kernel(sz, first, grad, *refs):
    refs = list(refs)
    meta, col, tiles, tcur, scur = refs[:5]
    refs = refs[5:]
    tprev = sprev = None
    if not first:
        tprev, sprev = refs[:2]
        refs = refs[2:]
    tnew, snew, psel, qsel = refs[:4]
    refs = refs[4:]
    if grad:
        gram = refs[0]
        refs = refs[1:]
    held, summed = refs
    count = meta[sz.live]
    steps = (count + UNROLL - 1) // UNROLL

    def clear(i, carry):
        summed[i] = jnp.zeros(summed.shape[1:], F32)
        return carry

    lax.fori_loop(0, sz.blocks, clear, 0, unroll=4)

    def block_row(i):
        cols = [col[m, i] for m in range(sz.nz)]
        wide = jnp.concatenate([tiles[i, m] for m in range(sz.nz)], axis=1)
        gathered = jnp.concatenate([tcur[c] for c in cols], axis=1)
        forward = nt(gathered, wide)
        if not first:
            forward = 2.0 * forward - tprev[i].astype(F32)
        held[i] = forward
        tnew[i] = forward.astype(BF16)
        terms = nn(scur[i], wide)
        for m in range(sz.nz):
            summed[cols[m]] = summed[cols[m]] + terms[:, m * sz.blk : (m + 1) * sz.blk]

    def step(g, carry):
        for u in range(UNROLL):
            block_row(g * UNROLL + u)
        return carry

    lax.fori_loop(0, steps, step, 0)

    def adjoint(i):
        total = summed[i]
        if not first:
            total = 2.0 * total - sprev[i].astype(F32)
        return total

    def finish(g, carry):
        for u in range(UNROLL):
            i = g * UNROLL + u
            snew[i] = adjoint(i).astype(BF16)
        return carry

    lax.fori_loop(0, steps, finish, 0)

    def dead(i, carry):
        tnew[i] = jnp.zeros(tnew.shape[1:], BF16)
        snew[i] = jnp.zeros(snew.shape[1:], BF16)
        return carry

    lax.fori_loop(count, sz.blocks, dead, 0)
    for j in range(sz.pairs):
        psel[j] = held[meta[sz.rows + j]]
        qsel[j] = adjoint(meta[sz.sends + j])
    if grad:

        def products(g, total):
            for u in range(0, UNROLL, 2):
                i = g * UNROLL + u
                left = [jnp.concatenate([tprev[k], tcur[k]], axis=0) for k in (i, i + 1)]
                right = [jnp.concatenate([sprev[k], scur[k]], axis=0) for k in (i, i + 1)]
                total = total + nt(jnp.concatenate(left, axis=1), jnp.concatenate(right, axis=1))
            return total

        side = 2 * sz.chan
        gram[...] = lax.fori_loop(0, steps, products, jnp.zeros((side, side), F32))


def local_products(sz, meta, col, tiles, tcur, scur, tprev=None, sprev=None, grad=False):
    first = tprev is None
    field = shape((sz.blocks, sz.chan, sz.blk), BF16)
    picked = shape((sz.pairs, sz.chan, sz.blk), F32)
    outs = [field, field, picked, picked]
    if grad:
        outs.append(shape((2 * sz.chan, 2 * sz.chan), F32))
    args = [meta, col, tiles, tcur, scur] + ([] if first else [tprev, sprev])
    return call(
        functools.partial(local_kernel, sz, first, grad),
        [SMEM, SMEM] + [VMEM] * (len(args) - 2),
        [VMEM] * len(outs),
        outs,
        [pltpu.VMEM((sz.blocks, sz.chan, sz.blk), F32)] * 2,
        4 * sz.blocks * sz.nz * sz.chan * sz.blk * sz.blk,
        12 << 20,
        24,
        "local",
    )(*args)


def add_coupled(sz, scale, meta, got, tiles, cross, psel, qsel, pacc, qacc):
    for j in range(sz.pairs):
        pacc[j] = psel[j]
        qacc[j] = qsel[j]
    for r, h, j in sz.couplings():
        factor = scale * meta[sz.flags + r].astype(F32)
        term = nt(got[r][pl.ds(h * sz.chan, sz.chan), :], cross[0, r, h])
        spot = meta[sz.first_row + j]
        pacc[spot] = pacc[spot] + factor * term
        term = nn(
            got[r][pl.ds(sz.half + h * sz.chan, sz.chan), :],
            tiles[r][pl.ds(2 * sz.half + h * sz.blk, sz.blk), :],
        )
        spot = meta[sz.first_send + j]
        qacc[spot] = qacc[spot] + scale * term


def patch(sz, meta, tbase, sbase, tnew, snew, pacc, qacc):
    def move(i, carry):
        tnew[i] = tbase[i]
        snew[i] = sbase[i]
        return carry

    lax.fori_loop(0, sz.blocks, move, 0, unroll=4)
    for j in range(sz.pairs):
        tnew[meta[sz.rows + j]] = pacc[meta[sz.first_row + j]].astype(BF16)
        snew[meta[sz.sends + j]] = qacc[meta[sz.first_send + j]].astype(BF16)


def join_kernel(sz, scale, grad, *refs):
    refs = list(refs)
    meta, cross, tbase, sbase, psel, qsel = refs[:6]
    refs = refs[6:]
    got, refs = refs[: sz.rounds], refs[sz.rounds :]
    tiles, refs = refs[: sz.rounds], refs[sz.rounds :]
    if grad:
        gram, sold = refs[:2]
        refs = refs[2:]
    tnew, snew = refs[:2]
    refs = refs[2:]
    pays, refs = refs[: sz.rounds], refs[sz.rounds :]
    if grad:
        partial, refs = refs[0], refs[1:]
    pacc, qacc = refs
    add_coupled(sz, scale, meta, got, tiles, cross, psel, qsel, pacc, qacc)
    patch(sz, meta, tbase, sbase, tnew, snew, pacc, qacc)
    for r, h, j in sz.couplings():
        pays[r][pl.ds(h * sz.chan, sz.chan), :] = tnew[meta[sz.sends + j]]
        pays[r][pl.ds(sz.half + h * sz.chan, sz.chan), :] = snew[meta[sz.rows + j]]
    if grad:
        count = meta[sz.live]
        steps = (count + UNROLL - 1) // UNROLL

        def products(g, total):
            for u in range(0, UNROLL, 2):
                i = g * UNROLL + u
                left = jnp.concatenate([tnew[i], tnew[i + 1]], axis=1)
                right = jnp.concatenate([sold[i], sold[i + 1]], axis=1)
                total = total + nt(left, right)
            return total

        last = lax.fori_loop(0, steps, products, jnp.zeros((sz.chan, sz.chan), F32))
        partial[...] = gram[...]
        partial[pl.ds(0, sz.chan), pl.ds(sz.chan, sz.chan)] = last


def join(sz, scale, meta, cross, tbase, sbase, psel, qsel, got, tiles, gram=None, sold=None):
    field = shape((sz.blocks, sz.chan, sz.blk), BF16)
    pay = shape((2 * sz.half, sz.blk), BF16)
    outs = [field, field] + [pay] * sz.rounds
    args = [meta, cross, tbase, sbase, psel, qsel, *got, *tiles]
    if gram is not None:
        args += [gram, sold]
        outs.append(shape(gram.shape, F32))
    outs = call(
        functools.partial(join_kernel, sz, scale, gram is not None),
        [SMEM] + [VMEM] * (len(args) - 1),
        [VMEM] * len(outs),
        outs,
        [pltpu.VMEM((sz.pairs, sz.chan, sz.blk), F32)] * 2,
        4 * sz.pairs * sz.chan * sz.blk * sz.blk,
        6 << 20,
        12,
        "join",
    )(*args)
    tail = outs[2 + sz.rounds :]
    return outs[0], outs[1], outs[2 : 2 + sz.rounds], tail


def output_kernel(sz, *refs):
    refs = list(refs)
    meta, cross, weight, tbase, sbase, psel, qsel = refs[:7]
    refs = refs[7:]
    got, refs = refs[: sz.rounds], refs[sz.rounds :]
    tiles, refs = refs[: sz.rounds], refs[sz.rounds :]
    t0, t1, t2, s0, s1, s2, out4, grad4, tlast, slast, pacc, qacc = refs
    add_coupled(sz, 2.0, meta, got, tiles, cross, psel, qsel, pacc, qacc)
    patch(sz, meta, tbase, sbase, tlast, slast, pacc, qacc)
    count = meta[sz.live]
    steps = (count + UNROLL - 1) // UNROLL
    orders = weight.shape[0]
    back = jnp.concatenate([weight[k].astype(F32) for k in range(orders)], axis=1).astype(BF16)
    ahead = jnp.concatenate([weight[k].astype(F32).T for k in range(orders)], axis=1).astype(BF16)
    groups = sz.chan // SUB

    def block(i):
        field = jnp.concatenate([t[i] for t in (t0, t1, t2, tlast)], axis=0)
        value = nn(ahead, field).astype(BF16)
        for t in range(groups):
            out4[t, i] = value[t * SUB : (t + 1) * SUB]
        field = jnp.concatenate([s[i] for s in (s0, s1, s2, slast)], axis=0)
        value = nn(back, field).astype(BF16)
        for t in range(groups):
            grad4[t, i] = value[t * SUB : (t + 1) * SUB]

    def step(g, carry):
        for u in range(UNROLL):
            block(g * UNROLL + u)
        return carry

    lax.fori_loop(0, steps, step, 0)

    def dead(i, carry):
        for t in range(groups):
            out4[t, i] = jnp.zeros((SUB, sz.blk), BF16)
            grad4[t, i] = jnp.zeros((SUB, sz.blk), BF16)
        return carry

    lax.fori_loop(count, sz.blocks, dead, 0)


def outputs(sz, meta, cross, weight, tbase, sbase, psel, qsel, got, tiles, fields):
    out = shape((sz.chan // SUB, sz.blocks, SUB, sz.blk), BF16)
    args = [meta, cross, weight, tbase, sbase, psel, qsel, *got, *tiles, *fields]
    return call(
        functools.partial(output_kernel, sz),
        [SMEM] + [VMEM] * (len(args) - 1),
        [VMEM] * 2,
        [out, out],
        [pltpu.VMEM((sz.blocks, sz.chan, sz.blk), BF16)] * 2
        + [pltpu.VMEM((sz.pairs, sz.chan, sz.blk), F32)] * 2,
        16 * sz.blocks * sz.chan * sz.chan * sz.blk,
        10 << 20,
        16,
        "outputs",
    )(*args)


def add_kernel(mine, theirs, out):
    out[...] = mine[...] + theirs[...]


def add(mine, theirs):
    return call(
        add_kernel,
        [VMEM, VMEM],
        VMEM,
        shape(mine.shape, F32),
        [],
        mine.size,
        12 * mine.size,
        2,
        "add",
    )(mine, theirs)


def weight_kernel(chan, gram, out):
    top, low = pl.ds(0, chan), pl.ds(chan, chan)
    zeroth, first = gram[top, top], gram[low, top]
    out[0] = zeroth
    out[1] = first
    out[2] = 2.0 * gram[low, low] - zeroth
    out[3] = 2.0 * gram[top, low] - first


def weight_gradient(sz, gram):
    return call(
        functools.partial(weight_kernel, sz.chan),
        [VMEM],
        VMEM,
        shape((4, sz.chan, sz.chan), F32),
        [],
        gram.size,
        8 * gram.size,
        2,
        "weight",
    )(gram)


def from_partner(values, bit):
    count = lax.axis_size("dom")
    route = []
    for low in range(count):
        high = low | 1 << bit
        if high != low and high < count:
            route += [(low, high), (high, low)]
    return lax.ppermute(values, "dom", route)


def total_over_devices(gram):
    count = lax.axis_size("dom")
    if count & (count - 1):
        return lax.psum(gram, "dom")
    for bit in range(count.bit_length() - 1):
        gram = add(gram, from_partner(gram, bit))
    return gram


def local(
    features,
    cheb_weight,
    lap_tiles,
    col_index,
    cross_tiles,
    send_index,
    row_index,
    pair_on,
    blk_live,
    cotangent,
):
    sz = Sizes(features, lap_tiles, cross_tiles)
    split = (sz.chan // SUB, SUB, sz.blocks, sz.blk)
    x4 = features.reshape(split).transpose(0, 2, 1, 3)
    u4 = cotangent.reshape(split).transpose(0, 2, 1, 3)
    col = col_index.T

    packed = pack(sz, x4, u4, cross_tiles, send_index, row_index, pair_on, blk_live)
    t0, s0, meta = packed[:3]
    tiles = [from_partner(pay, bit) for bit, pay in enumerate(packed[3:])]
    t1, s1, psel, qsel = local_products(sz, meta, col, lap_tiles, t0, s0)
    t1, s1, pays, _ = join(sz, 1.0, meta, cross_tiles, t1, s1, psel, qsel, tiles, tiles)

    got = [from_partner(pay, bit) for bit, pay in enumerate(pays)]
    t2, s2, psel, qsel, gram = local_products(
        sz, meta, col, lap_tiles, t1, s1, t0, s0, grad=True
    )
    t2, s2, pays, tail = join(
        sz, 2.0, meta, cross_tiles, t2, s2, psel, qsel, got, tiles, gram, s1
    )

    got = [from_partner(pay, bit) for bit, pay in enumerate(pays)]
    grad_w = weight_gradient(sz, total_over_devices(tail[0]))
    t3, s3, psel, qsel = local_products(sz, meta, col, lap_tiles, t2, s2, t1, s1)
    out4, grad4 = outputs(
        sz, meta, cross_tiles, cheb_weight, t3, s3, psel, qsel, got, tiles, (t0, t1, t2, s0, s1, s2)
    )
    conv_out = out4.transpose(0, 2, 1, 3).reshape(features.shape)
    grad_x = grad4.transpose(0, 2, 1, 3).reshape(features.shape)
    return (conv_out, grad_x, grad_w)


def solution(mesh):
    in_specs = (
        P(None, "dom"),
        P(),
        P("dom", None, None, None),
        P("dom", None),
        P("dom", None, None, None, None),
        P("dom", None, None),
        P("dom", None, None),
        P("dom", None),
        P("dom"),
        P(None, "dom"),
    )
    out_specs = (P(None, "dom"), P(None, "dom"), P())
    return jax.shard_map(local, mesh=mesh, in_specs=in_specs, out_specs=out_specs, check_vma=False)
```

time: 546 us -> 83.6 us (0.15)
  other arithmetic: 190 us -> 0.01 us
  waiting for transfers between devices: 125 us -> 11.9 us
  matrix products: 91 us -> 0 us
  local copies, waits for them, and re-layouts: 80.2 us -> 9.08 us
  Pallas kernels: 0 us -> 40.2 us
  starting transfers between devices: 37.6 us -> 20.6 us
  between operations: 15.7 us -> 1.54 us
    psum x1 -> x0, waiting for transfers between devices: 123 us -> none  [local(): grad_w = lax.psum(weight_terms, 'dom')]
    scatter-add x33 -> x0, other arithmetic: 118 us -> none  [the longest x3 60 us: local_adjoint(): jnp.zeros((channels, block_count, block_size), jnp.float32).at[:, col_index]]
    dot_general x39 -> x0, matrix products: 91 us -> none  [the longest x3 23.2 us: apply_forward(): jnp.einsum('inab,finb->fia', lap_tiles, gathered, preferred_element_type=...]
    gather x33 -> x0, local copies, waits for them, and re-layouts: 57.7 us -> none  [the longest x15 23.7 us: apply_adjoint(): slices = jnp.take(values, recv_rows[level], axis=1)]
    pallas_call x0 -> x13, Pallas kernels: none -> 40.2 us  [the longest x3 25.2 us: local_products(): call(functools.partial(local_kernel, sz, first, grad), [SMEM, SMEM] + [VM...]
    select_n x52 -> x0, other arithmetic: 39.5 us -> none  [the longest x20 13.8 us: apply_adjoint(): slices = jnp.take(values, recv_rows[level], axis=1)]
    ppermute x35 -> x20, starting transfers between devices: 37.5 us -> 20.6 us  [from_partner(): return lax.ppermute(values, 'dom', route)]
    ppermute x35 -> x20, waiting for transfers between devices: 2.58 us -> 11.9 us  [from_partner(): return lax.ppermute(values, 'dom', route)]
  transfers between devices with their start and end apart: 36 -> 20, of which waited for: 5 -> 4; matrix products, arithmetic and copies ran while one was open for 46% -> 0% of each run, Pallas kernels for 0% -> 30%
where the time goes in v1:
time: 83.6 us; the launch traced here: 83.3 us
  Pallas kernels  40.2 us (48%)
  starting transfers between devices  20.6 us (25%)
  waiting for transfers between devices  11.9 us (14%)
  local copies, waits for them, and re-layouts  9.08 us (11%)
  between operations  1.54 us (2%)
    pallas_call x3, Pallas kernels, local_products(): call(functools.partial(local_kernel, sz, first, grad), [SMEM, SMEM] + [VM...  25.2 us
    ppermute x20, starting transfers between devices, from_partner(): return lax.ppermute(values, 'dom', route)  20.6 us
    ppermute x20, waiting for transfers between devices, from_partner(): return lax.ppermute(values, 'dom', route)  11.9 us
    unnamed x24, local copies, waits for them, and re-layouts  9.08 us
    pallas_call x1, Pallas kernels, outputs(): call(functools.partial(output_kernel, sz), [SMEM] + [VMEM] * (len(args) -...  6.26 us
    pallas_call x2, Pallas kernels, join(): call(functools.partial(join_kernel, sz, scale, gram is not None), [SMEM]...  5.07 us
    pallas_call x1, Pallas kernels, pack(): call(functools.partial(pack_kernel, sz), [ANY, ANY, ANY, SMEM, SMEM, SMEM...  2.78 us
  transfers between devices with their start and end apart: 20, of which 4 were waited for; matrix products, arithmetic and copies ran while one was open for 0% of the time, Pallas kernels for 30%

profile of v1, /device:TPU:0, one launch (start us, length us, event | category | flops | bytes accessed | tf_op | source)
XLA Modules:
  0.0 83.3 jit_solution(14287489473097260226)
XLA Ops:
  0.6 0.8 copy.13.refs_3_
  1.4 0.8 copy.14.refs_4_
  2.8 0.0 copy-start.1
  2.8 1.0 %copy-done.1 = bf16[1,5,2,128,128]{4,3,2,1,0:T(8,128)(2,1)S(1)} copy-done((bf16[1,5,2,128,128]{4,3,2,1,0:T(8,128)(2,1)S(1)}, bf16[1,5,2,128,128]{4,3,2,1,0:T(8,128)(2,1)}, u32[]{:S(2)}) %copy-start.1) | copy-done | bytes 327704
  3.8 1.2 %copy-done.3 = bf16[64,8192]{1,0:T(8,128)(2,1)S(1)} copy-done((bf16[64,8192]{1,0:T(8,128)(2,1)S(1)}, bf16[64,8192]{1,0:T(8,128)(2,1)}, u32[]{:S(2)}) %copy-start.3) | copy-done | bytes 1048600
  5.0 1.2 %copy-done.4 = bf16[64,8192]{1,0:T(8,128)(2,1)S(1)} copy-done((bf16[64,8192]{1,0:T(8,128)(2,1)S(1)}, bf16[64,8192]{1,0:T(8,128)(2,1)}, u32[]{:S(2)}) %copy-start.4) | copy-done | bytes 1048600
  6.2 0.7 copy-done.8
  6.9 2.8 %pack.1 = (bf16[64,64,128]{2,1,0:T(8,128)(2,1)S(1)}, bf16[64,64,128]{2,1,0:T(8,128)(2,1)S(1)}, s32[46]{0:T(128)S(1)}, bf16[512,128]{1,0:T(8,128)(2,1)S(1)}, bf16...) custom-call(bf16[8,64,8,128]{3,2,1,0:T(8,128)(2,1)S(1)} %bitcast.15,, ...), custom_call_target="tpu_custom_call" | custom-call | flops 1000 | bytes 4194304 | tf_op jit(solution)/shard_map/pack/pallas_call | solution.py:123
  9.7 0.6 collective-permute-start
  10.2 2.8 %collective-permute-start.1 = (bf16[512,128]{1,0:T(8,128)(2,1)S(1)}, bf16[512,128]{1,0:T(8,128)(2,1)S(1)}, u32[]{:S(2)}, u32[]{:S(2)}) collective-permute-start(bf16[512,128]{1,0:T(8,128)(2,1)S(1)} %get-tuple-element.49), channel_id=1, source_target_pairs={{0,2},{2,0},{1,3},{3,1},{4,6},{6,4},{5,7},{7,5},{8,10},{10,8},{9,1... | collective-permute-start | bytes 393224 | tf_op jit(solution)/shard_map/ppermute | solution.py:437
  13.0 1.3 %collective-permute-start.2 = (bf16[512,128]{1,0:T(8,128)(2,1)S(1)}, bf16[512,128]{1,0:T(8,128)(2,1)S(1)}, u32[]{:S(2)}, u32[]{:S(2)}) collective-permute-start(bf16[512,128]{1,0:T(8,128)(2,1)S(1)} %get-tuple-element.50), channel_id=1, source_target_pairs={{0,4},{4,0},{1,5},{5,1},{2,6},{6,2},{3,7},{7,3},{8,12},{12,8},{9,1... | collective-permute-start | bytes 393224 | tf_op jit(solution)/shard_map/ppermute | solution.py:437
  14.3 1.6 %collective-permute-start.3 = (bf16[512,128]{1,0:T(8,128)(2,1)S(1)}, bf16[512,128]{1,0:T(8,128)(2,1)S(1)}, u32[]{:S(2)}, u32[]{:S(2)}) collective-permute-start(bf16[512,128]{1,0:T(8,128)(2,1)S(1)} %get-tuple-element.51), channel_id=1, source_target_pairs={{0,8},{8,0},{1,9},{9,1},{2,10},{10,2},{3,11},{11,3},{4,12},{12,4},... | collective-permute-start | bytes 393224 | tf_op jit(solution)/shard_map/ppermute | solution.py:437
  15.9 2.7 %collective-permute-start.4 = (bf16[512,128]{1,0:T(8,128)(2,1)S(1)}, bf16[512,128]{1,0:T(8,128)(2,1)S(1)}, u32[]{:S(2)}, u32[]{:S(2)}) collective-permute-start(bf16[512,128]{1,0:T(8,128)(2,1)S(1)} %get-tuple-element.52), channel_id=1, source_target_pairs={{0,16},{16,0},{1,17},{17,1},{2,18},{18,2},{3,19},{19,3},{4,20},{20... | collective-permute-start | bytes 393224 | tf_op jit(solution)/shard_map/ppermute | solution.py:437
  18.6 2.8 %copy-done = bf16[64,3,128,128]{3,2,1,0:T(8,128)(2,1)S(1)} copy-done((bf16[64,3,128,128]{3,2,1,0:T(8,128)(2,1)S(1)}, bf16[64,3,128,128]{3,2,1,0:T(8,128)(2,1)}, u32[]{:S(2)}) %copy-start) | copy-done | bytes 6291480
  21.4 0.7 copy-done.6
  22.1 7.2 %local.3 = (bf16[64,64,128]{2,1,0:T(8,128)(2,1)S(1)}, bf16[64,64,128]{2,1,0:T(8,128)(2,1)S(1)}, f32[10,64,128]{2,1,0:T(8,128)S(1)}, f32[10,64,128]{2,1,0:T(8,128)S(1)}) custom-call(s32[46]{0:T(128)S(1)} %get-tuple-element.41.refs_0_, s32[3,64]{1,0:T(4,128)S(1)} %bitcast.17, bf16[64,3,128,128]{3,2,1,0:T(8,128)(2,1)S(1)} %copy-done, ...), custom_call_target="tpu_custom_call" | custom-call | flops 805306368 | bytes 12582912 | tf_op jit(solution)/shard_map/local/pallas_call | solution.py:228
  29.3 0.0 collective-permute-done.refs_6_.refs_11_.refs_12_
  29.3 0.0 collective-permute-done.1.refs_7_.refs_12_.refs_13_
  29.3 0.0 collective-permute-done.2.refs_8_.refs_13_.refs_14_
  29.4 1.2 %join.2 = (bf16[64,64,128]{2,1,0:T(8,128)(2,1)S(1)}, bf16[64,64,128]{2,1,0:T(8,128)(2,1)S(1)}, bf16[256,128]{1,0:T(8,128)(2,1)S(1)}, bf16[256,128]{1,0:T(8,128)(...) custom-call(s32[46]{0:T(128)S(1)} %get-tuple-element.41.refs_0_, ...), custom_call_target="tpu_custom_call" | custom-call | flops 41943040 | bytes 6291456 | tf_op jit(solution)/shard_map/join/pallas_call | solution.py:315
  30.6 0.1 collective-permute-start.5
  30.7 0.1 collective-permute-start.6
  30.7 1.1 %collective-permute-start.7 = (bf16[256,128]{1,0:T(8,128)(2,1)S(1)}, bf16[256,128]{1,0:T(8,128)(2,1)S(1)}, u32[]{:S(2)}, u32[]{:S(2)}) collective-permute-start(bf16[256,128]{1,0:T(8,128)(2,1)S(1)} %get-tuple-element.61), channel_id=1, source_target_pairs={{0,4},{4,0},{1,5},{5,1},{2,6},{6,2},{3,7},{7,3},{8,12},{12,8},{9,1... | collective-permute-start | bytes 196616 | tf_op jit(solution)/shard_map/ppermute | solution.py:437
  31.8 0.5 collective-permute-start.8
  32.3 10.6 %local.4 = (bf16[64,64,128]{2,1,0:T(8,128)(2,1)S(1)}, bf16[64,64,128]{2,1,0:T(8,128)(2,1)S(1)}, f32[10,64,128]{2,1,0:T(8,128)S(1)}, f32[10,64,128]{2,1,0:T(8,128)S(1)}, f32[128,128]{1,0:T(8,128)S(1)}) custom-call(s32[46]{0:T(128)S(1)} %get-tuple-element.41.refs_0_, s32[3,64]{1,0:T(4,128)S(1)} %bitcast.18, bf16[64,3,128,128]{3,2,1,0:T(8,128)(2,1)S(1)} %copy-done, ...), custom_call_target="tpu_custom_call" | custom-call | flops 805306368 | bytes 12582912 | tf_op jit(solution)/shard_map/local/pallas_call | solution.py:228
  42.9 0.0 collective-permute-done.5.refs_6_
  43.0 0.0 collective-permute-done.8.refs_9_
  43.0 3.9 %join.3 = (bf16[64,64,128]{2,1,0:T(8,128)(2,1)S(1)}, bf16[64,64,128]{2,1,0:T(8,128)(2,1)S(1)}, bf16[256,128]{1,0:T(8,128)(2,1)S(1)}, bf16[256,128]{1,0:T(8,128)(...) custom-call(s32[46]{0:T(128)S(1)} %get-tuple-element.41.refs_0_, ...), custom_call_target="tpu_custom_call" | custom-call | flops 41943040 | bytes 6291456 | tf_op jit(solution)/shard_map/join/pallas_call | solution.py:315
  46.8 0.0 collective-permute-start.15
  46.9 1.2 %collective-permute-done.15.theirs = f32[128,128]{1,0:T(8,128)S(1)} collective-permute-done((f32[128,128]{1,0:T(8,128)S(1)}, f32[128,128]{1,0:T(8,128)S(1)}, u32[]{:S(2)}, u32[]{:S(2)}) %collective-permute-start.15) | collective-permute-done | bytes 65568 | tf_op jit(solution)/shard_map/ppermute | solution.py:437
  48.1 0.8 collective-permute-start.16
  48.9 3.6 %collective-permute-done.16.theirs = f32[128,128]{1,0:T(8,128)S(1)} collective-permute-done((f32[128,128]{1,0:T(8,128)S(1)}, f32[128,128]{1,0:T(8,128)S(1)}, u32[]{:S(2)}, u32[]{:S(2)}) %collective-permute-start.16) | collective-permute-done | bytes 65568 | tf_op jit(solution)/shard_map/ppermute | solution.py:437
  52.5 1.0 %collective-permute-start.17 = (f32[128,128]{1,0:T(8,128)S(1)}, f32[128,128]{1,0:T(8,128)S(1)}, u32[]{:S(2)}, u32[]{:S(2)}) collective-permute-start(f32[128,128]{1,0:T(8,128)S(1)} %add.6.mine), channel_id=1, source_target_pairs={{0,4},{4,0},{1,5},{5,1},{2,6},{6,2},{3,7},{7,3},{8,12},{12,8},{9,1... | collective-permute-start | bytes 196616 | tf_op jit(solution)/shard_map/ppermute | solution.py:437
  53.4 3.4 %collective-permute-done.17.theirs = f32[128,128]{1,0:T(8,128)S(1)} collective-permute-done((f32[128,128]{1,0:T(8,128)S(1)}, f32[128,128]{1,0:T(8,128)S(1)}, u32[]{:S(2)}, u32[]{:S(2)}) %collective-permute-start.17) | collective-permute-done | bytes 65568 | tf_op jit(solution)/shard_map/ppermute | solution.py:437
  56.8 0.7 collective-permute-start.18
  57.5 3.7 %collective-permute-done.18.theirs = f32[128,128]{1,0:T(8,128)S(1)} collective-permute-done((f32[128,128]{1,0:T(8,128)S(1)}, f32[128,128]{1,0:T(8,128)S(1)}, u32[]{:S(2)}, u32[]{:S(2)}) %collective-permute-start.18) | collective-permute-done | bytes 65568 | tf_op jit(solution)/shard_map/ppermute | solution.py:437
  61.2 1.6 %collective-permute-start.19 = (f32[128,128]{1,0:T(8,128)S(1)}, f32[128,128]{1,0:T(8,128)S(1)}, u32[]{:S(2)}, u32[]{:S(2)}) collective-permute-start(f32[128,128]{1,0:T(8,128)S(1)} %add.8.mine), channel_id=1, source_target_pairs={{0,16},{16,0},{1,17},{17,1},{2,18},{18,2},{3,19},{19,3},{4,20},{20... | collective-permute-start | bytes 196616 | tf_op jit(solution)/shard_map/ppermute | solution.py:437
  62.7 0.0 collective-permute-start.10
  62.7 2.2 %collective-permute-start.11 = (bf16[256,128]{1,0:T(8,128)(2,1)S(1)}, bf16[256,128]{1,0:T(8,128)(2,1)S(1)}, u32[]{:S(2)}, u32[]{:S(2)}) collective-permute-start(bf16[256,128]{1,0:T(8,128)(2,1)S(1)} %get-tuple-element.72), channel_id=1, source_target_pairs={{0,2},{2,0},{1,3},{3,1},{4,6},{6,4},{5,7},{7,5},{8,10},{10,8},{9,1... | collective-permute-start | bytes 196616 | tf_op jit(solution)/shard_map/ppermute | solution.py:437
  64.9 2.2 %collective-permute-start.12 = (bf16[256,128]{1,0:T(8,128)(2,1)S(1)}, bf16[256,128]{1,0:T(8,128)(2,1)S(1)}, u32[]{:S(2)}, u32[]{:S(2)}) collective-permute-start(bf16[256,128]{1,0:T(8,128)(2,1)S(1)} %get-tuple-element.73), channel_id=1, source_target_pairs={{0,4},{4,0},{1,5},{5,1},{2,6},{6,2},{3,7},{7,3},{8,12},{12,8},{9,1... | collective-permute-start | bytes 196616 | tf_op jit(solution)/shard_map/ppermute | solution.py:437
  67.2 0.0 collective-permute-done.19.theirs
  67.2 1.4 %collective-permute-start.14 = (bf16[256,128]{1,0:T(8,128)(2,1)S(1)}, bf16[256,128]{1,0:T(8,128)(2,1)S(1)}, u32[]{:S(2)}, u32[]{:S(2)}) collective-permute-start(bf16[256,128]{1,0:T(8,128)(2,1)S(1)} %get-tuple-element.75), channel_id=1, source_target_pairs={{0,16},{16,0},{1,17},{17,1},{2,18},{18,2},{3,19},{19,3},{4,20},{20... | collective-permute-start | bytes 196616 | tf_op jit(solution)/shard_map/ppermute | solution.py:437
  68.6 7.5 %local.5 = (bf16[64,64,128]{2,1,0:T(8,128)(2,1)S(1)}, bf16[64,64,128]{2,1,0:T(8,128)(2,1)S(1)}, f32[10,64,128]{2,1,0:T(8,128)S(1)}, f32[10,64,128]{2,1,0:T(8,128)S(1)}) custom-call(s32[46]{0:T(128)S(1)} %get-tuple-element.41.refs_0_, s32[3,64]{1,0:T(4,128)S(1)} %bitcast.19, bf16[64,3,128,128]{3,2,1,0:T(8,128)(2,1)S(1)} %bitcast.14, ...), custom_call_target="tpu_custom_call" | custom-call | flops 805306368 | bytes 12582912 | tf_op jit(solution)/shard_map/local/pallas_call | solution.py:228
  76.1 0.0 collective-permute-done.10.refs_7_
  76.1 0.0 collective-permute-done.12.refs_9_
  76.2 0.0 collective-permute-done.13.refs_10_
  76.2 6.3 %outputs.1 = (bf16[8,64,8,128]{3,2,1,0:T(8,128)(2,1)}, bf16[8,64,8,128]{3,2,1,0:T(8,128)(2,1)}) custom-call(s32[46]{0:T(128)S(1)} %get-tuple-element.41.refs_0_, bf16[1,5,2,128,128]{4,3,2,1,0:T(8,128)(2,1)S(1)} %copy-done.2, bf16[4,64,64]{2,1,0:T(8,128)(2,1)S(1)} %copy-done.5, bf16[64,64,128]{2,1,0:T(8,128)(2,1)S(1)} %get-tuple-element.67.refs_3_, ...), custom_call_target="tpu_custom_call" | custom-call | flops 536870912 | bytes 10485760 | tf_op jit(solution)/shard_map/outputs/pallas_call | solution.py:375
  82.4 0.8 weight.1
  (30 shorter events, 0.1 us)
Async XLA Ops:
  2.8 1.0 %copy-start.1 = (bf16[1,5,2,128,128]{4,3,2,1,0:T(8,128)(2,1)S(1)}, bf16[1,5,2,128,128]{4,3,2,1,0:T(8,128)(2,1)}, u32[]{:S(2)}) copy-start(bf16[1,5,2,128,128]{4,3,2,1,0:T(8,128)(2,1)} %refs_1_.5) | copy-start | bytes 983044
  3.8 1.2 %copy-start.3 = (bf16[64,8192]{1,0:T(8,128)(2,1)S(1)}, bf16[64,8192]{1,0:T(8,128)(2,1)}, u32[]{:S(2)}) copy-start(bf16[64,8192]{1,0:T(8,128)(2,1)} %param.10) | copy-start | bytes 3145732
  5.0 1.2 %copy-start.4 = (bf16[64,8192]{1,0:T(8,128)(2,1)S(1)}, bf16[64,8192]{1,0:T(8,128)(2,1)}, u32[]{:S(2)}) copy-start(bf16[64,8192]{1,0:T(8,128)(2,1)} %param.19) | copy-start | bytes 3145732
  6.2 0.7 copy-start.8
  6.9 22.5 %copy-start.2 = (bf16[1,5,2,128,128]{4,3,2,1,0:T(8,128)(2,1)S(1)}, bf16[1,5,2,128,128]{4,3,2,1,0:T(8,128)(2,1)}, u32[]{:S(2)}) copy-start(bf16[1,5,2,128,128]{4,3,2,1,0:T(8,128)(2,1)} %refs_1_.5) | copy-start | bytes 983044
  9.7 19.6 %collective-permute-start = (bf16[512,128]{1,0:T(8,128)(2,1)S(1)}, bf16[512,128]{1,0:T(8,128)(2,1)S(1)}, u32[]{:S(2)}, u32[]{:S(2)}) collective-permute-start(bf16[512,128]{1,0:T(8,128)(2,1)S(1)} %get-tuple-element.48), channel_id=1, source_target_pairs={{0,1},{1,0},{2,3},{3,2},{4,5},{5,4},{6,7},{7,6},{8,9},{9,8},{10,11... | collective-permute-start | bytes 393224 | tf_op jit(solution)/shard_map/ppermute | solution.py:437
  10.2 19.1 %collective-permute-start.1 = (bf16[512,128]{1,0:T(8,128)(2,1)S(1)}, bf16[512,128]{1,0:T(8,128)(2,1)S(1)}, u32[]{:S(2)}, u32[]{:S(2)}) collective-permute-start(bf16[512,128]{1,0:T(8,128)(2,1)S(1)} %get-tuple-element.49), channel_id=1, source_target_pairs={{0,2},{2,0},{1,3},{3,1},{4,6},{6,4},{5,7},{7,5},{8,10},{10,8},{9,1... | collective-permute-start | bytes 393224 | tf_op jit(solution)/shard_map/ppermute | solution.py:437
  13.0 16.3 %collective-permute-start.2 = (bf16[512,128]{1,0:T(8,128)(2,1)S(1)}, bf16[512,128]{1,0:T(8,128)(2,1)S(1)}, u32[]{:S(2)}, u32[]{:S(2)}) collective-permute-start(bf16[512,128]{1,0:T(8,128)(2,1)S(1)} %get-tuple-element.50), channel_id=1, source_target_pairs={{0,4},{4,0},{1,5},{5,1},{2,6},{6,2},{3,7},{7,3},{8,12},{12,8},{9,1... | collective-permute-start | bytes 393224 | tf_op jit(solution)/shard_map/ppermute | solution.py:437
  14.3 15.0 %collective-permute-start.3 = (bf16[512,128]{1,0:T(8,128)(2,1)S(1)}, bf16[512,128]{1,0:T(8,128)(2,1)S(1)}, u32[]{:S(2)}, u32[]{:S(2)}) collective-permute-start(bf16[512,128]{1,0:T(8,128)(2,1)S(1)} %get-tuple-element.51), channel_id=1, source_target_pairs={{0,8},{8,0},{1,9},{9,1},{2,10},{10,2},{3,11},{11,3},{4,12},{12,4},... | collective-permute-start | bytes 393224 | tf_op jit(solution)/shard_map/ppermute | solution.py:437
  15.9 13.4 %collective-permute-start.4 = (bf16[512,128]{1,0:T(8,128)(2,1)S(1)}, bf16[512,128]{1,0:T(8,128)(2,1)S(1)}, u32[]{:S(2)}, u32[]{:S(2)}) collective-permute-start(bf16[512,128]{1,0:T(8,128)(2,1)S(1)} %get-tuple-element.52), channel_id=1, source_target_pairs={{0,16},{16,0},{1,17},{17,1},{2,18},{18,2},{3,19},{19,3},{4,20},{20... | collective-permute-start | bytes 393224 | tf_op jit(solution)/shard_map/ppermute | solution.py:437
  18.6 2.8 %copy-start = (bf16[64,3,128,128]{3,2,1,0:T(8,128)(2,1)S(1)}, bf16[64,3,128,128]{3,2,1,0:T(8,128)(2,1)}, u32[]{:S(2)}) copy-start(bf16[64,3,128,128]{3,2,1,0:T(8,128)(2,1)} %refs_2_.8) | copy-start | bytes 18874372
  21.4 0.7 copy-start.6
  30.6 12.4 %collective-permute-start.5 = (bf16[256,128]{1,0:T(8,128)(2,1)S(1)}, bf16[256,128]{1,0:T(8,128)(2,1)S(1)}, u32[]{:S(2)}, u32[]{:S(2)}) collective-permute-start(bf16[256,128]{1,0:T(8,128)(2,1)S(1)} %get-tuple-element.59), channel_id=1, source_target_pairs={{0,1},{1,0},{2,3},{3,2},{4,5},{5,4},{6,7},{7,6},{8,9},{9,8},{10,11... | collective-permute-start | bytes 196616 | tf_op jit(solution)/shard_map/ppermute | solution.py:437
  30.7 12.3 %collective-permute-start.6 = (bf16[256,128]{1,0:T(8,128)(2,1)S(1)}, bf16[256,128]{1,0:T(8,128)(2,1)S(1)}, u32[]{:S(2)}, u32[]{:S(2)}) collective-permute-start(bf16[256,128]{1,0:T(8,128)(2,1)S(1)} %get-tuple-element.60), channel_id=1, source_target_pairs={{0,2},{2,0},{1,3},{3,1},{4,6},{6,4},{5,7},{7,5},{8,10},{10,8},{9,1... | collective-permute-start | bytes 196616 | tf_op jit(solution)/shard_map/ppermute | solution.py:437
  30.7 12.2 %collective-permute-start.7 = (bf16[256,128]{1,0:T(8,128)(2,1)S(1)}, bf16[256,128]{1,0:T(8,128)(2,1)S(1)}, u32[]{:S(2)}, u32[]{:S(2)}) collective-permute-start(bf16[256,128]{1,0:T(8,128)(2,1)S(1)} %get-tuple-element.61), channel_id=1, source_target_pairs={{0,4},{4,0},{1,5},{5,1},{2,6},{6,2},{3,7},{7,3},{8,12},{12,8},{9,1... | collective-permute-start | bytes 196616 | tf_op jit(solution)/shard_map/ppermute | solution.py:437
  31.8 11.1 %collective-permute-start.8 = (bf16[256,128]{1,0:T(8,128)(2,1)S(1)}, bf16[256,128]{1,0:T(8,128)(2,1)S(1)}, u32[]{:S(2)}, u32[]{:S(2)}) collective-permute-start(bf16[256,128]{1,0:T(8,128)(2,1)S(1)} %get-tuple-element.62), channel_id=1, source_target_pairs={{0,8},{8,0},{1,9},{9,1},{2,10},{10,2},{3,11},{11,3},{4,12},{12,4},... | collective-permute-start | bytes 196616 | tf_op jit(solution)/shard_map/ppermute | solution.py:437
  32.3 10.6 %collective-permute-start.9 = (bf16[256,128]{1,0:T(8,128)(2,1)S(1)}, bf16[256,128]{1,0:T(8,128)(2,1)S(1)}, u32[]{:S(2)}, u32[]{:S(2)}) collective-permute-start(bf16[256,128]{1,0:T(8,128)(2,1)S(1)} %get-tuple-element.63), channel_id=1, source_target_pairs={{0,16},{16,0},{1,17},{17,1},{2,18},{18,2},{3,19},{19,3},{4,20},{20... | collective-permute-start | bytes 196616 | tf_op jit(solution)/shard_map/ppermute | solution.py:437
  32.3 36.3 %slice-start = ((s8[6291456]{0:T(1024)(128)(4,1)}), s8[4194304]{0:T(1024)(128)(4,1)S(1)}, s32[]{:S(2)}) async-start(s8[6291456]{0:T(1024)(128)(4,1)} %bitcast.13), calls=%async_computation | async-start | bytes 8388608
  32.3 36.3 %slice-start.1 = ((s8[6291456]{0:T(1024)(128)(4,1)}), s8[2097152]{0:T(1024)(128)(4,1)S(1)}, s32[]{:S(2)}) async-start(s8[6291456]{0:T(1024)(128)(4,1)} %bitcast.13), calls=%async_computation.1 | async-start | bytes 4194304
  32.3 36.3 %copy-start.7 = (s32[64,3]{0,1:T(4,128)S(1)}, s32[64,3]{0,1:T(4,128)}, u32[]{:S(2)}) copy-start(s32[64,3]{0,1:T(4,128)} %param.13) | copy-start | bytes 2308
  46.8 29.4 %copy-start.5 = (bf16[4,64,64]{2,1,0:T(8,128)(2,1)S(1)}, bf16[4,64,64]{2,1,0:T(8,128)(2,1)}, u32[]{:S(2)}) copy-start(bf16[4,64,64]{2,1,0:T(8,128)(2,1)} %refs_2_.9) | copy-start | bytes 98308
  46.8 1.3 %collective-permute-start.15 = (f32[128,128]{1,0:T(8,128)S(1)}, f32[128,128]{1,0:T(8,128)S(1)}, u32[]{:S(2)}, u32[]{:S(2)}) collective-permute-start(f32[128,128]{1,0:T(8,128)S(1)} %get-tuple-element.78.mine), channel_id=1, source_target_pairs={{0,1},{1,0},{2,3},{3,2},{4,5},{5,4},{6,7},{7,6},{8,9},{9,8},{10,11... | collective-permute-start | bytes 196616 | tf_op jit(solution)/shard_map/ppermute | solution.py:437
  48.1 4.3 %collective-permute-start.16 = (f32[128,128]{1,0:T(8,128)S(1)}, f32[128,128]{1,0:T(8,128)S(1)}, u32[]{:S(2)}, u32[]{:S(2)}) collective-permute-start(f32[128,128]{1,0:T(8,128)S(1)} %add.5.mine), channel_id=1, source_target_pairs={{0,2},{2,0},{1,3},{3,1},{4,6},{6,4},{5,7},{7,5},{8,10},{10,8},{9,1... | collective-permute-start | bytes 196616 | tf_op jit(solution)/shard_map/ppermute | solution.py:437
  52.5 4.3 %collective-permute-start.17 = (f32[128,128]{1,0:T(8,128)S(1)}, f32[128,128]{1,0:T(8,128)S(1)}, u32[]{:S(2)}, u32[]{:S(2)}) collective-permute-start(f32[128,128]{1,0:T(8,128)S(1)} %add.6.mine), channel_id=1, source_target_pairs={{0,4},{4,0},{1,5},{5,1},{2,6},{6,2},{3,7},{7,3},{8,12},{12,8},{9,1... | collective-permute-start | bytes 196616 | tf_op jit(solution)/shard_map/ppermute | solution.py:437
  56.8 4.3 %collective-permute-start.18 = (f32[128,128]{1,0:T(8,128)S(1)}, f32[128,128]{1,0:T(8,128)S(1)}, u32[]{:S(2)}, u32[]{:S(2)}) collective-permute-start(f32[128,128]{1,0:T(8,128)S(1)} %add.7.mine), channel_id=1, source_target_pairs={{0,8},{8,0},{1,9},{9,1},{2,10},{10,2},{3,11},{11,3},{4,12},{12,4},... | collective-permute-start | bytes 196616 | tf_op jit(solution)/shard_map/ppermute | solution.py:437
  61.2 6.0 %collective-permute-start.19 = (f32[128,128]{1,0:T(8,128)S(1)}, f32[128,128]{1,0:T(8,128)S(1)}, u32[]{:S(2)}, u32[]{:S(2)}) collective-permute-start(f32[128,128]{1,0:T(8,128)S(1)} %add.8.mine), channel_id=1, source_target_pairs={{0,16},{16,0},{1,17},{17,1},{2,18},{18,2},{3,19},{19,3},{4,20},{20... | collective-permute-start | bytes 196616 | tf_op jit(solution)/shard_map/ppermute | solution.py:437
  62.7 13.4 %collective-permute-start.10 = (bf16[256,128]{1,0:T(8,128)(2,1)S(1)}, bf16[256,128]{1,0:T(8,128)(2,1)S(1)}, u32[]{:S(2)}, u32[]{:S(2)}) collective-permute-start(bf16[256,128]{1,0:T(8,128)(2,1)S(1)} %get-tuple-element.71), channel_id=1, source_target_pairs={{0,1},{1,0},{2,3},{3,2},{4,5},{5,4},{6,7},{7,6},{8,9},{9,8},{10,11... | collective-permute-start | bytes 196616 | tf_op jit(solution)/shard_map/ppermute | solution.py:437
  62.7 13.4 %collective-permute-start.11 = (bf16[256,128]{1,0:T(8,128)(2,1)S(1)}, bf16[256,128]{1,0:T(8,128)(2,1)S(1)}, u32[]{:S(2)}, u32[]{:S(2)}) collective-permute-start(bf16[256,128]{1,0:T(8,128)(2,1)S(1)} %get-tuple-element.72), channel_id=1, source_target_pairs={{0,2},{2,0},{1,3},{3,1},{4,6},{6,4},{5,7},{7,5},{8,10},{10,8},{9,1... | collective-permute-start | bytes 196616 | tf_op jit(solution)/shard_map/ppermute | solution.py:437
  64.9 11.2 %collective-permute-start.12 = (bf16[256,128]{1,0:T(8,128)(2,1)S(1)}, bf16[256,128]{1,0:T(8,128)(2,1)S(1)}, u32[]{:S(2)}, u32[]{:S(2)}) collective-permute-start(bf16[256,128]{1,0:T(8,128)(2,1)S(1)} %get-tuple-element.73), channel_id=1, source_target_pairs={{0,4},{4,0},{1,5},{5,1},{2,6},{6,2},{3,7},{7,3},{8,12},{12,8},{9,1... | collective-permute-start | bytes 196616 | tf_op jit(solution)/shard_map/ppermute | solution.py:437
  67.2 9.0 %collective-permute-start.13 = (bf16[256,128]{1,0:T(8,128)(2,1)S(1)}, bf16[256,128]{1,0:T(8,128)(2,1)S(1)}, u32[]{:S(2)}, u32[]{:S(2)}) collective-permute-start(bf16[256,128]{1,0:T(8,128)(2,1)S(1)} %get-tuple-element.74), channel_id=1, source_target_pairs={{0,8},{8,0},{1,9},{9,1},{2,10},{10,2},{3,11},{11,3},{4,12},{12,4},... | collective-permute-start | bytes 196616 | tf_op jit(solution)/shard_map/ppermute | solution.py:437
  67.2 9.0 %collective-permute-start.14 = (bf16[256,128]{1,0:T(8,128)(2,1)S(1)}, bf16[256,128]{1,0:T(8,128)(2,1)S(1)}, u32[]{:S(2)}, u32[]{:S(2)}) collective-permute-start(bf16[256,128]{1,0:T(8,128)(2,1)S(1)} %get-tuple-element.75), channel_id=1, source_target_pairs={{0,16},{16,0},{1,17},{17,1},{2,18},{18,2},{3,19},{19,3},{4,20},{20... | collective-permute-start | bytes 196616 | tf_op jit(solution)/shard_map/ppermute | solution.py:437

commit v2 on v0

v2 whole, which is shorter than its diff:
```python
import functools

import jax
import jax.numpy as jnp
from jax import lax
from jax.experimental import pallas as pl
from jax.experimental.pallas import tpu as pltpu
from jax.sharding import PartitionSpec as P

F32 = jnp.float32
BF16 = jnp.bfloat16
SUB = 8
LANES = 128
ROWS_FIRST = 8
ROWS = 16

VMEM = pl.BlockSpec(memory_space=pltpu.VMEM)
SMEM = pl.BlockSpec(memory_space=pltpu.SMEM)
HBM = pl.BlockSpec(memory_space=pltpu.HBM)
TOKEN = jax.ShapeDtypeStruct((SUB, LANES), F32)


def shape(dims, dtype):
    return jax.ShapeDtypeStruct(dims, dtype)


def nn(a, b):
    return lax.dot_general(a, b, (((1,), (0,)), ((), ())), preferred_element_type=F32)


class Sizes:
    def __init__(self, features, lap_tiles, cross_tiles):
        self.chan = features.shape[0]
        self.blocks, self.nz, self.blk = lap_tiles.shape[:3]
        self.rounds, self.hb = cross_tiles.shape[1:3]
        self.pairs = self.rounds * self.hb
        self.rows = 0
        self.sends = self.pairs
        self.first_row = 2 * self.pairs
        self.first_send = 3 * self.pairs
        self.flags = 4 * self.pairs
        self.live = self.flags + self.rounds
        self.meta = self.live + 1
        self.half = self.hb * self.chan
        self.field = shape((self.blocks, self.chan, self.blk), BF16)
        self.picked = shape((self.pairs, self.chan, self.blk), F32)
        self.pay = shape((2 * self.half, self.blk), BF16)

    def couplings(self):
        return [(r, h, r * self.hb + h) for r in range(self.rounds) for h in range(self.hb)]

    def forward_part(self, h):
        return pl.ds(h * self.chan, self.chan)

    def adjoint_part(self, h):
        return pl.ds(self.half + h * self.chan, self.chan)


def call(kernel, in_specs, out_specs, out_shape, scratch, flops, moved, limit, name, aliases=None):
    return pl.pallas_call(
        kernel,
        in_specs=in_specs,
        out_specs=out_specs,
        out_shape=out_shape,
        scratch_shapes=scratch,
        input_output_aliases=aliases or {},
        compiler_params=pltpu.CompilerParams(vmem_limit_bytes=limit << 20),
        cost_estimate=pl.CostEstimate(flops=flops, bytes_accessed=moved, transcendentals=0),
        name=name,
    )


def fill_pays(sz, meta, tnew, snew, cross, pays):
    for r, h, j in sz.couplings():
        pays[r][sz.forward_part(h), :] = tnew[meta[sz.sends + j]]
        term = nn(snew[meta[sz.rows + j]], cross[j])
        factor = meta[sz.flags + r].astype(F32)
        pays[r][sz.adjoint_part(h), :] = (factor * term).astype(BF16)


def pack_kernel(sz, *refs):
    x4, u4, coupling, send, row, pair, live, col = refs[:8]
    xb, ub, cross, meta, col_out = refs[8:13]
    pays = refs[13 : 13 + sz.rounds]
    send_s, row_s, pair_s, live_s, sem_x, sem_u, sem_t, sem_i = refs[13 + sz.rounds :]
    small = [
        pltpu.make_async_copy(send, send_s, sem_i.at[0]),
        pltpu.make_async_copy(row, row_s, sem_i.at[1]),
        pltpu.make_async_copy(pair, pair_s, sem_i.at[2]),
        pltpu.make_async_copy(live, live_s, sem_i.at[3]),
    ]
    copies = []
    for t in range(sz.chan // SUB):
        part = pl.ds(t * SUB, SUB)
        copies.append(pltpu.make_async_copy(x4.at[t], xb.at[:, part, :], sem_x.at[t]))
        copies.append(pltpu.make_async_copy(u4.at[t], ub.at[:, part, :], sem_u.at[t]))
    copies.append(pltpu.make_async_copy(coupling, cross, sem_t))
    copies.append(pltpu.make_async_copy(col, col_out, sem_i.at[4]))
    for copy in small + copies:
        copy.start()
    for copy in small:
        copy.wait()
    count = live_s[0]
    rows = [lax.rem(row_s[0, h, r], count) for r, h, _ in sz.couplings()]
    sends = [lax.rem(send_s[0, h, r], count) for r, h, _ in sz.couplings()]
    for values, spot, first in (
        (rows, sz.rows, sz.first_row),
        (sends, sz.sends, sz.first_send),
    ):
        for j, value in enumerate(values):
            earliest = jnp.int32(j)
            for q in reversed(range(j)):
                earliest = jnp.where(values[q] == value, q, earliest)
            meta[spot + j] = value
            meta[first + j] = earliest
    for r in range(sz.rounds):
        meta[sz.flags + r] = pair_s[0, r]
    meta[sz.live] = count
    for copy in copies:
        copy.wait()

    def clear(i, carry):
        xb[i] = jnp.zeros(xb.shape[1:], BF16)
        ub[i] = jnp.zeros(ub.shape[1:], BF16)
        return carry

    lax.fori_loop(count, sz.blocks, clear, 0)
    fill_pays(sz, meta, xb, ub, cross, pays)


def pack(sz, x4, u4, coupling, send, row, pair, live, col):
    groups = sz.chan // SUB
    cross = shape((sz.pairs, sz.blk, sz.blk), BF16)
    table = shape((sz.meta,), jnp.int32)
    return call(
        functools.partial(pack_kernel, sz),
        [HBM] * 8,
        [VMEM, VMEM, VMEM, SMEM, VMEM] + [VMEM] * sz.rounds,
        [sz.field, sz.field, cross, table, shape(col.shape, jnp.int32)] + [sz.pay] * sz.rounds,
        [
            pltpu.SMEM(send.shape, jnp.int32),
            pltpu.SMEM(row.shape, jnp.int32),
            pltpu.SMEM(pair.shape, jnp.int32),
            pltpu.SMEM(live.shape, jnp.int32),
            pltpu.SemaphoreType.DMA((groups,)),
            pltpu.SemaphoreType.DMA((groups,)),
            pltpu.SemaphoreType.DMA,
            pltpu.SemaphoreType.DMA((5,)),
        ],
        1000,
        4 << 20,
        8,
        "pack",
    )(x4, u4, coupling, send, row, pair, live, col)


def big_steps(count):
    return (count + ROWS - 1) // ROWS


def clear_sums(sz, summed):
    def clear(i, carry):
        summed[i] = jnp.zeros(summed.shape[1:], F32)
        return carry

    lax.fori_loop(0, sz.blocks, clear, 0, unroll=4)


def scatter_terms(sz, summed, cols, terms):
    for m in range(sz.nz):
        summed[cols[m]] = summed[cols[m]] + terms[:, m * sz.blk : (m + 1) * sz.blk]


def finish_local(sz, meta, held, adjoint, tnew, snew, psel, qsel):
    count = meta[sz.live]

    def finish(g, carry):
        for u in range(ROWS_FIRST):
            i = g * ROWS_FIRST + u
            snew[i] = adjoint(i).astype(BF16)
        return carry

    lax.fori_loop(0, (count + ROWS_FIRST - 1) // ROWS_FIRST, finish, 0)

    def dead(i, carry):
        tnew[i] = jnp.zeros(tnew.shape[1:], BF16)
        snew[i] = jnp.zeros(snew.shape[1:], BF16)
        return carry

    lax.fori_loop(count, sz.blocks, dead, 0)
    for j in range(sz.pairs):
        psel[j] = held[meta[sz.rows + j]]
        qsel[j] = adjoint(meta[sz.sends + j])


def first_kernel(
    sz, meta, col, tiles_hbm, t0, s0, tnew, snew, psel, qsel, tiles, turned, held, summed, sem
):
    count = meta[sz.live]
    steps = big_steps(count) * (ROWS // ROWS_FIRST)

    def fetch(g):
        part = pl.ds(g * ROWS_FIRST, ROWS_FIRST)
        return pltpu.make_async_copy(tiles_hbm.at[part], tiles.at[part], sem.at[g])

    def start(g, carry):
        fetch(g).start()
        return carry

    lax.fori_loop(0, steps, start, 0)
    clear_sums(sz, summed)

    def block_row(i):
        cols = [col[m, i] for m in range(sz.nz)]
        parts = [tiles[i, m] for m in range(sz.nz)]
        flipped = [part.T for part in parts]
        for m in range(sz.nz):
            turned[i, pl.ds(m * sz.blk, sz.blk), :] = flipped[m]
        gathered = jnp.concatenate([t0[c] for c in cols], axis=1)
        forward = nn(gathered, jnp.concatenate(flipped, axis=0))
        held[i] = forward
        tnew[i] = forward.astype(BF16)
        scatter_terms(sz, summed, cols, nn(s0[i], jnp.concatenate(parts, axis=1)))

    def step(g, carry):
        fetch(g).wait()
        for u in range(ROWS_FIRST):
            block_row(g * ROWS_FIRST + u)
        return carry

    lax.fori_loop(0, steps, step, 0)
    finish_local(sz, meta, held, lambda i: summed[i], tnew, snew, psel, qsel)


def first_products(sz, meta, col, tiles, t0, s0):
    turned = shape((sz.blocks, sz.nz * sz.blk, sz.blk), BF16)
    return call(
        functools.partial(first_kernel, sz),
        [SMEM, SMEM, HBM, VMEM, VMEM],
        [VMEM] * 6,
        [sz.field, sz.field, sz.picked, sz.picked, shape(tiles.shape, BF16), turned],
        [pltpu.VMEM((sz.blocks, sz.chan, sz.blk), F32)] * 2
        + [pltpu.SemaphoreType.DMA((sz.blocks // ROWS_FIRST,))],
        4 * sz.blocks * sz.nz * sz.chan * sz.blk * sz.blk,
        12 << 20,
        24,
        "first",
    )(meta, col, tiles, t0, s0)


def local_kernel(sz, grad, *refs):
    meta, col, tiles, turned, tcur, scur, tprev, sprev, _ = refs[:9]
    tnew, snew, psel, qsel, last = refs[9:14]
    held, summed = refs[-2:]
    count = meta[sz.live]
    clear_sums(sz, summed)

    def block_row(i):
        cols = [col[m, i] for m in range(sz.nz)]
        gathered = jnp.concatenate([tcur[c] for c in cols], axis=1)
        forward = 2.0 * nn(gathered, turned[i]) - tprev[i].astype(F32)
        held[i] = forward
        tnew[i] = forward.astype(BF16)
        wide = jnp.concatenate([tiles[i, m] for m in range(sz.nz)], axis=1)
        scatter_terms(sz, summed, cols, nn(scur[i], wide))

    def step(g, carry):
        for u in range(ROWS):
            block_row(g * ROWS + u)
        return carry

    lax.fori_loop(0, big_steps(count), step, 0)

    def adjoint(i):
        return 2.0 * summed[i] - sprev[i].astype(F32)

    finish_local(sz, meta, held, adjoint, tnew, snew, psel, qsel)
    if not grad:
        last[...] = jnp.zeros(last.shape, F32)
        return

    def products(g, total):
        left, right = [], []
        for u in range(ROWS_FIRST):
            i = g * ROWS_FIRST + u
            left.append(jnp.concatenate([tprev[i], tcur[i], tnew[i]], axis=0))
            right.append(jnp.concatenate([sprev[i], scur[i]], axis=0).T)
        return total + nn(jnp.concatenate(left, axis=1), jnp.concatenate(right, axis=0))

    steps = (count + ROWS_FIRST - 1) // ROWS_FIRST
    last[...] = lax.fori_loop(0, steps, products, jnp.zeros(last.shape, F32))


def local_products(sz, meta, col, tiles, turned, fields, token, grad):
    tail = shape((3 * sz.chan, 2 * sz.chan), F32) if grad else TOKEN
    return call(
        functools.partial(local_kernel, sz, grad),
        [SMEM, SMEM] + [VMEM] * 7,
        [VMEM] * 5,
        [sz.field, sz.field, sz.picked, sz.picked, tail],
        [pltpu.VMEM((sz.blocks, sz.chan, sz.blk), F32)] * 2,
        4 * sz.blocks * sz.nz * sz.chan * sz.blk * sz.blk,
        12 << 20,
        24,
        "local",
    )(meta, col, tiles, turned, *fields, token)


def add_coupled(sz, scale, meta, got, cross, psel, qsel, pacc, qacc):
    for j in range(sz.pairs):
        pacc[j] = psel[j]
        qacc[j] = qsel[j]
    terms = []
    for r, h, j in sz.couplings():
        factor = scale * meta[sz.flags + r].astype(F32)
        terms.append(factor * nn(got[r][sz.forward_part(h), :], cross[j].T))
        spot = meta[sz.first_row + j]
        pacc[spot] = pacc[spot] + terms[j]
        spot = meta[sz.first_send + j]
        qacc[spot] = qacc[spot] + scale * got[r][sz.adjoint_part(h), :].astype(F32)
    return terms


def join_kernel(sz, scale, grad, *refs):
    refs = list(refs)
    meta, cross, tbase, sbase, psel, qsel = refs[:6]
    got, refs = refs[6 : 6 + sz.rounds], refs[6 + sz.rounds :]
    if grad:
        gram, sold = refs[:2]
        refs = refs[2:]
    tnew, snew = refs[:2]
    pays, refs = refs[2 : 2 + sz.rounds], refs[2 + sz.rounds :]
    if grad:
        partial, refs = refs[0], refs[1:]
    pacc, qacc = refs
    terms = add_coupled(sz, scale, meta, got, cross, psel, qsel, pacc, qacc)

    def move(i, carry):
        tnew[i] = tbase[i]
        snew[i] = sbase[i]
        return carry

    lax.fori_loop(0, sz.blocks, move, 0, unroll=4)
    for j in range(sz.pairs):
        tnew[meta[sz.rows + j]] = pacc[meta[sz.first_row + j]].astype(BF16)
        snew[meta[sz.sends + j]] = qacc[meta[sz.first_send + j]].astype(BF16)
    fill_pays(sz, meta, tnew, snew, cross, pays)
    if grad:
        left = jnp.concatenate([term.astype(BF16) for term in terms], axis=1)
        right = [sold[meta[sz.rows + j]].T for j in range(sz.pairs)]
        extra = nn(left, jnp.concatenate(right, axis=0))
        one, two, three = (pl.ds(k * sz.chan, sz.chan) for k in range(3))
        partial[one, one] = gram[one, one]
        partial[two, :] = gram[two, :]
        partial[one, two] = gram[three, two] + extra


def join(sz, scale, meta, cross, base, got, gram=None, sold=None):
    outs = [sz.field, sz.field] + [sz.pay] * sz.rounds
    args = [meta, cross, *base, *got]
    if gram is not None:
        args += [gram, sold]
        outs.append(shape((2 * sz.chan, 2 * sz.chan), F32))
    outs = call(
        functools.partial(join_kernel, sz, scale, gram is not None),
        [SMEM] + [VMEM] * (len(args) - 1),
        [VMEM] * len(outs),
        outs,
        [pltpu.VMEM(sz.picked.shape, F32)] * 2,
        4 * sz.pairs * sz.chan * sz.blk * sz.blk,
        6 << 20,
        12,
        "join",
    )(*args)
    return outs[0], outs[1], outs[2 : 2 + sz.rounds], outs[2 + sz.rounds :]


def output_weights(weight):
    wide = [weight[k].astype(F32) for k in range(weight.shape[0])]
    ahead = jnp.concatenate([w.T for w in wide], axis=1).astype(BF16)
    back = jnp.concatenate(wide, axis=1).astype(BF16)
    return ahead, back


def output_kernel(sz, low, high, *refs):
    meta, weight = refs[:2]
    forward, adjoint = refs[2:6], refs[6:10]
    refs = refs[11:] if low == 0 else refs[13:]
    out4, grad4, token, held_out, held_grad, sem = refs
    count = meta[sz.live]
    ahead, back = output_weights(weight)
    groups = sz.chan // SUB

    def block(i):
        for left, fields, held in ((ahead, forward, held_out), (back, adjoint, held_grad)):
            value = nn(left, jnp.concatenate([f[i] for f in fields], axis=0)).astype(BF16)
            for t in range(groups):
                held[t, i - low] = value[t * SUB : (t + 1) * SUB]

    def step(g, carry):
        for u in range(ROWS_FIRST):
            block(g * ROWS_FIRST + u)
        return carry

    end = jnp.minimum((count + ROWS_FIRST - 1) // ROWS_FIRST, high // ROWS_FIRST)
    lax.fori_loop(low // ROWS_FIRST, end, step, 0)

    def dead(i, carry):
        for t in range(groups):
            held_out[t, i - low] = jnp.zeros((SUB, sz.blk), BF16)
            held_grad[t, i - low] = jnp.zeros((SUB, sz.blk), BF16)
        return carry

    lax.fori_loop(jnp.maximum(count, low), high, dead, 0)
    part = pl.ds(low, high - low)
    copies = [
        pltpu.make_async_copy(held_out, out4.at[:, part], sem.at[0]),
        pltpu.make_async_copy(held_grad, grad4.at[:, part], sem.at[1]),
    ]
    for copy in copies:
        copy.start()
    token[...] = jnp.zeros(token.shape, F32)
    for copy in copies:
        copy.wait()


def base_outputs(sz, low, high, meta, weight, forward, adjoint, token, before):
    out = shape((sz.chan // SUB, sz.blocks, SUB, sz.blk), BF16)
    args = [meta, weight, *forward, *adjoint, token]
    specs = [SMEM] + [VMEM] * (len(args) - 1)
    aliases = {}
    if low > 0:
        aliases = {len(args): 0, len(args) + 1: 1}
        args += before
        specs += [HBM] * 2
    held = pltpu.VMEM((sz.chan // SUB, high - low, SUB, sz.blk), BF16)
    return call(
        functools.partial(output_kernel, sz, low, high),
        specs,
        [HBM, HBM, VMEM],
        [out, out, TOKEN],
        [held, held, pltpu.SemaphoreType.DMA((2,))],
        16 * (high - low) * sz.chan * sz.chan * sz.blk,
        10 << 20,
        8,
        "outputs",
        aliases,
    )(*args)


def fix_kernel(sz, *refs):
    meta, cross, weight, psel, qsel = refs[:5]
    got, refs = refs[5 : 5 + sz.rounds], refs[5 + sz.rounds :]
    forward, adjoint = refs[:3], refs[3:6]
    mine, theirs = refs[6:8]
    out4, grad4, grad_w, pacc, qacc, held_out, held_grad, sem = refs[10:]
    add_coupled(sz, 2.0, meta, got, cross, psel, qsel, pacc, qacc)
    ahead, back = output_weights(weight)
    groups = sz.chan // SUB
    copies = []
    for j in range(sz.pairs):
        for left, fields, last, spot, first, held, out, s in (
            (ahead, forward, pacc, sz.rows, sz.first_row, held_out, out4, 0),
            (back, adjoint, qacc, sz.sends, sz.first_send, held_grad, grad4, 1),
        ):
            i, slot = meta[spot + j], meta[first + j]
            stack = [f[i] for f in fields] + [last[slot].astype(BF16)]
            value = nn(left, jnp.concatenate(stack, axis=0)).astype(BF16)
            for t in range(groups):
                held[j, t] = value[t * SUB : (t + 1) * SUB]
            copies.append((slot == j, pltpu.make_async_copy(held.at[j], out.at[:, i], sem.at[s, j])))
    for own, copy in copies:
        pl.when(own)(copy.start)
    one, two = pl.ds(0, sz.chan), pl.ds(sz.chan, sz.chan)

    def total(a, b):
        return mine[a, b] + theirs[a, b]

    zeroth, first = total(one, one), total(two, one)
    grad_w[0] = zeroth
    grad_w[1] = first
    grad_w[2] = 2.0 * total(two, two) - zeroth
    grad_w[3] = 2.0 * total(one, two) - first
    for own, copy in copies:
        pl.when(own)(copy.wait)


def fix_outputs(sz, meta, cross, weight, picked, got, forward, adjoint, mine, theirs, before):
    out = shape(before[0].shape, BF16)
    args = [meta, cross, weight, *picked, *got, *forward, *adjoint, mine, theirs]
    held = pltpu.VMEM((sz.pairs, sz.chan // SUB, SUB, sz.blk), BF16)
    return call(
        functools.partial(fix_kernel, sz),
        [SMEM] + [VMEM] * (len(args) - 1) + [HBM] * 2,
        [HBM, HBM, VMEM],
        [out, out, shape((4, sz.chan, sz.chan), F32)],
        [pltpu.VMEM(sz.picked.shape, F32)] * 2 + [held, held]
        + [pltpu.SemaphoreType.DMA((2, sz.pairs))],
        8 * sz.pairs * sz.chan * sz.blk * sz.blk,
        4 << 20,
        10,
        "fix",
        {len(args): 0, len(args) + 1: 1},
    )(*args, *before)


def add_kernel(gated, *refs):
    mine, theirs, _ = refs[:3]
    if gated:
        pay, out, token, pay_out = refs[3:]
        pay_out[...] = pay[...]
    else:
        out, token = refs[3:]
    out[...] = mine[...] + theirs[...]
    token[...] = jnp.zeros(token.shape, F32)


def add(mine, theirs, token, pay):
    outs = [shape(mine.shape, F32), TOKEN]
    args = [mine, theirs, token]
    if pay is not None:
        outs.append(shape(pay.shape, BF16))
        args.append(pay)
    return call(
        functools.partial(add_kernel, pay is not None),
        [VMEM] * len(args),
        [VMEM] * len(outs),
        outs,
        [],
        mine.size,
        12 * mine.size,
        2,
        "add",
    )(*args)


def from_partner(values, bit):
    count = lax.axis_size("dom")
    route = []
    for low in range(count):
        high = low | 1 << bit
        if high != low and high < count:
            route += [(low, high), (high, low)]
    return lax.ppermute(values, "dom", route)


def local(
    features,
    cheb_weight,
    lap_tiles,
    col_index,
    cross_tiles,
    send_index,
    row_index,
    pair_on,
    blk_live,
    cotangent,
):
    sz = Sizes(features, lap_tiles, cross_tiles)
    split = (sz.chan // SUB, SUB, sz.blocks, sz.blk)
    x4 = features.reshape(split).transpose(0, 2, 1, 3)
    u4 = cotangent.reshape(split).transpose(0, 2, 1, 3)
    coupling = cross_tiles.reshape(sz.pairs, sz.blk, sz.blk)
    send, row = send_index.transpose(0, 2, 1), row_index.transpose(0, 2, 1)

    packed = pack(sz, x4, u4, coupling, send, row, pair_on, blk_live, col_index.T)
    t0, s0, cross, meta, col = packed[:5]
    got = [from_partner(pay, bit) for bit, pay in enumerate(packed[5:])]
    *base, tiles, turned = first_products(sz, meta, col, lap_tiles, t0, s0)
    t1, s1, pays, _ = join(sz, 1.0, meta, cross, base, got)

    got = [from_partner(pay, bit) for bit, pay in enumerate(pays)]
    fields = (t1, s1, t0, s0)
    *base, gram = local_products(sz, meta, col, tiles, turned, fields, cross, True)
    t2, s2, pays, (mine,) = join(sz, 2.0, meta, cross, base, got, gram, s1)

    state = {}

    def window_products(token):
        fields = (t2, s2, t1, s1)
        *base, token = local_products(sz, meta, col, tiles, turned, fields, token, False)
        state["base"] = base
        return token

    def window_outputs(low, high):
        def window(token):
            forward = (t0, t1, t2, state["base"][0])
            adjoint = (s0, s1, s2, state["base"][1])
            out4, grad4, token = base_outputs(
                sz, low, high, meta, cheb_weight, forward, adjoint, token, state.get("outs", [])
            )
            state["outs"] = [out4, grad4]
            return token

        return window

    middle = sz.blocks // (2 * ROWS_FIRST) * ROWS_FIRST
    windows = [window_products, window_outputs(0, middle), window_outputs(middle, sz.blocks)]
    bits = list(reversed(range((lax.axis_size("dom") - 1).bit_length())))
    pays, got = list(pays), [None] * sz.rounds
    token = mine
    for at, bit in enumerate(bits):
        if bit < sz.rounds:
            got[bit] = from_partner(pays[bit], bit)
        theirs = from_partner(mine, bit)
        if at < len(windows):
            token = windows[at](token)
        if at + 1 < len(bits):
            later = bits[at + 1]
            gated = later < sz.rounds
            mine, token, *rest = add(mine, theirs, token, pays[later] if gated else None)
            if gated:
                pays[later] = rest[0]
    out4, grad4, grad_w = fix_outputs(
        sz,
        meta,
        cross,
        cheb_weight,
        state["base"][2:4],
        got,
        (t0, t1, t2),
        (s0, s1, s2),
        mine,
        theirs,
        state["outs"],
    )
    conv_out = out4.transpose(0, 2, 1, 3).reshape(features.shape)
    grad_x = grad4.transpose(0, 2, 1, 3).reshape(features.shape)
    return (conv_out, grad_x, grad_w)


def solution(mesh):
    in_specs = (
        P(None, "dom"),
        P(),
        P("dom", None, None, None),
        P("dom", None),
        P("dom", None, None, None, None),
        P("dom", None, None),
        P("dom", None, None),
        P("dom", None),
        P("dom"),
        P(None, "dom"),
    )
    out_specs = (P(None, "dom"), P(None, "dom"), P())
    return jax.shard_map(local, mesh=mesh, in_specs=in_specs, out_specs=out_specs, check_vma=False)
```

time: 546 us -> 65.3 us (0.12)
  other arithmetic: 190 us -> 0 us
  waiting for transfers between devices: 125 us -> 3.1 us
  matrix products: 91 us -> 0 us
  local copies, waits for them, and re-layouts: 80.2 us -> 8.89 us
  Pallas kernels: 0 us -> 29.8 us
  starting transfers between devices: 37.6 us -> 21.7 us
  between operations: 15.7 us -> 1.5 us
    psum x1 -> x0, waiting for transfers between devices: 123 us -> none  [local(): grad_w = lax.psum(weight_terms, 'dom')]
    scatter-add x33 -> x0, other arithmetic: 118 us -> none  [the longest x3 60 us: local_adjoint(): jnp.zeros((channels, block_count, block_size), jnp.float32).at[:, col_index]]
    dot_general x39 -> x0, matrix products: 91 us -> none  [the longest x3 23.2 us: apply_forward(): jnp.einsum('inab,finb->fia', lap_tiles, gathered, preferred_element_type=...]
    gather x33 -> x0, local copies, waits for them, and re-layouts: 57.7 us -> none  [the longest x15 23.7 us: apply_adjoint(): slices = jnp.take(values, recv_rows[level], axis=1)]
    select_n x52 -> x0, other arithmetic: 39.5 us -> none  [the longest x20 13.8 us: apply_adjoint(): slices = jnp.take(values, recv_rows[level], axis=1)]
    pallas_call x0 -> x13, Pallas kernels: none -> 29.8 us  [the longest x2 10.8 us: local_products(): call(functools.partial(local_kernel, sz, grad), [SMEM, SMEM] + [VMEM] * 7...]
    ppermute x35 -> x20, starting transfers between devices: 37.5 us -> 21.7 us  [from_partner(): return lax.ppermute(values, 'dom', route)]
    and x11 -> x0, other arithmetic: 8.75 us -> none  [the longest x5 4.63 us: apply_forward(): outgoing = jnp.take(values, send_rows[level], axis=1)]
  transfers between devices with their start and end apart: 36 -> 20, of which waited for: 5 -> 4; matrix products, arithmetic and copies ran while one was open for 46% -> 0% of each run, Pallas kernels for 0% -> 35%
where the time goes in v2:
time: 65.3 us; the launch traced here: 65 us
  Pallas kernels  29.8 us (46%)
  starting transfers between devices  21.7 us (33%)
  local copies, waits for them, and re-layouts  8.89 us (14%)
  waiting for transfers between devices  3.1 us (5%)
  between operations  1.5 us (2%)
    ppermute x20, starting transfers between devices, from_partner(): return lax.ppermute(values, 'dom', route)  21.7 us
    pallas_call x2, Pallas kernels, local_products(): call(functools.partial(local_kernel, sz, grad), [SMEM, SMEM] + [VMEM] * 7...  10.8 us
    unnamed x18, local copies, waits for them, and re-layouts  8.89 us
    pallas_call x2, Pallas kernels, base_outputs(): call(functools.partial(output_kernel, sz, low, high), specs, [HBM, HBM, V...  5.73 us
    pallas_call x1, Pallas kernels, first_products(): call(functools.partial(first_kernel, sz), [SMEM, SMEM, HBM, VMEM, VMEM],...  5.31 us
    ppermute x20, waiting for transfers between devices, from_partner(): return lax.ppermute(values, 'dom', route)  3.1 us
    pallas_call x2, Pallas kernels, join(): call(functools.partial(join_kernel, sz, scale, gram is not None), [SMEM]...  2.82 us
    pallas_call x1, Pallas kernels, fix_outputs(): call(functools.partial(fix_kernel, sz), [SMEM] + [VMEM] * (len(args) - 1)...  2.73 us
  transfers between devices with their start and end apart: 20, of which 4 were waited for; matrix products, arithmetic and copies ran while one was open for 0% of the time, Pallas kernels for 35%

profile of v2, /device:TPU:0, one launch (start us, length us, event | category | flops | bytes accessed | tf_op | source)
XLA Modules:
  0.0 65.0 jit_solution(17119624471796634683)
XLA Ops:
  1.3 1.2 %copy-done.1 = bf16[64,8192]{1,0:T(8,128)(2,1)S(1)} copy-done((bf16[64,8192]{1,0:T(8,128)(2,1)S(1)}, bf16[64,8192]{1,0:T(8,128)(2,1)}, u32[]{:S(2)}) %copy-start.1) | copy-done | bytes 1048600
  2.5 1.2 %copy-done.2 = bf16[64,8192]{1,0:T(8,128)(2,1)S(1)} copy-done((bf16[64,8192]{1,0:T(8,128)(2,1)S(1)}, bf16[64,8192]{1,0:T(8,128)(2,1)}, u32[]{:S(2)}) %copy-start.2) | copy-done | bytes 1048600
  3.7 1.0 %copy-done.4 = bf16[1,5,2,128,128]{4,3,2,1,0:T(8,128)(2,1)S(1)} copy-done((bf16[1,5,2,128,128]{4,3,2,1,0:T(8,128)(2,1)S(1)}, bf16[1,5,2,128,128]{4,3,2,1,0:T(8,128)(2,1)}, u32[]{:S(2)}) %copy-start.4) | copy-done | bytes 327704
  4.7 0.7 %copy-done.5 = s32[64,3]{0,1:T(4,128)S(1)} copy-done((s32[64,3]{0,1:T(4,128)S(1)}, s32[64,3]{0,1:T(4,128)}, u32[]{:S(2)}) %copy-start.5) | copy-done | bytes 792
  5.4 0.7 %copy-done.6 = s32[1,5,2]{1,2,0:T(2,128)S(1)} copy-done((s32[1,5,2]{1,2,0:T(2,128)S(1)}, s32[1,5,2]{1,2,0:T(2,128)}, u32[]{:S(2)}) %copy-start.6) | copy-done | bytes 64
  6.1 0.7 %copy-done.7 = s32[1,5,2]{1,2,0:T(2,128)S(1)} copy-done((s32[1,5,2]{1,2,0:T(2,128)S(1)}, s32[1,5,2]{1,2,0:T(2,128)}, u32[]{:S(2)}) %copy-start.7) | copy-done | bytes 64
  6.7 0.7 %copy-done.8 = s32[1,5]{1,0:T(1,128)S(1)} copy-done((s32[1,5]{1,0:T(1,128)S(1)}, s32[1,5]{1,0:T(1,128)}, u32[]{:S(2)}) %copy-start.8) | copy-done | bytes 44
  7.4 1.7 %pack.1 = (bf16[64,64,128]{2,1,0:T(8,128)(2,1)S(1)}, bf16[64,64,128]{2,1,0:T(8,128)(2,1)S(1)}, bf16[10,128,128]{2,1,0:T(8,128)(2,1)S(1)}, s32[46]{0:T(128)S(1)},...) custom-call(bf16[8,64,8,128]{3,2,1,0:T(8,128)(2,1)S(1)} %bitcast.16,, ...), custom_call_target="tpu_custom_call" | custom-call | flops 1000 | bytes 4194304 | tf_op jit(solution)/shard_map/pack/pallas_call | solution.py:135
  9.1 0.6 collective-permute-start
  9.7 2.7 %collective-permute-start.1 = (bf16[256,128]{1,0:T(8,128)(2,1)S(1)}, bf16[256,128]{1,0:T(8,128)(2,1)S(1)}, u32[]{:S(2)}, u32[]{:S(2)}) collective-permute-start(bf16[256,128]{1,0:T(8,128)(2,1)S(1)} %get-tuple-element.76), channel_id=1, source_target_pairs={{0,2},{2,0},{1,3},{3,1},{4,6},{6,4},{5,7},{7,5},{8,10},{10,8},{9,1... | collective-permute-start | bytes 196616 | tf_op jit(solution)/shard_map/ppermute | solution.py:544
  12.4 1.6 %collective-permute-start.2 = (bf16[256,128]{1,0:T(8,128)(2,1)S(1)}, bf16[256,128]{1,0:T(8,128)(2,1)S(1)}, u32[]{:S(2)}, u32[]{:S(2)}) collective-permute-start(bf16[256,128]{1,0:T(8,128)(2,1)S(1)} %get-tuple-element.77), channel_id=1, source_target_pairs={{0,4},{4,0},{1,5},{5,1},{2,6},{6,2},{3,7},{7,3},{8,12},{12,8},{9,1... | collective-permute-start | bytes 196616 | tf_op jit(solution)/shard_map/ppermute | solution.py:544
  14.0 1.3 %collective-permute-start.3 = (bf16[256,128]{1,0:T(8,128)(2,1)S(1)}, bf16[256,128]{1,0:T(8,128)(2,1)S(1)}, u32[]{:S(2)}, u32[]{:S(2)}) collective-permute-start(bf16[256,128]{1,0:T(8,128)(2,1)S(1)} %get-tuple-element.78), channel_id=1, source_target_pairs={{0,8},{8,0},{1,9},{9,1},{2,10},{10,2},{3,11},{11,3},{4,12},{12,4},... | collective-permute-start | bytes 196616 | tf_op jit(solution)/shard_map/ppermute | solution.py:544
  15.3 2.9 %collective-permute-start.4 = (bf16[256,128]{1,0:T(8,128)(2,1)S(1)}, bf16[256,128]{1,0:T(8,128)(2,1)S(1)}, u32[]{:S(2)}, u32[]{:S(2)}) collective-permute-start(bf16[256,128]{1,0:T(8,128)(2,1)S(1)} %get-tuple-element.79), channel_id=1, source_target_pairs={{0,16},{16,0},{1,17},{17,1},{2,18},{18,2},{3,19},{19,3},{4,20},{20... | collective-permute-start | bytes 196616 | tf_op jit(solution)/shard_map/ppermute | solution.py:544
  18.2 2.8 %copy-done = bf16[64,3,128,128]{3,2,1,0:T(8,128)(2,1)S(1)} copy-done((bf16[64,3,128,128]{3,2,1,0:T(8,128)(2,1)S(1)}, bf16[64,3,128,128]{3,2,1,0:T(8,128)(2,1)}, u32[]{:S(2)}) %copy-start) | copy-done | bytes 6291480
  21.0 5.3 %first.1 = (bf16[64,64,128]{2,1,0:T(8,128)(2,1)S(1)}, bf16[64,64,128]{2,1,0:T(8,128)(2,1)S(1)}, f32[10,64,128]{2,1,0:T(8,128)S(1)}, f32[10,64,128]{2,1,0:T(8,128...) custom-call(s32[46]{0:T(128)S(1)} %get-tuple-element.64.meta.refs_0_, ...), custom_call_target="tpu_custom_call" | custom-call | flops 805306368 | bytes 12582912 | tf_op jit(solution)/shard_map/first/pallas_call | solution.py:237
  26.3 0.0 collective-permute-done.refs_6_
  26.3 0.0 collective-permute-done.1.refs_7_
  26.3 0.0 collective-permute-done.2.refs_8_
  26.3 0.0 collective-permute-done.3.refs_9_
  26.4 0.0 collective-permute-done.4.refs_10_
  26.4 1.3 %join.2 = (bf16[64,64,128]{2,1,0:T(8,128)(2,1)S(1)}, bf16[64,64,128]{2,1,0:T(8,128)(2,1)S(1)}, bf16[256,128]{1,0:T(8,128)(2,1)S(1)}, bf16[256,128]{1,0:T(8,128)(...) custom-call(s32[46]{0:T(128)S(1)} %get-tuple-element.64.meta.refs_0_, ...), custom_call_target="tpu_custom_call" | custom-call | flops 41943040 | bytes 6291456 | tf_op jit(solution)/shard_map/join/pallas_call | solution.py:364
  27.7 0.1 collective-permute-start.5
  27.8 0.1 collective-permute-start.6
  27.9 0.4 collective-permute-start.7
  28.2 0.9 %collective-permute-start.8 = (bf16[256,128]{1,0:T(8,128)(2,1)S(1)}, bf16[256,128]{1,0:T(8,128)(2,1)S(1)}, u32[]{:S(2)}, u32[]{:S(2)}) collective-permute-start(bf16[256,128]{1,0:T(8,128)(2,1)S(1)} %get-tuple-element.89), channel_id=1, source_target_pairs={{0,8},{8,0},{1,9},{9,1},{2,10},{10,2},{3,11},{11,3},{4,12},{12,4},... | collective-permute-start | bytes 196616 | tf_op jit(solution)/shard_map/ppermute | solution.py:544
  29.2 0.0 collective-permute-start.9
  29.2 6.7 %local.2 = (bf16[64,64,128]{2,1,0:T(8,128)(2,1)S(1)}, bf16[64,64,128]{2,1,0:T(8,128)(2,1)S(1)}, f32[10,64,128]{2,1,0:T(8,128)S(1)}, f32[10,64,128]{2,1,0:T(8,128)S(1)}, f32[192,128]{1,0:T(8,128)S(1)}) custom-call(s32[46]{0:T(128)S(1)} %get-tuple-element.64.meta.refs_0_, s32[3,64]{1,0:T(4,128)S(1)} %get-tuple-element.66.col.refs_1_, ...), custom_call_target="tpu_custom_call" | custom-call | flops 805306368 | bytes 12582912 | tf_op jit(solution)/shard_map/local/pallas_call | solution.py:296
  35.9 0.0 collective-permute-done.7.refs_8_
  36.0 1.5 %join.3 = (bf16[64,64,128]{2,1,0:T(8,128)(2,1)S(1)}, bf16[64,64,128]{2,1,0:T(8,128)(2,1)S(1)}, bf16[256,128]{1,0:T(8,128)(2,1)S(1)}, bf16[256,128]{1,0:T(8,128)(...) custom-call(s32[46]{0:T(128)S(1)} %get-tuple-element.64.meta.refs_0_, ...), custom_call_target="tpu_custom_call" | custom-call | flops 41943040 | bytes 6291456 | tf_op jit(solution)/shard_map/join/pallas_call | solution.py:364
  37.5 1.7 %collective-permute-start.10 = (f32[128,128]{1,0:T(8,128)S(1)}, f32[128,128]{1,0:T(8,128)S(1)}, u32[]{:S(2)}, u32[]{:S(2)}) collective-permute-start(f32[128,128]{1,0:T(8,128)S(1)} %get-tuple-element.94.refs_8_.refs_0_), channel_id=1, source_target_pairs={{0,16},{16,0},{1,17},{17,1},{2,18},{18,2},{3,19},{19,3},{4,20},{20... | collective-permute-start | bytes 196616 | tf_op jit(solution)/shard_map/ppermute | solution.py:544
  39.1 4.1 %local.3 = (bf16[64,64,128]{2,1,0:T(8,128)(2,1)S(1)}, bf16[64,64,128]{2,1,0:T(8,128)(2,1)S(1)}, f32[10,64,128]{2,1,0:T(8,128)S(1)}, f32[10,64,128]{2,1,0:T(8,128)S(1)}, f32[8,128]{1,0:T(8,128)S(1)}) custom-call(s32[46]{0:T(128)S(1)} %get-tuple-element.64.meta.refs_0_, s32[3,64]{1,0:T(4,128)S(1)} %get-tuple-element.66.col.refs_1_, ...), custom_call_target="tpu_custom_call" | custom-call | flops 805306368 | bytes 12582912 | tf_op jit(solution)/shard_map/local/pallas_call | solution.py:296
  43.3 0.1 collective-permute-done.10.refs_1_
  43.4 0.1 collective-permute-start.11
  43.5 2.9 %outputs.2 = (bf16[8,64,8,128]{3,2,1,0:T(8,128)(2,1)}, bf16[8,64,8,128]{3,2,1,0:T(8,128)(2,1)}, f32[8,128]{1,0:T(8,128)S(1)}) custom-call(s32[46]{0:T(128)S(1)} %get-tuple-element.64.meta.refs_0_, bf16[4,64,64]{2,1,0:T(8,128)(2,1)S(1)} %copy-done.3, bf16[64,64,128]{2,1,0:T(8,128)(2,1)S(1)} %get-tuple-element.67.t0.refs_6_.refs_2_.refs_10_, ...), custom_call_target="tpu_custom_call" | custom-call | flops 268435456 | bytes 10485760 | tf_op jit(solution)/shard_map/outputs/pallas_call | solution.py:437
  46.4 1.4 %collective-permute-done.11.refs_1_ = f32[128,128]{1,0:T(8,128)S(1)} collective-permute-done((f32[128,128]{1,0:T(8,128)S(1)}, f32[128,128]{1,0:T(8,128)S(1)}, u32[]{:S(2)}, u32[]{:S(2)}) %collective-permute-start.11) | collective-permute-done | bytes 65568 | tf_op jit(solution)/shard_map/ppermute | solution.py:544
  47.8 2.1 %collective-permute-start.12 = (f32[128,128]{1,0:T(8,128)S(1)}, f32[128,128]{1,0:T(8,128)S(1)}, u32[]{:S(2)}, u32[]{:S(2)}) collective-permute-start(f32[128,128]{1,0:T(8,128)S(1)} %get-tuple-element.105.refs_0_), channel_id=1, source_target_pairs={{0,4},{4,0},{1,5},{5,1},{2,6},{6,2},{3,7},{7,3},{8,12},{12,8},{9,1... | collective-permute-start | bytes 196616 | tf_op jit(solution)/shard_map/ppermute | solution.py:544
  49.9 2.9 %outputs.3 = (bf16[8,64,8,128]{3,2,1,0:T(8,128)(2,1)}, bf16[8,64,8,128]{3,2,1,0:T(8,128)(2,1)}, f32[8,128]{1,0:T(8,128)S(1)}) custom-call(s32[46]{0:T(128)S(1)} %get-tuple-element.64.meta.refs_0_, bf16[4,64,64]{2,1,0:T(8,128)(2,1)S(1)} %copy-done.3, ...), custom_call_target="tpu_custom_call", output_to_operand_aliasing={{0}: (11, {}), {1}: (12, {})} | custom-call | flops 268435456 | bytes 10485760 | tf_op jit(solution)/shard_map/outputs/pallas_call | solution.py:437
  52.8 0.0 collective-permute-done.12.refs_1_
  52.8 0.9 %collective-permute-start.13 = (f32[128,128]{1,0:T(8,128)S(1)}, f32[128,128]{1,0:T(8,128)S(1)}, u32[]{:S(2)}, u32[]{:S(2)}) collective-permute-start(f32[128,128]{1,0:T(8,128)S(1)} %get-tuple-element.111.refs_0_), channel_id=1, source_target_pairs={{0,2},{2,0},{1,3},{3,1},{4,6},{6,4},{5,7},{7,5},{8,10},{10,8},{9,1... | collective-permute-start | bytes 196616 | tf_op jit(solution)/shard_map/ppermute | solution.py:544
  53.7 2.5 %collective-permute-start.18 = (bf16[256,128]{1,0:T(8,128)(2,1)S(1)}, bf16[256,128]{1,0:T(8,128)(2,1)S(1)}, u32[]{:S(2)}, u32[]{:S(2)}) collective-permute-start(bf16[256,128]{1,0:T(8,128)(2,1)S(1)} %get-tuple-element.118), channel_id=1, source_target_pairs={{0,16},{16,0},{1,17},{17,1},{2,18},{18,2},{3,19},{19,3},{4,20},{20... | collective-permute-start | bytes 196616 | tf_op jit(solution)/shard_map/ppermute | solution.py:544
  56.2 1.4 %collective-permute-start.17 = (bf16[256,128]{1,0:T(8,128)(2,1)S(1)}, bf16[256,128]{1,0:T(8,128)(2,1)S(1)}, u32[]{:S(2)}, u32[]{:S(2)}) collective-permute-start(bf16[256,128]{1,0:T(8,128)(2,1)S(1)} %get-tuple-element.117), channel_id=1, source_target_pairs={{0,8},{8,0},{1,9},{9,1},{2,10},{10,2},{3,11},{11,3},{4,12},{12,4},... | collective-permute-start | bytes 196616 | tf_op jit(solution)/shard_map/ppermute | solution.py:544
  57.6 0.4 collective-permute-start.16
  58.0 1.6 %collective-permute-start.15 = (bf16[256,128]{1,0:T(8,128)(2,1)S(1)}, bf16[256,128]{1,0:T(8,128)(2,1)S(1)}, u32[]{:S(2)}, u32[]{:S(2)}) collective-permute-start(bf16[256,128]{1,0:T(8,128)(2,1)S(1)} %get-tuple-element.115), channel_id=1, source_target_pairs={{0,2},{2,0},{1,3},{3,1},{4,6},{6,4},{5,7},{7,5},{8,10},{10,8},{9,1... | collective-permute-start | bytes 196616 | tf_op jit(solution)/shard_map/ppermute | solution.py:544
  59.6 0.6 add.7
  60.2 0.5 collective-permute-start.19
  60.7 1.1 %collective-permute-done.16.refs_7_ = bf16[256,128]{1,0:T(8,128)(2,1)S(1)} collective-permute-done((bf16[256,128]{1,0:T(8,128)(2,1)S(1)}, bf16[256,128]{1,0:T(8,128)(2,1)S(1)}, u32[]{:S(2)}, u32[]{:S(2)}) %collective-permute-start.16) | collective-permute-done | bytes 65568 | tf_op jit(solution)/shard_map/ppermute | solution.py:544
  61.8 0.4 collective-permute-done.15.refs_6_
  62.3 2.7 %fix.1 = (bf16[8,64,8,128]{3,2,1,0:T(8,128)(2,1)}, bf16[8,64,8,128]{3,2,1,0:T(8,128)(2,1)}, f32[4,64,64]{2,1,0:T(8,128)}) custom-call(s32[46]{0:T(128)S(1)} %get-tuple-element.64.meta.refs_0_, bf16[10,128,128]{2,1,0:T(8,128)(2,1)S(1)} %get-tuple-element.65.refs_1_.refs_8_, ...), custom_call_target="tpu_custom_call", output_to_operand_aliasing={{0}: (18, {}), {1}: (19, {})} | custom-call | flops 83886080 | bytes 4194304 | tf_op jit(solution)/shard_map/fix/pallas_call | solution.py:492
  (23 shorter events, 0.1 us)
Async XLA Ops:
  1.3 1.2 %copy-start.1 = (bf16[64,8192]{1,0:T(8,128)(2,1)S(1)}, bf16[64,8192]{1,0:T(8,128)(2,1)}, u32[]{:S(2)}) copy-start(bf16[64,8192]{1,0:T(8,128)(2,1)} %param.10) | copy-start | bytes 3145732
  2.5 1.2 %copy-start.2 = (bf16[64,8192]{1,0:T(8,128)(2,1)S(1)}, bf16[64,8192]{1,0:T(8,128)(2,1)}, u32[]{:S(2)}) copy-start(bf16[64,8192]{1,0:T(8,128)(2,1)} %param.19) | copy-start | bytes 3145732
  3.7 1.0 %copy-start.4 = (bf16[1,5,2,128,128]{4,3,2,1,0:T(8,128)(2,1)S(1)}, bf16[1,5,2,128,128]{4,3,2,1,0:T(8,128)(2,1)}, u32[]{:S(2)}) copy-start(bf16[1,5,2,128,128]{4,3,2,1,0:T(8,128)(2,1)} %param.14) | copy-start | bytes 983044
  4.7 0.7 %copy-start.5 = (s32[64,3]{0,1:T(4,128)S(1)}, s32[64,3]{0,1:T(4,128)}, u32[]{:S(2)}) copy-start(s32[64,3]{0,1:T(4,128)} %param.13) | copy-start | bytes 2308
  5.4 0.7 %copy-start.6 = (s32[1,5,2]{1,2,0:T(2,128)S(1)}, s32[1,5,2]{1,2,0:T(2,128)}, u32[]{:S(2)}) copy-start(s32[1,5,2]{1,2,0:T(2,128)} %param.15) | copy-start | bytes 124
  6.1 0.7 %copy-start.7 = (s32[1,5,2]{1,2,0:T(2,128)S(1)}, s32[1,5,2]{1,2,0:T(2,128)}, u32[]{:S(2)}) copy-start(s32[1,5,2]{1,2,0:T(2,128)} %param.16) | copy-start | bytes 124
  6.7 0.7 %copy-start.8 = (s32[1,5]{1,0:T(1,128)S(1)}, s32[1,5]{1,0:T(1,128)}, u32[]{:S(2)}) copy-start(s32[1,5]{1,0:T(1,128)} %refs_5_.1) | copy-start | bytes 64
  9.1 17.2 %collective-permute-start = (bf16[256,128]{1,0:T(8,128)(2,1)S(1)}, bf16[256,128]{1,0:T(8,128)(2,1)S(1)}, u32[]{:S(2)}, u32[]{:S(2)}) collective-permute-start(bf16[256,128]{1,0:T(8,128)(2,1)S(1)} %get-tuple-element.75), channel_id=1, source_target_pairs={{0,1},{1,0},{2,3},{3,2},{4,5},{5,4},{6,7},{7,6},{8,9},{9,8},{10,11... | collective-permute-start | bytes 196616 | tf_op jit(solution)/shard_map/ppermute | solution.py:544
  9.7 16.7 %collective-permute-start.1 = (bf16[256,128]{1,0:T(8,128)(2,1)S(1)}, bf16[256,128]{1,0:T(8,128)(2,1)S(1)}, u32[]{:S(2)}, u32[]{:S(2)}) collective-permute-start(bf16[256,128]{1,0:T(8,128)(2,1)S(1)} %get-tuple-element.76), channel_id=1, source_target_pairs={{0,2},{2,0},{1,3},{3,1},{4,6},{6,4},{5,7},{7,5},{8,10},{10,8},{9,1... | collective-permute-start | bytes 196616 | tf_op jit(solution)/shard_map/ppermute | solution.py:544
  12.4 13.9 %collective-permute-start.2 = (bf16[256,128]{1,0:T(8,128)(2,1)S(1)}, bf16[256,128]{1,0:T(8,128)(2,1)S(1)}, u32[]{:S(2)}, u32[]{:S(2)}) collective-permute-start(bf16[256,128]{1,0:T(8,128)(2,1)S(1)} %get-tuple-element.77), channel_id=1, source_target_pairs={{0,4},{4,0},{1,5},{5,1},{2,6},{6,2},{3,7},{7,3},{8,12},{12,8},{9,1... | collective-permute-start | bytes 196616 | tf_op jit(solution)/shard_map/ppermute | solution.py:544
  14.0 12.3 %collective-permute-start.3 = (bf16[256,128]{1,0:T(8,128)(2,1)S(1)}, bf16[256,128]{1,0:T(8,128)(2,1)S(1)}, u32[]{:S(2)}, u32[]{:S(2)}) collective-permute-start(bf16[256,128]{1,0:T(8,128)(2,1)S(1)} %get-tuple-element.78), channel_id=1, source_target_pairs={{0,8},{8,0},{1,9},{9,1},{2,10},{10,2},{3,11},{11,3},{4,12},{12,4},... | collective-permute-start | bytes 196616 | tf_op jit(solution)/shard_map/ppermute | solution.py:544
  15.3 11.0 %collective-permute-start.4 = (bf16[256,128]{1,0:T(8,128)(2,1)S(1)}, bf16[256,128]{1,0:T(8,128)(2,1)S(1)}, u32[]{:S(2)}, u32[]{:S(2)}) collective-permute-start(bf16[256,128]{1,0:T(8,128)(2,1)S(1)} %get-tuple-element.79), channel_id=1, source_target_pairs={{0,16},{16,0},{1,17},{17,1},{2,18},{18,2},{3,19},{19,3},{4,20},{20... | collective-permute-start | bytes 196616 | tf_op jit(solution)/shard_map/ppermute | solution.py:544
  18.2 2.8 %copy-start = (bf16[64,3,128,128]{3,2,1,0:T(8,128)(2,1)S(1)}, bf16[64,3,128,128]{3,2,1,0:T(8,128)(2,1)}, u32[]{:S(2)}) copy-start(bf16[64,3,128,128]{3,2,1,0:T(8,128)(2,1)} %tiles_hbm.1) | copy-start | bytes 18874372
  27.7 8.2 %collective-permute-start.5 = (bf16[256,128]{1,0:T(8,128)(2,1)S(1)}, bf16[256,128]{1,0:T(8,128)(2,1)S(1)}, u32[]{:S(2)}, u32[]{:S(2)}) collective-permute-start(bf16[256,128]{1,0:T(8,128)(2,1)S(1)} %get-tuple-element.86), channel_id=1, source_target_pairs={{0,1},{1,0},{2,3},{3,2},{4,5},{5,4},{6,7},{7,6},{8,9},{9,8},{10,11... | collective-permute-start | bytes 196616 | tf_op jit(solution)/shard_map/ppermute | solution.py:544
  27.8 8.1 %collective-permute-start.6 = (bf16[256,128]{1,0:T(8,128)(2,1)S(1)}, bf16[256,128]{1,0:T(8,128)(2,1)S(1)}, u32[]{:S(2)}, u32[]{:S(2)}) collective-permute-start(bf16[256,128]{1,0:T(8,128)(2,1)S(1)} %get-tuple-element.87), channel_id=1, source_target_pairs={{0,2},{2,0},{1,3},{3,1},{4,6},{6,4},{5,7},{7,5},{8,10},{10,8},{9,1... | collective-permute-start | bytes 196616 | tf_op jit(solution)/shard_map/ppermute | solution.py:544
  27.9 8.1 %collective-permute-start.7 = (bf16[256,128]{1,0:T(8,128)(2,1)S(1)}, bf16[256,128]{1,0:T(8,128)(2,1)S(1)}, u32[]{:S(2)}, u32[]{:S(2)}) collective-permute-start(bf16[256,128]{1,0:T(8,128)(2,1)S(1)} %get-tuple-element.88), channel_id=1, source_target_pairs={{0,4},{4,0},{1,5},{5,1},{2,6},{6,2},{3,7},{7,3},{8,12},{12,8},{9,1... | collective-permute-start | bytes 196616 | tf_op jit(solution)/shard_map/ppermute | solution.py:544
  28.2 7.7 %collective-permute-start.8 = (bf16[256,128]{1,0:T(8,128)(2,1)S(1)}, bf16[256,128]{1,0:T(8,128)(2,1)S(1)}, u32[]{:S(2)}, u32[]{:S(2)}) collective-permute-start(bf16[256,128]{1,0:T(8,128)(2,1)S(1)} %get-tuple-element.89), channel_id=1, source_target_pairs={{0,8},{8,0},{1,9},{9,1},{2,10},{10,2},{3,11},{11,3},{4,12},{12,4},... | collective-permute-start | bytes 196616 | tf_op jit(solution)/shard_map/ppermute | solution.py:544
  29.2 6.8 %collective-permute-start.9 = (bf16[256,128]{1,0:T(8,128)(2,1)S(1)}, bf16[256,128]{1,0:T(8,128)(2,1)S(1)}, u32[]{:S(2)}, u32[]{:S(2)}) collective-permute-start(bf16[256,128]{1,0:T(8,128)(2,1)S(1)} %get-tuple-element.90), channel_id=1, source_target_pairs={{0,16},{16,0},{1,17},{17,1},{2,18},{18,2},{3,19},{19,3},{4,20},{20... | collective-permute-start | bytes 196616 | tf_op jit(solution)/shard_map/ppermute | solution.py:544
  37.5 6.0 %collective-permute-start.10 = (f32[128,128]{1,0:T(8,128)S(1)}, f32[128,128]{1,0:T(8,128)S(1)}, u32[]{:S(2)}, u32[]{:S(2)}) collective-permute-start(f32[128,128]{1,0:T(8,128)S(1)} %get-tuple-element.94.refs_8_.refs_0_), channel_id=1, source_target_pairs={{0,16},{16,0},{1,17},{17,1},{2,18},{18,2},{3,19},{19,3},{4,20},{20... | collective-permute-start | bytes 196616 | tf_op jit(solution)/shard_map/ppermute | solution.py:544
  39.1 4.4 %copy-start.3 = (bf16[4,64,64]{2,1,0:T(8,128)(2,1)S(1)}, bf16[4,64,64]{2,1,0:T(8,128)(2,1)}, u32[]{:S(2)}) copy-start(bf16[4,64,64]{2,1,0:T(8,128)(2,1)} %refs_2_.1) | copy-start | bytes 98308
  43.4 4.3 %collective-permute-start.11 = (f32[128,128]{1,0:T(8,128)S(1)}, f32[128,128]{1,0:T(8,128)S(1)}, u32[]{:S(2)}, u32[]{:S(2)}) collective-permute-start(f32[128,128]{1,0:T(8,128)S(1)} %get-tuple-element.99.refs_0_), channel_id=1, source_target_pairs={{0,8},{8,0},{1,9},{9,1},{2,10},{10,2},{3,11},{11,3},{4,12},{12,4},... | collective-permute-start | bytes 196616 | tf_op jit(solution)/shard_map/ppermute | solution.py:544
  47.8 5.0 %collective-permute-start.12 = (f32[128,128]{1,0:T(8,128)S(1)}, f32[128,128]{1,0:T(8,128)S(1)}, u32[]{:S(2)}, u32[]{:S(2)}) collective-permute-start(f32[128,128]{1,0:T(8,128)S(1)} %get-tuple-element.105.refs_0_), channel_id=1, source_target_pairs={{0,4},{4,0},{1,5},{5,1},{2,6},{6,2},{3,7},{7,3},{8,12},{12,8},{9,1... | collective-permute-start | bytes 196616 | tf_op jit(solution)/shard_map/ppermute | solution.py:544
  52.8 6.7 %collective-permute-start.13 = (f32[128,128]{1,0:T(8,128)S(1)}, f32[128,128]{1,0:T(8,128)S(1)}, u32[]{:S(2)}, u32[]{:S(2)}) collective-permute-start(f32[128,128]{1,0:T(8,128)S(1)} %get-tuple-element.111.refs_0_), channel_id=1, source_target_pairs={{0,2},{2,0},{1,3},{3,1},{4,6},{6,4},{5,7},{7,5},{8,10},{10,8},{9,1... | collective-permute-start | bytes 196616 | tf_op jit(solution)/shard_map/ppermute | solution.py:544
  53.7 6.5 %collective-permute-start.18 = (bf16[256,128]{1,0:T(8,128)(2,1)S(1)}, bf16[256,128]{1,0:T(8,128)(2,1)S(1)}, u32[]{:S(2)}, u32[]{:S(2)}) collective-permute-start(bf16[256,128]{1,0:T(8,128)(2,1)S(1)} %get-tuple-element.118), channel_id=1, source_target_pairs={{0,16},{16,0},{1,17},{17,1},{2,18},{18,2},{3,19},{19,3},{4,20},{20... | collective-permute-start | bytes 196616 | tf_op jit(solution)/shard_map/ppermute | solution.py:544
  56.2 4.5 %collective-permute-start.17 = (bf16[256,128]{1,0:T(8,128)(2,1)S(1)}, bf16[256,128]{1,0:T(8,128)(2,1)S(1)}, u32[]{:S(2)}, u32[]{:S(2)}) collective-permute-start(bf16[256,128]{1,0:T(8,128)(2,1)S(1)} %get-tuple-element.117), channel_id=1, source_target_pairs={{0,8},{8,0},{1,9},{9,1},{2,10},{10,2},{3,11},{11,3},{4,12},{12,4},... | collective-permute-start | bytes 196616 | tf_op jit(solution)/shard_map/ppermute | solution.py:544
  57.6 4.3 %collective-permute-start.16 = (bf16[256,128]{1,0:T(8,128)(2,1)S(1)}, bf16[256,128]{1,0:T(8,128)(2,1)S(1)}, u32[]{:S(2)}, u32[]{:S(2)}) collective-permute-start(bf16[256,128]{1,0:T(8,128)(2,1)S(1)} %get-tuple-element.116), channel_id=1, source_target_pairs={{0,4},{4,0},{1,5},{5,1},{2,6},{6,2},{3,7},{7,3},{8,12},{12,8},{9,1... | collective-permute-start | bytes 196616 | tf_op jit(solution)/shard_map/ppermute | solution.py:544
  58.0 4.3 %collective-permute-start.15 = (bf16[256,128]{1,0:T(8,128)(2,1)S(1)}, bf16[256,128]{1,0:T(8,128)(2,1)S(1)}, u32[]{:S(2)}, u32[]{:S(2)}) collective-permute-start(bf16[256,128]{1,0:T(8,128)(2,1)S(1)} %get-tuple-element.115), channel_id=1, source_target_pairs={{0,2},{2,0},{1,3},{3,1},{4,6},{6,4},{5,7},{7,5},{8,10},{10,8},{9,1... | collective-permute-start | bytes 196616 | tf_op jit(solution)/shard_map/ppermute | solution.py:544
  60.2 2.1 %collective-permute-start.14 = (bf16[256,128]{1,0:T(8,128)(2,1)S(1)}, bf16[256,128]{1,0:T(8,128)(2,1)S(1)}, u32[]{:S(2)}, u32[]{:S(2)}) collective-permute-start(bf16[256,128]{1,0:T(8,128)(2,1)S(1)} %get-tuple-element.114), channel_id=1, source_target_pairs={{0,1},{1,0},{2,3},{3,2},{4,5},{5,4},{6,7},{7,6},{8,9},{9,8},{10,11... | collective-permute-start | bytes 196616 | tf_op jit(solution)/shard_map/ppermute | solution.py:544
  60.2 2.1 %collective-permute-start.19 = (f32[128,128]{1,0:T(8,128)S(1)}, f32[128,128]{1,0:T(8,128)S(1)}, u32[]{:S(2)}, u32[]{:S(2)}) collective-permute-start(f32[128,128]{1,0:T(8,128)S(1)} %get-tuple-element.119.refs_16_), channel_id=1, source_target_pairs={{0,1},{1,0},{2,3},{3,2},{4,5},{5,4},{6,7},{7,6},{8,9},{9,8},{10,11... | collective-permute-start | bytes 196616 | tf_op jit(solution)/shard_map/ppermute | solution.py:544

commit v3 on v2

--- a/solution.py
+++ b/solution.py
@@ -79,15 +79,14 @@
 
 
 def pack_kernel(sz, *refs):
-    x4, u4, coupling, send, row, pair, live, col = refs[:8]
+    x4, u4, coupling, send, row, pair, live_s, col = refs[:8]
     xb, ub, cross, meta, col_out = refs[8:13]
     pays = refs[13 : 13 + sz.rounds]
-    send_s, row_s, pair_s, live_s, sem_x, sem_u, sem_t, sem_i = refs[13 + sz.rounds :]
+    send_s, row_s, pair_s, sem_x, sem_u, sem_t, sem_i = refs[13 + sz.rounds :]
     small = [
         pltpu.make_async_copy(send, send_s, sem_i.at[0]),
         pltpu.make_async_copy(row, row_s, sem_i.at[1]),
         pltpu.make_async_copy(pair, pair_s, sem_i.at[2]),
-        pltpu.make_async_copy(live, live_s, sem_i.at[3]),
     ]
     copies = []
     for t in range(sz.chan // SUB):
@@ -95,7 +94,7 @@
         copies.append(pltpu.make_async_copy(x4.at[t], xb.at[:, part, :], sem_x.at[t]))
         copies.append(pltpu.make_async_copy(u4.at[t], ub.at[:, part, :], sem_u.at[t]))
     copies.append(pltpu.make_async_copy(coupling, cross, sem_t))
-    copies.append(pltpu.make_async_copy(col, col_out, sem_i.at[4]))
+    copies.append(pltpu.make_async_copy(col, col_out, sem_i.at[3]))
     for copy in small + copies:
         copy.start()
     for copy in small:
@@ -128,30 +127,35 @@
     fill_pays(sz, meta, xb, ub, cross, pays)
 
 
-def pack(sz, x4, u4, coupling, send, row, pair, live, col):
+def keep(array):
+    return pltpu.with_memory_space_constraint(array, pltpu.HBM)
+
+
+def pack(sz, *args):
+    args = [array if array.size == 1 else keep(array) for array in args]
+    _, _, _, send, row, pair, live, col = args
     groups = sz.chan // SUB
     cross = shape((sz.pairs, sz.blk, sz.blk), BF16)
     table = shape((sz.meta,), jnp.int32)
     return call(
         functools.partial(pack_kernel, sz),
-        [HBM] * 8,
+        [HBM] * 6 + [SMEM, HBM],
         [VMEM, VMEM, VMEM, SMEM, VMEM] + [VMEM] * sz.rounds,
         [sz.field, sz.field, cross, table, shape(col.shape, jnp.int32)] + [sz.pay] * sz.rounds,
         [
             pltpu.SMEM(send.shape, jnp.int32),
             pltpu.SMEM(row.shape, jnp.int32),
             pltpu.SMEM(pair.shape, jnp.int32),
-            pltpu.SMEM(live.shape, jnp.int32),
             pltpu.SemaphoreType.DMA((groups,)),
             pltpu.SemaphoreType.DMA((groups,)),
             pltpu.SemaphoreType.DMA,
-            pltpu.SemaphoreType.DMA((5,)),
+            pltpu.SemaphoreType.DMA((4,)),
         ],
         1000,
         4 << 20,
         8,
         "pack",
-    )(x4, u4, coupling, send, row, pair, live, col)
+    )(*args)
 
 
 def big_steps(count):
@@ -245,7 +249,7 @@
         12 << 20,
         24,
         "first",
-    )(meta, col, tiles, t0, s0)
+    )(meta, col, keep(tiles), t0, s0)
 
 
 def local_kernel(sz, grad, *refs):
@@ -504,25 +508,24 @@
     )(*args, *before)
 
 
-def add_kernel(gated, *refs):
-    mine, theirs, _ = refs[:3]
+def add_kernel(gated, inputs, *refs):
+    mine, theirs = refs[:2]
+    out, token = refs[inputs : inputs + 2]
     if gated:
-        pay, out, token, pay_out = refs[3:]
-        pay_out[...] = pay[...]
-    else:
-        out, token = refs[3:]
+        refs[-1][...] = refs[2][...]
     out[...] = mine[...] + theirs[...]
     token[...] = jnp.zeros(token.shape, F32)
 
 
-def add(mine, theirs, token, pay):
+def add(mine, theirs, pay, after):
     outs = [shape(mine.shape, F32), TOKEN]
-    args = [mine, theirs, token]
+    args = [mine, theirs]
     if pay is not None:
         outs.append(shape(pay.shape, BF16))
         args.append(pay)
+    args += after
     return call(
-        functools.partial(add_kernel, pay is not None),
+        functools.partial(add_kernel, pay is not None, len(args)),
         [VMEM] * len(args),
         [VMEM] * len(outs),
         outs,
@@ -608,7 +611,8 @@
         if at + 1 < len(bits):
             later = bits[at + 1]
             gated = later < sz.rounds
-            mine, token, *rest = add(mine, theirs, token, pays[later] if gated else None)
+            after = [token] + ([got[bit]] if bit < sz.rounds else [])
+            mine, token, *rest = add(mine, theirs, pays[later] if gated else None, after)
             if gated:
                 pays[later] = rest[0]
     out4, grad4, grad_w = fix_outputs(

time: 65.3 us -> 60.1 us (0.920)
  local copies, waits for them, and re-layouts: 8.89 us -> 0.01 us
  waiting for transfers between devices: 3.1 us -> 9.77 us
  Pallas kernels: 29.8 us -> 27.6 us
    unnamed x18 -> x2, local copies, waits for them, and re-layouts: 8.89 us -> 0.01 us
    ppermute x20, waiting for transfers between devices: 3.1 us -> 9.77 us  [from_partner(): return lax.ppermute(values, 'dom', route)]
    pallas_call x2, Pallas kernels: 10.8 us -> 8.6 us  [local_products(): call(functools.partial(local_kernel, sz, grad), [SMEM, SMEM] + [VMEM] * 7...]
    pallas_call x5, Pallas kernels: 2.34 us -> 3.4 us  [the longest x1 2.75 us: pack(): call(functools.partial(pack_kernel, sz), [HBM] * 6 + [SMEM, HBM], [VMEM,...]
    pallas_call x2, Pallas kernels: 5.73 us -> 5.04 us  [base_outputs(): call(functools.partial(output_kernel, sz, low, high), specs, [HBM, HBM, V...]
  transfers between devices with their start and end apart: 20 -> 20, of which waited for: 4 -> 8; matrix products, arithmetic and copies ran while one was open for 0% -> 0% of each run, Pallas kernels for 35% -> 31%
where the time goes in v3:
time: 60.1 us; the launch traced here: 60.2 us
  Pallas kernels  27.6 us (46%)
  starting transfers between devices  21.3 us (35%)
  waiting for transfers between devices  9.77 us (16%)
  between operations  1.47 us (2%)
    ppermute x20, starting transfers between devices, from_partner(): return lax.ppermute(values, 'dom', route)  21.3 us
    ppermute x20, waiting for transfers between devices, from_partner(): return lax.ppermute(values, 'dom', route)  9.77 us
    pallas_call x2, Pallas kernels, local_products(): call(functools.partial(local_kernel, sz, grad), [SMEM, SMEM] + [VMEM] * 7...  8.6 us
    pallas_call x2, Pallas kernels, base_outputs(): call(functools.partial(output_kernel, sz, low, high), specs, [HBM, HBM, V...  5.04 us
    pallas_call x1, Pallas kernels, first_products(): call(functools.partial(first_kernel, sz), [SMEM, SMEM, HBM, VMEM, VMEM],...  5.04 us
    pallas_call x2, Pallas kernels, join(): call(functools.partial(join_kernel, sz, scale, gram is not None), [SMEM]...  2.81 us
    pallas_call x1, Pallas kernels, pack(): call(functools.partial(pack_kernel, sz), [HBM] * 6 + [SMEM, HBM], [VMEM,...  2.75 us
    pallas_call x1, Pallas kernels, fix_outputs(): call(functools.partial(fix_kernel, sz), [SMEM] + [VMEM] * (len(args) - 1)...  2.73 us
  transfers between devices with their start and end apart: 20, of which 8 were waited for; matrix products, arithmetic and copies ran while one was open for 0% of the time, Pallas kernels for 31%

profile of v3, /device:TPU:0, one launch (start us, length us, event | category | flops | bytes accessed | tf_op | source)
XLA Modules:
  0.0 60.2 jit_solution(14289757283837409653)
XLA Ops:
  1.3 2.7 %pack.1 = (bf16[64,64,128]{2,1,0:T(8,128)(2,1)S(1)}, bf16[64,64,128]{2,1,0:T(8,128)(2,1)S(1)}, bf16[10,128,128]{2,1,0:T(8,128)(2,1)S(1)}, s32[46]{0:T(128)S(1)},...) custom-call(bf16[8,64,8,128]{3,2,1,0:T(8,128)(2,1)} %bitcast.18, ...), custom_call_target="tpu_custom_call" | custom-call | flops 1000 | bytes 4194304 | tf_op jit(solution)/shard_map/pack/pallas_call | solution.py:140
  4.0 0.6 %collective-permute-start = (bf16[256,128]{1,0:T(8,128)(2,1)S(1)}, bf16[256,128]{1,0:T(8,128)(2,1)S(1)}, u32[]{:S(2)}, u32[]{:S(2)}) collective-permute-start(bf16[256,128]{1,0:T(8,128)(2,1)S(1)} %get-tuple-element.75), channel_id=1, source_target_pairs={{0,1},{1,0},{2,3},{3,2},{4,5},{5,4},{6,7},{7,6},{8,9},{9,8},{10,11... | collective-permute-start | bytes 196616 | tf_op jit(solution)/shard_map/ppermute | solution.py:547
  4.6 2.4 %collective-permute-start.1 = (bf16[256,128]{1,0:T(8,128)(2,1)S(1)}, bf16[256,128]{1,0:T(8,128)(2,1)S(1)}, u32[]{:S(2)}, u32[]{:S(2)}) collective-permute-start(bf16[256,128]{1,0:T(8,128)(2,1)S(1)} %get-tuple-element.76), channel_id=1, source_target_pairs={{0,2},{2,0},{1,3},{3,1},{4,6},{6,4},{5,7},{7,5},{8,10},{10,8},{9,1... | collective-permute-start | bytes 196616 | tf_op jit(solution)/shard_map/ppermute | solution.py:547
  7.0 1.7 %collective-permute-start.2 = (bf16[256,128]{1,0:T(8,128)(2,1)S(1)}, bf16[256,128]{1,0:T(8,128)(2,1)S(1)}, u32[]{:S(2)}, u32[]{:S(2)}) collective-permute-start(bf16[256,128]{1,0:T(8,128)(2,1)S(1)} %get-tuple-element.77), channel_id=1, source_target_pairs={{0,4},{4,0},{1,5},{5,1},{2,6},{6,2},{3,7},{7,3},{8,12},{12,8},{9,1... | collective-permute-start | bytes 196616 | tf_op jit(solution)/shard_map/ppermute | solution.py:547
  8.7 1.4 %collective-permute-start.3 = (bf16[256,128]{1,0:T(8,128)(2,1)S(1)}, bf16[256,128]{1,0:T(8,128)(2,1)S(1)}, u32[]{:S(2)}, u32[]{:S(2)}) collective-permute-start(bf16[256,128]{1,0:T(8,128)(2,1)S(1)} %get-tuple-element.78), channel_id=1, source_target_pairs={{0,8},{8,0},{1,9},{9,1},{2,10},{10,2},{3,11},{11,3},{4,12},{12,4},... | collective-permute-start | bytes 196616 | tf_op jit(solution)/shard_map/ppermute | solution.py:547
  10.1 2.5 %collective-permute-start.4 = (bf16[256,128]{1,0:T(8,128)(2,1)S(1)}, bf16[256,128]{1,0:T(8,128)(2,1)S(1)}, u32[]{:S(2)}, u32[]{:S(2)}) collective-permute-start(bf16[256,128]{1,0:T(8,128)(2,1)S(1)} %get-tuple-element.79), channel_id=1, source_target_pairs={{0,16},{16,0},{1,17},{17,1},{2,18},{18,2},{3,19},{19,3},{4,20},{20... | collective-permute-start | bytes 196616 | tf_op jit(solution)/shard_map/ppermute | solution.py:547
  12.6 5.0 %first.1 = (bf16[64,64,128]{2,1,0:T(8,128)(2,1)S(1)}, bf16[64,64,128]{2,1,0:T(8,128)(2,1)S(1)}, f32[10,64,128]{2,1,0:T(8,128)S(1)}, f32[10,64,128]{2,1,0:T(8,128...) custom-call(s32[46]{0:T(128)S(1)} %get-tuple-element.64.meta.refs_0_, ...), custom_call_target="tpu_custom_call" | custom-call | flops 805306368 | bytes 12582912 | tf_op jit(solution)/shard_map/first/pallas_call | solution.py:241
  17.7 0.0 collective-permute-done.refs_6_
  17.7 0.0 collective-permute-done.1.refs_7_
  17.7 0.0 collective-permute-done.2.refs_8_
  17.7 0.0 collective-permute-done.3.refs_9_
  17.7 0.0 collective-permute-done.4.refs_10_
  17.7 1.3 %join.2 = (bf16[64,64,128]{2,1,0:T(8,128)(2,1)S(1)}, bf16[64,64,128]{2,1,0:T(8,128)(2,1)S(1)}, bf16[256,128]{1,0:T(8,128)(2,1)S(1)}, bf16[256,128]{1,0:T(8,128)(...) custom-call(s32[46]{0:T(128)S(1)} %get-tuple-element.64.meta.refs_0_, ...), custom_call_target="tpu_custom_call" | custom-call | flops 41943040 | bytes 6291456 | tf_op jit(solution)/shard_map/join/pallas_call | solution.py:368
  19.0 0.1 collective-permute-start.5
  19.1 1.4 %collective-permute-start.6 = (bf16[256,128]{1,0:T(8,128)(2,1)S(1)}, bf16[256,128]{1,0:T(8,128)(2,1)S(1)}, u32[]{:S(2)}, u32[]{:S(2)}) collective-permute-start(bf16[256,128]{1,0:T(8,128)(2,1)S(1)} %get-tuple-element.87), channel_id=1, source_target_pairs={{0,2},{2,0},{1,3},{3,1},{4,6},{6,4},{5,7},{7,5},{8,10},{10,8},{9,1... | collective-permute-start | bytes 196616 | tf_op jit(solution)/shard_map/ppermute | solution.py:547
  20.6 0.0 collective-permute-start.7
  20.6 0.8 %collective-permute-start.8 = (bf16[256,128]{1,0:T(8,128)(2,1)S(1)}, bf16[256,128]{1,0:T(8,128)(2,1)S(1)}, u32[]{:S(2)}, u32[]{:S(2)}) collective-permute-start(bf16[256,128]{1,0:T(8,128)(2,1)S(1)} %get-tuple-element.89), channel_id=1, source_target_pairs={{0,8},{8,0},{1,9},{9,1},{2,10},{10,2},{3,11},{11,3},{4,12},{12,4},... | collective-permute-start | bytes 196616 | tf_op jit(solution)/shard_map/ppermute | solution.py:547
  21.4 0.5 collective-permute-start.9
  21.9 5.1 %local.2 = (bf16[64,64,128]{2,1,0:T(8,128)(2,1)S(1)}, bf16[64,64,128]{2,1,0:T(8,128)(2,1)S(1)}, f32[10,64,128]{2,1,0:T(8,128)S(1)}, f32[10,64,128]{2,1,0:T(8,128)S(1)}, f32[192,128]{1,0:T(8,128)S(1)}) custom-call(s32[46]{0:T(128)S(1)} %get-tuple-element.64.meta.refs_0_, s32[3,64]{1,0:T(4,128)S(1)} %get-tuple-element.66.col.refs_1_, ...), custom_call_target="tpu_custom_call" | custom-call | flops 805306368 | bytes 12582912 | tf_op jit(solution)/shard_map/local/pallas_call | solution.py:300
  27.1 0.0 collective-permute-done.5.refs_6_
  27.1 0.0 collective-permute-done.7.refs_8_
  27.1 0.0 collective-permute-done.8.refs_9_
  27.1 0.4 collective-permute-done.9.refs_10_
  27.5 1.5 %join.3 = (bf16[64,64,128]{2,1,0:T(8,128)(2,1)S(1)}, bf16[64,64,128]{2,1,0:T(8,128)(2,1)S(1)}, bf16[256,128]{1,0:T(8,128)(2,1)S(1)}, bf16[256,128]{1,0:T(8,128)(...) custom-call(s32[46]{0:T(128)S(1)} %get-tuple-element.64.meta.refs_0_, ...), custom_call_target="tpu_custom_call" | custom-call | flops 41943040 | bytes 6291456 | tf_op jit(solution)/shard_map/join/pallas_call | solution.py:368
  29.0 0.4 collective-permute-start.11
  29.4 2.6 %collective-permute-start.10 = (f32[128,128]{1,0:T(8,128)S(1)}, f32[128,128]{1,0:T(8,128)S(1)}, u32[]{:S(2)}, u32[]{:S(2)}) collective-permute-start(f32[128,128]{1,0:T(8,128)S(1)} %get-tuple-element.94.refs_8_.refs_0_), channel_id=1, source_target_pairs={{0,16},{16,0},{1,17},{17,1},{2,18},{18,2},{3,19},{19,3},{4,20},{20... | collective-permute-start | bytes 196616 | tf_op jit(solution)/shard_map/ppermute | solution.py:547
  32.0 3.5 %local.3 = (bf16[64,64,128]{2,1,0:T(8,128)(2,1)S(1)}, bf16[64,64,128]{2,1,0:T(8,128)(2,1)S(1)}, f32[10,64,128]{2,1,0:T(8,128)S(1)}, f32[10,64,128]{2,1,0:T(8,128)S(1)}, f32[8,128]{1,0:T(8,128)S(1)}) custom-call(s32[46]{0:T(128)S(1)} %get-tuple-element.64.meta.refs_0_, s32[3,64]{1,0:T(4,128)S(1)} %get-tuple-element.66.col.refs_1_, ...), custom_call_target="tpu_custom_call" | custom-call | flops 805306368 | bytes 12582912 | tf_op jit(solution)/shard_map/local/pallas_call | solution.py:300
  35.5 0.0 collective-permute-done.11.refs_4_.refs_9_
  35.5 2.2 %collective-permute-done.10.refs_1_ = f32[128,128]{1,0:T(8,128)S(1)} collective-permute-done((f32[128,128]{1,0:T(8,128)S(1)}, f32[128,128]{1,0:T(8,128)S(1)}, u32[]{:S(2)}, u32[]{:S(2)}) %collective-permute-start.10) | collective-permute-done | bytes 65568 | tf_op jit(solution)/shard_map/ppermute | solution.py:547
  37.7 1.1 %collective-permute-start.13 = (bf16[256,128]{1,0:T(8,128)(2,1)S(1)}, bf16[256,128]{1,0:T(8,128)(2,1)S(1)}, u32[]{:S(2)}, u32[]{:S(2)}) collective-permute-start(bf16[256,128]{1,0:T(8,128)(2,1)S(1)} %get-tuple-element.106), channel_id=1, source_target_pairs={{0,8},{8,0},{1,9},{9,1},{2,10},{10,2},{3,11},{11,3},{4,12},{12,4},... | collective-permute-start | bytes 196616 | tf_op jit(solution)/shard_map/ppermute | solution.py:547
  38.8 1.0 %collective-permute-start.12 = (f32[128,128]{1,0:T(8,128)S(1)}, f32[128,128]{1,0:T(8,128)S(1)}, u32[]{:S(2)}, u32[]{:S(2)}) collective-permute-start(f32[128,128]{1,0:T(8,128)S(1)} %get-tuple-element.100.refs_0_), channel_id=1, source_target_pairs={{0,8},{8,0},{1,9},{9,1},{2,10},{10,2},{3,11},{11,3},{4,12},{12,4},... | collective-permute-start | bytes 196616 | tf_op jit(solution)/shard_map/ppermute | solution.py:547
  39.8 2.9 %outputs.2 = (bf16[8,64,8,128]{3,2,1,0:T(8,128)(2,1)}, bf16[8,64,8,128]{3,2,1,0:T(8,128)(2,1)}, f32[8,128]{1,0:T(8,128)S(1)}) custom-call(s32[46]{0:T(128)S(1)} %get-tuple-element.64.meta.refs_0_, bf16[4,64,64]{2,1,0:T(8,128)(2,1)S(1)} %copy-done, bf16[64,64,128]{2,1,0:T(8,128)(2,1)S(1)} %get-tuple-element.67.t0.refs_6_.refs_2_.refs_10_, ...), custom_call_target="tpu_custom_call" | custom-call | flops 268435456 | bytes 10485760 | tf_op jit(solution)/shard_map/outputs/pallas_call | solution.py:441
  42.7 0.0 collective-permute-done.13.refs_4_.refs_8_
  42.7 0.7 %collective-permute-done.12.refs_1_ = f32[128,128]{1,0:T(8,128)S(1)} collective-permute-done((f32[128,128]{1,0:T(8,128)S(1)}, f32[128,128]{1,0:T(8,128)S(1)}, u32[]{:S(2)}, u32[]{:S(2)}) %collective-permute-start.12) | collective-permute-done | bytes 65568 | tf_op jit(solution)/shard_map/ppermute | solution.py:547
  43.4 2.1 %collective-permute-start.15 = (bf16[256,128]{1,0:T(8,128)(2,1)S(1)}, bf16[256,128]{1,0:T(8,128)(2,1)S(1)}, u32[]{:S(2)}, u32[]{:S(2)}) collective-permute-start(bf16[256,128]{1,0:T(8,128)(2,1)S(1)} %get-tuple-element.113), channel_id=1, source_target_pairs={{0,4},{4,0},{1,5},{5,1},{2,6},{6,2},{3,7},{7,3},{8,12},{12,8},{9,1... | collective-permute-start | bytes 196616 | tf_op jit(solution)/shard_map/ppermute | solution.py:547
  45.5 0.1 collective-permute-start.14
  45.6 2.2 %outputs.3 = (bf16[8,64,8,128]{3,2,1,0:T(8,128)(2,1)}, bf16[8,64,8,128]{3,2,1,0:T(8,128)(2,1)}, f32[8,128]{1,0:T(8,128)S(1)}) custom-call(s32[46]{0:T(128)S(1)} %get-tuple-element.64.meta.refs_0_, bf16[4,64,64]{2,1,0:T(8,128)(2,1)S(1)} %copy-done, ...), custom_call_target="tpu_custom_call", output_to_operand_aliasing={{0}: (11, {}), {1}: (12, {})} | custom-call | flops 268435456 | bytes 10485760 | tf_op jit(solution)/shard_map/outputs/pallas_call | solution.py:441
  47.8 2.0 %collective-permute-done.14.refs_1_ = f32[128,128]{1,0:T(8,128)S(1)} collective-permute-done((f32[128,128]{1,0:T(8,128)S(1)}, f32[128,128]{1,0:T(8,128)S(1)}, u32[]{:S(2)}, u32[]{:S(2)}) %collective-permute-start.14) | collective-permute-done | bytes 65568 | tf_op jit(solution)/shard_map/ppermute | solution.py:547
  49.8 1.4 %collective-permute-start.17 = (bf16[256,128]{1,0:T(8,128)(2,1)S(1)}, bf16[256,128]{1,0:T(8,128)(2,1)S(1)}, u32[]{:S(2)}, u32[]{:S(2)}) collective-permute-start(bf16[256,128]{1,0:T(8,128)(2,1)S(1)} %get-tuple-element.117), channel_id=1, source_target_pairs={{0,2},{2,0},{1,3},{3,1},{4,6},{6,4},{5,7},{7,5},{8,10},{10,8},{9,1... | collective-permute-start | bytes 196616 | tf_op jit(solution)/shard_map/ppermute | solution.py:547
  51.2 0.7 %collective-permute-start.16 = (f32[128,128]{1,0:T(8,128)S(1)}, f32[128,128]{1,0:T(8,128)S(1)}, u32[]{:S(2)}, u32[]{:S(2)}) collective-permute-start(f32[128,128]{1,0:T(8,128)S(1)} %get-tuple-element.114.refs_0_), channel_id=1, source_target_pairs={{0,2},{2,0},{1,3},{3,1},{4,6},{6,4},{5,7},{7,5},{8,10},{10,8},{9,1... | collective-permute-start | bytes 196616 | tf_op jit(solution)/shard_map/ppermute | solution.py:547
  51.8 2.2 %collective-permute-done.17.refs_4_.refs_6_ = bf16[256,128]{1,0:T(8,128)(2,1)S(1)} collective-permute-done((bf16[256,128]{1,0:T(8,128)(2,1)S(1)}, bf16[256,128]{1,0:T(8,128)(2,1)S(1)}, u32[]{:S(2)}, u32[]{:S(2)}) %collective-permute-start.17) | collective-permute-done | bytes 65568 | tf_op jit(solution)/shard_map/ppermute | solution.py:547
  54.1 1.4 %collective-permute-done.16.refs_1_ = f32[128,128]{1,0:T(8,128)S(1)} collective-permute-done((f32[128,128]{1,0:T(8,128)S(1)}, f32[128,128]{1,0:T(8,128)S(1)}, u32[]{:S(2)}, u32[]{:S(2)}) %collective-permute-start.16) | collective-permute-done | bytes 65568 | tf_op jit(solution)/shard_map/ppermute | solution.py:547
  55.4 0.6 %add.7 = (f32[128,128]{1,0:T(8,128)S(1)}, f32[8,128]{1,0:T(8,128)}, bf16[256,128]{1,0:T(8,128)(2,1)S(1)}) custom-call(f32[128,128]{1,0:T(8,128)S(1)} %get-tuple-element.114.refs_0_, f32[128,128]{1,0:T(8,128)S(1)} %collective-permute-done.16.refs_1_, bf16[256,128]{1,0:T(8,128)(2,1)S(1)} %get-tuple-element.115.refs_2_, ...), custom_call_target="tpu_custom_call" | custom-call | flops 16384 | bytes 196608 | tf_op jit(solution)/shard_map/add/pallas_call | solution.py:527
  56.0 0.0 collective-permute-start.18
  56.0 0.5 collective-permute-start.19
  56.6 0.7 %collective-permute-done.18.refs_5_ = bf16[256,128]{1,0:T(8,128)(2,1)S(1)} collective-permute-done((bf16[256,128]{1,0:T(8,128)(2,1)S(1)}, bf16[256,128]{1,0:T(8,128)(2,1)S(1)}, u32[]{:S(2)}, u32[]{:S(2)}) %collective-permute-start.18) | collective-permute-done | bytes 65568 | tf_op jit(solution)/shard_map/ppermute | solution.py:547
  57.3 0.2 collective-permute-done.19.refs_17_
  57.5 2.7 %fix.1 = (bf16[8,64,8,128]{3,2,1,0:T(8,128)(2,1)}, bf16[8,64,8,128]{3,2,1,0:T(8,128)(2,1)}, f32[4,64,64]{2,1,0:T(8,128)}) custom-call(s32[46]{0:T(128)S(1)} %get-tuple-element.64.meta.refs_0_, bf16[10,128,128]{2,1,0:T(8,128)(2,1)S(1)} %get-tuple-element.65.refs_1_.refs_8_, ...), custom_call_target="tpu_custom_call", output_to_operand_aliasing={{0}: (18, {}), {1}: (19, {})} | custom-call | flops 83886080 | bytes 4194304 | tf_op jit(solution)/shard_map/fix/pallas_call | solution.py:496
  (7 shorter events, 0.1 us)
Async XLA Ops:
  4.0 13.6 %collective-permute-start = (bf16[256,128]{1,0:T(8,128)(2,1)S(1)}, bf16[256,128]{1,0:T(8,128)(2,1)S(1)}, u32[]{:S(2)}, u32[]{:S(2)}) collective-permute-start(bf16[256,128]{1,0:T(8,128)(2,1)S(1)} %get-tuple-element.75), channel_id=1, source_target_pairs={{0,1},{1,0},{2,3},{3,2},{4,5},{5,4},{6,7},{7,6},{8,9},{9,8},{10,11... | collective-permute-start | bytes 196616 | tf_op jit(solution)/shard_map/ppermute | solution.py:547
  4.6 13.0 %collective-permute-start.1 = (bf16[256,128]{1,0:T(8,128)(2,1)S(1)}, bf16[256,128]{1,0:T(8,128)(2,1)S(1)}, u32[]{:S(2)}, u32[]{:S(2)}) collective-permute-start(bf16[256,128]{1,0:T(8,128)(2,1)S(1)} %get-tuple-element.76), channel_id=1, source_target_pairs={{0,2},{2,0},{1,3},{3,1},{4,6},{6,4},{5,7},{7,5},{8,10},{10,8},{9,1... | collective-permute-start | bytes 196616 | tf_op jit(solution)/shard_map/ppermute | solution.py:547
  7.0 10.7 %collective-permute-start.2 = (bf16[256,128]{1,0:T(8,128)(2,1)S(1)}, bf16[256,128]{1,0:T(8,128)(2,1)S(1)}, u32[]{:S(2)}, u32[]{:S(2)}) collective-permute-start(bf16[256,128]{1,0:T(8,128)(2,1)S(1)} %get-tuple-element.77), channel_id=1, source_target_pairs={{0,4},{4,0},{1,5},{5,1},{2,6},{6,2},{3,7},{7,3},{8,12},{12,8},{9,1... | collective-permute-start | bytes 196616 | tf_op jit(solution)/shard_map/ppermute | solution.py:547
  8.7 8.9 %collective-permute-start.3 = (bf16[256,128]{1,0:T(8,128)(2,1)S(1)}, bf16[256,128]{1,0:T(8,128)(2,1)S(1)}, u32[]{:S(2)}, u32[]{:S(2)}) collective-permute-start(bf16[256,128]{1,0:T(8,128)(2,1)S(1)} %get-tuple-element.78), channel_id=1, source_target_pairs={{0,8},{8,0},{1,9},{9,1},{2,10},{10,2},{3,11},{11,3},{4,12},{12,4},... | collective-permute-start | bytes 196616 | tf_op jit(solution)/shard_map/ppermute | solution.py:547
  10.1 7.5 %collective-permute-start.4 = (bf16[256,128]{1,0:T(8,128)(2,1)S(1)}, bf16[256,128]{1,0:T(8,128)(2,1)S(1)}, u32[]{:S(2)}, u32[]{:S(2)}) collective-permute-start(bf16[256,128]{1,0:T(8,128)(2,1)S(1)} %get-tuple-element.79), channel_id=1, source_target_pairs={{0,16},{16,0},{1,17},{17,1},{2,18},{18,2},{3,19},{19,3},{4,20},{20... | collective-permute-start | bytes 196616 | tf_op jit(solution)/shard_map/ppermute | solution.py:547
  19.0 8.0 %collective-permute-start.5 = (bf16[256,128]{1,0:T(8,128)(2,1)S(1)}, bf16[256,128]{1,0:T(8,128)(2,1)S(1)}, u32[]{:S(2)}, u32[]{:S(2)}) collective-permute-start(bf16[256,128]{1,0:T(8,128)(2,1)S(1)} %get-tuple-element.86), channel_id=1, source_target_pairs={{0,1},{1,0},{2,3},{3,2},{4,5},{5,4},{6,7},{7,6},{8,9},{9,8},{10,11... | collective-permute-start | bytes 196616 | tf_op jit(solution)/shard_map/ppermute | solution.py:547
  19.1 8.0 %collective-permute-start.6 = (bf16[256,128]{1,0:T(8,128)(2,1)S(1)}, bf16[256,128]{1,0:T(8,128)(2,1)S(1)}, u32[]{:S(2)}, u32[]{:S(2)}) collective-permute-start(bf16[256,128]{1,0:T(8,128)(2,1)S(1)} %get-tuple-element.87), channel_id=1, source_target_pairs={{0,2},{2,0},{1,3},{3,1},{4,6},{6,4},{5,7},{7,5},{8,10},{10,8},{9,1... | collective-permute-start | bytes 196616 | tf_op jit(solution)/shard_map/ppermute | solution.py:547
  20.6 6.5 %collective-permute-start.7 = (bf16[256,128]{1,0:T(8,128)(2,1)S(1)}, bf16[256,128]{1,0:T(8,128)(2,1)S(1)}, u32[]{:S(2)}, u32[]{:S(2)}) collective-permute-start(bf16[256,128]{1,0:T(8,128)(2,1)S(1)} %get-tuple-element.88), channel_id=1, source_target_pairs={{0,4},{4,0},{1,5},{5,1},{2,6},{6,2},{3,7},{7,3},{8,12},{12,8},{9,1... | collective-permute-start | bytes 196616 | tf_op jit(solution)/shard_map/ppermute | solution.py:547
  20.6 6.5 %collective-permute-start.8 = (bf16[256,128]{1,0:T(8,128)(2,1)S(1)}, bf16[256,128]{1,0:T(8,128)(2,1)S(1)}, u32[]{:S(2)}, u32[]{:S(2)}) collective-permute-start(bf16[256,128]{1,0:T(8,128)(2,1)S(1)} %get-tuple-element.89), channel_id=1, source_target_pairs={{0,8},{8,0},{1,9},{9,1},{2,10},{10,2},{3,11},{11,3},{4,12},{12,4},... | collective-permute-start | bytes 196616 | tf_op jit(solution)/shard_map/ppermute | solution.py:547
  21.4 6.1 %collective-permute-start.9 = (bf16[256,128]{1,0:T(8,128)(2,1)S(1)}, bf16[256,128]{1,0:T(8,128)(2,1)S(1)}, u32[]{:S(2)}, u32[]{:S(2)}) collective-permute-start(bf16[256,128]{1,0:T(8,128)(2,1)S(1)} %get-tuple-element.90), channel_id=1, source_target_pairs={{0,16},{16,0},{1,17},{17,1},{2,18},{18,2},{3,19},{19,3},{4,20},{20... | collective-permute-start | bytes 196616 | tf_op jit(solution)/shard_map/ppermute | solution.py:547
  29.0 6.5 %collective-permute-start.11 = (bf16[256,128]{1,0:T(8,128)(2,1)S(1)}, bf16[256,128]{1,0:T(8,128)(2,1)S(1)}, u32[]{:S(2)}, u32[]{:S(2)}) collective-permute-start(bf16[256,128]{1,0:T(8,128)(2,1)S(1)} %get-tuple-element.99), channel_id=1, source_target_pairs={{0,16},{16,0},{1,17},{17,1},{2,18},{18,2},{3,19},{19,3},{4,20},{20... | collective-permute-start | bytes 196616 | tf_op jit(solution)/shard_map/ppermute | solution.py:547
  29.4 8.3 %collective-permute-start.10 = (f32[128,128]{1,0:T(8,128)S(1)}, f32[128,128]{1,0:T(8,128)S(1)}, u32[]{:S(2)}, u32[]{:S(2)}) collective-permute-start(f32[128,128]{1,0:T(8,128)S(1)} %get-tuple-element.94.refs_8_.refs_0_), channel_id=1, source_target_pairs={{0,16},{16,0},{1,17},{17,1},{2,18},{18,2},{3,19},{19,3},{4,20},{20... | collective-permute-start | bytes 196616 | tf_op jit(solution)/shard_map/ppermute | solution.py:547
  32.0 7.8 %copy-start = (bf16[4,64,64]{2,1,0:T(8,128)(2,1)S(1)}, bf16[4,64,64]{2,1,0:T(8,128)(2,1)}, u32[]{:S(2)}) copy-start(bf16[4,64,64]{2,1,0:T(8,128)(2,1)} %refs_2_.1) | copy-start | bytes 98308
  37.7 5.0 %collective-permute-start.13 = (bf16[256,128]{1,0:T(8,128)(2,1)S(1)}, bf16[256,128]{1,0:T(8,128)(2,1)S(1)}, u32[]{:S(2)}, u32[]{:S(2)}) collective-permute-start(bf16[256,128]{1,0:T(8,128)(2,1)S(1)} %get-tuple-element.106), channel_id=1, source_target_pairs={{0,8},{8,0},{1,9},{9,1},{2,10},{10,2},{3,11},{11,3},{4,12},{12,4},... | collective-permute-start | bytes 196616 | tf_op jit(solution)/shard_map/ppermute | solution.py:547
  38.8 4.6 %collective-permute-start.12 = (f32[128,128]{1,0:T(8,128)S(1)}, f32[128,128]{1,0:T(8,128)S(1)}, u32[]{:S(2)}, u32[]{:S(2)}) collective-permute-start(f32[128,128]{1,0:T(8,128)S(1)} %get-tuple-element.100.refs_0_), channel_id=1, source_target_pairs={{0,8},{8,0},{1,9},{9,1},{2,10},{10,2},{3,11},{11,3},{4,12},{12,4},... | collective-permute-start | bytes 196616 | tf_op jit(solution)/shard_map/ppermute | solution.py:547
  43.4 4.4 %collective-permute-start.15 = (bf16[256,128]{1,0:T(8,128)(2,1)S(1)}, bf16[256,128]{1,0:T(8,128)(2,1)S(1)}, u32[]{:S(2)}, u32[]{:S(2)}) collective-permute-start(bf16[256,128]{1,0:T(8,128)(2,1)S(1)} %get-tuple-element.113), channel_id=1, source_target_pairs={{0,4},{4,0},{1,5},{5,1},{2,6},{6,2},{3,7},{7,3},{8,12},{12,8},{9,1... | collective-permute-start | bytes 196616 | tf_op jit(solution)/shard_map/ppermute | solution.py:547
  45.5 4.3 %collective-permute-start.14 = (f32[128,128]{1,0:T(8,128)S(1)}, f32[128,128]{1,0:T(8,128)S(1)}, u32[]{:S(2)}, u32[]{:S(2)}) collective-permute-start(f32[128,128]{1,0:T(8,128)S(1)} %get-tuple-element.107.refs_0_), channel_id=1, source_target_pairs={{0,4},{4,0},{1,5},{5,1},{2,6},{6,2},{3,7},{7,3},{8,12},{12,8},{9,1... | collective-permute-start | bytes 196616 | tf_op jit(solution)/shard_map/ppermute | solution.py:547
  49.8 4.3 %collective-permute-start.17 = (bf16[256,128]{1,0:T(8,128)(2,1)S(1)}, bf16[256,128]{1,0:T(8,128)(2,1)S(1)}, u32[]{:S(2)}, u32[]{:S(2)}) collective-permute-start(bf16[256,128]{1,0:T(8,128)(2,1)S(1)} %get-tuple-element.117), channel_id=1, source_target_pairs={{0,2},{2,0},{1,3},{3,1},{4,6},{6,4},{5,7},{7,5},{8,10},{10,8},{9,1... | collective-permute-start | bytes 196616 | tf_op jit(solution)/shard_map/ppermute | solution.py:547
  51.2 4.3 %collective-permute-start.16 = (f32[128,128]{1,0:T(8,128)S(1)}, f32[128,128]{1,0:T(8,128)S(1)}, u32[]{:S(2)}, u32[]{:S(2)}) collective-permute-start(f32[128,128]{1,0:T(8,128)S(1)} %get-tuple-element.114.refs_0_), channel_id=1, source_target_pairs={{0,2},{2,0},{1,3},{3,1},{4,6},{6,4},{5,7},{7,5},{8,10},{10,8},{9,1... | collective-permute-start | bytes 196616 | tf_op jit(solution)/shard_map/ppermute | solution.py:547
  56.0 1.3 %collective-permute-start.18 = (bf16[256,128]{1,0:T(8,128)(2,1)S(1)}, bf16[256,128]{1,0:T(8,128)(2,1)S(1)}, u32[]{:S(2)}, u32[]{:S(2)}) collective-permute-start(bf16[256,128]{1,0:T(8,128)(2,1)S(1)} %get-tuple-element.118), channel_id=1, source_target_pairs={{0,1},{1,0},{2,3},{3,2},{4,5},{5,4},{6,7},{7,6},{8,9},{9,8},{10,11... | collective-permute-start | bytes 196616 | tf_op jit(solution)/shard_map/ppermute | solution.py:547
  56.0 1.4 %collective-permute-start.19 = (f32[128,128]{1,0:T(8,128)S(1)}, f32[128,128]{1,0:T(8,128)S(1)}, u32[]{:S(2)}, u32[]{:S(2)}) collective-permute-start(f32[128,128]{1,0:T(8,128)S(1)} %get-tuple-element.119.refs_16_), channel_id=1, source_target_pairs={{0,1},{1,0},{2,3},{3,2},{4,5},{5,4},{6,7},{7,6},{8,9},{9,8},{10,11... | collective-permute-start | bytes 196616 | tf_op jit(solution)/shard_map/ppermute | solution.py:547

commit v4 on v3

--- a/solution.py
+++ b/solution.py
@@ -6,6 +6,7 @@
 from jax.experimental import pallas as pl
 from jax.experimental.pallas import tpu as pltpu
 from jax.sharding import PartitionSpec as P
+
 
 F32 = jnp.float32
 BF16 = jnp.bfloat16
@@ -56,7 +57,7 @@
         return pl.ds(self.half + h * self.chan, self.chan)
 
 
-def call(kernel, in_specs, out_specs, out_shape, scratch, flops, moved, limit, name, aliases=None):
+def call(kernel, in_specs, out_specs, out_shape, scratch, flops, moved, limit, aliases=None):
     return pl.pallas_call(
         kernel,
         in_specs=in_specs,
@@ -66,7 +67,6 @@
         input_output_aliases=aliases or {},
         compiler_params=pltpu.CompilerParams(vmem_limit_bytes=limit << 20),
         cost_estimate=pl.CostEstimate(flops=flops, bytes_accessed=moved, transcendentals=0),
-        name=name,
     )
 
 
@@ -80,22 +80,22 @@
 
 def pack_kernel(sz, *refs):
     x4, u4, coupling, send, row, pair, live_s, col = refs[:8]
-    xb, ub, cross, meta, col_out = refs[8:13]
-    pays = refs[13 : 13 + sz.rounds]
-    send_s, row_s, pair_s, sem_x, sem_u, sem_t, sem_i = refs[13 + sz.rounds :]
+    xb, ub, cross, across, meta, col_out = refs[8:14]
+    pays = refs[14 : 14 + sz.rounds]
+    send_s, row_s, pair_s, sem_x, sem_u, sem_t, sem_i = refs[14 + sz.rounds :]
     small = [
         pltpu.make_async_copy(send, send_s, sem_i.at[0]),
         pltpu.make_async_copy(row, row_s, sem_i.at[1]),
         pltpu.make_async_copy(pair, pair_s, sem_i.at[2]),
     ]
+    tiles = pltpu.make_async_copy(coupling, cross, sem_t)
     copies = []
     for t in range(sz.chan // SUB):
         part = pl.ds(t * SUB, SUB)
         copies.append(pltpu.make_async_copy(x4.at[t], xb.at[:, part, :], sem_x.at[t]))
         copies.append(pltpu.make_async_copy(u4.at[t], ub.at[:, part, :], sem_u.at[t]))
-    copies.append(pltpu.make_async_copy(coupling, cross, sem_t))
     copies.append(pltpu.make_async_copy(col, col_out, sem_i.at[3]))
-    for copy in small + copies:
+    for copy in small + [tiles] + copies:
         copy.start()
     for copy in small:
         copy.wait()
@@ -115,6 +115,9 @@
     for r in range(sz.rounds):
         meta[sz.flags + r] = pair_s[0, r]
     meta[sz.live] = count
+    tiles.wait()
+    for j in range(sz.pairs):
+        across[j] = cross[j].T
     for copy in copies:
         copy.wait()
 
@@ -133,15 +136,16 @@
 
 def pack(sz, *args):
     args = [array if array.size == 1 else keep(array) for array in args]
-    _, _, _, send, row, pair, live, col = args
+    _, _, _, send, row, pair, _, col = args
     groups = sz.chan // SUB
     cross = shape((sz.pairs, sz.blk, sz.blk), BF16)
     table = shape((sz.meta,), jnp.int32)
     return call(
         functools.partial(pack_kernel, sz),
         [HBM] * 6 + [SMEM, HBM],
-        [VMEM, VMEM, VMEM, SMEM, VMEM] + [VMEM] * sz.rounds,
-        [sz.field, sz.field, cross, table, shape(col.shape, jnp.int32)] + [sz.pay] * sz.rounds,
+        [VMEM] * 4 + [SMEM, VMEM] + [VMEM] * sz.rounds,
+        [sz.field, sz.field, cross, cross, table, shape(col.shape, jnp.int32)]
+        + [sz.pay] * sz.rounds,
         [
             pltpu.SMEM(send.shape, jnp.int32),
             pltpu.SMEM(row.shape, jnp.int32),
@@ -154,7 +158,6 @@
         1000,
         4 << 20,
         8,
-        "pack",
     )(*args)
 
 
@@ -198,10 +201,11 @@
 
 
 def first_kernel(
-    sz, meta, col, tiles_hbm, t0, s0, tnew, snew, psel, qsel, tiles, turned, held, summed, sem
+    sz, meta, col, tiles_hbm, t0, s0, tnew, snew, psel, qsel, tiles, turned, gram, held, summed, sem
 ):
     count = meta[sz.live]
-    steps = big_steps(count) * (ROWS // ROWS_FIRST)
+    steps = big_steps(count)
+    loads = steps * (ROWS // ROWS_FIRST)
 
     def fetch(g):
         part = pl.ds(g * ROWS_FIRST, ROWS_FIRST)
@@ -211,8 +215,15 @@
         fetch(g).start()
         return carry
 
-    lax.fori_loop(0, steps, start, 0)
+    lax.fori_loop(0, loads, start, 0)
     clear_sums(sz, summed)
+
+    def products(g, total):
+        spots = [g * ROWS + u for u in range(ROWS)]
+        left = jnp.concatenate([t0[i] for i in spots], axis=1)
+        return total + nn(left, jnp.concatenate([s0[i].T for i in spots], axis=0))
+
+    gram[...] = lax.fori_loop(0, steps, products, jnp.zeros(gram.shape, F32))
 
     def block_row(i):
         cols = [col[m, i] for m in range(sz.nz)]
@@ -227,9 +238,10 @@
         scatter_terms(sz, summed, cols, nn(s0[i], jnp.concatenate(parts, axis=1)))
 
     def step(g, carry):
-        fetch(g).wait()
-        for u in range(ROWS_FIRST):
-            block_row(g * ROWS_FIRST + u)
+        for part in range(ROWS // ROWS_FIRST):
+            fetch(g * (ROWS // ROWS_FIRST) + part).wait()
+        for u in range(ROWS):
+            block_row(g * ROWS + u)
         return carry
 
     lax.fori_loop(0, steps, step, 0)
@@ -241,14 +253,14 @@
     return call(
         functools.partial(first_kernel, sz),
         [SMEM, SMEM, HBM, VMEM, VMEM],
-        [VMEM] * 6,
-        [sz.field, sz.field, sz.picked, sz.picked, shape(tiles.shape, BF16), turned],
+        [VMEM] * 7,
+        [sz.field, sz.field, sz.picked, sz.picked, shape(tiles.shape, BF16), turned]
+        + [shape((sz.chan, sz.chan), F32)],
         [pltpu.VMEM((sz.blocks, sz.chan, sz.blk), F32)] * 2
         + [pltpu.SemaphoreType.DMA((sz.blocks // ROWS_FIRST,))],
         4 * sz.blocks * sz.nz * sz.chan * sz.blk * sz.blk,
         12 << 20,
         24,
-        "first",
     )(meta, col, keep(tiles), t0, s0)
 
 
@@ -285,18 +297,17 @@
 
     def products(g, total):
         left, right = [], []
-        for u in range(ROWS_FIRST):
-            i = g * ROWS_FIRST + u
-            left.append(jnp.concatenate([tprev[i], tcur[i], tnew[i]], axis=0))
+        for u in range(ROWS):
+            i = g * ROWS + u
+            left.append(jnp.concatenate([tcur[i], tnew[i]], axis=0))
             right.append(jnp.concatenate([sprev[i], scur[i]], axis=0).T)
         return total + nn(jnp.concatenate(left, axis=1), jnp.concatenate(right, axis=0))
 
-    steps = (count + ROWS_FIRST - 1) // ROWS_FIRST
-    last[...] = lax.fori_loop(0, steps, products, jnp.zeros(last.shape, F32))
+    last[...] = lax.fori_loop(0, big_steps(count), products, jnp.zeros(last.shape, F32))
 
 
 def local_products(sz, meta, col, tiles, turned, fields, token, grad):
-    tail = shape((3 * sz.chan, 2 * sz.chan), F32) if grad else TOKEN
+    tail = shape((2 * sz.chan, 2 * sz.chan), F32) if grad else TOKEN
     return call(
         functools.partial(local_kernel, sz, grad),
         [SMEM, SMEM] + [VMEM] * 7,
@@ -306,38 +317,83 @@
         4 * sz.blocks * sz.nz * sz.chan * sz.blk * sz.blk,
         12 << 20,
         24,
-        "local",
     )(meta, col, tiles, turned, *fields, token)
 
 
-def add_coupled(sz, scale, meta, got, cross, psel, qsel, pacc, qacc):
+def add_coupled(sz, scale, meta, got, across, psel, qsel, pacc, qacc, which):
     for j in range(sz.pairs):
         pacc[j] = psel[j]
         qacc[j] = qsel[j]
-    terms = []
+    terms = {}
     for r, h, j in sz.couplings():
-        factor = scale * meta[sz.flags + r].astype(F32)
-        terms.append(factor * nn(got[r][sz.forward_part(h), :], cross[j].T))
-        spot = meta[sz.first_row + j]
-        pacc[spot] = pacc[spot] + terms[j]
-        spot = meta[sz.first_send + j]
-        qacc[spot] = qacc[spot] + scale * got[r][sz.adjoint_part(h), :].astype(F32)
+        if r in which:
+            factor = scale * meta[sz.flags + r].astype(F32)
+            terms[j] = factor * nn(got[r][sz.forward_part(h), :], across[j])
+            spot = meta[sz.first_row + j]
+            pacc[spot] = pacc[spot] + terms[j]
+            spot = meta[sz.first_send + j]
+            qacc[spot] = qacc[spot] + scale * got[r][sz.adjoint_part(h), :].astype(F32)
     return terms
 
 
-def join_kernel(sz, scale, grad, *refs):
-    refs = list(refs)
-    meta, cross, tbase, sbase, psel, qsel = refs[:6]
-    got, refs = refs[6 : 6 + sz.rounds], refs[6 + sz.rounds :]
-    if grad:
-        gram, sold = refs[:2]
-        refs = refs[2:]
-    tnew, snew = refs[:2]
-    pays, refs = refs[2 : 2 + sz.rounds], refs[2 + sz.rounds :]
-    if grad:
-        partial, refs = refs[0], refs[1:]
-    pacc, qacc = refs
-    terms = add_coupled(sz, scale, meta, got, cross, psel, qsel, pacc, qacc)
+def couple_kernel(sz, scale, which, *refs):
+    meta, across, psel, qsel = refs[:4]
+    got = dict(zip(which, refs[4 : 4 + len(which)]))
+    pacc, qacc = refs[-2:]
+    add_coupled(sz, scale, meta, got, across, psel, qsel, pacc, qacc, which)
+
+
+def couple(sz, scale, meta, across, picked, got, which, after):
+    args = [meta, across, *picked, *(got[r] for r in which), *after]
+    return call(
+        functools.partial(couple_kernel, sz, scale, which),
+        [SMEM] + [VMEM] * (len(args) - 1),
+        [VMEM] * 2,
+        [sz.picked] * 2,
+        [],
+        2 * len(which) * sz.hb * sz.chan * sz.blk * sz.blk,
+        2 << 20,
+        6,
+    )(*args)
+
+
+def correct_kernel(sz, axis, *refs):
+    meta, across, psel, qsel, gram0, gram, sold = refs[:7]
+    got, refs = refs[7 : 7 + sz.rounds], refs[7 + sz.rounds :]
+    pacc, qacc, keep_half, give_half, whole = refs
+    which = range(sz.rounds)
+    terms = add_coupled(sz, 2.0, meta, got, across, psel, qsel, pacc, qacc, which)
+    left = jnp.concatenate([terms[j].astype(BF16) for j in range(sz.pairs)], axis=1)
+    right = [sold[meta[sz.rows + j]].T for j in range(sz.pairs)]
+    extra = nn(left, jnp.concatenate(right, axis=0))
+    one, two = pl.ds(0, sz.chan), pl.ds(sz.chan, sz.chan)
+    whole[one, one] = gram0[...]
+    whole[two, one] = gram[one, one]
+    whole[two, two] = gram[one, two]
+    whole[one, two] = gram[two, two] + extra
+    odd = lax.rem(lax.axis_index(axis), 2)
+    keep_half[...] = whole[pl.ds(pl.multiple_of(odd * sz.chan, sz.chan), sz.chan), :]
+    give_half[...] = whole[pl.ds(pl.multiple_of((1 - odd) * sz.chan, sz.chan), sz.chan), :]
+
+
+def correct(sz, axis, meta, across, picked, got, gram0, gram, sold):
+    args = [meta, across, *picked, gram0, gram, sold, *got]
+    half = shape((sz.chan, 2 * sz.chan), F32)
+    return call(
+        functools.partial(correct_kernel, sz, axis),
+        [SMEM] + [VMEM] * (len(args) - 1),
+        [VMEM] * 4,
+        [sz.picked, sz.picked, half, half],
+        [pltpu.VMEM((2 * sz.chan, 2 * sz.chan), F32)],
+        4 * sz.pairs * sz.chan * sz.blk * sz.blk,
+        3 << 20,
+        8,
+    )(*args)
+
+
+def join_kernel(sz, *refs):
+    meta, cross, tbase, sbase, pacc, qacc, tnew, snew = refs[:8]
+    pays = refs[8:]
 
     def move(i, carry):
         tnew[i] = tbase[i]
@@ -349,34 +405,22 @@
         tnew[meta[sz.rows + j]] = pacc[meta[sz.first_row + j]].astype(BF16)
         snew[meta[sz.sends + j]] = qacc[meta[sz.first_send + j]].astype(BF16)
     fill_pays(sz, meta, tnew, snew, cross, pays)
-    if grad:
-        left = jnp.concatenate([term.astype(BF16) for term in terms], axis=1)
-        right = [sold[meta[sz.rows + j]].T for j in range(sz.pairs)]
-        extra = nn(left, jnp.concatenate(right, axis=0))
-        one, two, three = (pl.ds(k * sz.chan, sz.chan) for k in range(3))
-        partial[one, one] = gram[one, one]
-        partial[two, :] = gram[two, :]
-        partial[one, two] = gram[three, two] + extra
-
-
-def join(sz, scale, meta, cross, base, got, gram=None, sold=None):
+
+
+def join(sz, meta, cross, base, picked):
+    args = [meta, cross, *base, *picked]
     outs = [sz.field, sz.field] + [sz.pay] * sz.rounds
-    args = [meta, cross, *base, *got]
-    if gram is not None:
-        args += [gram, sold]
-        outs.append(shape((2 * sz.chan, 2 * sz.chan), F32))
     outs = call(
-        functools.partial(join_kernel, sz, scale, gram is not None),
+        functools.partial(join_kernel, sz),
         [SMEM] + [VMEM] * (len(args) - 1),
         [VMEM] * len(outs),
         outs,
-        [pltpu.VMEM(sz.picked.shape, F32)] * 2,
-        4 * sz.pairs * sz.chan * sz.blk * sz.blk,
-        6 << 20,
-        12,
-        "join",
+        [],
+        2 * sz.pairs * sz.chan * sz.blk * sz.blk,
+        5 << 20,
+        8,
     )(*args)
-    return outs[0], outs[1], outs[2 : 2 + sz.rounds], outs[2 + sz.rounds :]
+    return outs[0], outs[1], outs[2:]
 
 
 def output_weights(weight):
@@ -447,18 +491,17 @@
         16 * (high - low) * sz.chan * sz.chan * sz.blk,
         10 << 20,
         8,
-        "outputs",
         aliases,
     )(*args)
 
 
-def fix_kernel(sz, *refs):
-    meta, cross, weight, psel, qsel = refs[:5]
-    got, refs = refs[5 : 5 + sz.rounds], refs[5 + sz.rounds :]
+def fix_kernel(sz, axis, which, *refs):
+    meta, across, weight, psel, qsel = refs[:5]
+    got, refs = dict(zip(which, refs[5 : 5 + len(which)])), refs[5 + len(which) :]
     forward, adjoint = refs[:3], refs[3:6]
     mine, theirs = refs[6:8]
     out4, grad4, grad_w, pacc, qacc, held_out, held_grad, sem = refs[10:]
-    add_coupled(sz, 2.0, meta, got, cross, psel, qsel, pacc, qacc)
+    add_coupled(sz, 2.0, meta, got, across, psel, qsel, pacc, qacc, which)
     ahead, back = output_weights(weight)
     groups = sz.chan // SUB
     copies = []
@@ -475,26 +518,27 @@
             copies.append((slot == j, pltpu.make_async_copy(held.at[j], out.at[:, i], sem.at[s, j])))
     for own, copy in copies:
         pl.when(own)(copy.start)
-    one, two = pl.ds(0, sz.chan), pl.ds(sz.chan, sz.chan)
-
-    def total(a, b):
-        return mine[a, b] + theirs[a, b]
-
-    zeroth, first = total(one, one), total(two, one)
+    odd = lax.rem(lax.axis_index(axis), 2) == 1
+    top = jnp.where(odd, theirs[...], mine[...])
+    low = jnp.where(odd, mine[...], theirs[...])
+    zeroth, first = top[:, : sz.chan], low[:, : sz.chan]
     grad_w[0] = zeroth
     grad_w[1] = first
-    grad_w[2] = 2.0 * total(two, two) - zeroth
-    grad_w[3] = 2.0 * total(one, two) - first
+    grad_w[2] = 2.0 * low[:, sz.chan :] - zeroth
+    grad_w[3] = 2.0 * top[:, sz.chan :] - first
     for own, copy in copies:
         pl.when(own)(copy.wait)
 
 
-def fix_outputs(sz, meta, cross, weight, picked, got, forward, adjoint, mine, theirs, before):
+def fix_outputs(
+    sz, axis, meta, across, weight, picked, got, which, forward, adjoint, mine, theirs, before
+):
     out = shape(before[0].shape, BF16)
-    args = [meta, cross, weight, *picked, *got, *forward, *adjoint, mine, theirs]
+    late = [got[r] for r in which]
+    args = [meta, across, weight, *picked, *late, *forward, *adjoint, mine, theirs]
     held = pltpu.VMEM((sz.pairs, sz.chan // SUB, SUB, sz.blk), BF16)
     return call(
-        functools.partial(fix_kernel, sz),
+        functools.partial(fix_kernel, sz, axis, which),
         [SMEM] + [VMEM] * (len(args) - 1) + [HBM] * 2,
         [HBM, HBM, VMEM],
         [out, out, shape((4, sz.chan, sz.chan), F32)],
@@ -503,7 +547,6 @@
         8 * sz.pairs * sz.chan * sz.blk * sz.blk,
         4 << 20,
         10,
-        "fix",
         {len(args): 0, len(args) + 1: 1},
     )(*args, *before)
 
@@ -533,7 +576,6 @@
         mine.size,
         12 * mine.size,
         2,
-        "add",
     )(*args)
 
 
@@ -567,22 +609,27 @@
     send, row = send_index.transpose(0, 2, 1), row_index.transpose(0, 2, 1)
 
     packed = pack(sz, x4, u4, coupling, send, row, pair_on, blk_live, col_index.T)
-    t0, s0, cross, meta, col = packed[:5]
-    got = [from_partner(pay, bit) for bit, pay in enumerate(packed[5:])]
-    *base, tiles, turned = first_products(sz, meta, col, lap_tiles, t0, s0)
-    t1, s1, pays, _ = join(sz, 1.0, meta, cross, base, got)
+    t0, s0, cross, across, meta, col = packed[:6]
+    everyone = range(sz.rounds)
+    got = [from_partner(pay, bit) for bit, pay in enumerate(packed[6:])]
+    *base, psel, qsel, tiles, turned, gram0 = first_products(sz, meta, col, lap_tiles, t0, s0)
+    picked = couple(sz, 1.0, meta, across, (psel, qsel), got, everyone, [])
+    t1, s1, pays = join(sz, meta, cross, base, picked)
 
     got = [from_partner(pay, bit) for bit, pay in enumerate(pays)]
     fields = (t1, s1, t0, s0)
-    *base, gram = local_products(sz, meta, col, tiles, turned, fields, cross, True)
-    t2, s2, pays, (mine,) = join(sz, 2.0, meta, cross, base, got, gram, s1)
+    *base, psel, qsel, gram = local_products(sz, meta, col, tiles, turned, fields, cross, True)
+    *picked, mine, given = correct(
+        sz, "dom", meta, across, (psel, qsel), got, gram0, gram, s1
+    )
+    theirs = from_partner(given, 0)
+    t2, s2, pays = join(sz, meta, cross, base, picked)
 
     state = {}
 
     def window_products(token):
         fields = (t2, s2, t1, s1)
-        *base, token = local_products(sz, meta, col, tiles, turned, fields, token, False)
-        state["base"] = base
+        *state["base"], token = local_products(sz, meta, col, tiles, turned, fields, token, False)
         return token
 
     def window_outputs(low, high):
@@ -599,29 +646,39 @@
 
     middle = sz.blocks // (2 * ROWS_FIRST) * ROWS_FIRST
     windows = [window_products, window_outputs(0, middle), window_outputs(middle, sz.blocks)]
-    bits = list(reversed(range((lax.axis_size("dom") - 1).bit_length())))
+    bits = list(reversed(range(1, (lax.axis_size("dom") - 1).bit_length())))
     pays, got = list(pays), [None] * sz.rounds
-    token = mine
+    got[0] = from_partner(pays[0], 0)
+    early = [bit for bit in bits[:-1] if bit < sz.rounds]
+    late = [bit for bit in everyone if bit not in early]
+    mine, token, *rest = add(mine, theirs, pays[bits[0]] if bits[0] < sz.rounds else None, [])
     for at, bit in enumerate(bits):
         if bit < sz.rounds:
+            pays[bit] = rest[0]
+        theirs = from_partner(mine, bit)
+        if bit < sz.rounds:
             got[bit] = from_partner(pays[bit], bit)
-        theirs = from_partner(mine, bit)
         if at < len(windows):
             token = windows[at](token)
-        if at + 1 < len(bits):
-            later = bits[at + 1]
-            gated = later < sz.rounds
-            after = [token] + ([got[bit]] if bit < sz.rounds else [])
-            mine, token, *rest = add(mine, theirs, pays[later] if gated else None, after)
-            if gated:
-                pays[later] = rest[0]
+        last = at + 1 == len(bits)
+        if last:
+            picked = couple(sz, 2.0, meta, across, state["base"][2:4], got, early, [token])
+            token = picked[0]
+        gated = not last and bits[at + 1] < sz.rounds
+        after = [token] + ([got[bit]] if bit < sz.rounds and not last else [])
+        if at == 0:
+            after.append(got[0])
+        mine, token, *rest = add(mine, theirs, pays[bits[at + 1]] if gated else None, after)
+    theirs = from_partner(mine, 0)
     out4, grad4, grad_w = fix_outputs(
         sz,
+        "dom",
         meta,
-        cross,
+        across,
         cheb_weight,
-        state["base"][2:4],
+        picked,
         got,
+        late,
         (t0, t1, t2),
         (s0, s1, s2),
         mine,

time: 60.1 us -> 58.1 us (0.967)
  waiting for transfers between devices: 9.77 us -> 6.95 us
  Pallas kernels: 27.6 us -> 28.3 us
    ppermute x20 -> x21, waiting for transfers between devices: 9.77 us -> 6.95 us  [from_partner(): return lax.ppermute(values, 'dom', route)]
    pallas_call x4 -> x7, Pallas kernels: 8.29 us -> 9.84 us  [the longest x1 2.79 us: pack(): call(functools.partial(pack_kernel, sz), [HBM] * 6 + [SMEM, HBM], [VMEM]...]
    pallas_call x2, Pallas kernels: 8.6 us -> 7.96 us  [local_products(): call(functools.partial(local_kernel, sz, grad), [SMEM, SMEM] + [VMEM] * 7...]
    ppermute x20 -> x21, starting transfers between devices: 21.3 us -> 21.2 us  [from_partner(): return lax.ppermute(values, 'dom', route)]
  transfers between devices with their start and end apart: 20 -> 21, of which waited for: 8 -> 5; matrix products, arithmetic and copies ran while one was open for 0% -> 0% of each run, Pallas kernels for 31% -> 35%
where the time goes in v4:
time: 58.1 us; the launch traced here: 58 us
  Pallas kernels  28.3 us (49%)
  starting transfers between devices  21.2 us (36%)
  waiting for transfers between devices  6.95 us (12%)
  between operations  1.51 us (3%)
    ppermute x21, starting transfers between devices, from_partner(): return lax.ppermute(values, 'dom', route)  21.2 us
    pallas_call x2, Pallas kernels, local_products(): call(functools.partial(local_kernel, sz, grad), [SMEM, SMEM] + [VMEM] * 7...  7.96 us
    ppermute x21, waiting for transfers between devices, from_partner(): return lax.ppermute(values, 'dom', route)  6.95 us
    pallas_call x2, Pallas kernels, base_outputs(): call(functools.partial(output_kernel, sz, low, high), specs, [HBM, HBM, V...  5.28 us
    pallas_call x1, Pallas kernels, first_products(): call(functools.partial(first_kernel, sz), [SMEM, SMEM, HBM, VMEM, VMEM],...  4.59 us
    pallas_call x1, Pallas kernels, pack(): call(functools.partial(pack_kernel, sz), [HBM] * 6 + [SMEM, HBM], [VMEM]...  2.79 us
    pallas_call x1, Pallas kernels, fix_outputs(): call(functools.partial(fix_kernel, sz, axis, which), [SMEM] + [VMEM] * (l...  2.58 us
    pallas_call x2, Pallas kernels, join(): call(functools.partial(join_kernel, sz), [SMEM] + [VMEM] * (len(args) - 1...  1.92 us
  transfers between devices with their start and end apart: 21, of which 5 were waited for; matrix products, arithmetic and copies ran while one was open for 0% of the time, Pallas kernels for 35%

profile of v4, /device:TPU:0, one launch (start us, length us, event | category | flops | bytes accessed | tf_op | source)
XLA Modules:
  0.0 58.0 jit_solution(1405601943931823802)
XLA Ops:
  1.3 2.8 %shard_map.121 = (bf16[64,64,128]{2,1,0:T(8,128)(2,1)S(1)}, bf16[64,64,128]{2,1,0:T(8,128)(2,1)S(1)}, bf16[10,128,128]{2,1,0:T(8,128)(2,1)S(1)}, bf16[10,128,128...) custom-call(bf16[8,64,8,128]{3,2,1,0:T(8,128)(2,1)} %bitcast.18, ...), custom_call_target="tpu_custom_call" | custom-call | flops 1000 | bytes 4194304 | tf_op jit(solution)/shard_map/pallas_call | solution.py:143
  4.1 0.8 %collective-permute-start = (bf16[256,128]{1,0:T(8,128)(2,1)S(1)}, bf16[256,128]{1,0:T(8,128)(2,1)S(1)}, u32[]{:S(2)}, u32[]{:S(2)}) collective-permute-start(bf16[256,128]{1,0:T(8,128)(2,1)S(1)} %get-tuple-element.87), channel_id=1, source_target_pairs={{0,1},{1,0},{2,3},{3,2},{4,5},{5,4},{6,7},{7,6},{8,9},{9,8},{10,11... | collective-permute-start | bytes 196616 | tf_op jit(solution)/shard_map/ppermute | solution.py:589
  4.9 2.3 %collective-permute-start.1 = (bf16[256,128]{1,0:T(8,128)(2,1)S(1)}, bf16[256,128]{1,0:T(8,128)(2,1)S(1)}, u32[]{:S(2)}, u32[]{:S(2)}) collective-permute-start(bf16[256,128]{1,0:T(8,128)(2,1)S(1)} %get-tuple-element.88), channel_id=1, source_target_pairs={{0,2},{2,0},{1,3},{3,1},{4,6},{6,4},{5,7},{7,5},{8,10},{10,8},{9,1... | collective-permute-start | bytes 196616 | tf_op jit(solution)/shard_map/ppermute | solution.py:589
  7.2 1.7 %collective-permute-start.2 = (bf16[256,128]{1,0:T(8,128)(2,1)S(1)}, bf16[256,128]{1,0:T(8,128)(2,1)S(1)}, u32[]{:S(2)}, u32[]{:S(2)}) collective-permute-start(bf16[256,128]{1,0:T(8,128)(2,1)S(1)} %get-tuple-element.89), channel_id=1, source_target_pairs={{0,4},{4,0},{1,5},{5,1},{2,6},{6,2},{3,7},{7,3},{8,12},{12,8},{9,1... | collective-permute-start | bytes 196616 | tf_op jit(solution)/shard_map/ppermute | solution.py:589
  8.9 1.3 %collective-permute-start.3 = (bf16[256,128]{1,0:T(8,128)(2,1)S(1)}, bf16[256,128]{1,0:T(8,128)(2,1)S(1)}, u32[]{:S(2)}, u32[]{:S(2)}) collective-permute-start(bf16[256,128]{1,0:T(8,128)(2,1)S(1)} %get-tuple-element.90), channel_id=1, source_target_pairs={{0,8},{8,0},{1,9},{9,1},{2,10},{10,2},{3,11},{11,3},{4,12},{12,4},... | collective-permute-start | bytes 196616 | tf_op jit(solution)/shard_map/ppermute | solution.py:589
  10.1 2.6 %collective-permute-start.4 = (bf16[256,128]{1,0:T(8,128)(2,1)S(1)}, bf16[256,128]{1,0:T(8,128)(2,1)S(1)}, u32[]{:S(2)}, u32[]{:S(2)}) collective-permute-start(bf16[256,128]{1,0:T(8,128)(2,1)S(1)} %get-tuple-element.91), channel_id=1, source_target_pairs={{0,16},{16,0},{1,17},{17,1},{2,18},{18,2},{3,19},{19,3},{4,20},{20... | collective-permute-start | bytes 196616 | tf_op jit(solution)/shard_map/ppermute | solution.py:589
  12.7 4.6 %shard_map.122 = (bf16[64,64,128]{2,1,0:T(8,128)(2,1)S(1)}, bf16[64,64,128]{2,1,0:T(8,128)(2,1)S(1)}, f32[10,64,128]{2,1,0:T(8,128)S(1)}, f32[10,64,128]{2,1,0:T...) custom-call(s32[46]{0:T(128)S(1)} %get-tuple-element.75.meta.refs_0_, ...), custom_call_target="tpu_custom_call" | custom-call | flops 805306368 | bytes 12582912 | tf_op jit(solution)/shard_map/pallas_call | solution.py:253
  17.3 0.0 collective-permute-done.refs_4_
  17.3 0.0 collective-permute-done.1.refs_5_
  17.4 0.0 collective-permute-done.3.refs_7_
  17.4 0.0 collective-permute-done.4.refs_8_
  17.4 0.8 %shard_map.123 = (f32[10,64,128]{2,1,0:T(8,128)S(1)}, f32[10,64,128]{2,1,0:T(8,128)S(1)}) custom-call(s32[46]{0:T(128)S(1)} %get-tuple-element.75.meta.refs_0_, bf16[10,128,128]{2,1,0:T(8,128)(2,1)S(1)} %get-tuple-element.76.refs_1_, f32[10,64,128]{2,1,0:T(8,128)S(1)} %get-tuple-element.85.refs_2_, f32[10,64,128]{2,1,0:T(8,128)S(1)} %get-tuple-element.86.refs_3_, ...), custom_call_target="tpu_custom_call" | custom-call | flops 20971520 | bytes 2097152 | tf_op jit(solution)/shard_map/pallas_call | solution.py:348
  18.2 1.0 %shard_map.124 = (bf16[64,64,128]{2,1,0:T(8,128)(2,1)S(1)}, bf16[64,64,128]{2,1,0:T(8,128)(2,1)S(1)}, bf16[256,128]{1,0:T(8,128)(2,1)S(1)}, bf16[256,128]{1,0:T(...) custom-call(s32[46]{0:T(128)S(1)} %get-tuple-element.75.meta.refs_0_, ...), custom_call_target="tpu_custom_call" | custom-call | flops 20971520 | bytes 5242880 | tf_op jit(solution)/shard_map/pallas_call | solution.py:413
  19.1 0.1 collective-permute-start.5
  19.2 0.7 %collective-permute-start.6 = (bf16[256,128]{1,0:T(8,128)(2,1)S(1)}, bf16[256,128]{1,0:T(8,128)(2,1)S(1)}, u32[]{:S(2)}, u32[]{:S(2)}) collective-permute-start(bf16[256,128]{1,0:T(8,128)(2,1)S(1)} %get-tuple-element.103), channel_id=1, source_target_pairs={{0,2},{2,0},{1,3},{3,1},{4,6},{6,4},{5,7},{7,5},{8,10},{10,8},{9,1... | collective-permute-start | bytes 196616 | tf_op jit(solution)/shard_map/ppermute | solution.py:589
  19.9 1.2 %collective-permute-start.7 = (bf16[256,128]{1,0:T(8,128)(2,1)S(1)}, bf16[256,128]{1,0:T(8,128)(2,1)S(1)}, u32[]{:S(2)}, u32[]{:S(2)}) collective-permute-start(bf16[256,128]{1,0:T(8,128)(2,1)S(1)} %get-tuple-element.104), channel_id=1, source_target_pairs={{0,4},{4,0},{1,5},{5,1},{2,6},{6,2},{3,7},{7,3},{8,12},{12,8},{9,1... | collective-permute-start | bytes 196616 | tf_op jit(solution)/shard_map/ppermute | solution.py:589
  21.2 0.5 collective-permute-start.8
  21.6 0.2 collective-permute-start.9
  21.8 4.5 %shard_map.125 = (bf16[64,64,128]{2,1,0:T(8,128)(2,1)S(1)}, bf16[64,64,128]{2,1,0:T(8,128)(2,1)S(1)}, f32[10,64,128]{2,1,0:T(8,128)S(1)}, f32[10,64,128]{2,1,0:T(8,128)S(1)}, f32[128,128]{1,0:T(8,128)S(1)}) custom-call(s32[46]{0:T(128)S(1)} %get-tuple-element.75.meta.refs_0_, s32[3,64]{1,0:T(4,128)S(1)} %get-tuple-element.77.col.refs_1_, ...), custom_call_target="tpu_custom_call" | custom-call | flops 805306368 | bytes 12582912 | tf_op jit(solution)/shard_map/pallas_call | solution.py:311
  26.3 0.0 collective-permute-done.5.refs_7_
  26.3 0.0 collective-permute-done.6.refs_8_
  26.4 0.0 collective-permute-done.8.refs_10_
  26.4 1.6 %collective-permute-done.9.refs_11_ = bf16[256,128]{1,0:T(8,128)(2,1)S(1)} collective-permute-done((bf16[256,128]{1,0:T(8,128)(2,1)S(1)}, bf16[256,128]{1,0:T(8,128)(2,1)S(1)}, u32[]{:S(2)}, u32[]{:S(2)}) %collective-permute-start.9) | collective-permute-done | bytes 65568 | tf_op jit(solution)/shard_map/ppermute | solution.py:589
  28.0 1.0 %shard_map.126 = (f32[10,64,128]{2,1,0:T(8,128)S(1)}, f32[10,64,128]{2,1,0:T(8,128)S(1)}, f32[64,128]{1,0:T(8,128)S(1)}, f32[64,128]{1,0:T(8,128)S(1)}) custom-call(s32[46]{0:T(128)S(1)} %get-tuple-element.75.meta.refs_0_, bf16[10,128,128]{2,1,0:T(8,128)(2,1)S(1)} %get-tuple-element.76.refs_1_, f32[10,64,128]{2,1,0:T(8,128)S(1)} %get-tuple-element.98.refs_2_, ...), custom_call_target="tpu_custom_call" | custom-call | flops 41943040 | bytes 3145728 | tf_op jit(solution)/shard_map/pallas_call | solution.py:382
  29.0 0.1 collective-permute-start.10
  29.1 1.0 %shard_map.127 = (bf16[64,64,128]{2,1,0:T(8,128)(2,1)S(1)}, bf16[64,64,128]{2,1,0:T(8,128)(2,1)S(1)}, bf16[256,128]{1,0:T(8,128)(2,1)S(1)}, bf16[256,128]{1,0:T(...) custom-call(s32[46]{0:T(128)S(1)} %get-tuple-element.75.meta.refs_0_, ...), custom_call_target="tpu_custom_call" | custom-call | flops 20971520 | bytes 5242880 | tf_op jit(solution)/shard_map/pallas_call | solution.py:413
  30.1 0.6 collective-permute-start.13
  30.6 0.0 collective-permute-done.10.refs_1_
  30.6 2.2 %collective-permute-start.12 = (f32[64,128]{1,0:T(8,128)S(1)}, f32[64,128]{1,0:T(8,128)S(1)}, u32[]{:S(2)}, u32[]{:S(2)}) collective-permute-start(f32[64,128]{1,0:T(8,128)S(1)} %get-tuple-element.118.refs_0_), channel_id=1, source_target_pairs={{0,16},{16,0},{1,17},{17,1},{2,18},{18,2},{3,19},{19,3},{4,20},{20... | collective-permute-start | bytes 98312 | tf_op jit(solution)/shard_map/ppermute | solution.py:589
  32.9 0.7 %collective-permute-start.11 = (bf16[256,128]{1,0:T(8,128)(2,1)S(1)}, bf16[256,128]{1,0:T(8,128)(2,1)S(1)}, u32[]{:S(2)}, u32[]{:S(2)}) collective-permute-start(bf16[256,128]{1,0:T(8,128)(2,1)S(1)} %get-tuple-element.117), channel_id=1, source_target_pairs={{0,16},{16,0},{1,17},{17,1},{2,18},{18,2},{3,19},{19,3},{4,20},{20... | collective-permute-start | bytes 196616 | tf_op jit(solution)/shard_map/ppermute | solution.py:589
  33.6 3.4 %shard_map.129 = (bf16[64,64,128]{2,1,0:T(8,128)(2,1)S(1)}, bf16[64,64,128]{2,1,0:T(8,128)(2,1)S(1)}, f32[10,64,128]{2,1,0:T(8,128)S(1)}, f32[10,64,128]{2,1,0:T(8,128)S(1)}, f32[8,128]{1,0:T(8,128)S(1)}) custom-call(s32[46]{0:T(128)S(1)} %get-tuple-element.75.meta.refs_0_, s32[3,64]{1,0:T(4,128)S(1)} %get-tuple-element.77.col.refs_1_, ...), custom_call_target="tpu_custom_call" | custom-call | flops 805306368 | bytes 12582912 | tf_op jit(solution)/shard_map/pallas_call | solution.py:311
  37.1 0.0 collective-permute-done.12.refs_1_
  37.1 1.8 %collective-permute-done.11.refs_4_ = bf16[256,128]{1,0:T(8,128)(2,1)S(1)} collective-permute-done((bf16[256,128]{1,0:T(8,128)(2,1)S(1)}, bf16[256,128]{1,0:T(8,128)(2,1)S(1)}, u32[]{:S(2)}, u32[]{:S(2)}) %collective-permute-start.11) | collective-permute-done | bytes 65568 | tf_op jit(solution)/shard_map/ppermute | solution.py:589
  38.9 0.1 collective-permute-start.14
  39.1 2.0 %collective-permute-start.15 = (f32[64,128]{1,0:T(8,128)S(1)}, f32[64,128]{1,0:T(8,128)S(1)}, u32[]{:S(2)}, u32[]{:S(2)}) collective-permute-start(f32[64,128]{1,0:T(8,128)S(1)} %get-tuple-element.123.refs_0_), channel_id=1, source_target_pairs={{0,8},{8,0},{1,9},{9,1},{2,10},{10,2},{3,11},{11,3},{4,12},{12,4},... | collective-permute-start | bytes 98312 | tf_op jit(solution)/shard_map/ppermute | solution.py:589
  41.0 2.9 %shard_map.131 = (bf16[8,64,8,128]{3,2,1,0:T(8,128)(2,1)}, bf16[8,64,8,128]{3,2,1,0:T(8,128)(2,1)}, f32[8,128]{1,0:T(8,128)S(1)}) custom-call(s32[46]{0:T(128)S(1)} %get-tuple-element.75.meta.refs_0_, bf16[4,64,64]{2,1,0:T(8,128)(2,1)S(1)} %copy-done, bf16[64,64,128]{2,1,0:T(8,128)(2,1)S(1)} %get-tuple-element.78.t0.refs_6_.refs_2_.refs_7_, ...), custom_call_target="tpu_custom_call" | custom-call | flops 268435456 | bytes 10485760 | tf_op jit(solution)/shard_map/pallas_call | solution.py:485
  44.0 1.7 %collective-permute-start.16 = (bf16[256,128]{1,0:T(8,128)(2,1)S(1)}, bf16[256,128]{1,0:T(8,128)(2,1)S(1)}, u32[]{:S(2)}, u32[]{:S(2)}) collective-permute-start(bf16[256,128]{1,0:T(8,128)(2,1)S(1)} %get-tuple-element.129), channel_id=1, source_target_pairs={{0,4},{4,0},{1,5},{5,1},{2,6},{6,2},{3,7},{7,3},{8,12},{12,8},{9,1... | collective-permute-start | bytes 196616 | tf_op jit(solution)/shard_map/ppermute | solution.py:589
  45.6 0.4 collective-permute-start.17
  46.1 2.4 %shard_map.133 = (bf16[8,64,8,128]{3,2,1,0:T(8,128)(2,1)}, bf16[8,64,8,128]{3,2,1,0:T(8,128)(2,1)}, f32[8,128]{1,0:T(8,128)S(1)}) custom-call(s32[46]{0:T(128)S(1)} %get-tuple-element.75.meta.refs_0_, bf16[4,64,64]{2,1,0:T(8,128)(2,1)S(1)} %copy-done, ...), custom_call_target="tpu_custom_call", output_to_operand_aliasing={{0}: (11, {}), {1}: (12, {})} | custom-call | flops 268435456 | bytes 10485760 | tf_op jit(solution)/shard_map/pallas_call | solution.py:485
  48.5 1.1 %collective-permute-done.17.refs_1_ = f32[64,128]{1,0:T(8,128)S(1)} collective-permute-done((f32[64,128]{1,0:T(8,128)S(1)}, f32[64,128]{1,0:T(8,128)S(1)}, u32[]{:S(2)}, u32[]{:S(2)}) %collective-permute-start.17) | collective-permute-done | bytes 32800 | tf_op jit(solution)/shard_map/ppermute | solution.py:589
  49.6 1.6 %collective-permute-start.19 = (f32[64,128]{1,0:T(8,128)S(1)}, f32[64,128]{1,0:T(8,128)S(1)}, u32[]{:S(2)}, u32[]{:S(2)}) collective-permute-start(f32[64,128]{1,0:T(8,128)S(1)} %get-tuple-element.140.refs_0_), channel_id=1, source_target_pairs={{0,2},{2,0},{1,3},{3,1},{4,6},{6,4},{5,7},{7,5},{8,10},{10,8},{9,1... | collective-permute-start | bytes 98312 | tf_op jit(solution)/shard_map/ppermute | solution.py:589
  51.1 0.5 collective-permute-start.18
  51.6 0.8 %shard_map.135 = (f32[10,64,128]{2,1,0:T(8,128)S(1)}, f32[10,64,128]{2,1,0:T(8,128)S(1)}) custom-call(s32[46]{0:T(128)S(1)} %get-tuple-element.75.meta.refs_0_, bf16[10,128,128]{2,1,0:T(8,128)(2,1)S(1)} %get-tuple-element.76.refs_1_, f32[10,64,128]{2,1,0:T(8,128)S(1)} %get-tuple-element.115.refs_2_, f32[10,64,128]{2,1,0:T(8,128)S(1)} %get-tuple-element.116.refs_3_, ...), custom_call_target="tpu_custom_call" | custom-call | flops 12582912 | bytes 2097152 | tf_op jit(solution)/shard_map/pallas_call | solution.py:348
  52.4 1.1 %collective-permute-done.19.refs_1_ = f32[64,128]{1,0:T(8,128)S(1)} collective-permute-done((f32[64,128]{1,0:T(8,128)S(1)}, f32[64,128]{1,0:T(8,128)S(1)}, u32[]{:S(2)}, u32[]{:S(2)}) %collective-permute-start.19) | collective-permute-done | bytes 32800 | tf_op jit(solution)/shard_map/ppermute | solution.py:589
  53.5 0.6 %shard_map.136 = (f32[64,128]{1,0:T(8,128)S(1)}, f32[8,128]{1,0:T(8,128)}) custom-call(f32[64,128]{1,0:T(8,128)S(1)} %get-tuple-element.140.refs_0_, f32[64,128]{1,0:T(8,128)S(1)} %collective-permute-done.19.refs_1_, f32[10,64,128]{2,1,0:T(8,128)S(1)} %get-tuple-element.137.refs_2_.refs_3_), custom_call_target="tpu_custom_call" | custom-call | flops 8192 | bytes 98304 | tf_op jit(solution)/shard_map/pallas_call | solution.py:570
  54.1 1.2 %collective-permute-done.20.refs_14_ = f32[64,128]{1,0:T(8,128)S(1)} collective-permute-done((f32[64,128]{1,0:T(8,128)S(1)}, f32[64,128]{1,0:T(8,128)S(1)}, u32[]{:S(2)}, u32[]{:S(2)}) %collective-permute-start.20) | collective-permute-done | bytes 32800 | tf_op jit(solution)/shard_map/ppermute | solution.py:589
  55.3 0.0 collective-permute-done.18.refs_6_
  55.4 2.6 %shard_map.137 = (bf16[8,64,8,128]{3,2,1,0:T(8,128)(2,1)}, bf16[8,64,8,128]{3,2,1,0:T(8,128)(2,1)}, f32[4,64,64]{2,1,0:T(8,128)}) custom-call(s32[46]{0:T(128)S(1)} %get-tuple-element.75.meta.refs_0_, bf16[10,128,128]{2,1,0:T(8,128)(2,1)S(1)} %get-tuple-element.76.refs_1_, ...), custom_call_target="tpu_custom_call", output_to_operand_aliasing={{0}: (15, {}), {1}: (16, {})} | custom-call | flops 83886080 | bytes 4194304 | tf_op jit(solution)/shard_map/pallas_call | solution.py:540
  (13 shorter events, 0.1 us)
Async XLA Ops:
  4.1 13.3 %collective-permute-start = (bf16[256,128]{1,0:T(8,128)(2,1)S(1)}, bf16[256,128]{1,0:T(8,128)(2,1)S(1)}, u32[]{:S(2)}, u32[]{:S(2)}) collective-permute-start(bf16[256,128]{1,0:T(8,128)(2,1)S(1)} %get-tuple-element.87), channel_id=1, source_target_pairs={{0,1},{1,0},{2,3},{3,2},{4,5},{5,4},{6,7},{7,6},{8,9},{9,8},{10,11... | collective-permute-start | bytes 196616 | tf_op jit(solution)/shard_map/ppermute | solution.py:589
  4.9 12.5 %collective-permute-start.1 = (bf16[256,128]{1,0:T(8,128)(2,1)S(1)}, bf16[256,128]{1,0:T(8,128)(2,1)S(1)}, u32[]{:S(2)}, u32[]{:S(2)}) collective-permute-start(bf16[256,128]{1,0:T(8,128)(2,1)S(1)} %get-tuple-element.88), channel_id=1, source_target_pairs={{0,2},{2,0},{1,3},{3,1},{4,6},{6,4},{5,7},{7,5},{8,10},{10,8},{9,1... | collective-permute-start | bytes 196616 | tf_op jit(solution)/shard_map/ppermute | solution.py:589
  7.2 10.2 %collective-permute-start.2 = (bf16[256,128]{1,0:T(8,128)(2,1)S(1)}, bf16[256,128]{1,0:T(8,128)(2,1)S(1)}, u32[]{:S(2)}, u32[]{:S(2)}) collective-permute-start(bf16[256,128]{1,0:T(8,128)(2,1)S(1)} %get-tuple-element.89), channel_id=1, source_target_pairs={{0,4},{4,0},{1,5},{5,1},{2,6},{6,2},{3,7},{7,3},{8,12},{12,8},{9,1... | collective-permute-start | bytes 196616 | tf_op jit(solution)/shard_map/ppermute | solution.py:589
  8.9 8.5 %collective-permute-start.3 = (bf16[256,128]{1,0:T(8,128)(2,1)S(1)}, bf16[256,128]{1,0:T(8,128)(2,1)S(1)}, u32[]{:S(2)}, u32[]{:S(2)}) collective-permute-start(bf16[256,128]{1,0:T(8,128)(2,1)S(1)} %get-tuple-element.90), channel_id=1, source_target_pairs={{0,8},{8,0},{1,9},{9,1},{2,10},{10,2},{3,11},{11,3},{4,12},{12,4},... | collective-permute-start | bytes 196616 | tf_op jit(solution)/shard_map/ppermute | solution.py:589
  10.1 7.2 %collective-permute-start.4 = (bf16[256,128]{1,0:T(8,128)(2,1)S(1)}, bf16[256,128]{1,0:T(8,128)(2,1)S(1)}, u32[]{:S(2)}, u32[]{:S(2)}) collective-permute-start(bf16[256,128]{1,0:T(8,128)(2,1)S(1)} %get-tuple-element.91), channel_id=1, source_target_pairs={{0,16},{16,0},{1,17},{17,1},{2,18},{18,2},{3,19},{19,3},{4,20},{20... | collective-permute-start | bytes 196616 | tf_op jit(solution)/shard_map/ppermute | solution.py:589
  19.1 7.2 %collective-permute-start.5 = (bf16[256,128]{1,0:T(8,128)(2,1)S(1)}, bf16[256,128]{1,0:T(8,128)(2,1)S(1)}, u32[]{:S(2)}, u32[]{:S(2)}) collective-permute-start(bf16[256,128]{1,0:T(8,128)(2,1)S(1)} %get-tuple-element.102), channel_id=1, source_target_pairs={{0,1},{1,0},{2,3},{3,2},{4,5},{5,4},{6,7},{7,6},{8,9},{9,8},{10,11... | collective-permute-start | bytes 196616 | tf_op jit(solution)/shard_map/ppermute | solution.py:589
  19.2 7.1 %collective-permute-start.6 = (bf16[256,128]{1,0:T(8,128)(2,1)S(1)}, bf16[256,128]{1,0:T(8,128)(2,1)S(1)}, u32[]{:S(2)}, u32[]{:S(2)}) collective-permute-start(bf16[256,128]{1,0:T(8,128)(2,1)S(1)} %get-tuple-element.103), channel_id=1, source_target_pairs={{0,2},{2,0},{1,3},{3,1},{4,6},{6,4},{5,7},{7,5},{8,10},{10,8},{9,1... | collective-permute-start | bytes 196616 | tf_op jit(solution)/shard_map/ppermute | solution.py:589
  19.9 6.4 %collective-permute-start.7 = (bf16[256,128]{1,0:T(8,128)(2,1)S(1)}, bf16[256,128]{1,0:T(8,128)(2,1)S(1)}, u32[]{:S(2)}, u32[]{:S(2)}) collective-permute-start(bf16[256,128]{1,0:T(8,128)(2,1)S(1)} %get-tuple-element.104), channel_id=1, source_target_pairs={{0,4},{4,0},{1,5},{5,1},{2,6},{6,2},{3,7},{7,3},{8,12},{12,8},{9,1... | collective-permute-start | bytes 196616 | tf_op jit(solution)/shard_map/ppermute | solution.py:589
  21.2 5.2 %collective-permute-start.8 = (bf16[256,128]{1,0:T(8,128)(2,1)S(1)}, bf16[256,128]{1,0:T(8,128)(2,1)S(1)}, u32[]{:S(2)}, u32[]{:S(2)}) collective-permute-start(bf16[256,128]{1,0:T(8,128)(2,1)S(1)} %get-tuple-element.105), channel_id=1, source_target_pairs={{0,8},{8,0},{1,9},{9,1},{2,10},{10,2},{3,11},{11,3},{4,12},{12,4},... | collective-permute-start | bytes 196616 | tf_op jit(solution)/shard_map/ppermute | solution.py:589
  21.6 6.4 %collective-permute-start.9 = (bf16[256,128]{1,0:T(8,128)(2,1)S(1)}, bf16[256,128]{1,0:T(8,128)(2,1)S(1)}, u32[]{:S(2)}, u32[]{:S(2)}) collective-permute-start(bf16[256,128]{1,0:T(8,128)(2,1)S(1)} %get-tuple-element.106), channel_id=1, source_target_pairs={{0,16},{16,0},{1,17},{17,1},{2,18},{18,2},{3,19},{19,3},{4,20},{20... | collective-permute-start | bytes 196616 | tf_op jit(solution)/shard_map/ppermute | solution.py:589
  29.0 1.6 %collective-permute-start.10 = (f32[64,128]{1,0:T(8,128)S(1)}, f32[64,128]{1,0:T(8,128)S(1)}, u32[]{:S(2)}, u32[]{:S(2)}) collective-permute-start(f32[64,128]{1,0:T(8,128)S(1)} %get-tuple-element.112), channel_id=1, source_target_pairs={{0,1},{1,0},{2,3},{3,2},{4,5},{5,4},{6,7},{7,6},{8,9},{9,8},{10,11... | collective-permute-start | bytes 98312 | tf_op jit(solution)/shard_map/ppermute | solution.py:589
  30.1 7.0 %collective-permute-start.13 = (bf16[256,128]{1,0:T(8,128)(2,1)S(1)}, bf16[256,128]{1,0:T(8,128)(2,1)S(1)}, u32[]{:S(2)}, u32[]{:S(2)}) collective-permute-start(bf16[256,128]{1,0:T(8,128)(2,1)S(1)} %get-tuple-element.121), channel_id=1, source_target_pairs={{0,1},{1,0},{2,3},{3,2},{4,5},{5,4},{6,7},{7,6},{8,9},{9,8},{10,11... | collective-permute-start | bytes 196616 | tf_op jit(solution)/shard_map/ppermute | solution.py:589
  30.6 6.5 %collective-permute-start.12 = (f32[64,128]{1,0:T(8,128)S(1)}, f32[64,128]{1,0:T(8,128)S(1)}, u32[]{:S(2)}, u32[]{:S(2)}) collective-permute-start(f32[64,128]{1,0:T(8,128)S(1)} %get-tuple-element.118.refs_0_), channel_id=1, source_target_pairs={{0,16},{16,0},{1,17},{17,1},{2,18},{18,2},{3,19},{19,3},{4,20},{20... | collective-permute-start | bytes 98312 | tf_op jit(solution)/shard_map/ppermute | solution.py:589
  32.9 6.1 %collective-permute-start.11 = (bf16[256,128]{1,0:T(8,128)(2,1)S(1)}, bf16[256,128]{1,0:T(8,128)(2,1)S(1)}, u32[]{:S(2)}, u32[]{:S(2)}) collective-permute-start(bf16[256,128]{1,0:T(8,128)(2,1)S(1)} %get-tuple-element.117), channel_id=1, source_target_pairs={{0,16},{16,0},{1,17},{17,1},{2,18},{18,2},{3,19},{19,3},{4,20},{20... | collective-permute-start | bytes 196616 | tf_op jit(solution)/shard_map/ppermute | solution.py:589
  33.6 7.4 %copy-start = (bf16[4,64,64]{2,1,0:T(8,128)(2,1)S(1)}, bf16[4,64,64]{2,1,0:T(8,128)(2,1)}, u32[]{:S(2)}) copy-start(bf16[4,64,64]{2,1,0:T(8,128)(2,1)} %refs_2_.1) | copy-start | bytes 98308
  38.9 5.0 %collective-permute-start.14 = (bf16[256,128]{1,0:T(8,128)(2,1)S(1)}, bf16[256,128]{1,0:T(8,128)(2,1)S(1)}, u32[]{:S(2)}, u32[]{:S(2)}) collective-permute-start(bf16[256,128]{1,0:T(8,128)(2,1)S(1)} %get-tuple-element.122), channel_id=1, source_target_pairs={{0,8},{8,0},{1,9},{9,1},{2,10},{10,2},{3,11},{11,3},{4,12},{12,4},... | collective-permute-start | bytes 196616 | tf_op jit(solution)/shard_map/ppermute | solution.py:589
  39.1 4.9 %collective-permute-start.15 = (f32[64,128]{1,0:T(8,128)S(1)}, f32[64,128]{1,0:T(8,128)S(1)}, u32[]{:S(2)}, u32[]{:S(2)}) collective-permute-start(f32[64,128]{1,0:T(8,128)S(1)} %get-tuple-element.123.refs_0_), channel_id=1, source_target_pairs={{0,8},{8,0},{1,9},{9,1},{2,10},{10,2},{3,11},{11,3},{4,12},{12,4},... | collective-permute-start | bytes 98312 | tf_op jit(solution)/shard_map/ppermute | solution.py:589
  44.0 5.6 %collective-permute-start.16 = (bf16[256,128]{1,0:T(8,128)(2,1)S(1)}, bf16[256,128]{1,0:T(8,128)(2,1)S(1)}, u32[]{:S(2)}, u32[]{:S(2)}) collective-permute-start(bf16[256,128]{1,0:T(8,128)(2,1)S(1)} %get-tuple-element.129), channel_id=1, source_target_pairs={{0,4},{4,0},{1,5},{5,1},{2,6},{6,2},{3,7},{7,3},{8,12},{12,8},{9,1... | collective-permute-start | bytes 196616 | tf_op jit(solution)/shard_map/ppermute | solution.py:589
  45.6 3.9 %collective-permute-start.17 = (f32[64,128]{1,0:T(8,128)S(1)}, f32[64,128]{1,0:T(8,128)S(1)}, u32[]{:S(2)}, u32[]{:S(2)}) collective-permute-start(f32[64,128]{1,0:T(8,128)S(1)} %get-tuple-element.130.refs_0_), channel_id=1, source_target_pairs={{0,4},{4,0},{1,5},{5,1},{2,6},{6,2},{3,7},{7,3},{8,12},{12,8},{9,1... | collective-permute-start | bytes 98312 | tf_op jit(solution)/shard_map/ppermute | solution.py:589
  49.6 4.0 %collective-permute-start.19 = (f32[64,128]{1,0:T(8,128)S(1)}, f32[64,128]{1,0:T(8,128)S(1)}, u32[]{:S(2)}, u32[]{:S(2)}) collective-permute-start(f32[64,128]{1,0:T(8,128)S(1)} %get-tuple-element.140.refs_0_), channel_id=1, source_target_pairs={{0,2},{2,0},{1,3},{3,1},{4,6},{6,4},{5,7},{7,5},{8,10},{10,8},{9,1... | collective-permute-start | bytes 98312 | tf_op jit(solution)/shard_map/ppermute | solution.py:589
  51.1 4.3 %collective-permute-start.18 = (bf16[256,128]{1,0:T(8,128)(2,1)S(1)}, bf16[256,128]{1,0:T(8,128)(2,1)S(1)}, u32[]{:S(2)}, u32[]{:S(2)}) collective-permute-start(bf16[256,128]{1,0:T(8,128)(2,1)S(1)} %get-tuple-element.139), channel_id=1, source_target_pairs={{0,2},{2,0},{1,3},{3,1},{4,6},{6,4},{5,7},{7,5},{8,10},{10,8},{9,1... | collective-permute-start | bytes 196616 | tf_op jit(solution)/shard_map/ppermute | solution.py:589
  54.1 1.2 %collective-permute-start.20 = (f32[64,128]{1,0:T(8,128)S(1)}, f32[64,128]{1,0:T(8,128)S(1)}, u32[]{:S(2)}, u32[]{:S(2)}) collective-permute-start(f32[64,128]{1,0:T(8,128)S(1)} %get-tuple-element.141.refs_13_), channel_id=1, source_target_pairs={{0,1},{1,0},{2,3},{3,2},{4,5},{5,4},{6,7},{7,6},{8,9},{9,8},{10,11... | collective-permute-start | bytes 98312 | tf_op jit(solution)/shard_map/ppermute | solution.py:589

commit v5 on v4

--- a/solution.py
+++ b/solution.py
@@ -553,15 +553,16 @@
 
 def add_kernel(gated, inputs, *refs):
     mine, theirs = refs[:2]
-    out, token = refs[inputs : inputs + 2]
+    outs = refs[inputs:]
     if gated:
-        refs[-1][...] = refs[2][...]
-    out[...] = mine[...] + theirs[...]
-    token[...] = jnp.zeros(token.shape, F32)
-
-
-def add(mine, theirs, pay, after):
-    outs = [shape(mine.shape, F32), TOKEN]
+        outs[2][...] = refs[2][...]
+    outs[0][...] = mine[...] + theirs[...]
+    if len(outs) > 1:
+        outs[1][...] = jnp.zeros(outs[1].shape, F32)
+
+
+def add(mine, theirs, pay, after, last=False):
+    outs = [shape(mine.shape, F32)] + ([] if last else [TOKEN])
     args = [mine, theirs]
     if pay is not None:
         outs.append(shape(pay.shape, BF16))
@@ -652,6 +653,7 @@
     early = [bit for bit in bits[:-1] if bit < sz.rounds]
     late = [bit for bit in everyone if bit not in early]
     mine, token, *rest = add(mine, theirs, pays[bits[0]] if bits[0] < sz.rounds else None, [])
+    held = [got[0]]
     for at, bit in enumerate(bits):
         if bit < sz.rounds:
             pays[bit] = rest[0]
@@ -665,10 +667,12 @@
             picked = couple(sz, 2.0, meta, across, state["base"][2:4], got, early, [token])
             token = picked[0]
         gated = not last and bits[at + 1] < sz.rounds
-        after = [token] + ([got[bit]] if bit < sz.rounds and not last else [])
-        if at == 0:
-            after.append(got[0])
-        mine, token, *rest = add(mine, theirs, pays[bits[at + 1]] if gated else None, after)
+        after = [token] + held
+        held = [got[bit]] if bit < sz.rounds else []
+        if last:
+            (mine,) = add(mine, theirs, None, after, True)
+        else:
+            mine, token, *rest = add(mine, theirs, pays[bits[at + 1]] if gated else None, after)
     theirs = from_partner(mine, 0)
     out4, grad4, grad_w = fix_outputs(
         sz,

time: 58.1 us -> 56.2 us (0.967)
  waiting for transfers between devices: 6.95 us -> 5.58 us
  Pallas kernels: 28.3 us -> 27.7 us
    ppermute x21, waiting for transfers between devices: 6.95 us -> 5.58 us  [from_partner(): return lax.ppermute(values, 'dom', route)]
    pallas_call x5, Pallas kernels: 0.64 us -> 0.06 us  [add(): call(functools.partial(add_kernel, pay is not None, len(args)), [VMEM] *...]
  transfers between devices with their start and end apart: 21 -> 21, of which waited for: 5 -> 4; matrix products, arithmetic and copies ran while one was open for 0% -> 0% of each run, Pallas kernels for 35% -> 35%
where the time goes in v5:
time: 56.2 us; the launch traced here: 56 us
  Pallas kernels  27.7 us (49%)
  starting transfers between devices  21.2 us (38%)
  waiting for transfers between devices  5.58 us (10%)
  between operations  1.52 us (3%)
    ppermute x21, starting transfers between devices, from_partner(): return lax.ppermute(values, 'dom', route)  21.2 us
    pallas_call x2, Pallas kernels, local_products(): call(functools.partial(local_kernel, sz, grad), [SMEM, SMEM] + [VMEM] * 7...  7.96 us
    ppermute x21, waiting for transfers between devices, from_partner(): return lax.ppermute(values, 'dom', route)  5.58 us
    pallas_call x2, Pallas kernels, base_outputs(): call(functools.partial(output_kernel, sz, low, high), specs, [HBM, HBM, V...  5.28 us
    pallas_call x1, Pallas kernels, first_products(): call(functools.partial(first_kernel, sz), [SMEM, SMEM, HBM, VMEM, VMEM],...  4.59 us
    pallas_call x1, Pallas kernels, pack(): call(functools.partial(pack_kernel, sz), [HBM] * 6 + [SMEM, HBM], [VMEM]...  2.79 us
    pallas_call x1, Pallas kernels, fix_outputs(): call(functools.partial(fix_kernel, sz, axis, which), [SMEM] + [VMEM] * (l...  2.58 us
    pallas_call x2, Pallas kernels, join(): call(functools.partial(join_kernel, sz), [SMEM] + [VMEM] * (len(args) - 1...  1.92 us
  transfers between devices with their start and end apart: 21, of which 4 were waited for; matrix products, arithmetic and copies ran while one was open for 0% of the time, Pallas kernels for 35%

profile of v5, /device:TPU:0, one launch (start us, length us, event | category | flops | bytes accessed | tf_op | source)
XLA Modules:
  0.0 56.0 jit_solution(15046616622938378922)
XLA Ops:
  1.3 2.8 %shard_map.121 = (bf16[64,64,128]{2,1,0:T(8,128)(2,1)S(1)}, bf16[64,64,128]{2,1,0:T(8,128)(2,1)S(1)}, bf16[10,128,128]{2,1,0:T(8,128)(2,1)S(1)}, bf16[10,128,128...) custom-call(bf16[8,64,8,128]{3,2,1,0:T(8,128)(2,1)} %bitcast.18, ...), custom_call_target="tpu_custom_call" | custom-call | flops 1000 | bytes 4194304 | tf_op jit(solution)/shard_map/pallas_call | solution.py:143
  4.1 0.8 %collective-permute-start = (bf16[256,128]{1,0:T(8,128)(2,1)S(1)}, bf16[256,128]{1,0:T(8,128)(2,1)S(1)}, u32[]{:S(2)}, u32[]{:S(2)}) collective-permute-start(bf16[256,128]{1,0:T(8,128)(2,1)S(1)} %get-tuple-element.86), channel_id=1, source_target_pairs={{0,1},{1,0},{2,3},{3,2},{4,5},{5,4},{6,7},{7,6},{8,9},{9,8},{10,11... | collective-permute-start | bytes 196616 | tf_op jit(solution)/shard_map/ppermute | solution.py:590
  4.9 2.3 %collective-permute-start.1 = (bf16[256,128]{1,0:T(8,128)(2,1)S(1)}, bf16[256,128]{1,0:T(8,128)(2,1)S(1)}, u32[]{:S(2)}, u32[]{:S(2)}) collective-permute-start(bf16[256,128]{1,0:T(8,128)(2,1)S(1)} %get-tuple-element.87), channel_id=1, source_target_pairs={{0,2},{2,0},{1,3},{3,1},{4,6},{6,4},{5,7},{7,5},{8,10},{10,8},{9,1... | collective-permute-start | bytes 196616 | tf_op jit(solution)/shard_map/ppermute | solution.py:590
  7.2 1.7 %collective-permute-start.2 = (bf16[256,128]{1,0:T(8,128)(2,1)S(1)}, bf16[256,128]{1,0:T(8,128)(2,1)S(1)}, u32[]{:S(2)}, u32[]{:S(2)}) collective-permute-start(bf16[256,128]{1,0:T(8,128)(2,1)S(1)} %get-tuple-element.88), channel_id=1, source_target_pairs={{0,4},{4,0},{1,5},{5,1},{2,6},{6,2},{3,7},{7,3},{8,12},{12,8},{9,1... | collective-permute-start | bytes 196616 | tf_op jit(solution)/shard_map/ppermute | solution.py:590
  8.9 1.3 %collective-permute-start.3 = (bf16[256,128]{1,0:T(8,128)(2,1)S(1)}, bf16[256,128]{1,0:T(8,128)(2,1)S(1)}, u32[]{:S(2)}, u32[]{:S(2)}) collective-permute-start(bf16[256,128]{1,0:T(8,128)(2,1)S(1)} %get-tuple-element.89), channel_id=1, source_target_pairs={{0,8},{8,0},{1,9},{9,1},{2,10},{10,2},{3,11},{11,3},{4,12},{12,4},... | collective-permute-start | bytes 196616 | tf_op jit(solution)/shard_map/ppermute | solution.py:590
  10.1 2.6 %collective-permute-start.4 = (bf16[256,128]{1,0:T(8,128)(2,1)S(1)}, bf16[256,128]{1,0:T(8,128)(2,1)S(1)}, u32[]{:S(2)}, u32[]{:S(2)}) collective-permute-start(bf16[256,128]{1,0:T(8,128)(2,1)S(1)} %get-tuple-element.90), channel_id=1, source_target_pairs={{0,16},{16,0},{1,17},{17,1},{2,18},{18,2},{3,19},{19,3},{4,20},{20... | collective-permute-start | bytes 196616 | tf_op jit(solution)/shard_map/ppermute | solution.py:590
  12.7 4.6 %shard_map.122 = (bf16[64,64,128]{2,1,0:T(8,128)(2,1)S(1)}, bf16[64,64,128]{2,1,0:T(8,128)(2,1)S(1)}, f32[10,64,128]{2,1,0:T(8,128)S(1)}, f32[10,64,128]{2,1,0:T...) custom-call(s32[46]{0:T(128)S(1)} %get-tuple-element.74.meta.refs_0_, ...), custom_call_target="tpu_custom_call" | custom-call | flops 805306368 | bytes 12582912 | tf_op jit(solution)/shard_map/pallas_call | solution.py:253
  17.3 0.0 collective-permute-done.refs_4_
  17.3 0.0 collective-permute-done.1.refs_5_
  17.4 0.0 collective-permute-done.3.refs_7_
  17.4 0.0 collective-permute-done.4.refs_8_
  17.4 0.8 %shard_map.123 = (f32[10,64,128]{2,1,0:T(8,128)S(1)}, f32[10,64,128]{2,1,0:T(8,128)S(1)}) custom-call(s32[46]{0:T(128)S(1)} %get-tuple-element.74.meta.refs_0_, bf16[10,128,128]{2,1,0:T(8,128)(2,1)S(1)} %get-tuple-element.75.refs_1_, f32[10,64,128]{2,1,0:T(8,128)S(1)} %get-tuple-element.84.refs_2_, f32[10,64,128]{2,1,0:T(8,128)S(1)} %get-tuple-element.85.refs_3_, ...), custom_call_target="tpu_custom_call" | custom-call | flops 20971520 | bytes 2097152 | tf_op jit(solution)/shard_map/pallas_call | solution.py:348
  18.2 1.0 %shard_map.124 = (bf16[64,64,128]{2,1,0:T(8,128)(2,1)S(1)}, bf16[64,64,128]{2,1,0:T(8,128)(2,1)S(1)}, bf16[256,128]{1,0:T(8,128)(2,1)S(1)}, bf16[256,128]{1,0:T(...) custom-call(s32[46]{0:T(128)S(1)} %get-tuple-element.74.meta.refs_0_, ...), custom_call_target="tpu_custom_call" | custom-call | flops 20971520 | bytes 5242880 | tf_op jit(solution)/shard_map/pallas_call | solution.py:413
  19.1 0.1 collective-permute-start.5
  19.2 0.7 %collective-permute-start.6 = (bf16[256,128]{1,0:T(8,128)(2,1)S(1)}, bf16[256,128]{1,0:T(8,128)(2,1)S(1)}, u32[]{:S(2)}, u32[]{:S(2)}) collective-permute-start(bf16[256,128]{1,0:T(8,128)(2,1)S(1)} %get-tuple-element.102), channel_id=1, source_target_pairs={{0,2},{2,0},{1,3},{3,1},{4,6},{6,4},{5,7},{7,5},{8,10},{10,8},{9,1... | collective-permute-start | bytes 196616 | tf_op jit(solution)/shard_map/ppermute | solution.py:590
  19.9 1.2 %collective-permute-start.7 = (bf16[256,128]{1,0:T(8,128)(2,1)S(1)}, bf16[256,128]{1,0:T(8,128)(2,1)S(1)}, u32[]{:S(2)}, u32[]{:S(2)}) collective-permute-start(bf16[256,128]{1,0:T(8,128)(2,1)S(1)} %get-tuple-element.103), channel_id=1, source_target_pairs={{0,4},{4,0},{1,5},{5,1},{2,6},{6,2},{3,7},{7,3},{8,12},{12,8},{9,1... | collective-permute-start | bytes 196616 | tf_op jit(solution)/shard_map/ppermute | solution.py:590
  21.2 0.5 collective-permute-start.8
  21.6 0.2 collective-permute-start.9
  21.8 4.5 %shard_map.125 = (bf16[64,64,128]{2,1,0:T(8,128)(2,1)S(1)}, bf16[64,64,128]{2,1,0:T(8,128)(2,1)S(1)}, f32[10,64,128]{2,1,0:T(8,128)S(1)}, f32[10,64,128]{2,1,0:T(8,128)S(1)}, f32[128,128]{1,0:T(8,128)S(1)}) custom-call(s32[46]{0:T(128)S(1)} %get-tuple-element.74.meta.refs_0_, s32[3,64]{1,0:T(4,128)S(1)} %get-tuple-element.76.col.refs_1_, ...), custom_call_target="tpu_custom_call" | custom-call | flops 805306368 | bytes 12582912 | tf_op jit(solution)/shard_map/pallas_call | solution.py:311
  26.3 0.0 collective-permute-done.5.refs_7_
  26.3 0.0 collective-permute-done.6.refs_8_
  26.4 0.0 collective-permute-done.8.refs_10_
  26.4 1.6 %collective-permute-done.9.refs_11_ = bf16[256,128]{1,0:T(8,128)(2,1)S(1)} collective-permute-done((bf16[256,128]{1,0:T(8,128)(2,1)S(1)}, bf16[256,128]{1,0:T(8,128)(2,1)S(1)}, u32[]{:S(2)}, u32[]{:S(2)}) %collective-permute-start.9) | collective-permute-done | bytes 65568 | tf_op jit(solution)/shard_map/ppermute | solution.py:590
  28.0 1.0 %shard_map.126 = (f32[10,64,128]{2,1,0:T(8,128)S(1)}, f32[10,64,128]{2,1,0:T(8,128)S(1)}, f32[64,128]{1,0:T(8,128)S(1)}, f32[64,128]{1,0:T(8,128)S(1)}) custom-call(s32[46]{0:T(128)S(1)} %get-tuple-element.74.meta.refs_0_, bf16[10,128,128]{2,1,0:T(8,128)(2,1)S(1)} %get-tuple-element.75.refs_1_, f32[10,64,128]{2,1,0:T(8,128)S(1)} %get-tuple-element.97.refs_2_, ...), custom_call_target="tpu_custom_call" | custom-call | flops 41943040 | bytes 3145728 | tf_op jit(solution)/shard_map/pallas_call | solution.py:382
  29.0 0.1 collective-permute-start.10
  29.1 1.0 %shard_map.127 = (bf16[64,64,128]{2,1,0:T(8,128)(2,1)S(1)}, bf16[64,64,128]{2,1,0:T(8,128)(2,1)S(1)}, bf16[256,128]{1,0:T(8,128)(2,1)S(1)}, bf16[256,128]{1,0:T(...) custom-call(s32[46]{0:T(128)S(1)} %get-tuple-element.74.meta.refs_0_, ...), custom_call_target="tpu_custom_call" | custom-call | flops 20971520 | bytes 5242880 | tf_op jit(solution)/shard_map/pallas_call | solution.py:413
  30.1 0.6 collective-permute-start.13
  30.6 0.0 collective-permute-done.10.refs_1_
  30.6 2.2 %collective-permute-start.12 = (f32[64,128]{1,0:T(8,128)S(1)}, f32[64,128]{1,0:T(8,128)S(1)}, u32[]{:S(2)}, u32[]{:S(2)}) collective-permute-start(f32[64,128]{1,0:T(8,128)S(1)} %get-tuple-element.117.refs_0_), channel_id=1, source_target_pairs={{0,16},{16,0},{1,17},{17,1},{2,18},{18,2},{3,19},{19,3},{4,20},{20... | collective-permute-start | bytes 98312 | tf_op jit(solution)/shard_map/ppermute | solution.py:590
  32.9 0.7 %collective-permute-start.11 = (bf16[256,128]{1,0:T(8,128)(2,1)S(1)}, bf16[256,128]{1,0:T(8,128)(2,1)S(1)}, u32[]{:S(2)}, u32[]{:S(2)}) collective-permute-start(bf16[256,128]{1,0:T(8,128)(2,1)S(1)} %get-tuple-element.116), channel_id=1, source_target_pairs={{0,16},{16,0},{1,17},{17,1},{2,18},{18,2},{3,19},{19,3},{4,20},{20... | collective-permute-start | bytes 196616 | tf_op jit(solution)/shard_map/ppermute | solution.py:590
  33.6 3.4 %shard_map.129 = (bf16[64,64,128]{2,1,0:T(8,128)(2,1)S(1)}, bf16[64,64,128]{2,1,0:T(8,128)(2,1)S(1)}, f32[10,64,128]{2,1,0:T(8,128)S(1)}, f32[10,64,128]{2,1,0:T(8,128)S(1)}, f32[8,128]{1,0:T(8,128)S(1)}) custom-call(s32[46]{0:T(128)S(1)} %get-tuple-element.74.meta.refs_0_, s32[3,64]{1,0:T(4,128)S(1)} %get-tuple-element.76.col.refs_1_, ...), custom_call_target="tpu_custom_call" | custom-call | flops 805306368 | bytes 12582912 | tf_op jit(solution)/shard_map/pallas_call | solution.py:311
  37.1 0.0 collective-permute-done.12.refs_1_
  37.1 1.9 %collective-permute-start.15 = (f32[64,128]{1,0:T(8,128)S(1)}, f32[64,128]{1,0:T(8,128)S(1)}, u32[]{:S(2)}, u32[]{:S(2)}) collective-permute-start(f32[64,128]{1,0:T(8,128)S(1)} %get-tuple-element.122.refs_0_), channel_id=1, source_target_pairs={{0,8},{8,0},{1,9},{9,1},{2,10},{10,2},{3,11},{11,3},{4,12},{12,4},... | collective-permute-start | bytes 98312 | tf_op jit(solution)/shard_map/ppermute | solution.py:590
  39.0 0.2 collective-permute-start.14
  39.2 2.9 %shard_map.131 = (bf16[8,64,8,128]{3,2,1,0:T(8,128)(2,1)}, bf16[8,64,8,128]{3,2,1,0:T(8,128)(2,1)}, f32[8,128]{1,0:T(8,128)S(1)}) custom-call(s32[46]{0:T(128)S(1)} %get-tuple-element.74.meta.refs_0_, bf16[4,64,64]{2,1,0:T(8,128)(2,1)S(1)} %copy-done, bf16[64,64,128]{2,1,0:T(8,128)(2,1)S(1)} %get-tuple-element.77.t0.refs_6_.refs_2_.refs_7_, ...), custom_call_target="tpu_custom_call" | custom-call | flops 268435456 | bytes 10485760 | tf_op jit(solution)/shard_map/pallas_call | solution.py:485
  42.1 0.0 collective-permute-done.11.refs_4_
  42.1 0.0 collective-permute-done.15.refs_1_
  42.1 2.0 %collective-permute-start.16 = (bf16[256,128]{1,0:T(8,128)(2,1)S(1)}, bf16[256,128]{1,0:T(8,128)(2,1)S(1)}, u32[]{:S(2)}, u32[]{:S(2)}) collective-permute-start(bf16[256,128]{1,0:T(8,128)(2,1)S(1)} %get-tuple-element.128), channel_id=1, source_target_pairs={{0,4},{4,0},{1,5},{5,1},{2,6},{6,2},{3,7},{7,3},{8,12},{12,8},{9,1... | collective-permute-start | bytes 196616 | tf_op jit(solution)/shard_map/ppermute | solution.py:590
  44.1 0.1 collective-permute-start.17
  44.2 2.4 %shard_map.133 = (bf16[8,64,8,128]{3,2,1,0:T(8,128)(2,1)}, bf16[8,64,8,128]{3,2,1,0:T(8,128)(2,1)}, f32[8,128]{1,0:T(8,128)S(1)}) custom-call(s32[46]{0:T(128)S(1)} %get-tuple-element.74.meta.refs_0_, bf16[4,64,64]{2,1,0:T(8,128)(2,1)S(1)} %copy-done, ...), custom_call_target="tpu_custom_call", output_to_operand_aliasing={{0}: (11, {}), {1}: (12, {})} | custom-call | flops 268435456 | bytes 10485760 | tf_op jit(solution)/shard_map/pallas_call | solution.py:485
  46.6 1.4 %collective-permute-done.17.refs_1_ = f32[64,128]{1,0:T(8,128)S(1)} collective-permute-done((f32[64,128]{1,0:T(8,128)S(1)}, f32[64,128]{1,0:T(8,128)S(1)}, u32[]{:S(2)}, u32[]{:S(2)}) %collective-permute-start.17) | collective-permute-done | bytes 32800 | tf_op jit(solution)/shard_map/ppermute | solution.py:590
  48.1 1.1 %collective-permute-start.19 = (f32[64,128]{1,0:T(8,128)S(1)}, f32[64,128]{1,0:T(8,128)S(1)}, u32[]{:S(2)}, u32[]{:S(2)}) collective-permute-start(f32[64,128]{1,0:T(8,128)S(1)} %get-tuple-element.139.refs_0_), channel_id=1, source_target_pairs={{0,2},{2,0},{1,3},{3,1},{4,6},{6,4},{5,7},{7,5},{8,10},{10,8},{9,1... | collective-permute-start | bytes 98312 | tf_op jit(solution)/shard_map/ppermute | solution.py:590
  49.2 1.0 %collective-permute-start.18 = (bf16[256,128]{1,0:T(8,128)(2,1)S(1)}, bf16[256,128]{1,0:T(8,128)(2,1)S(1)}, u32[]{:S(2)}, u32[]{:S(2)}) collective-permute-start(bf16[256,128]{1,0:T(8,128)(2,1)S(1)} %get-tuple-element.138), channel_id=1, source_target_pairs={{0,2},{2,0},{1,3},{3,1},{4,6},{6,4},{5,7},{7,5},{8,10},{10,8},{9,1... | collective-permute-start | bytes 196616 | tf_op jit(solution)/shard_map/ppermute | solution.py:590
  50.2 0.8 %shard_map.135 = (f32[10,64,128]{2,1,0:T(8,128)S(1)}, f32[10,64,128]{2,1,0:T(8,128)S(1)}) custom-call(s32[46]{0:T(128)S(1)} %get-tuple-element.74.meta.refs_0_, bf16[10,128,128]{2,1,0:T(8,128)(2,1)S(1)} %get-tuple-element.75.refs_1_, f32[10,64,128]{2,1,0:T(8,128)S(1)} %get-tuple-element.114.refs_2_, f32[10,64,128]{2,1,0:T(8,128)S(1)} %get-tuple-element.115.refs_3_, ...), custom_call_target="tpu_custom_call" | custom-call | flops 12582912 | bytes 2097152 | tf_op jit(solution)/shard_map/pallas_call | solution.py:348
  50.9 1.1 %collective-permute-done.19.refs_1_ = f32[64,128]{1,0:T(8,128)S(1)} collective-permute-done((f32[64,128]{1,0:T(8,128)S(1)}, f32[64,128]{1,0:T(8,128)S(1)}, u32[]{:S(2)}, u32[]{:S(2)}) %collective-permute-start.19) | collective-permute-done | bytes 32800 | tf_op jit(solution)/shard_map/ppermute | solution.py:590
  52.1 0.0 collective-permute-start.20
  52.1 1.4 %collective-permute-done.18.refs_6_ = bf16[256,128]{1,0:T(8,128)(2,1)S(1)} collective-permute-done((bf16[256,128]{1,0:T(8,128)(2,1)S(1)}, bf16[256,128]{1,0:T(8,128)(2,1)S(1)}, u32[]{:S(2)}, u32[]{:S(2)}) %collective-permute-start.18) | collective-permute-done | bytes 65568 | tf_op jit(solution)/shard_map/ppermute | solution.py:590
  53.4 2.6 %shard_map.137 = (bf16[8,64,8,128]{3,2,1,0:T(8,128)(2,1)}, bf16[8,64,8,128]{3,2,1,0:T(8,128)(2,1)}, f32[4,64,64]{2,1,0:T(8,128)}) custom-call(s32[46]{0:T(128)S(1)} %get-tuple-element.74.meta.refs_0_, bf16[10,128,128]{2,1,0:T(8,128)(2,1)S(1)} %get-tuple-element.75.refs_1_, ...), custom_call_target="tpu_custom_call", output_to_operand_aliasing={{0}: (15, {}), {1}: (16, {})} | custom-call | flops 83886080 | bytes 4194304 | tf_op jit(solution)/shard_map/pallas_call | solution.py:540
  (13 shorter events, 0.1 us)
Async XLA Ops:
  4.1 13.3 %collective-permute-start = (bf16[256,128]{1,0:T(8,128)(2,1)S(1)}, bf16[256,128]{1,0:T(8,128)(2,1)S(1)}, u32[]{:S(2)}, u32[]{:S(2)}) collective-permute-start(bf16[256,128]{1,0:T(8,128)(2,1)S(1)} %get-tuple-element.86), channel_id=1, source_target_pairs={{0,1},{1,0},{2,3},{3,2},{4,5},{5,4},{6,7},{7,6},{8,9},{9,8},{10,11... | collective-permute-start | bytes 196616 | tf_op jit(solution)/shard_map/ppermute | solution.py:590
  4.9 12.5 %collective-permute-start.1 = (bf16[256,128]{1,0:T(8,128)(2,1)S(1)}, bf16[256,128]{1,0:T(8,128)(2,1)S(1)}, u32[]{:S(2)}, u32[]{:S(2)}) collective-permute-start(bf16[256,128]{1,0:T(8,128)(2,1)S(1)} %get-tuple-element.87), channel_id=1, source_target_pairs={{0,2},{2,0},{1,3},{3,1},{4,6},{6,4},{5,7},{7,5},{8,10},{10,8},{9,1... | collective-permute-start | bytes 196616 | tf_op jit(solution)/shard_map/ppermute | solution.py:590
  7.2 10.2 %collective-permute-start.2 = (bf16[256,128]{1,0:T(8,128)(2,1)S(1)}, bf16[256,128]{1,0:T(8,128)(2,1)S(1)}, u32[]{:S(2)}, u32[]{:S(2)}) collective-permute-start(bf16[256,128]{1,0:T(8,128)(2,1)S(1)} %get-tuple-element.88), channel_id=1, source_target_pairs={{0,4},{4,0},{1,5},{5,1},{2,6},{6,2},{3,7},{7,3},{8,12},{12,8},{9,1... | collective-permute-start | bytes 196616 | tf_op jit(solution)/shard_map/ppermute | solution.py:590
  8.9 8.5 %collective-permute-start.3 = (bf16[256,128]{1,0:T(8,128)(2,1)S(1)}, bf16[256,128]{1,0:T(8,128)(2,1)S(1)}, u32[]{:S(2)}, u32[]{:S(2)}) collective-permute-start(bf16[256,128]{1,0:T(8,128)(2,1)S(1)} %get-tuple-element.89), channel_id=1, source_target_pairs={{0,8},{8,0},{1,9},{9,1},{2,10},{10,2},{3,11},{11,3},{4,12},{12,4},... | collective-permute-start | bytes 196616 | tf_op jit(solution)/shard_map/ppermute | solution.py:590
  10.1 7.2 %collective-permute-start.4 = (bf16[256,128]{1,0:T(8,128)(2,1)S(1)}, bf16[256,128]{1,0:T(8,128)(2,1)S(1)}, u32[]{:S(2)}, u32[]{:S(2)}) collective-permute-start(bf16[256,128]{1,0:T(8,128)(2,1)S(1)} %get-tuple-element.90), channel_id=1, source_target_pairs={{0,16},{16,0},{1,17},{17,1},{2,18},{18,2},{3,19},{19,3},{4,20},{20... | collective-permute-start | bytes 196616 | tf_op jit(solution)/shard_map/ppermute | solution.py:590
  19.1 7.2 %collective-permute-start.5 = (bf16[256,128]{1,0:T(8,128)(2,1)S(1)}, bf16[256,128]{1,0:T(8,128)(2,1)S(1)}, u32[]{:S(2)}, u32[]{:S(2)}) collective-permute-start(bf16[256,128]{1,0:T(8,128)(2,1)S(1)} %get-tuple-element.101), channel_id=1, source_target_pairs={{0,1},{1,0},{2,3},{3,2},{4,5},{5,4},{6,7},{7,6},{8,9},{9,8},{10,11... | collective-permute-start | bytes 196616 | tf_op jit(solution)/shard_map/ppermute | solution.py:590
  19.2 7.1 %collective-permute-start.6 = (bf16[256,128]{1,0:T(8,128)(2,1)S(1)}, bf16[256,128]{1,0:T(8,128)(2,1)S(1)}, u32[]{:S(2)}, u32[]{:S(2)}) collective-permute-start(bf16[256,128]{1,0:T(8,128)(2,1)S(1)} %get-tuple-element.102), channel_id=1, source_target_pairs={{0,2},{2,0},{1,3},{3,1},{4,6},{6,4},{5,7},{7,5},{8,10},{10,8},{9,1... | collective-permute-start | bytes 196616 | tf_op jit(solution)/shard_map/ppermute | solution.py:590
  19.9 6.4 %collective-permute-start.7 = (bf16[256,128]{1,0:T(8,128)(2,1)S(1)}, bf16[256,128]{1,0:T(8,128)(2,1)S(1)}, u32[]{:S(2)}, u32[]{:S(2)}) collective-permute-start(bf16[256,128]{1,0:T(8,128)(2,1)S(1)} %get-tuple-element.103), channel_id=1, source_target_pairs={{0,4},{4,0},{1,5},{5,1},{2,6},{6,2},{3,7},{7,3},{8,12},{12,8},{9,1... | collective-permute-start | bytes 196616 | tf_op jit(solution)/shard_map/ppermute | solution.py:590
  21.2 5.2 %collective-permute-start.8 = (bf16[256,128]{1,0:T(8,128)(2,1)S(1)}, bf16[256,128]{1,0:T(8,128)(2,1)S(1)}, u32[]{:S(2)}, u32[]{:S(2)}) collective-permute-start(bf16[256,128]{1,0:T(8,128)(2,1)S(1)} %get-tuple-element.104), channel_id=1, source_target_pairs={{0,8},{8,0},{1,9},{9,1},{2,10},{10,2},{3,11},{11,3},{4,12},{12,4},... | collective-permute-start | bytes 196616 | tf_op jit(solution)/shard_map/ppermute | solution.py:590
  21.6 6.4 %collective-permute-start.9 = (bf16[256,128]{1,0:T(8,128)(2,1)S(1)}, bf16[256,128]{1,0:T(8,128)(2,1)S(1)}, u32[]{:S(2)}, u32[]{:S(2)}) collective-permute-start(bf16[256,128]{1,0:T(8,128)(2,1)S(1)} %get-tuple-element.105), channel_id=1, source_target_pairs={{0,16},{16,0},{1,17},{17,1},{2,18},{18,2},{3,19},{19,3},{4,20},{20... | collective-permute-start | bytes 196616 | tf_op jit(solution)/shard_map/ppermute | solution.py:590
  29.0 1.6 %collective-permute-start.10 = (f32[64,128]{1,0:T(8,128)S(1)}, f32[64,128]{1,0:T(8,128)S(1)}, u32[]{:S(2)}, u32[]{:S(2)}) collective-permute-start(f32[64,128]{1,0:T(8,128)S(1)} %get-tuple-element.111), channel_id=1, source_target_pairs={{0,1},{1,0},{2,3},{3,2},{4,5},{5,4},{6,7},{7,6},{8,9},{9,8},{10,11... | collective-permute-start | bytes 98312 | tf_op jit(solution)/shard_map/ppermute | solution.py:590
  30.1 7.0 %collective-permute-start.13 = (bf16[256,128]{1,0:T(8,128)(2,1)S(1)}, bf16[256,128]{1,0:T(8,128)(2,1)S(1)}, u32[]{:S(2)}, u32[]{:S(2)}) collective-permute-start(bf16[256,128]{1,0:T(8,128)(2,1)S(1)} %get-tuple-element.120), channel_id=1, source_target_pairs={{0,1},{1,0},{2,3},{3,2},{4,5},{5,4},{6,7},{7,6},{8,9},{9,8},{10,11... | collective-permute-start | bytes 196616 | tf_op jit(solution)/shard_map/ppermute | solution.py:590
  30.6 6.5 %collective-permute-start.12 = (f32[64,128]{1,0:T(8,128)S(1)}, f32[64,128]{1,0:T(8,128)S(1)}, u32[]{:S(2)}, u32[]{:S(2)}) collective-permute-start(f32[64,128]{1,0:T(8,128)S(1)} %get-tuple-element.117.refs_0_), channel_id=1, source_target_pairs={{0,16},{16,0},{1,17},{17,1},{2,18},{18,2},{3,19},{19,3},{4,20},{20... | collective-permute-start | bytes 98312 | tf_op jit(solution)/shard_map/ppermute | solution.py:590
  32.9 9.2 %collective-permute-start.11 = (bf16[256,128]{1,0:T(8,128)(2,1)S(1)}, bf16[256,128]{1,0:T(8,128)(2,1)S(1)}, u32[]{:S(2)}, u32[]{:S(2)}) collective-permute-start(bf16[256,128]{1,0:T(8,128)(2,1)S(1)} %get-tuple-element.116), channel_id=1, source_target_pairs={{0,16},{16,0},{1,17},{17,1},{2,18},{18,2},{3,19},{19,3},{4,20},{20... | collective-permute-start | bytes 196616 | tf_op jit(solution)/shard_map/ppermute | solution.py:590
  33.6 5.6 %copy-start = (bf16[4,64,64]{2,1,0:T(8,128)(2,1)S(1)}, bf16[4,64,64]{2,1,0:T(8,128)(2,1)}, u32[]{:S(2)}) copy-start(bf16[4,64,64]{2,1,0:T(8,128)(2,1)} %refs_2_.1) | copy-start | bytes 98308
  37.1 5.0 %collective-permute-start.15 = (f32[64,128]{1,0:T(8,128)S(1)}, f32[64,128]{1,0:T(8,128)S(1)}, u32[]{:S(2)}, u32[]{:S(2)}) collective-permute-start(f32[64,128]{1,0:T(8,128)S(1)} %get-tuple-element.122.refs_0_), channel_id=1, source_target_pairs={{0,8},{8,0},{1,9},{9,1},{2,10},{10,2},{3,11},{11,3},{4,12},{12,4},... | collective-permute-start | bytes 98312 | tf_op jit(solution)/shard_map/ppermute | solution.py:590
  39.0 7.6 %collective-permute-start.14 = (bf16[256,128]{1,0:T(8,128)(2,1)S(1)}, bf16[256,128]{1,0:T(8,128)(2,1)S(1)}, u32[]{:S(2)}, u32[]{:S(2)}) collective-permute-start(bf16[256,128]{1,0:T(8,128)(2,1)S(1)} %get-tuple-element.121), channel_id=1, source_target_pairs={{0,8},{8,0},{1,9},{9,1},{2,10},{10,2},{3,11},{11,3},{4,12},{12,4},... | collective-permute-start | bytes 196616 | tf_op jit(solution)/shard_map/ppermute | solution.py:590
  42.1 8.0 %collective-permute-start.16 = (bf16[256,128]{1,0:T(8,128)(2,1)S(1)}, bf16[256,128]{1,0:T(8,128)(2,1)S(1)}, u32[]{:S(2)}, u32[]{:S(2)}) collective-permute-start(bf16[256,128]{1,0:T(8,128)(2,1)S(1)} %get-tuple-element.128), channel_id=1, source_target_pairs={{0,4},{4,0},{1,5},{5,1},{2,6},{6,2},{3,7},{7,3},{8,12},{12,8},{9,1... | collective-permute-start | bytes 196616 | tf_op jit(solution)/shard_map/ppermute | solution.py:590
  44.1 3.9 %collective-permute-start.17 = (f32[64,128]{1,0:T(8,128)S(1)}, f32[64,128]{1,0:T(8,128)S(1)}, u32[]{:S(2)}, u32[]{:S(2)}) collective-permute-start(f32[64,128]{1,0:T(8,128)S(1)} %get-tuple-element.129.refs_0_), channel_id=1, source_target_pairs={{0,4},{4,0},{1,5},{5,1},{2,6},{6,2},{3,7},{7,3},{8,12},{12,8},{9,1... | collective-permute-start | bytes 98312 | tf_op jit(solution)/shard_map/ppermute | solution.py:590
  48.1 4.0 %collective-permute-start.19 = (f32[64,128]{1,0:T(8,128)S(1)}, f32[64,128]{1,0:T(8,128)S(1)}, u32[]{:S(2)}, u32[]{:S(2)}) collective-permute-start(f32[64,128]{1,0:T(8,128)S(1)} %get-tuple-element.139.refs_0_), channel_id=1, source_target_pairs={{0,2},{2,0},{1,3},{3,1},{4,6},{6,4},{5,7},{7,5},{8,10},{10,8},{9,1... | collective-permute-start | bytes 98312 | tf_op jit(solution)/shard_map/ppermute | solution.py:590
  49.2 4.3 %collective-permute-start.18 = (bf16[256,128]{1,0:T(8,128)(2,1)S(1)}, bf16[256,128]{1,0:T(8,128)(2,1)S(1)}, u32[]{:S(2)}, u32[]{:S(2)}) collective-permute-start(bf16[256,128]{1,0:T(8,128)(2,1)S(1)} %get-tuple-element.138), channel_id=1, source_target_pairs={{0,2},{2,0},{1,3},{3,1},{4,6},{6,4},{5,7},{7,5},{8,10},{10,8},{9,1... | collective-permute-start | bytes 196616 | tf_op jit(solution)/shard_map/ppermute | solution.py:590
  52.1 1.4 %collective-permute-start.20 = (f32[64,128]{1,0:T(8,128)S(1)}, f32[64,128]{1,0:T(8,128)S(1)}, u32[]{:S(2)}, u32[]{:S(2)}) collective-permute-start(f32[64,128]{1,0:T(8,128)S(1)} %shard_map.136.refs_13_), channel_id=1, source_target_pairs={{0,1},{1,0},{2,3},{3,2},{4,5},{5,4},{6,7},{7,6},{8,9},{9,8},{10,11... | collective-permute-start | bytes 98312 | tf_op jit(solution)/shard_map/ppermute | solution.py:590

commit v6 on v5

--- a/solution.py
+++ b/solution.py
@@ -165,6 +165,10 @@
     return (count + ROWS - 1) // ROWS
 
 
+def table_scratch(sz, col):
+    return [pltpu.SMEM((sz.meta,), jnp.int32), pltpu.SMEM(col.shape, jnp.int32)]
+
+
 def clear_sums(sz, summed):
     def clear(i, carry):
         summed[i] = jnp.zeros(summed.shape[1:], F32)
@@ -182,12 +186,12 @@
     count = meta[sz.live]
 
     def finish(g, carry):
-        for u in range(ROWS_FIRST):
-            i = g * ROWS_FIRST + u
+        for u in range(ROWS):
+            i = g * ROWS + u
             snew[i] = adjoint(i).astype(BF16)
         return carry
 
-    lax.fori_loop(0, (count + ROWS_FIRST - 1) // ROWS_FIRST, finish, 0)
+    lax.fori_loop(0, big_steps(count), finish, 0)
 
     def dead(i, carry):
         tnew[i] = jnp.zeros(tnew.shape[1:], BF16)
@@ -200,9 +204,17 @@
         qsel[j] = adjoint(meta[sz.sends + j])
 
 
-def first_kernel(
-    sz, meta, col, tiles_hbm, t0, s0, tnew, snew, psel, qsel, tiles, turned, gram, held, summed, sem
-):
+def first_kernel(sz, *refs):
+    meta_in, col_in, tiles_hbm, t0, s0 = refs[:5]
+    tnew, snew, psel, qsel, tiles, turned, gram, held, summed, meta, col, sem, sem_i = refs[5:]
+    small = [
+        pltpu.make_async_copy(meta_in, meta, sem_i.at[0]),
+        pltpu.make_async_copy(col_in, col, sem_i.at[1]),
+    ]
+    for copy in small:
+        copy.start()
+    for copy in small:
+        copy.wait()
     count = meta[sz.live]
     steps = big_steps(count)
     loads = steps * (ROWS // ROWS_FIRST)
@@ -252,12 +264,13 @@
     turned = shape((sz.blocks, sz.nz * sz.blk, sz.blk), BF16)
     return call(
         functools.partial(first_kernel, sz),
-        [SMEM, SMEM, HBM, VMEM, VMEM],
+        [VMEM, VMEM, HBM, VMEM, VMEM],
         [VMEM] * 7,
         [sz.field, sz.field, sz.picked, sz.picked, shape(tiles.shape, BF16), turned]
         + [shape((sz.chan, sz.chan), F32)],
         [pltpu.VMEM((sz.blocks, sz.chan, sz.blk), F32)] * 2
-        + [pltpu.SemaphoreType.DMA((sz.blocks // ROWS_FIRST,))],
+        + table_scratch(sz, col)
+        + [pltpu.SemaphoreType.DMA((sz.blocks // ROWS_FIRST,)), pltpu.SemaphoreType.DMA((2,))],
         4 * sz.blocks * sz.nz * sz.chan * sz.blk * sz.blk,
         12 << 20,
         24,
@@ -265,11 +278,19 @@
 
 
 def local_kernel(sz, grad, *refs):
-    meta, col, tiles, turned, tcur, scur, tprev, sprev, _ = refs[:9]
+    meta_in, col_in, tiles, turned, tcur, scur, tprev, sprev, _ = refs[:9]
     tnew, snew, psel, qsel, last = refs[9:14]
-    held, summed = refs[-2:]
+    held, summed, meta, col, sem = refs[14:]
+    small = [
+        pltpu.make_async_copy(meta_in, meta, sem.at[0]),
+        pltpu.make_async_copy(col_in, col, sem.at[1]),
+    ]
+    for copy in small:
+        copy.start()
+    clear_sums(sz, summed)
+    for copy in small:
+        copy.wait()
     count = meta[sz.live]
-    clear_sums(sz, summed)
 
     def block_row(i):
         cols = [col[m, i] for m in range(sz.nz)]
@@ -310,10 +331,12 @@
     tail = shape((2 * sz.chan, 2 * sz.chan), F32) if grad else TOKEN
     return call(
         functools.partial(local_kernel, sz, grad),
-        [SMEM, SMEM] + [VMEM] * 7,
+        [VMEM] * 9,
         [VMEM] * 5,
         [sz.field, sz.field, sz.picked, sz.picked, tail],
-        [pltpu.VMEM((sz.blocks, sz.chan, sz.blk), F32)] * 2,
+        [pltpu.VMEM((sz.blocks, sz.chan, sz.blk), F32)] * 2
+        + table_scratch(sz, col)
+        + [pltpu.SemaphoreType.DMA((2,))],
         4 * sz.blocks * sz.nz * sz.chan * sz.blk * sz.blk,
         12 << 20,
         24,
@@ -334,27 +357,6 @@
             spot = meta[sz.first_send + j]
             qacc[spot] = qacc[spot] + scale * got[r][sz.adjoint_part(h), :].astype(F32)
     return terms
-
-
-def couple_kernel(sz, scale, which, *refs):
-    meta, across, psel, qsel = refs[:4]
-    got = dict(zip(which, refs[4 : 4 + len(which)]))
-    pacc, qacc = refs[-2:]
-    add_coupled(sz, scale, meta, got, across, psel, qsel, pacc, qacc, which)
-
-
-def couple(sz, scale, meta, across, picked, got, which, after):
-    args = [meta, across, *picked, *(got[r] for r in which), *after]
-    return call(
-        functools.partial(couple_kernel, sz, scale, which),
-        [SMEM] + [VMEM] * (len(args) - 1),
-        [VMEM] * 2,
-        [sz.picked] * 2,
-        [],
-        2 * len(which) * sz.hb * sz.chan * sz.blk * sz.blk,
-        2 << 20,
-        6,
-    )(*args)
 
 
 def correct_kernel(sz, axis, *refs):
@@ -391,34 +393,40 @@
     )(*args)
 
 
-def join_kernel(sz, *refs):
-    meta, cross, tbase, sbase, pacc, qacc, tnew, snew = refs[:8]
-    pays = refs[8:]
-
-    def move(i, carry):
-        tnew[i] = tbase[i]
-        snew[i] = sbase[i]
-        return carry
-
-    lax.fori_loop(0, sz.blocks, move, 0, unroll=4)
+def patch(sz, meta, cross, tnew, snew, pacc, qacc, pays):
     for j in range(sz.pairs):
         tnew[meta[sz.rows + j]] = pacc[meta[sz.first_row + j]].astype(BF16)
         snew[meta[sz.sends + j]] = qacc[meta[sz.first_send + j]].astype(BF16)
     fill_pays(sz, meta, tnew, snew, cross, pays)
 
 
-def join(sz, meta, cross, base, picked):
-    args = [meta, cross, *base, *picked]
+def start_kernel(sz, *refs):
+    meta, cross, _, _, across, psel, qsel = refs[:7]
+    got, refs = refs[7 : 7 + sz.rounds], refs[7 + sz.rounds :]
+    tnew, snew = refs[:2]
+    pacc, qacc = refs[-2:]
+    add_coupled(sz, 1.0, meta, got, across, psel, qsel, pacc, qacc, range(sz.rounds))
+    patch(sz, meta, cross, tnew, snew, pacc, qacc, refs[2:-2])
+
+
+def join_kernel(sz, *refs):
+    meta, cross, _, _, pacc, qacc, tnew, snew = refs[:8]
+    patch(sz, meta, cross, tnew, snew, pacc, qacc, refs[8:])
+
+
+def join(sz, meta, cross, base, rest, first):
+    args = [meta, cross, *base, *rest]
     outs = [sz.field, sz.field] + [sz.pay] * sz.rounds
     outs = call(
-        functools.partial(join_kernel, sz),
+        functools.partial(start_kernel if first else join_kernel, sz),
         [SMEM] + [VMEM] * (len(args) - 1),
         [VMEM] * len(outs),
         outs,
-        [],
+        [pltpu.VMEM(sz.picked.shape, F32)] * 2 if first else [],
         2 * sz.pairs * sz.chan * sz.blk * sz.blk,
         5 << 20,
         8,
+        {2: 0, 3: 1},
     )(*args)
     return outs[0], outs[1], outs[2:]
 
@@ -430,94 +438,141 @@
     return ahead, back
 
 
-def output_kernel(sz, low, high, *refs):
-    meta, weight = refs[:2]
-    forward, adjoint = refs[2:6], refs[6:10]
-    refs = refs[11:] if low == 0 else refs[13:]
-    out4, grad4, token, held_out, held_grad, sem = refs
-    count = meta[sz.live]
-    ahead, back = output_weights(weight)
-    groups = sz.chan // SUB
-
-    def block(i):
-        for left, fields, held in ((ahead, forward, held_out), (back, adjoint, held_grad)):
-            value = nn(left, jnp.concatenate([f[i] for f in fields], axis=0)).astype(BF16)
-            for t in range(groups):
-                held[t, i - low] = value[t * SUB : (t + 1) * SUB]
-
-    def step(g, carry):
-        for u in range(ROWS_FIRST):
-            block(g * ROWS_FIRST + u)
-        return carry
-
-    end = jnp.minimum((count + ROWS_FIRST - 1) // ROWS_FIRST, high // ROWS_FIRST)
-    lax.fori_loop(low // ROWS_FIRST, end, step, 0)
-
-    def dead(i, carry):
-        for t in range(groups):
-            held_out[t, i - low] = jnp.zeros((SUB, sz.blk), BF16)
-            held_grad[t, i - low] = jnp.zeros((SUB, sz.blk), BF16)
-        return carry
-
-    lax.fori_loop(jnp.maximum(count, low), high, dead, 0)
-    part = pl.ds(low, high - low)
-    copies = [
-        pltpu.make_async_copy(held_out, out4.at[:, part], sem.at[0]),
-        pltpu.make_async_copy(held_grad, grad4.at[:, part], sem.at[1]),
-    ]
+def output_block(sz, left, fields, held, spot):
+    value = nn(left[...], jnp.concatenate(fields, axis=0)).astype(BF16)
+    for t in range(sz.chan // SUB):
+        held[(t,) + spot if len(spot) == 1 else (spot[1], t)] = value[t * SUB : (t + 1) * SUB]
+
+
+def output_kernel(sz, low, *refs):
+    forward, adjoint = refs[:4], refs[4:8]
+    if low == 0:
+        weight, ahead, back, held_out, held_grad = refs[8], *refs[10:]
+        wide_ahead, wide_back = output_weights(weight)
+        ahead[...] = wide_ahead
+        back[...] = wide_back
+        copies = []
+    else:
+        ahead, back, before_out, before_grad = refs[8:12]
+        held_out, held_grad, out4, grad4, sem = refs[13:]
+        part = pl.ds(0, low)
+        copies = [
+            pltpu.make_async_copy(before_out, out4.at[:, part], sem.at[0]),
+            pltpu.make_async_copy(before_grad, grad4.at[:, part], sem.at[1]),
+        ]
     for copy in copies:
         copy.start()
-    token[...] = jnp.zeros(token.shape, F32)
+
+    def step(g, carry):
+        for u in range(ROWS):
+            n = g * ROWS + u
+            output_block(sz, ahead, [f[low + n] for f in forward], held_out, (n,))
+            output_block(sz, back, [f[low + n] for f in adjoint], held_grad, (n,))
+        return carry
+
+    lax.fori_loop(0, held_out.shape[1] // ROWS, step, 0)
     for copy in copies:
         copy.wait()
 
 
-def base_outputs(sz, low, high, meta, weight, forward, adjoint, token, before):
-    out = shape((sz.chan // SUB, sz.blocks, SUB, sz.blk), BF16)
-    args = [meta, weight, *forward, *adjoint, token]
-    specs = [SMEM] + [VMEM] * (len(args) - 1)
-    aliases = {}
-    if low > 0:
-        aliases = {len(args): 0, len(args) + 1: 1}
-        args += before
-        specs += [HBM] * 2
-    held = pltpu.VMEM((sz.chan // SUB, high - low, SUB, sz.blk), BF16)
+def output_weight_shape(sz, orders):
+    return shape((sz.chan, orders * sz.chan), BF16)
+
+
+def base_outputs(sz, low, high, forward, adjoint, rest, token, orders):
+    groups = sz.chan // SUB
+    held = shape((groups, high - low, SUB, sz.blk), BF16)
+    whole = shape((groups, sz.blocks, SUB, sz.blk), BF16)
+    args = [*forward, *adjoint, *rest, token]
+    if low == 0:
+        outs = [output_weight_shape(sz, orders)] * 2 + [held, held]
+        specs = [VMEM] * 4
+    else:
+        outs = [held, held, whole, whole]
+        specs = [VMEM] * 2 + [HBM] * 2
     return call(
-        functools.partial(output_kernel, sz, low, high),
+        functools.partial(output_kernel, sz, low),
+        [VMEM] * len(args),
         specs,
-        [HBM, HBM, VMEM],
-        [out, out, TOKEN],
-        [held, held, pltpu.SemaphoreType.DMA((2,))],
+        outs,
+        [pltpu.SemaphoreType.DMA((2,))] if low else [],
         16 * (high - low) * sz.chan * sz.chan * sz.blk,
-        10 << 20,
+        6 << 20,
         8,
-        aliases,
     )(*args)
 
 
+def fixed_blocks(sz, meta, which, ahead, back, forward, adjoint, pacc, qacc, held, outs, sem):
+    copies, seen = [], ([], [])
+    for r, h, j in sz.couplings():
+        if r not in which:
+            continue
+        for side, (left, fields, last, spot, first) in enumerate(
+            (
+                (ahead, forward, pacc, sz.rows, sz.first_row),
+                (back, adjoint, qacc, sz.sends, sz.first_send),
+            )
+        ):
+            i, slot = meta[spot + j], meta[first + j]
+            stack = [f[i] for f in fields] + [last[slot].astype(BF16)]
+            output_block(sz, left, stack, held[side], (None, j))
+            fresh = jnp.bool_(True)
+            for other in seen[side]:
+                fresh = jnp.logical_and(fresh, other != i)
+            seen[side].append(i)
+            copy = pltpu.make_async_copy(
+                held[side].at[j], outs[side].at[:, i], sem.at[side, j]
+            )
+            copies.append((fresh, copy))
+    return copies
+
+
+def run_copies(copies):
+    for fresh, copy in copies:
+        pl.when(fresh)(copy.start)
+
+
+def end_copies(copies):
+    for fresh, copy in copies:
+        pl.when(fresh)(copy.wait)
+
+
+def early_kernel(sz, which, low, *refs):
+    meta, across, psel, qsel, ahead, back = refs[:6]
+    got, refs = dict(zip(which, refs[6 : 6 + len(which)])), refs[6 + len(which) :]
+    forward, adjoint = refs[:3], refs[3:6]
+    before_out, before_grad = refs[6:8]
+    pacc, qacc, out4, grad4, held_out, held_grad, sem, sem_base = refs[11:]
+    part = pl.ds(low, before_out.shape[1])
+    base = [
+        pltpu.make_async_copy(before_out, out4.at[:, part], sem_base.at[0]),
+        pltpu.make_async_copy(before_grad, grad4.at[:, part], sem_base.at[1]),
+    ]
+    for copy in base:
+        copy.start()
+    add_coupled(sz, 2.0, meta, got, across, psel, qsel, pacc, qacc, which)
+    held, outs = (held_out, held_grad), (out4, grad4)
+    copies = fixed_blocks(
+        sz, meta, which, ahead, back, forward, adjoint, pacc, qacc, held, outs, sem
+    )
+    for copy in base:
+        copy.wait()
+    run_copies(copies)
+    end_copies(copies)
+
+
 def fix_kernel(sz, axis, which, *refs):
-    meta, across, weight, psel, qsel = refs[:5]
-    got, refs = dict(zip(which, refs[5 : 5 + len(which)])), refs[5 + len(which) :]
+    meta, across, psel, qsel, ahead, back = refs[:6]
+    got, refs = dict(zip(which, refs[6 : 6 + len(which)])), refs[6 + len(which) :]
     forward, adjoint = refs[:3], refs[3:6]
     mine, theirs = refs[6:8]
     out4, grad4, grad_w, pacc, qacc, held_out, held_grad, sem = refs[10:]
     add_coupled(sz, 2.0, meta, got, across, psel, qsel, pacc, qacc, which)
-    ahead, back = output_weights(weight)
-    groups = sz.chan // SUB
-    copies = []
-    for j in range(sz.pairs):
-        for left, fields, last, spot, first, held, out, s in (
-            (ahead, forward, pacc, sz.rows, sz.first_row, held_out, out4, 0),
-            (back, adjoint, qacc, sz.sends, sz.first_send, held_grad, grad4, 1),
-        ):
-            i, slot = meta[spot + j], meta[first + j]
-            stack = [f[i] for f in fields] + [last[slot].astype(BF16)]
-            value = nn(left, jnp.concatenate(stack, axis=0)).astype(BF16)
-            for t in range(groups):
-                held[j, t] = value[t * SUB : (t + 1) * SUB]
-            copies.append((slot == j, pltpu.make_async_copy(held.at[j], out.at[:, i], sem.at[s, j])))
-    for own, copy in copies:
-        pl.when(own)(copy.start)
+    held, outs = (held_out, held_grad), (out4, grad4)
+    copies = fixed_blocks(
+        sz, meta, which, ahead, back, forward, adjoint, pacc, qacc, held, outs, sem
+    )
+    run_copies(copies)
     odd = lax.rem(lax.axis_index(axis), 2) == 1
     top = jnp.where(odd, theirs[...], mine[...])
     low = jnp.where(odd, mine[...], theirs[...])
@@ -526,29 +581,34 @@
     grad_w[1] = first
     grad_w[2] = 2.0 * low[:, sz.chan :] - zeroth
     grad_w[3] = 2.0 * top[:, sz.chan :] - first
-    for own, copy in copies:
-        pl.when(own)(copy.wait)
-
-
-def fix_outputs(
-    sz, axis, meta, across, weight, picked, got, which, forward, adjoint, mine, theirs, before
-):
-    out = shape(before[0].shape, BF16)
+    end_copies(copies)
+
+
+def fix_outputs(sz, kernel, meta, across, picked, weights, got, which, fields, rest, token, outs, limit):
     late = [got[r] for r in which]
-    args = [meta, across, weight, *picked, *late, *forward, *adjoint, mine, theirs]
+    args = [meta, across, *picked, *weights, *late, *fields, *rest, *token]
+    whole = [shape(out.shape, BF16) for out in outs]
     held = pltpu.VMEM((sz.pairs, sz.chan // SUB, SUB, sz.blk), BF16)
+    scratch = [held, held, pltpu.SemaphoreType.DMA((2, sz.pairs))]
+    if token:
+        results = [sz.picked, sz.picked] + whole
+        specs, at = [VMEM] * 2 + [HBM] * 2, 2
+        scratch.append(pltpu.SemaphoreType.DMA((2,)))
+    else:
+        results = whole + [shape((4, sz.chan, sz.chan), F32)]
+        specs, at = [HBM] * 2 + [VMEM], 0
+        scratch = [pltpu.VMEM(sz.picked.shape, F32)] * 2 + scratch
     return call(
-        functools.partial(fix_kernel, sz, axis, which),
+        kernel,
         [SMEM] + [VMEM] * (len(args) - 1) + [HBM] * 2,
-        [HBM, HBM, VMEM],
-        [out, out, shape((4, sz.chan, sz.chan), F32)],
-        [pltpu.VMEM(sz.picked.shape, F32)] * 2 + [held, held]
-        + [pltpu.SemaphoreType.DMA((2, sz.pairs))],
+        specs,
+        results,
+        scratch,
         8 * sz.pairs * sz.chan * sz.blk * sz.blk,
         4 << 20,
-        10,
-        {len(args): 0, len(args) + 1: 1},
-    )(*args, *before)
+        limit,
+        {len(args): at, len(args) + 1: at + 1},
+    )(*args, *outs)
 
 
 def add_kernel(gated, inputs, *refs):
@@ -614,8 +674,7 @@
     everyone = range(sz.rounds)
     got = [from_partner(pay, bit) for bit, pay in enumerate(packed[6:])]
     *base, psel, qsel, tiles, turned, gram0 = first_products(sz, meta, col, lap_tiles, t0, s0)
-    picked = couple(sz, 1.0, meta, across, (psel, qsel), got, everyone, [])
-    t1, s1, pays = join(sz, meta, cross, base, picked)
+    t1, s1, pays = join(sz, meta, cross, base, [across, psel, qsel, *got], True)
 
     got = [from_partner(pay, bit) for bit, pay in enumerate(pays)]
     fields = (t1, s1, t0, s0)
@@ -624,7 +683,7 @@
         sz, "dom", meta, across, (psel, qsel), got, gram0, gram, s1
     )
     theirs = from_partner(given, 0)
-    t2, s2, pays = join(sz, meta, cross, base, picked)
+    t2, s2, pays = join(sz, meta, cross, base, picked, False)
 
     state = {}
 
@@ -633,24 +692,31 @@
         *state["base"], token = local_products(sz, meta, col, tiles, turned, fields, token, False)
         return token
 
-    def window_outputs(low, high):
-        def window(token):
-            forward = (t0, t1, t2, state["base"][0])
-            adjoint = (s0, s1, s2, state["base"][1])
-            out4, grad4, token = base_outputs(
-                sz, low, high, meta, cheb_weight, forward, adjoint, token, state.get("outs", [])
-            )
-            state["outs"] = [out4, grad4]
-            return token
-
-        return window
-
-    middle = sz.blocks // (2 * ROWS_FIRST) * ROWS_FIRST
-    windows = [window_products, window_outputs(0, middle), window_outputs(middle, sz.blocks)]
+    middle = sz.blocks // (2 * ROWS) * ROWS
+    orders = cheb_weight.shape[0]
+
+    def window_low(token):
+        forward, adjoint = (t0, t1, t2, state["base"][0]), (s0, s1, s2, state["base"][1])
+        *state["weights"], left, right = base_outputs(
+            sz, 0, middle, forward, adjoint, [cheb_weight], token, orders
+        )
+        state["low"] = [left, right]
+        return state["weights"][0]
+
+    def window_high(token):
+        forward, adjoint = (t0, t1, t2, state["base"][0]), (s0, s1, s2, state["base"][1])
+        rest = state["weights"] + state["low"]
+        left, right, out4, grad4 = base_outputs(
+            sz, middle, sz.blocks, forward, adjoint, rest, token, orders
+        )
+        state["high"], state["outs"] = [left, right], [out4, grad4]
+        return left
+
+    windows = [window_products, window_low, window_high]
     bits = list(reversed(range(1, (lax.axis_size("dom") - 1).bit_length())))
     pays, got = list(pays), [None] * sz.rounds
     got[0] = from_partner(pays[0], 0)
-    early = [bit for bit in bits[:-1] if bit < sz.rounds]
+    early = [0] + [bit for bit in bits[:-1] if bit < sz.rounds]
     late = [bit for bit in everyone if bit not in early]
     mine, token, *rest = add(mine, theirs, pays[bits[0]] if bits[0] < sz.rounds else None, [])
     held = [got[0]]
@@ -664,7 +730,21 @@
             token = windows[at](token)
         last = at + 1 == len(bits)
         if last:
-            picked = couple(sz, 2.0, meta, across, state["base"][2:4], got, early, [token])
+            *picked, out4, grad4 = fix_outputs(
+                sz,
+                functools.partial(early_kernel, sz, early, middle),
+                meta,
+                across,
+                state["base"][2:4],
+                state["weights"],
+                got,
+                early,
+                (t0, t1, t2, s0, s1, s2),
+                state["high"],
+                [token],
+                state["outs"],
+                10,
+            )
             token = picked[0]
         gated = not last and bits[at + 1] < sz.rounds
         after = [token] + held
@@ -676,18 +756,18 @@
     theirs = from_partner(mine, 0)
     out4, grad4, grad_w = fix_outputs(
         sz,
-        "dom",
+        functools.partial(fix_kernel, sz, "dom", late),
         meta,
         across,
-        cheb_weight,
         picked,
+        state["weights"],
         got,
         late,
-        (t0, t1, t2),
-        (s0, s1, s2),
-        mine,
-        theirs,
-        state["outs"],
+        (t0, t1, t2, s0, s1, s2),
+        [mine, theirs],
+        [],
+        [out4, grad4],
+        10,
     )
     conv_out = out4.transpose(0, 2, 1, 3).reshape(features.shape)
     grad_x = grad4.transpose(0, 2, 1, 3).reshape(features.shape)

time: 56.2 us -> 54.6 us (0.972)
  Pallas kernels: 27.7 us -> 25 us
  waiting for transfers between devices: 5.58 us -> 6.63 us
    pallas_call x10 -> x9, Pallas kernels: 23.9 us -> 21.2 us  [the longest x2 7.72 us: local_products(): call(functools.partial(local_kernel, sz, grad), [VMEM] * 9, [VMEM] * 5, [...]
    ppermute x21, waiting for transfers between devices: 5.58 us -> 6.63 us  [from_partner(): return lax.ppermute(values, 'dom', route)]
  transfers between devices with their start and end apart: 21 -> 21, of which waited for: 4 -> 5; matrix products, arithmetic and copies ran while one was open for 0% -> 0% of each run, Pallas kernels for 35% -> 33%
where the time goes in v6:
time: 54.6 us; the launch traced here: 54.4 us
  Pallas kernels  25 us (46%)
  starting transfers between devices  21.2 us (39%)
  waiting for transfers between devices  6.63 us (12%)
  between operations  1.52 us (3%)
    ppermute x21, starting transfers between devices, from_partner(): return lax.ppermute(values, 'dom', route)  21.2 us
    pallas_call x2, Pallas kernels, local_products(): call(functools.partial(local_kernel, sz, grad), [VMEM] * 9, [VMEM] * 5, [...  7.72 us
    ppermute x21, waiting for transfers between devices, from_partner(): return lax.ppermute(values, 'dom', route)  6.63 us
    pallas_call x2, Pallas kernels, fix_outputs(): call(kernel, [SMEM] + [VMEM] * (len(args) - 1) + [HBM] * 2, specs, result...  5.03 us
    pallas_call x1, Pallas kernels, first_products(): call(functools.partial(first_kernel, sz), [VMEM, VMEM, HBM, VMEM, VMEM],...  4.59 us
    pallas_call x1, Pallas kernels, pack(): call(functools.partial(pack_kernel, sz), [HBM] * 6 + [SMEM, HBM], [VMEM]...  2.79 us
    pallas_call x2, Pallas kernels, base_outputs(): call(functools.partial(output_kernel, sz, low), [VMEM] * len(args), specs...  2.07 us
    pallas_call x2, Pallas kernels, join(): call(functools.partial(start_kernel if first else join_kernel, sz), [SMEM...  1.74 us
  transfers between devices with their start and end apart: 21, of which 5 were waited for; matrix products, arithmetic and copies ran while one was open for 0% of the time, Pallas kernels for 33%

profile of v6, /device:TPU:0, one launch (start us, length us, event | category | flops | bytes accessed | tf_op | source)
XLA Modules:
  0.0 54.4 jit_solution(10211586828159439087)
XLA Ops:
  1.3 2.8 %shard_map.121 = (bf16[64,64,128]{2,1,0:T(8,128)(2,1)S(1)}, bf16[64,64,128]{2,1,0:T(8,128)(2,1)S(1)}, bf16[10,128,128]{2,1,0:T(8,128)(2,1)S(1)}, bf16[10,128,128...) custom-call(bf16[8,64,8,128]{3,2,1,0:T(8,128)(2,1)} %bitcast.18, ...), custom_call_target="tpu_custom_call" | custom-call | flops 1000 | bytes 4194304 | tf_op jit(solution)/shard_map/pallas_call | solution.py:143
  4.1 0.8 %collective-permute-start = (bf16[256,128]{1,0:T(8,128)(2,1)S(1)}, bf16[256,128]{1,0:T(8,128)(2,1)S(1)}, u32[]{:S(2)}, u32[]{:S(2)}) collective-permute-start(bf16[256,128]{1,0:T(8,128)(2,1)S(1)} %get-tuple-element.88), channel_id=1, source_target_pairs={{0,1},{1,0},{2,3},{3,2},{4,5},{5,4},{6,7},{7,6},{8,9},{9,8},{10,11... | collective-permute-start | bytes 196616 | tf_op jit(solution)/shard_map/ppermute | solution.py:650
  4.9 2.3 %collective-permute-start.1 = (bf16[256,128]{1,0:T(8,128)(2,1)S(1)}, bf16[256,128]{1,0:T(8,128)(2,1)S(1)}, u32[]{:S(2)}, u32[]{:S(2)}) collective-permute-start(bf16[256,128]{1,0:T(8,128)(2,1)S(1)} %get-tuple-element.89), channel_id=1, source_target_pairs={{0,2},{2,0},{1,3},{3,1},{4,6},{6,4},{5,7},{7,5},{8,10},{10,8},{9,1... | collective-permute-start | bytes 196616 | tf_op jit(solution)/shard_map/ppermute | solution.py:650
  7.2 1.7 %collective-permute-start.2 = (bf16[256,128]{1,0:T(8,128)(2,1)S(1)}, bf16[256,128]{1,0:T(8,128)(2,1)S(1)}, u32[]{:S(2)}, u32[]{:S(2)}) collective-permute-start(bf16[256,128]{1,0:T(8,128)(2,1)S(1)} %get-tuple-element.90), channel_id=1, source_target_pairs={{0,4},{4,0},{1,5},{5,1},{2,6},{6,2},{3,7},{7,3},{8,12},{12,8},{9,1... | collective-permute-start | bytes 196616 | tf_op jit(solution)/shard_map/ppermute | solution.py:650
  8.9 1.3 %collective-permute-start.3 = (bf16[256,128]{1,0:T(8,128)(2,1)S(1)}, bf16[256,128]{1,0:T(8,128)(2,1)S(1)}, u32[]{:S(2)}, u32[]{:S(2)}) collective-permute-start(bf16[256,128]{1,0:T(8,128)(2,1)S(1)} %get-tuple-element.91), channel_id=1, source_target_pairs={{0,8},{8,0},{1,9},{9,1},{2,10},{10,2},{3,11},{11,3},{4,12},{12,4},... | collective-permute-start | bytes 196616 | tf_op jit(solution)/shard_map/ppermute | solution.py:650
  10.1 2.6 %collective-permute-start.4 = (bf16[256,128]{1,0:T(8,128)(2,1)S(1)}, bf16[256,128]{1,0:T(8,128)(2,1)S(1)}, u32[]{:S(2)}, u32[]{:S(2)}) collective-permute-start(bf16[256,128]{1,0:T(8,128)(2,1)S(1)} %get-tuple-element.92), channel_id=1, source_target_pairs={{0,16},{16,0},{1,17},{17,1},{2,18},{18,2},{3,19},{19,3},{4,20},{20... | collective-permute-start | bytes 196616 | tf_op jit(solution)/shard_map/ppermute | solution.py:650
  12.7 4.6 %shard_map.122 = (bf16[64,64,128]{2,1,0:T(8,128)(2,1)S(1)}, bf16[64,64,128]{2,1,0:T(8,128)(2,1)S(1)}, f32[10,64,128]{2,1,0:T(8,128)S(1)}, f32[10,64,128]{2,1,0:T...) custom-call(s32[46]{0:T(128)S(1)} %get-tuple-element.76.refs_0_, ...), custom_call_target="tpu_custom_call" | custom-call | flops 805306368 | bytes 12582912 | tf_op jit(solution)/shard_map/pallas_call | solution.py:265
  17.3 0.0 collective-permute-done.refs_7_
  17.3 0.0 collective-permute-done.1.refs_8_
  17.3 0.0 collective-permute-done.2.refs_9_
  17.4 0.0 collective-permute-done.4.refs_11_
  17.4 0.9 %shard_map.123 = (bf16[64,64,128]{2,1,0:T(8,128)(2,1)S(1)}, bf16[64,64,128]{2,1,0:T(8,128)(2,1)S(1)}, bf16[256,128]{1,0:T(8,128)(2,1)S(1)}, bf16[256,128]{1,0:T(...) custom-call(s32[46]{0:T(128)S(1)} %get-tuple-element.76.refs_0_, ...), custom_call_target="tpu_custom_call", output_to_operand_aliasing={{0}: (2, {}), {1}: (3, {})} | custom-call | flops 20971520 | bytes 5242880 | tf_op jit(solution)/shard_map/pallas_call | solution.py:420
  18.3 0.1 collective-permute-start.5
  18.4 0.7 %collective-permute-start.6 = (bf16[256,128]{1,0:T(8,128)(2,1)S(1)}, bf16[256,128]{1,0:T(8,128)(2,1)S(1)}, u32[]{:S(2)}, u32[]{:S(2)}) collective-permute-start(bf16[256,128]{1,0:T(8,128)(2,1)S(1)} %get-tuple-element.102), channel_id=1, source_target_pairs={{0,2},{2,0},{1,3},{3,1},{4,6},{6,4},{5,7},{7,5},{8,10},{10,8},{9,1... | collective-permute-start | bytes 196616 | tf_op jit(solution)/shard_map/ppermute | solution.py:650
  19.1 1.2 %collective-permute-start.7 = (bf16[256,128]{1,0:T(8,128)(2,1)S(1)}, bf16[256,128]{1,0:T(8,128)(2,1)S(1)}, u32[]{:S(2)}, u32[]{:S(2)}) collective-permute-start(bf16[256,128]{1,0:T(8,128)(2,1)S(1)} %get-tuple-element.103), channel_id=1, source_target_pairs={{0,4},{4,0},{1,5},{5,1},{2,6},{6,2},{3,7},{7,3},{8,12},{12,8},{9,1... | collective-permute-start | bytes 196616 | tf_op jit(solution)/shard_map/ppermute | solution.py:650
  20.4 0.4 collective-permute-start.8
  20.8 0.2 collective-permute-start.9
  21.0 4.4 %shard_map.124 = (bf16[64,64,128]{2,1,0:T(8,128)(2,1)S(1)}, bf16[64,64,128]{2,1,0:T(8,128)(2,1)S(1)}, f32[10,64,128]{2,1,0:T(8,128)S(1)}, f32[10,64,128]{2,1,0:T(8,128)S(1)}, f32[128,128]{1,0:T(8,128)S(1)}) custom-call(s32[46]{0:T(128)S(1)} %get-tuple-element.76.refs_0_, s32[3,64]{1,0:T(4,128)S(1)} %get-tuple-element.78.refs_1_, ...), custom_call_target="tpu_custom_call" | custom-call | flops 805306368 | bytes 12582912 | tf_op jit(solution)/shard_map/pallas_call | solution.py:332
  25.4 0.0 collective-permute-done.5.refs_7_
  25.4 0.0 collective-permute-done.7.refs_9_
  25.4 0.0 collective-permute-done.8.refs_10_
  25.4 1.8 %collective-permute-done.9.refs_11_ = bf16[256,128]{1,0:T(8,128)(2,1)S(1)} collective-permute-done((bf16[256,128]{1,0:T(8,128)(2,1)S(1)}, bf16[256,128]{1,0:T(8,128)(2,1)S(1)}, u32[]{:S(2)}, u32[]{:S(2)}) %collective-permute-start.9) | collective-permute-done | bytes 65568 | tf_op jit(solution)/shard_map/ppermute | solution.py:650
  27.2 1.0 %shard_map.125 = (f32[10,64,128]{2,1,0:T(8,128)S(1)}, f32[10,64,128]{2,1,0:T(8,128)S(1)}, f32[64,128]{1,0:T(8,128)S(1)}, f32[64,128]{1,0:T(8,128)S(1)}) custom-call(s32[46]{0:T(128)S(1)} %get-tuple-element.76.refs_0_, bf16[10,128,128]{2,1,0:T(8,128)(2,1)S(1)} %get-tuple-element.77.refs_4_.refs_1_, f32[10,64,128]{2,1,0:T(8,128)S(1)} %get-tuple-element.97.refs_2_, ...), custom_call_target="tpu_custom_call" | custom-call | flops 41943040 | bytes 3145728 | tf_op jit(solution)/shard_map/pallas_call | solution.py:384
  28.2 0.1 collective-permute-start.10
  28.3 0.8 %shard_map.126 = (bf16[64,64,128]{2,1,0:T(8,128)(2,1)S(1)}, bf16[64,64,128]{2,1,0:T(8,128)(2,1)S(1)}, bf16[256,128]{1,0:T(8,128)(2,1)S(1)}, bf16[256,128]{1,0:T(...) custom-call(s32[46]{0:T(128)S(1)} %get-tuple-element.76.refs_0_, ...), custom_call_target="tpu_custom_call", output_to_operand_aliasing={{0}: (2, {}), {1}: (3, {})} | custom-call | flops 20971520 | bytes 5242880 | tf_op jit(solution)/shard_map/pallas_call | solution.py:420
  29.1 0.6 %collective-permute-start.12 = (bf16[256,128]{1,0:T(8,128)(2,1)S(1)}, bf16[256,128]{1,0:T(8,128)(2,1)S(1)}, u32[]{:S(2)}, u32[]{:S(2)}) collective-permute-start(bf16[256,128]{1,0:T(8,128)(2,1)S(1)} %get-tuple-element.121), channel_id=1, source_target_pairs={{0,1},{1,0},{2,3},{3,2},{4,5},{5,4},{6,7},{7,6},{8,9},{9,8},{10,11... | collective-permute-start | bytes 196616 | tf_op jit(solution)/shard_map/ppermute | solution.py:650
  29.7 2.1 %collective-permute-start.11 = (f32[64,128]{1,0:T(8,128)S(1)}, f32[64,128]{1,0:T(8,128)S(1)}, u32[]{:S(2)}, u32[]{:S(2)}) collective-permute-start(f32[64,128]{1,0:T(8,128)S(1)} %get-tuple-element.118.refs_0_), channel_id=1, source_target_pairs={{0,16},{16,0},{1,17},{17,1},{2,18},{18,2},{3,19},{19,3},{4,20},{20... | collective-permute-start | bytes 98312 | tf_op jit(solution)/shard_map/ppermute | solution.py:650
  31.8 0.9 %collective-permute-start.13 = (bf16[256,128]{1,0:T(8,128)(2,1)S(1)}, bf16[256,128]{1,0:T(8,128)(2,1)S(1)}, u32[]{:S(2)}, u32[]{:S(2)}) collective-permute-start(bf16[256,128]{1,0:T(8,128)(2,1)S(1)} %get-tuple-element.125), channel_id=1, source_target_pairs={{0,16},{16,0},{1,17},{17,1},{2,18},{18,2},{3,19},{19,3},{4,20},{20... | collective-permute-start | bytes 196616 | tf_op jit(solution)/shard_map/ppermute | solution.py:650
  32.7 3.3 %shard_map.128 = (bf16[64,64,128]{2,1,0:T(8,128)(2,1)S(1)}, bf16[64,64,128]{2,1,0:T(8,128)(2,1)S(1)}, f32[10,64,128]{2,1,0:T(8,128)S(1)}, f32[10,64,128]{2,1,0:T(8,128)S(1)}, f32[8,128]{1,0:T(8,128)S(1)}) custom-call(s32[46]{0:T(128)S(1)} %get-tuple-element.76.refs_0_, s32[3,64]{1,0:T(4,128)S(1)} %get-tuple-element.78.refs_1_, ...), custom_call_target="tpu_custom_call" | custom-call | flops 805306368 | bytes 12582912 | tf_op jit(solution)/shard_map/pallas_call | solution.py:332
  36.0 0.0 collective-permute-done.12.refs_4_.refs_6_
  36.0 0.0 collective-permute-done.11.refs_1_
  36.0 1.8 %collective-permute-start.15 = (f32[64,128]{1,0:T(8,128)S(1)}, f32[64,128]{1,0:T(8,128)S(1)}, u32[]{:S(2)}, u32[]{:S(2)}) collective-permute-start(f32[64,128]{1,0:T(8,128)S(1)} %get-tuple-element.127.refs_0_), channel_id=1, source_target_pairs={{0,8},{8,0},{1,9},{9,1},{2,10},{10,2},{3,11},{11,3},{4,12},{12,4},... | collective-permute-start | bytes 98312 | tf_op jit(solution)/shard_map/ppermute | solution.py:650
  37.9 0.3 collective-permute-start.14
  38.1 1.1 %shard_map.130 = (bf16[64,256]{1,0:T(8,128)(2,1)S(1)}, bf16[64,256]{1,0:T(8,128)(2,1)S(1)}, bf16[8,32,8,128]{3,2,1,0:T(8,128)(2,1)S(1)}, bf16[8,32,8,128]{3,2,1,0:T(8,128)(2,1)S(1)}) custom-call(bf16[64,64,128]{2,1,0:T(8,128)(2,1)S(1)} %get-tuple-element.79.refs_3_.refs_6_.refs_0_.refs_10_.refs_7_, ...), custom_call_target="tpu_custom_call" | custom-call | flops 268435456 | bytes 6291456 | tf_op jit(solution)/shard_map/pallas_call | solution.py:493
  39.2 0.0 collective-permute-done.13.refs_4_.refs_7_
  39.2 1.1 %collective-permute-done.15.refs_1_ = f32[64,128]{1,0:T(8,128)S(1)} collective-permute-done((f32[64,128]{1,0:T(8,128)S(1)}, f32[64,128]{1,0:T(8,128)S(1)}, u32[]{:S(2)}, u32[]{:S(2)}) %collective-permute-start.15) | collective-permute-done | bytes 32800 | tf_op jit(solution)/shard_map/ppermute | solution.py:650
  40.4 1.7 %collective-permute-start.16 = (bf16[256,128]{1,0:T(8,128)(2,1)S(1)}, bf16[256,128]{1,0:T(8,128)(2,1)S(1)}, u32[]{:S(2)}, u32[]{:S(2)}) collective-permute-start(bf16[256,128]{1,0:T(8,128)(2,1)S(1)} %get-tuple-element.129), channel_id=1, source_target_pairs={{0,4},{4,0},{1,5},{5,1},{2,6},{6,2},{3,7},{7,3},{8,12},{12,8},{9,1... | collective-permute-start | bytes 196616 | tf_op jit(solution)/shard_map/ppermute | solution.py:650
  42.0 0.4 collective-permute-start.17
  42.5 1.0 %shard_map.132 = (bf16[8,32,8,128]{3,2,1,0:T(8,128)(2,1)S(1)}, bf16[8,32,8,128]{3,2,1,0:T(8,128)(2,1)S(1)}, bf16[8,64,8,128]{3,2,1,0:T(8,128)(2,1)}, bf16[8,64,8,128]{3,2,1,0:T(8,128)(2,1)}) custom-call(bf16[64,64,128]{2,1,0:T(8,128)(2,1)S(1)} %get-tuple-element.79.refs_3_.refs_6_.refs_0_.refs_10_.refs_7_, ...), custom_call_target="tpu_custom_call" | custom-call | flops 268435456 | bytes 6291456 | tf_op jit(solution)/shard_map/pallas_call | solution.py:493
  43.5 2.5 %collective-permute-done.17.refs_1_ = f32[64,128]{1,0:T(8,128)S(1)} collective-permute-done((f32[64,128]{1,0:T(8,128)S(1)}, f32[64,128]{1,0:T(8,128)S(1)}, u32[]{:S(2)}, u32[]{:S(2)}) %collective-permute-start.17) | collective-permute-done | bytes 32800 | tf_op jit(solution)/shard_map/ppermute | solution.py:650
  46.0 0.9 %collective-permute-start.19 = (f32[64,128]{1,0:T(8,128)S(1)}, f32[64,128]{1,0:T(8,128)S(1)}, u32[]{:S(2)}, u32[]{:S(2)}) collective-permute-start(f32[64,128]{1,0:T(8,128)S(1)} %get-tuple-element.143.refs_0_), channel_id=1, source_target_pairs={{0,2},{2,0},{1,3},{3,1},{4,6},{6,4},{5,7},{7,5},{8,10},{10,8},{9,1... | collective-permute-start | bytes 98312 | tf_op jit(solution)/shard_map/ppermute | solution.py:650
  46.9 1.1 %collective-permute-start.18 = (bf16[256,128]{1,0:T(8,128)(2,1)S(1)}, bf16[256,128]{1,0:T(8,128)(2,1)S(1)}, u32[]{:S(2)}, u32[]{:S(2)}) collective-permute-start(bf16[256,128]{1,0:T(8,128)(2,1)S(1)} %get-tuple-element.142), channel_id=1, source_target_pairs={{0,2},{2,0},{1,3},{3,1},{4,6},{6,4},{5,7},{7,5},{8,10},{10,8},{9,1... | collective-permute-start | bytes 196616 | tf_op jit(solution)/shard_map/ppermute | solution.py:650
  48.1 0.0 collective-permute-done.16.refs_9_.refs_3_
  48.1 2.7 %shard_map.134 = (f32[10,64,128]{2,1,0:T(8,128)S(1)}, f32[10,64,128]{2,1,0:T(8,128)S(1)}, bf16[8,64,8,128]{3,2,1,0:T(8,128)(2,1)}, bf16[8,64,8,128]{3,2,1,0:T(8,128)(2,1)}) custom-call(s32[46]{0:T(128)S(1)} %get-tuple-element.76.refs_0_, bf16[10,128,128]{2,1,0:T(8,128)(2,1)S(1)} %get-tuple-element.77.refs_4_.refs_1_, ...), custom_call_target="tpu_custom_call", output_to_operand_aliasing={{2}: (19, {}), {3}: (20, {})} | custom-call | flops 83886080 | bytes 4194304 | tf_op jit(solution)/shard_map/pallas_call | solution.py:601
  50.8 0.1 collective-permute-start.20
  50.9 0.3 collective-permute-done.18.refs_6_
  51.2 0.9 %collective-permute-done.20.refs_14_ = f32[64,128]{1,0:T(8,128)S(1)} collective-permute-done((f32[64,128]{1,0:T(8,128)S(1)}, f32[64,128]{1,0:T(8,128)S(1)}, u32[]{:S(2)}, u32[]{:S(2)}) %collective-permute-start.20) | collective-permute-done | bytes 32800 | tf_op jit(solution)/shard_map/ppermute | solution.py:650
  52.1 2.3 %shard_map.136 = (bf16[8,64,8,128]{3,2,1,0:T(8,128)(2,1)}, bf16[8,64,8,128]{3,2,1,0:T(8,128)(2,1)}, f32[4,64,64]{2,1,0:T(8,128)}) custom-call(s32[46]{0:T(128)S(1)} %get-tuple-element.76.refs_0_, bf16[10,128,128]{2,1,0:T(8,128)(2,1)S(1)} %get-tuple-element.77.refs_4_.refs_1_, ...), custom_call_target="tpu_custom_call", output_to_operand_aliasing={{0}: (15, {}), {1}: (16, {})} | custom-call | flops 83886080 | bytes 4194304 | tf_op jit(solution)/shard_map/pallas_call | solution.py:601
  (12 shorter events, 0.1 us)
Async XLA Ops:
  4.1 13.3 %collective-permute-start = (bf16[256,128]{1,0:T(8,128)(2,1)S(1)}, bf16[256,128]{1,0:T(8,128)(2,1)S(1)}, u32[]{:S(2)}, u32[]{:S(2)}) collective-permute-start(bf16[256,128]{1,0:T(8,128)(2,1)S(1)} %get-tuple-element.88), channel_id=1, source_target_pairs={{0,1},{1,0},{2,3},{3,2},{4,5},{5,4},{6,7},{7,6},{8,9},{9,8},{10,11... | collective-permute-start | bytes 196616 | tf_op jit(solution)/shard_map/ppermute | solution.py:650
  4.9 12.5 %collective-permute-start.1 = (bf16[256,128]{1,0:T(8,128)(2,1)S(1)}, bf16[256,128]{1,0:T(8,128)(2,1)S(1)}, u32[]{:S(2)}, u32[]{:S(2)}) collective-permute-start(bf16[256,128]{1,0:T(8,128)(2,1)S(1)} %get-tuple-element.89), channel_id=1, source_target_pairs={{0,2},{2,0},{1,3},{3,1},{4,6},{6,4},{5,7},{7,5},{8,10},{10,8},{9,1... | collective-permute-start | bytes 196616 | tf_op jit(solution)/shard_map/ppermute | solution.py:650
  7.2 10.2 %collective-permute-start.2 = (bf16[256,128]{1,0:T(8,128)(2,1)S(1)}, bf16[256,128]{1,0:T(8,128)(2,1)S(1)}, u32[]{:S(2)}, u32[]{:S(2)}) collective-permute-start(bf16[256,128]{1,0:T(8,128)(2,1)S(1)} %get-tuple-element.90), channel_id=1, source_target_pairs={{0,4},{4,0},{1,5},{5,1},{2,6},{6,2},{3,7},{7,3},{8,12},{12,8},{9,1... | collective-permute-start | bytes 196616 | tf_op jit(solution)/shard_map/ppermute | solution.py:650
  8.9 8.5 %collective-permute-start.3 = (bf16[256,128]{1,0:T(8,128)(2,1)S(1)}, bf16[256,128]{1,0:T(8,128)(2,1)S(1)}, u32[]{:S(2)}, u32[]{:S(2)}) collective-permute-start(bf16[256,128]{1,0:T(8,128)(2,1)S(1)} %get-tuple-element.91), channel_id=1, source_target_pairs={{0,8},{8,0},{1,9},{9,1},{2,10},{10,2},{3,11},{11,3},{4,12},{12,4},... | collective-permute-start | bytes 196616 | tf_op jit(solution)/shard_map/ppermute | solution.py:650
  10.1 7.2 %collective-permute-start.4 = (bf16[256,128]{1,0:T(8,128)(2,1)S(1)}, bf16[256,128]{1,0:T(8,128)(2,1)S(1)}, u32[]{:S(2)}, u32[]{:S(2)}) collective-permute-start(bf16[256,128]{1,0:T(8,128)(2,1)S(1)} %get-tuple-element.92), channel_id=1, source_target_pairs={{0,16},{16,0},{1,17},{17,1},{2,18},{18,2},{3,19},{19,3},{4,20},{20... | collective-permute-start | bytes 196616 | tf_op jit(solution)/shard_map/ppermute | solution.py:650
  18.3 7.1 %collective-permute-start.5 = (bf16[256,128]{1,0:T(8,128)(2,1)S(1)}, bf16[256,128]{1,0:T(8,128)(2,1)S(1)}, u32[]{:S(2)}, u32[]{:S(2)}) collective-permute-start(bf16[256,128]{1,0:T(8,128)(2,1)S(1)} %get-tuple-element.101), channel_id=1, source_target_pairs={{0,1},{1,0},{2,3},{3,2},{4,5},{5,4},{6,7},{7,6},{8,9},{9,8},{10,11... | collective-permute-start | bytes 196616 | tf_op jit(solution)/shard_map/ppermute | solution.py:650
  18.4 7.0 %collective-permute-start.6 = (bf16[256,128]{1,0:T(8,128)(2,1)S(1)}, bf16[256,128]{1,0:T(8,128)(2,1)S(1)}, u32[]{:S(2)}, u32[]{:S(2)}) collective-permute-start(bf16[256,128]{1,0:T(8,128)(2,1)S(1)} %get-tuple-element.102), channel_id=1, source_target_pairs={{0,2},{2,0},{1,3},{3,1},{4,6},{6,4},{5,7},{7,5},{8,10},{10,8},{9,1... | collective-permute-start | bytes 196616 | tf_op jit(solution)/shard_map/ppermute | solution.py:650
  19.1 6.3 %collective-permute-start.7 = (bf16[256,128]{1,0:T(8,128)(2,1)S(1)}, bf16[256,128]{1,0:T(8,128)(2,1)S(1)}, u32[]{:S(2)}, u32[]{:S(2)}) collective-permute-start(bf16[256,128]{1,0:T(8,128)(2,1)S(1)} %get-tuple-element.103), channel_id=1, source_target_pairs={{0,4},{4,0},{1,5},{5,1},{2,6},{6,2},{3,7},{7,3},{8,12},{12,8},{9,1... | collective-permute-start | bytes 196616 | tf_op jit(solution)/shard_map/ppermute | solution.py:650
  20.4 5.1 %collective-permute-start.8 = (bf16[256,128]{1,0:T(8,128)(2,1)S(1)}, bf16[256,128]{1,0:T(8,128)(2,1)S(1)}, u32[]{:S(2)}, u32[]{:S(2)}) collective-permute-start(bf16[256,128]{1,0:T(8,128)(2,1)S(1)} %get-tuple-element.104), channel_id=1, source_target_pairs={{0,8},{8,0},{1,9},{9,1},{2,10},{10,2},{3,11},{11,3},{4,12},{12,4},... | collective-permute-start | bytes 196616 | tf_op jit(solution)/shard_map/ppermute | solution.py:650
  20.8 6.4 %collective-permute-start.9 = (bf16[256,128]{1,0:T(8,128)(2,1)S(1)}, bf16[256,128]{1,0:T(8,128)(2,1)S(1)}, u32[]{:S(2)}, u32[]{:S(2)}) collective-permute-start(bf16[256,128]{1,0:T(8,128)(2,1)S(1)} %get-tuple-element.105), channel_id=1, source_target_pairs={{0,16},{16,0},{1,17},{17,1},{2,18},{18,2},{3,19},{19,3},{4,20},{20... | collective-permute-start | bytes 196616 | tf_op jit(solution)/shard_map/ppermute | solution.py:650
  28.2 1.4 %collective-permute-start.10 = (f32[64,128]{1,0:T(8,128)S(1)}, f32[64,128]{1,0:T(8,128)S(1)}, u32[]{:S(2)}, u32[]{:S(2)}) collective-permute-start(f32[64,128]{1,0:T(8,128)S(1)} %get-tuple-element.111), channel_id=1, source_target_pairs={{0,1},{1,0},{2,3},{3,2},{4,5},{5,4},{6,7},{7,6},{8,9},{9,8},{10,11... | collective-permute-start | bytes 98312 | tf_op jit(solution)/shard_map/ppermute | solution.py:650
  29.1 6.9 %collective-permute-start.12 = (bf16[256,128]{1,0:T(8,128)(2,1)S(1)}, bf16[256,128]{1,0:T(8,128)(2,1)S(1)}, u32[]{:S(2)}, u32[]{:S(2)}) collective-permute-start(bf16[256,128]{1,0:T(8,128)(2,1)S(1)} %get-tuple-element.121), channel_id=1, source_target_pairs={{0,1},{1,0},{2,3},{3,2},{4,5},{5,4},{6,7},{7,6},{8,9},{9,8},{10,11... | collective-permute-start | bytes 196616 | tf_op jit(solution)/shard_map/ppermute | solution.py:650
  29.7 6.3 %collective-permute-start.11 = (f32[64,128]{1,0:T(8,128)S(1)}, f32[64,128]{1,0:T(8,128)S(1)}, u32[]{:S(2)}, u32[]{:S(2)}) collective-permute-start(f32[64,128]{1,0:T(8,128)S(1)} %get-tuple-element.118.refs_0_), channel_id=1, source_target_pairs={{0,16},{16,0},{1,17},{17,1},{2,18},{18,2},{3,19},{19,3},{4,20},{20... | collective-permute-start | bytes 98312 | tf_op jit(solution)/shard_map/ppermute | solution.py:650
  31.8 7.4 %collective-permute-start.13 = (bf16[256,128]{1,0:T(8,128)(2,1)S(1)}, bf16[256,128]{1,0:T(8,128)(2,1)S(1)}, u32[]{:S(2)}, u32[]{:S(2)}) collective-permute-start(bf16[256,128]{1,0:T(8,128)(2,1)S(1)} %get-tuple-element.125), channel_id=1, source_target_pairs={{0,16},{16,0},{1,17},{17,1},{2,18},{18,2},{3,19},{19,3},{4,20},{20... | collective-permute-start | bytes 196616 | tf_op jit(solution)/shard_map/ppermute | solution.py:650
  32.7 5.5 %copy-start = (bf16[4,64,64]{2,1,0:T(8,128)(2,1)S(1)}, bf16[4,64,64]{2,1,0:T(8,128)(2,1)}, u32[]{:S(2)}) copy-start(bf16[4,64,64]{2,1,0:T(8,128)(2,1)} %refs_8_.1) | copy-start | bytes 98308
  36.0 4.3 %collective-permute-start.15 = (f32[64,128]{1,0:T(8,128)S(1)}, f32[64,128]{1,0:T(8,128)S(1)}, u32[]{:S(2)}, u32[]{:S(2)}) collective-permute-start(f32[64,128]{1,0:T(8,128)S(1)} %get-tuple-element.127.refs_0_), channel_id=1, source_target_pairs={{0,8},{8,0},{1,9},{9,1},{2,10},{10,2},{3,11},{11,3},{4,12},{12,4},... | collective-permute-start | bytes 98312 | tf_op jit(solution)/shard_map/ppermute | solution.py:650
  37.9 5.6 %collective-permute-start.14 = (bf16[256,128]{1,0:T(8,128)(2,1)S(1)}, bf16[256,128]{1,0:T(8,128)(2,1)S(1)}, u32[]{:S(2)}, u32[]{:S(2)}) collective-permute-start(bf16[256,128]{1,0:T(8,128)(2,1)S(1)} %get-tuple-element.126), channel_id=1, source_target_pairs={{0,8},{8,0},{1,9},{9,1},{2,10},{10,2},{3,11},{11,3},{4,12},{12,4},... | collective-permute-start | bytes 196616 | tf_op jit(solution)/shard_map/ppermute | solution.py:650
  40.4 7.7 %collective-permute-start.16 = (bf16[256,128]{1,0:T(8,128)(2,1)S(1)}, bf16[256,128]{1,0:T(8,128)(2,1)S(1)}, u32[]{:S(2)}, u32[]{:S(2)}) collective-permute-start(bf16[256,128]{1,0:T(8,128)(2,1)S(1)} %get-tuple-element.129), channel_id=1, source_target_pairs={{0,4},{4,0},{1,5},{5,1},{2,6},{6,2},{3,7},{7,3},{8,12},{12,8},{9,1... | collective-permute-start | bytes 196616 | tf_op jit(solution)/shard_map/ppermute | solution.py:650
  42.0 3.9 %collective-permute-start.17 = (f32[64,128]{1,0:T(8,128)S(1)}, f32[64,128]{1,0:T(8,128)S(1)}, u32[]{:S(2)}, u32[]{:S(2)}) collective-permute-start(f32[64,128]{1,0:T(8,128)S(1)} %get-tuple-element.135.refs_0_), channel_id=1, source_target_pairs={{0,4},{4,0},{1,5},{5,1},{2,6},{6,2},{3,7},{7,3},{8,12},{12,8},{9,1... | collective-permute-start | bytes 98312 | tf_op jit(solution)/shard_map/ppermute | solution.py:650
  46.0 4.8 %collective-permute-start.19 = (f32[64,128]{1,0:T(8,128)S(1)}, f32[64,128]{1,0:T(8,128)S(1)}, u32[]{:S(2)}, u32[]{:S(2)}) collective-permute-start(f32[64,128]{1,0:T(8,128)S(1)} %get-tuple-element.143.refs_0_), channel_id=1, source_target_pairs={{0,2},{2,0},{1,3},{3,1},{4,6},{6,4},{5,7},{7,5},{8,10},{10,8},{9,1... | collective-permute-start | bytes 98312 | tf_op jit(solution)/shard_map/ppermute | solution.py:650
  46.9 4.3 %collective-permute-start.18 = (bf16[256,128]{1,0:T(8,128)(2,1)S(1)}, bf16[256,128]{1,0:T(8,128)(2,1)S(1)}, u32[]{:S(2)}, u32[]{:S(2)}) collective-permute-start(bf16[256,128]{1,0:T(8,128)(2,1)S(1)} %get-tuple-element.142), channel_id=1, source_target_pairs={{0,2},{2,0},{1,3},{3,1},{4,6},{6,4},{5,7},{7,5},{8,10},{10,8},{9,1... | collective-permute-start | bytes 196616 | tf_op jit(solution)/shard_map/ppermute | solution.py:650
  50.8 1.3 %collective-permute-start.20 = (f32[64,128]{1,0:T(8,128)S(1)}, f32[64,128]{1,0:T(8,128)S(1)}, u32[]{:S(2)}, u32[]{:S(2)}) collective-permute-start(f32[64,128]{1,0:T(8,128)S(1)} %shard_map.135.refs_13_), channel_id=1, source_target_pairs={{0,1},{1,0},{2,3},{3,2},{4,5},{5,4},{6,7},{7,6},{8,9},{9,8},{10,11... | collective-permute-start | bytes 98312 | tf_op jit(solution)/shard_map/ppermute | solution.py:650

commit v7 on v6

--- a/solution.py
+++ b/solution.py
@@ -277,20 +277,8 @@
     )(meta, col, keep(tiles), t0, s0)
 
 
-def local_kernel(sz, grad, *refs):
-    meta_in, col_in, tiles, turned, tcur, scur, tprev, sprev, _ = refs[:9]
-    tnew, snew, psel, qsel, last = refs[9:14]
-    held, summed, meta, col, sem = refs[14:]
-    small = [
-        pltpu.make_async_copy(meta_in, meta, sem.at[0]),
-        pltpu.make_async_copy(col_in, col, sem.at[1]),
-    ]
-    for copy in small:
-        copy.start()
-    clear_sums(sz, summed)
-    for copy in small:
-        copy.wait()
-    count = meta[sz.live]
+def row_products(sz, col, low, high, arrays, tnew, held, summed):
+    tiles, turned, tcur, scur, tprev = arrays
 
     def block_row(i):
         cols = [col[m, i] for m in range(sz.nz)]
@@ -306,15 +294,34 @@
             block_row(g * ROWS + u)
         return carry
 
-    lax.fori_loop(0, big_steps(count), step, 0)
+    lax.fori_loop(low, high, step, 0)
+
+
+def start_table(meta_in, col_in, meta, col, sem):
+    small = [
+        pltpu.make_async_copy(meta_in, meta, sem.at[0]),
+        pltpu.make_async_copy(col_in, col, sem.at[1]),
+    ]
+    for copy in small:
+        copy.start()
+    return small
+
+
+def local_kernel(sz, *refs):
+    meta_in, col_in, tiles, turned, tcur, scur, tprev, sprev = refs[:8]
+    tnew, snew, psel, qsel, gram, held, summed, meta, col, sem = refs[8:]
+    small = start_table(meta_in, col_in, meta, col, sem)
+    clear_sums(sz, summed)
+    for copy in small:
+        copy.wait()
+    steps = big_steps(meta[sz.live])
+    arrays = (tiles, turned, tcur, scur, tprev)
+    row_products(sz, col, 0, steps, arrays, tnew, held, summed)
 
     def adjoint(i):
         return 2.0 * summed[i] - sprev[i].astype(F32)
 
     finish_local(sz, meta, held, adjoint, tnew, snew, psel, qsel)
-    if not grad:
-        last[...] = jnp.zeros(last.shape, F32)
-        return
 
     def products(g, total):
         left, right = [], []
@@ -324,47 +331,104 @@
             right.append(jnp.concatenate([sprev[i], scur[i]], axis=0).T)
         return total + nn(jnp.concatenate(left, axis=1), jnp.concatenate(right, axis=0))
 
-    last[...] = lax.fori_loop(0, big_steps(count), products, jnp.zeros(last.shape, F32))
-
-
-def local_products(sz, meta, col, tiles, turned, fields, token, grad):
-    tail = shape((2 * sz.chan, 2 * sz.chan), F32) if grad else TOKEN
+    gram[...] = lax.fori_loop(0, steps, products, jnp.zeros(gram.shape, F32))
+
+
+def local_products(sz, meta, col, tiles, turned, fields):
+    gram = shape((2 * sz.chan, 2 * sz.chan), F32)
     return call(
-        functools.partial(local_kernel, sz, grad),
-        [VMEM] * 9,
+        functools.partial(local_kernel, sz),
+        [VMEM] * 8,
         [VMEM] * 5,
-        [sz.field, sz.field, sz.picked, sz.picked, tail],
+        [sz.field, sz.field, sz.picked, sz.picked, gram],
         [pltpu.VMEM((sz.blocks, sz.chan, sz.blk), F32)] * 2
         + table_scratch(sz, col)
         + [pltpu.SemaphoreType.DMA((2,))],
         4 * sz.blocks * sz.nz * sz.chan * sz.blk * sz.blk,
         12 << 20,
         24,
-    )(meta, col, tiles, turned, *fields, token)
-
-
-def add_coupled(sz, scale, meta, got, across, psel, qsel, pacc, qacc, which):
+    )(meta, col, tiles, turned, *fields)
+
+
+def early_rows_kernel(sz, *refs):
+    meta_in, col_in, tiles, turned, tcur, scur, tprev, _ = refs[:8]
+    tnew, held, summed, meta, col, sem = refs[8:]
+    small = start_table(meta_in, col_in, meta, col, sem)
+    clear_sums(sz, summed)
+    for copy in small:
+        copy.wait()
+    cut = (3 * big_steps(meta[sz.live])) // 4
+    arrays = (tiles, turned, tcur, scur, tprev)
+    row_products(sz, col, 0, cut, arrays, tnew, held, summed)
+
+
+def late_rows_kernel(sz, *refs):
+    meta_in, col_in, tiles, turned, tcur, scur, tprev, sprev = refs[:8]
+    tnew, held, summed, snew, psel, qsel, meta, col, sem = refs[12:]
+    for copy in start_table(meta_in, col_in, meta, col, sem):
+        copy.wait()
+    steps = big_steps(meta[sz.live])
+    arrays = (tiles, turned, tcur, scur, tprev)
+    row_products(sz, col, (3 * steps) // 4, steps, arrays, tnew, held, summed)
+
+    def adjoint(i):
+        return 2.0 * summed[i] - sprev[i].astype(F32)
+
+    finish_local(sz, meta, held, adjoint, tnew, snew, psel, qsel)
+
+
+def part_products(sz, meta, col, tiles, turned, fields, before, token):
+    sums = shape((sz.blocks, sz.chan, sz.blk), F32)
+    args = [meta, col, tiles, turned, *fields]
+    outs, aliases = [sz.field, sums, sums], {}
+    if before is None:
+        args[-1] = token
+    else:
+        aliases = {len(args) + k: k for k in range(3)}
+        args += [*before, token]
+        outs += [sz.field, sz.picked, sz.picked]
+    return call(
+        functools.partial(early_rows_kernel if before is None else late_rows_kernel, sz),
+        [VMEM] * len(args),
+        [VMEM] * len(outs),
+        outs,
+        table_scratch(sz, col) + [pltpu.SemaphoreType.DMA((2,))],
+        2 * sz.blocks * sz.nz * sz.chan * sz.blk * sz.blk,
+        6 << 20,
+        8,
+        aliases,
+    )(*args)
+
+
+def add_coupled(sz, scale, table, got, across, psel, qsel, pacc, qacc, which):
+    meta_in, meta, sem = table
+    copy = pltpu.make_async_copy(meta_in, meta, sem)
+    copy.start()
     for j in range(sz.pairs):
         pacc[j] = psel[j]
         qacc[j] = qsel[j]
-    terms = {}
-    for r, h, j in sz.couplings():
-        if r in which:
-            factor = scale * meta[sz.flags + r].astype(F32)
-            terms[j] = factor * nn(got[r][sz.forward_part(h), :], across[j])
-            spot = meta[sz.first_row + j]
-            pacc[spot] = pacc[spot] + terms[j]
-            spot = meta[sz.first_send + j]
-            qacc[spot] = qacc[spot] + scale * got[r][sz.adjoint_part(h), :].astype(F32)
+    some = [(r, h, j) for r, h, j in sz.couplings() if r in which]
+    terms = {j: nn(got[r][sz.forward_part(h), :], across[j]) for r, h, j in some}
+    copy.wait()
+    for r, h, j in some:
+        terms[j] = (scale * meta[sz.flags + r].astype(F32)) * terms[j]
+        spot = meta[sz.first_row + j]
+        pacc[spot] = pacc[spot] + terms[j]
+        spot = meta[sz.first_send + j]
+        qacc[spot] = qacc[spot] + scale * got[r][sz.adjoint_part(h), :].astype(F32)
     return terms
 
 
+def table_copy(sz):
+    return [pltpu.SMEM((sz.meta,), jnp.int32), pltpu.SemaphoreType.DMA]
+
+
 def correct_kernel(sz, axis, *refs):
-    meta, across, psel, qsel, gram0, gram, sold = refs[:7]
+    meta_in, across, psel, qsel, gram0, gram, sold = refs[:7]
     got, refs = refs[7 : 7 + sz.rounds], refs[7 + sz.rounds :]
-    pacc, qacc, keep_half, give_half, whole = refs
-    which = range(sz.rounds)
-    terms = add_coupled(sz, 2.0, meta, got, across, psel, qsel, pacc, qacc, which)
+    pacc, qacc, keep_half, give_half, whole, meta, sem = refs
+    which, table = range(sz.rounds), (meta_in, meta, sem)
+    terms = add_coupled(sz, 2.0, table, got, across, psel, qsel, pacc, qacc, which)
     left = jnp.concatenate([terms[j].astype(BF16) for j in range(sz.pairs)], axis=1)
     right = [sold[meta[sz.rows + j]].T for j in range(sz.pairs)]
     extra = nn(left, jnp.concatenate(right, axis=0))
@@ -383,10 +447,10 @@
     half = shape((sz.chan, 2 * sz.chan), F32)
     return call(
         functools.partial(correct_kernel, sz, axis),
-        [SMEM] + [VMEM] * (len(args) - 1),
+        [VMEM] * len(args),
         [VMEM] * 4,
         [sz.picked, sz.picked, half, half],
-        [pltpu.VMEM((2 * sz.chan, 2 * sz.chan), F32)],
+        [pltpu.VMEM((2 * sz.chan, 2 * sz.chan), F32)] + table_copy(sz),
         4 * sz.pairs * sz.chan * sz.blk * sz.blk,
         3 << 20,
         8,
@@ -401,12 +465,13 @@
 
 
 def start_kernel(sz, *refs):
-    meta, cross, _, _, across, psel, qsel = refs[:7]
+    meta_in, cross, _, _, across, psel, qsel = refs[:7]
     got, refs = refs[7 : 7 + sz.rounds], refs[7 + sz.rounds :]
     tnew, snew = refs[:2]
-    pacc, qacc = refs[-2:]
-    add_coupled(sz, 1.0, meta, got, across, psel, qsel, pacc, qacc, range(sz.rounds))
-    patch(sz, meta, cross, tnew, snew, pacc, qacc, refs[2:-2])
+    pacc, qacc, meta, sem = refs[-4:]
+    table = (meta_in, meta, sem)
+    add_coupled(sz, 1.0, table, got, across, psel, qsel, pacc, qacc, range(sz.rounds))
+    patch(sz, meta, cross, tnew, snew, pacc, qacc, refs[2:-4])
 
 
 def join_kernel(sz, *refs):
@@ -419,10 +484,10 @@
     outs = [sz.field, sz.field] + [sz.pay] * sz.rounds
     outs = call(
         functools.partial(start_kernel if first else join_kernel, sz),
-        [SMEM] + [VMEM] * (len(args) - 1),
+        [VMEM if first else SMEM] + [VMEM] * (len(args) - 1),
         [VMEM] * len(outs),
         outs,
-        [pltpu.VMEM(sz.picked.shape, F32)] * 2 if first else [],
+        [pltpu.VMEM(sz.picked.shape, F32)] * 2 + table_copy(sz) if first else [],
         2 * sz.pairs * sz.chan * sz.blk * sz.blk,
         5 << 20,
         8,
@@ -444,170 +509,168 @@
         held[(t,) + spot if len(spot) == 1 else (spot[1], t)] = value[t * SUB : (t + 1) * SUB]
 
 
-def output_kernel(sz, low, *refs):
-    forward, adjoint = refs[:4], refs[4:8]
-    if low == 0:
-        weight, ahead, back, held_out, held_grad = refs[8], *refs[10:]
-        wide_ahead, wide_back = output_weights(weight)
-        ahead[...] = wide_ahead
-        back[...] = wide_back
-        copies = []
-    else:
-        ahead, back, before_out, before_grad = refs[8:12]
-        held_out, held_grad, out4, grad4, sem = refs[13:]
-        part = pl.ds(0, low)
-        copies = [
-            pltpu.make_async_copy(before_out, out4.at[:, part], sem.at[0]),
-            pltpu.make_async_copy(before_grad, grad4.at[:, part], sem.at[1]),
-        ]
+def output_kernel(sz, middle, *refs):
+    forward, adjoint, weight = refs[:4], refs[4:8], refs[8]
+    ahead, back, high_out, high_grad, out4, grad4, low_out, low_grad, sem = refs[10:]
+    wide_ahead, wide_back = output_weights(weight)
+    ahead[...] = wide_ahead
+    back[...] = wide_back
+
+    def half(low, count, held_out, held_grad):
+        def step(g, carry):
+            for u in range(ROWS):
+                n = g * ROWS + u
+                output_block(sz, ahead, [f[low + n] for f in forward], held_out, (n,))
+                output_block(sz, back, [f[low + n] for f in adjoint], held_grad, (n,))
+            return carry
+
+        lax.fori_loop(0, count // ROWS, step, 0)
+
+    half(0, middle, low_out, low_grad)
+    part = pl.ds(0, middle)
+    copies = [
+        pltpu.make_async_copy(low_out, out4.at[:, part], sem.at[0]),
+        pltpu.make_async_copy(low_grad, grad4.at[:, part], sem.at[1]),
+    ]
     for copy in copies:
         copy.start()
-
-    def step(g, carry):
-        for u in range(ROWS):
-            n = g * ROWS + u
-            output_block(sz, ahead, [f[low + n] for f in forward], held_out, (n,))
-            output_block(sz, back, [f[low + n] for f in adjoint], held_grad, (n,))
-        return carry
-
-    lax.fori_loop(0, held_out.shape[1] // ROWS, step, 0)
+    half(middle, sz.blocks - middle, high_out, high_grad)
     for copy in copies:
         copy.wait()
 
 
-def output_weight_shape(sz, orders):
-    return shape((sz.chan, orders * sz.chan), BF16)
-
-
-def base_outputs(sz, low, high, forward, adjoint, rest, token, orders):
+def base_outputs(sz, middle, forward, adjoint, weight, token):
     groups = sz.chan // SUB
-    held = shape((groups, high - low, SUB, sz.blk), BF16)
+    high = shape((groups, sz.blocks - middle, SUB, sz.blk), BF16)
     whole = shape((groups, sz.blocks, SUB, sz.blk), BF16)
-    args = [*forward, *adjoint, *rest, token]
-    if low == 0:
-        outs = [output_weight_shape(sz, orders)] * 2 + [held, held]
-        specs = [VMEM] * 4
-    else:
-        outs = [held, held, whole, whole]
-        specs = [VMEM] * 2 + [HBM] * 2
+    wide = shape((sz.chan, weight.shape[0] * sz.chan), BF16)
+    args = [*forward, *adjoint, weight, token]
     return call(
-        functools.partial(output_kernel, sz, low),
+        functools.partial(output_kernel, sz, middle),
         [VMEM] * len(args),
-        specs,
-        outs,
-        [pltpu.SemaphoreType.DMA((2,))] if low else [],
-        16 * (high - low) * sz.chan * sz.chan * sz.blk,
+        [VMEM] * 4 + [HBM] * 2,
+        [wide, wide, high, high, whole, whole],
+        [pltpu.VMEM((groups, middle, SUB, sz.blk), BF16)] * 2 + [pltpu.SemaphoreType.DMA((2,))],
+        16 * sz.blocks * sz.chan * sz.chan * sz.blk,
         6 << 20,
-        8,
+        10,
     )(*args)
 
 
-def fixed_blocks(sz, meta, which, ahead, back, forward, adjoint, pacc, qacc, held, outs, sem):
-    copies, seen = [], ([], [])
+def fixed_blocks(sz, meta, which, weights, fields, last, held):
     for r, h, j in sz.couplings():
-        if r not in which:
-            continue
-        for side, (left, fields, last, spot, first) in enumerate(
-            (
-                (ahead, forward, pacc, sz.rows, sz.first_row),
-                (back, adjoint, qacc, sz.sends, sz.first_send),
-            )
-        ):
-            i, slot = meta[spot + j], meta[first + j]
-            stack = [f[i] for f in fields] + [last[slot].astype(BF16)]
-            output_block(sz, left, stack, held[side], (None, j))
-            fresh = jnp.bool_(True)
-            for other in seen[side]:
-                fresh = jnp.logical_and(fresh, other != i)
-            seen[side].append(i)
-            copy = pltpu.make_async_copy(
-                held[side].at[j], outs[side].at[:, i], sem.at[side, j]
-            )
-            copies.append((fresh, copy))
+        if r in which:
+            for side, spot, first in ((0, sz.rows, sz.first_row), (1, sz.sends, sz.first_send)):
+                i = meta[spot + j]
+                stack = [f[i] for f in fields[3 * side : 3 * side + 3]]
+                stack.append(last[side][meta[first + j]].astype(BF16))
+                output_block(sz, weights[side], stack, held[side], (None, j))
+
+
+def fixed_copies(sz, meta, which, over, held, outs, sem):
+    copies = []
+    for side, spot in ((0, sz.rows), (1, sz.sends)):
+        seen = [meta[spot + j] for r, h, j in sz.couplings() if r in over]
+        for r, h, j in sz.couplings():
+            if r in which:
+                i = meta[spot + j]
+                fresh = jnp.bool_(True)
+                for other in seen:
+                    fresh = jnp.logical_and(fresh, other != i)
+                seen.append(i)
+                copy = pltpu.make_async_copy(
+                    held[side].at[j], outs[side].at[:, i], sem.at[side, j]
+                )
+                copies.append((fresh, copy))
     return copies
 
 
-def run_copies(copies):
-    for fresh, copy in copies:
-        pl.when(fresh)(copy.start)
-
-
-def end_copies(copies):
-    for fresh, copy in copies:
-        pl.when(fresh)(copy.wait)
-
-
 def early_kernel(sz, which, low, *refs):
-    meta, across, psel, qsel, ahead, back = refs[:6]
-    got, refs = dict(zip(which, refs[6 : 6 + len(which)])), refs[6 + len(which) :]
-    forward, adjoint = refs[:3], refs[3:6]
-    before_out, before_grad = refs[6:8]
-    pacc, qacc, out4, grad4, held_out, held_grad, sem, sem_base = refs[11:]
-    part = pl.ds(low, before_out.shape[1])
+    meta_in, across, psel, qsel = refs[:4]
+    got, refs = dict(zip(which, refs[4 : 4 + len(which)])), refs[4 + len(which) :]
+    weights, fields, high = refs[:2], refs[2:8], refs[8:10]
+    pacc, qacc, held_out, held_grad, out4, grad4, meta, sem, sem_base = refs[13:]
+    part = pl.ds(low, high[0].shape[1])
     base = [
-        pltpu.make_async_copy(before_out, out4.at[:, part], sem_base.at[0]),
-        pltpu.make_async_copy(before_grad, grad4.at[:, part], sem_base.at[1]),
+        pltpu.make_async_copy(high[0], out4.at[:, part], sem_base.at[0]),
+        pltpu.make_async_copy(high[1], grad4.at[:, part], sem_base.at[1]),
     ]
     for copy in base:
         copy.start()
-    add_coupled(sz, 2.0, meta, got, across, psel, qsel, pacc, qacc, which)
-    held, outs = (held_out, held_grad), (out4, grad4)
-    copies = fixed_blocks(
-        sz, meta, which, ahead, back, forward, adjoint, pacc, qacc, held, outs, sem
-    )
+    add_coupled(sz, 2.0, (meta_in, meta, sem), got, across, psel, qsel, pacc, qacc, which)
+    fixed_blocks(sz, meta, which, weights, fields, (pacc, qacc), (held_out, held_grad))
     for copy in base:
         copy.wait()
-    run_copies(copies)
-    end_copies(copies)
-
-
-def fix_kernel(sz, axis, which, *refs):
-    meta, across, psel, qsel, ahead, back = refs[:6]
-    got, refs = dict(zip(which, refs[6 : 6 + len(which)])), refs[6 + len(which) :]
-    forward, adjoint = refs[:3], refs[3:6]
-    mine, theirs = refs[6:8]
-    out4, grad4, grad_w, pacc, qacc, held_out, held_grad, sem = refs[10:]
-    add_coupled(sz, 2.0, meta, got, across, psel, qsel, pacc, qacc, which)
+
+
+def early_outputs(sz, low, meta, across, picked, got, which, weights, fields, high, token, outs):
+    args = [meta, across, *picked, *(got[r] for r in which), *weights, *fields, *high, token]
+    whole = [shape(out.shape, BF16) for out in outs]
+    held = shape((sz.pairs, sz.chan // SUB, SUB, sz.blk), BF16)
+    return call(
+        functools.partial(early_kernel, sz, which, low),
+        [VMEM] * len(args) + [HBM] * 2,
+        [VMEM] * 4 + [HBM] * 2,
+        [sz.picked, sz.picked, held, held] + whole,
+        table_copy(sz) + [pltpu.SemaphoreType.DMA((2,))],
+        8 * sz.pairs * sz.chan * sz.blk * sz.blk,
+        4 << 20,
+        8,
+        {len(args): 4, len(args) + 1: 5},
+    )(*args, *outs)
+
+
+def fix_kernel(sz, axis, early, late, *refs):
+    meta_in, across, psel, qsel = refs[:4]
+    got, refs = dict(zip(late, refs[4 : 4 + len(late)])), refs[4 + len(late) :]
+    weights, fields, fixed = refs[:2], refs[2:8], refs[8:10]
+    mine, theirs = refs[10:12]
+    out4, grad4, grad_w, pacc, qacc, held_out, held_grad, total, meta, sem, sem_out, sem_w = refs[14:]
     held, outs = (held_out, held_grad), (out4, grad4)
-    copies = fixed_blocks(
-        sz, meta, which, ahead, back, forward, adjoint, pacc, qacc, held, outs, sem
-    )
-    run_copies(copies)
     odd = lax.rem(lax.axis_index(axis), 2) == 1
     top = jnp.where(odd, theirs[...], mine[...])
     low = jnp.where(odd, mine[...], theirs[...])
     zeroth, first = top[:, : sz.chan], low[:, : sz.chan]
-    grad_w[0] = zeroth
-    grad_w[1] = first
-    grad_w[2] = 2.0 * low[:, sz.chan :] - zeroth
-    grad_w[3] = 2.0 * top[:, sz.chan :] - first
-    end_copies(copies)
-
-
-def fix_outputs(sz, kernel, meta, across, picked, weights, got, which, fields, rest, token, outs, limit):
-    late = [got[r] for r in which]
-    args = [meta, across, *picked, *weights, *late, *fields, *rest, *token]
+    total[0] = zeroth
+    total[1] = first
+    total[2] = 2.0 * low[:, sz.chan :] - zeroth
+    total[3] = 2.0 * top[:, sz.chan :] - first
+    weight_copy = pltpu.make_async_copy(total, grad_w, sem_w)
+    weight_copy.start()
+    add_coupled(sz, 2.0, (meta_in, meta, sem), got, across, psel, qsel, pacc, qacc, late)
+    copies = fixed_copies(sz, meta, early, late, fixed, outs, sem_out)
+    for fresh, copy in copies:
+        pl.when(fresh)(copy.start)
+    fixed_blocks(sz, meta, late, weights, fields, (pacc, qacc), held)
+    last = fixed_copies(sz, meta, late, [], held, outs, sem_out)
+    for fresh, copy in last:
+        pl.when(fresh)(copy.start)
+    for fresh, copy in copies + last:
+        pl.when(fresh)(copy.wait)
+    weight_copy.wait()
+
+
+def fix_outputs(
+    sz, axis, meta, across, picked, got, early, late, weights, fields, fixed, mine, theirs, outs
+):
+    args = [meta, across, *picked, *(got[r] for r in late), *weights, *fields, *fixed]
+    args += [mine, theirs]
     whole = [shape(out.shape, BF16) for out in outs]
     held = pltpu.VMEM((sz.pairs, sz.chan // SUB, SUB, sz.blk), BF16)
-    scratch = [held, held, pltpu.SemaphoreType.DMA((2, sz.pairs))]
-    if token:
-        results = [sz.picked, sz.picked] + whole
-        specs, at = [VMEM] * 2 + [HBM] * 2, 2
-        scratch.append(pltpu.SemaphoreType.DMA((2,)))
-    else:
-        results = whole + [shape((4, sz.chan, sz.chan), F32)]
-        specs, at = [HBM] * 2 + [VMEM], 0
-        scratch = [pltpu.VMEM(sz.picked.shape, F32)] * 2 + scratch
+    total = (4, sz.chan, sz.chan)
     return call(
-        kernel,
-        [SMEM] + [VMEM] * (len(args) - 1) + [HBM] * 2,
-        specs,
-        results,
-        scratch,
-        8 * sz.pairs * sz.chan * sz.blk * sz.blk,
-        4 << 20,
-        limit,
-        {len(args): at, len(args) + 1: at + 1},
+        functools.partial(fix_kernel, sz, axis, early, late),
+        [VMEM] * len(args) + [HBM] * 2,
+        [HBM] * 3,
+        whole + [shape(total, F32)],
+        [pltpu.VMEM(sz.picked.shape, F32)] * 2
+        + [held, held, pltpu.VMEM(total, F32)]
+        + table_copy(sz)
+        + [pltpu.SemaphoreType.DMA((2, sz.pairs)), pltpu.SemaphoreType.DMA],
+        8 * len(late) * sz.hb * sz.chan * sz.blk * sz.blk,
+        2 << 20,
+        8,
+        {len(args): 0, len(args) + 1: 1},
     )(*args, *outs)
 
 
@@ -678,7 +741,7 @@
 
     got = [from_partner(pay, bit) for bit, pay in enumerate(pays)]
     fields = (t1, s1, t0, s0)
-    *base, psel, qsel, gram = local_products(sz, meta, col, tiles, turned, fields, cross, True)
+    *base, psel, qsel, gram = local_products(sz, meta, col, tiles, turned, fields)
     *picked, mine, given = correct(
         sz, "dom", meta, across, (psel, qsel), got, gram0, gram, s1
     )
@@ -687,34 +750,33 @@
 
     state = {}
 
-    def window_products(token):
+    middle = sz.blocks // (2 * ROWS) * ROWS
+
+    def window_early_rows(token):
         fields = (t2, s2, t1, s1)
-        *state["base"], token = local_products(sz, meta, col, tiles, turned, fields, token, False)
-        return token
-
-    middle = sz.blocks // (2 * ROWS) * ROWS
-    orders = cheb_weight.shape[0]
-
-    def window_low(token):
-        forward, adjoint = (t0, t1, t2, state["base"][0]), (s0, s1, s2, state["base"][1])
-        *state["weights"], left, right = base_outputs(
-            sz, 0, middle, forward, adjoint, [cheb_weight], token, orders
+        state["part"] = part_products(sz, meta, col, tiles, turned, fields, None, token)
+        return None
+
+    def window_late_rows(token):
+        fields = (t2, s2, t1, s1)
+        t3, _, _, s3, *state["picked"] = part_products(
+            sz, meta, col, tiles, turned, fields, state["part"], token
         )
-        state["low"] = [left, right]
-        return state["weights"][0]
-
-    def window_high(token):
-        forward, adjoint = (t0, t1, t2, state["base"][0]), (s0, s1, s2, state["base"][1])
-        rest = state["weights"] + state["low"]
-        left, right, out4, grad4 = base_outputs(
-            sz, middle, sz.blocks, forward, adjoint, rest, token, orders
+        state["last"] = (t3, s3)
+        return state["picked"][0]
+
+    def window_outputs(token):
+        t3, s3 = state["last"]
+        *state["weights"], left, right, out4, grad4 = base_outputs(
+            sz, middle, (t0, t1, t2, t3), (s0, s1, s2, s3), cheb_weight, token
         )
         state["high"], state["outs"] = [left, right], [out4, grad4]
-        return left
-
-    windows = [window_products, window_low, window_high]
+        return state["weights"][0]
+
+    windows = [window_early_rows, window_late_rows, window_outputs]
     bits = list(reversed(range(1, (lax.axis_size("dom") - 1).bit_length())))
     pays, got = list(pays), [None] * sz.rounds
+    history = (t0, t1, t2, s0, s1, s2)
     got[0] = from_partner(pays[0], 0)
     early = [0] + [bit for bit in bits[:-1] if bit < sz.rounds]
     late = [bit for bit in everyone if bit not in early]
@@ -730,24 +792,23 @@
             token = windows[at](token)
         last = at + 1 == len(bits)
         if last:
-            *picked, out4, grad4 = fix_outputs(
+            *picked, left, right, out4, grad4 = early_outputs(
                 sz,
-                functools.partial(early_kernel, sz, early, middle),
+                middle,
                 meta,
                 across,
-                state["base"][2:4],
-                state["weights"],
+                state["picked"],
                 got,
                 early,
-                (t0, t1, t2, s0, s1, s2),
+                state["weights"],
+                history,
                 state["high"],
-                [token],
+                token,
                 state["outs"],
-                10,
             )
             token = picked[0]
         gated = not last and bits[at + 1] < sz.rounds
-        after = [token] + held
+        after = ([] if token is None else [token]) + held
         held = [got[bit]] if bit < sz.rounds else []
         if last:
             (mine,) = add(mine, theirs, None, after, True)
@@ -756,18 +817,19 @@
     theirs = from_partner(mine, 0)
     out4, grad4, grad_w = fix_outputs(
         sz,
-        functools.partial(fix_kernel, sz, "dom", late),
+        "dom",
         meta,
         across,
         picked,
+        got,
+        early,
+        late,
         state["weights"],
-        got,
-        late,
-        (t0, t1, t2, s0, s1, s2),
-        [mine, theirs],
-        [],
+        history,
+        [left, right],
+        mine,
+        theirs,
         [out4, grad4],
-        10,
     )
     conv_out = out4.transpose(0, 2, 1, 3).reshape(features.shape)
     grad_x = grad4.transpose(0, 2, 1, 3).reshape(features.shape)

time: 54.6 us -> 50.6 us (0.927)
  waiting for transfers between devices: 6.63 us -> 4.63 us
  Pallas kernels: 25 us -> 23.1 us
    ppermute x21, waiting for transfers between devices: 6.63 us -> 4.63 us  [from_partner(): return lax.ppermute(values, 'dom', route)]
    pallas_call x9, Pallas kernels: 17.6 us -> 15.7 us  [the longest x1 4.5 us: local_products(): call(functools.partial(local_kernel, sz), [VMEM] * 8, [VMEM] * 5, [sz.fie...]
  transfers between devices with their start and end apart: 21 -> 21, of which waited for: 5 -> 5; matrix products, arithmetic and copies ran while one was open for 0% -> 0% of each run, Pallas kernels for 33% -> 34%
where the time goes in v7:
time: 50.6 us; the launch traced here: 50.5 us
  Pallas kernels  23.1 us (46%)
  starting transfers between devices  21.2 us (42%)
  waiting for transfers between devices  4.63 us (9%)
  between operations  1.52 us (3%)
    ppermute x21, starting transfers between devices, from_partner(): return lax.ppermute(values, 'dom', route)  21.2 us
    ppermute x21, waiting for transfers between devices, from_partner(): return lax.ppermute(values, 'dom', route)  4.63 us
    pallas_call x1, Pallas kernels, first_products(): call(functools.partial(first_kernel, sz), [VMEM, VMEM, HBM, VMEM, VMEM],...  4.59 us
    pallas_call x1, Pallas kernels, local_products(): call(functools.partial(local_kernel, sz), [VMEM] * 8, [VMEM] * 5, [sz.fie...  4.5 us
    pallas_call x2, Pallas kernels, part_products(): call(functools.partial(early_rows_kernel if before is None else late_rows...  3.91 us
    pallas_call x1, Pallas kernels, pack(): call(functools.partial(pack_kernel, sz), [HBM] * 6 + [SMEM, HBM], [VMEM]...  2.8 us
    pallas_call x1, Pallas kernels, base_outputs(): call(functools.partial(output_kernel, sz, middle), [VMEM] * len(args), [V...  2.09 us
    pallas_call x2, Pallas kernels, join(): call(functools.partial(start_kernel if first else join_kernel, sz), [VMEM...  1.7 us
  transfers between devices with their start and end apart: 21, of which 5 were waited for; matrix products, arithmetic and copies ran while one was open for 0% of the time, Pallas kernels for 34%

profile of v7, /device:TPU:0, one launch (start us, length us, event | category | flops | bytes accessed | tf_op | source)
XLA Modules:
  0.0 50.5 jit_solution(2821972260044097000)
XLA Ops:
  1.3 2.8 %shard_map.121 = (bf16[64,64,128]{2,1,0:T(8,128)(2,1)S(1)}, bf16[64,64,128]{2,1,0:T(8,128)(2,1)S(1)}, bf16[10,128,128]{2,1,0:T(8,128)(2,1)S(1)}, bf16[10,128,128...) custom-call(bf16[8,64,8,128]{3,2,1,0:T(8,128)(2,1)} %bitcast.18, ...), custom_call_target="tpu_custom_call" | custom-call | flops 1000 | bytes 4194304 | tf_op jit(solution)/shard_map/pallas_call | solution.py:143
  4.1 0.8 %collective-permute-start = (bf16[256,128]{1,0:T(8,128)(2,1)S(1)}, bf16[256,128]{1,0:T(8,128)(2,1)S(1)}, u32[]{:S(2)}, u32[]{:S(2)}) collective-permute-start(bf16[256,128]{1,0:T(8,128)(2,1)S(1)} %get-tuple-element.90), channel_id=1, source_target_pairs={{0,1},{1,0},{2,3},{3,2},{4,5},{5,4},{6,7},{7,6},{8,9},{9,8},{10,11... | collective-permute-start | bytes 196616 | tf_op jit(solution)/shard_map/ppermute | solution.py:713
  4.9 2.3 %collective-permute-start.1 = (bf16[256,128]{1,0:T(8,128)(2,1)S(1)}, bf16[256,128]{1,0:T(8,128)(2,1)S(1)}, u32[]{:S(2)}, u32[]{:S(2)}) collective-permute-start(bf16[256,128]{1,0:T(8,128)(2,1)S(1)} %get-tuple-element.91), channel_id=1, source_target_pairs={{0,2},{2,0},{1,3},{3,1},{4,6},{6,4},{5,7},{7,5},{8,10},{10,8},{9,1... | collective-permute-start | bytes 196616 | tf_op jit(solution)/shard_map/ppermute | solution.py:713
  7.2 1.7 %collective-permute-start.2 = (bf16[256,128]{1,0:T(8,128)(2,1)S(1)}, bf16[256,128]{1,0:T(8,128)(2,1)S(1)}, u32[]{:S(2)}, u32[]{:S(2)}) collective-permute-start(bf16[256,128]{1,0:T(8,128)(2,1)S(1)} %get-tuple-element.92), channel_id=1, source_target_pairs={{0,4},{4,0},{1,5},{5,1},{2,6},{6,2},{3,7},{7,3},{8,12},{12,8},{9,1... | collective-permute-start | bytes 196616 | tf_op jit(solution)/shard_map/ppermute | solution.py:713
  8.9 1.3 %collective-permute-start.3 = (bf16[256,128]{1,0:T(8,128)(2,1)S(1)}, bf16[256,128]{1,0:T(8,128)(2,1)S(1)}, u32[]{:S(2)}, u32[]{:S(2)}) collective-permute-start(bf16[256,128]{1,0:T(8,128)(2,1)S(1)} %get-tuple-element.93), channel_id=1, source_target_pairs={{0,8},{8,0},{1,9},{9,1},{2,10},{10,2},{3,11},{11,3},{4,12},{12,4},... | collective-permute-start | bytes 196616 | tf_op jit(solution)/shard_map/ppermute | solution.py:713
  10.1 2.6 %collective-permute-start.4 = (bf16[256,128]{1,0:T(8,128)(2,1)S(1)}, bf16[256,128]{1,0:T(8,128)(2,1)S(1)}, u32[]{:S(2)}, u32[]{:S(2)}) collective-permute-start(bf16[256,128]{1,0:T(8,128)(2,1)S(1)} %get-tuple-element.94), channel_id=1, source_target_pairs={{0,16},{16,0},{1,17},{17,1},{2,18},{18,2},{3,19},{19,3},{4,20},{20... | collective-permute-start | bytes 196616 | tf_op jit(solution)/shard_map/ppermute | solution.py:713
  12.7 4.6 %shard_map.122 = (bf16[64,64,128]{2,1,0:T(8,128)(2,1)S(1)}, bf16[64,64,128]{2,1,0:T(8,128)(2,1)S(1)}, f32[10,64,128]{2,1,0:T(8,128)S(1)}, f32[10,64,128]{2,1,0:T...) custom-call(s32[46]{0:T(128)S(1)} %get-tuple-element.78.refs_0_, ...), custom_call_target="tpu_custom_call" | custom-call | flops 805306368 | bytes 12582912 | tf_op jit(solution)/shard_map/pallas_call | solution.py:265
  17.3 0.0 collective-permute-done.refs_7_
  17.3 0.0 collective-permute-done.1.refs_8_
  17.4 0.0 collective-permute-done.2.refs_9_
  17.4 0.0 collective-permute-done.3.refs_10_
  17.4 0.9 %shard_map.123 = (bf16[64,64,128]{2,1,0:T(8,128)(2,1)S(1)}, bf16[64,64,128]{2,1,0:T(8,128)(2,1)S(1)}, bf16[256,128]{1,0:T(8,128)(2,1)S(1)}, bf16[256,128]{1,0:T(...) custom-call(s32[46]{0:T(128)S(1)} %get-tuple-element.78.refs_0_, ...), custom_call_target="tpu_custom_call", output_to_operand_aliasing={{0}: (2, {}), {1}: (3, {})} | custom-call | flops 20971520 | bytes 5242880 | tf_op jit(solution)/shard_map/pallas_call | solution.py:485
  18.3 0.1 collective-permute-start.5
  18.4 0.7 %collective-permute-start.6 = (bf16[256,128]{1,0:T(8,128)(2,1)S(1)}, bf16[256,128]{1,0:T(8,128)(2,1)S(1)}, u32[]{:S(2)}, u32[]{:S(2)}) collective-permute-start(bf16[256,128]{1,0:T(8,128)(2,1)S(1)} %get-tuple-element.104), channel_id=1, source_target_pairs={{0,2},{2,0},{1,3},{3,1},{4,6},{6,4},{5,7},{7,5},{8,10},{10,8},{9,1... | collective-permute-start | bytes 196616 | tf_op jit(solution)/shard_map/ppermute | solution.py:713
  19.1 1.2 %collective-permute-start.7 = (bf16[256,128]{1,0:T(8,128)(2,1)S(1)}, bf16[256,128]{1,0:T(8,128)(2,1)S(1)}, u32[]{:S(2)}, u32[]{:S(2)}) collective-permute-start(bf16[256,128]{1,0:T(8,128)(2,1)S(1)} %get-tuple-element.105), channel_id=1, source_target_pairs={{0,4},{4,0},{1,5},{5,1},{2,6},{6,2},{3,7},{7,3},{8,12},{12,8},{9,1... | collective-permute-start | bytes 196616 | tf_op jit(solution)/shard_map/ppermute | solution.py:713
  20.3 0.4 collective-permute-start.8
  20.8 0.2 collective-permute-start.9
  20.9 4.5 %shard_map.124 = (bf16[64,64,128]{2,1,0:T(8,128)(2,1)S(1)}, bf16[64,64,128]{2,1,0:T(8,128)(2,1)S(1)}, f32[10,64,128]{2,1,0:T(8,128)S(1)}, f32[10,64,128]{2,1,0:T(8,128)S(1)}, f32[128,128]{1,0:T(8,128)S(1)}) custom-call(s32[46]{0:T(128)S(1)} %get-tuple-element.78.refs_0_, s32[3,64]{1,0:T(4,128)S(1)} %get-tuple-element.80.refs_1_, ...), custom_call_target="tpu_custom_call" | custom-call | flops 805306368 | bytes 12582912 | tf_op jit(solution)/shard_map/pallas_call | solution.py:339
  25.4 0.0 collective-permute-done.5.refs_7_
  25.5 0.0 collective-permute-done.6.refs_8_
  25.5 0.0 collective-permute-done.8.refs_10_
  25.5 1.7 %collective-permute-done.9.refs_11_ = bf16[256,128]{1,0:T(8,128)(2,1)S(1)} collective-permute-done((bf16[256,128]{1,0:T(8,128)(2,1)S(1)}, bf16[256,128]{1,0:T(8,128)(2,1)S(1)}, u32[]{:S(2)}, u32[]{:S(2)}) %collective-permute-start.9) | collective-permute-done | bytes 65568 | tf_op jit(solution)/shard_map/ppermute | solution.py:713
  27.2 0.9 %shard_map.125 = (f32[10,64,128]{2,1,0:T(8,128)S(1)}, f32[10,64,128]{2,1,0:T(8,128)S(1)}, f32[64,128]{1,0:T(8,128)S(1)}, f32[64,128]{1,0:T(8,128)S(1)}) custom-call(s32[46]{0:T(128)S(1)} %get-tuple-element.78.refs_0_, bf16[10,128,128]{2,1,0:T(8,128)(2,1)S(1)} %get-tuple-element.79.refs_4_.refs_1_, f32[10,64,128]{2,1,0:T(8,128)S(1)} %get-tuple-element.99.refs_2_, ...), custom_call_target="tpu_custom_call" | custom-call | flops 41943040 | bytes 3145728 | tf_op jit(solution)/shard_map/pallas_call | solution.py:448
  28.1 0.1 collective-permute-start.10
  28.2 0.8 %shard_map.126 = (bf16[64,64,128]{2,1,0:T(8,128)(2,1)S(1)}, bf16[64,64,128]{2,1,0:T(8,128)(2,1)S(1)}, bf16[256,128]{1,0:T(8,128)(2,1)S(1)}, bf16[256,128]{1,0:T(...) custom-call(s32[46]{0:T(128)S(1)} %get-tuple-element.78.refs_0_, ...), custom_call_target="tpu_custom_call", output_to_operand_aliasing={{0}: (2, {}), {1}: (3, {})} | custom-call | flops 20971520 | bytes 5242880 | tf_op jit(solution)/shard_map/pallas_call | solution.py:485
  29.0 0.6 %collective-permute-start.12 = (bf16[256,128]{1,0:T(8,128)(2,1)S(1)}, bf16[256,128]{1,0:T(8,128)(2,1)S(1)}, u32[]{:S(2)}, u32[]{:S(2)}) collective-permute-start(bf16[256,128]{1,0:T(8,128)(2,1)S(1)} %get-tuple-element.121), channel_id=1, source_target_pairs={{0,1},{1,0},{2,3},{3,2},{4,5},{5,4},{6,7},{7,6},{8,9},{9,8},{10,11... | collective-permute-start | bytes 196616 | tf_op jit(solution)/shard_map/ppermute | solution.py:713
  29.6 0.0 collective-permute-done.10.refs_1_
  29.6 2.2 %collective-permute-start.11 = (f32[64,128]{1,0:T(8,128)S(1)}, f32[64,128]{1,0:T(8,128)S(1)}, u32[]{:S(2)}, u32[]{:S(2)}) collective-permute-start(f32[64,128]{1,0:T(8,128)S(1)} %get-tuple-element.119.refs_0_), channel_id=1, source_target_pairs={{0,16},{16,0},{1,17},{17,1},{2,18},{18,2},{3,19},{19,3},{4,20},{20... | collective-permute-start | bytes 98312 | tf_op jit(solution)/shard_map/ppermute | solution.py:713
  31.8 0.8 %collective-permute-start.13 = (bf16[256,128]{1,0:T(8,128)(2,1)S(1)}, bf16[256,128]{1,0:T(8,128)(2,1)S(1)}, u32[]{:S(2)}, u32[]{:S(2)}) collective-permute-start(bf16[256,128]{1,0:T(8,128)(2,1)S(1)} %get-tuple-element.125), channel_id=1, source_target_pairs={{0,16},{16,0},{1,17},{17,1},{2,18},{18,2},{3,19},{19,3},{4,20},{20... | collective-permute-start | bytes 196616 | tf_op jit(solution)/shard_map/ppermute | solution.py:713
  32.6 2.1 %shard_map.128 = (bf16[64,64,128]{2,1,0:T(8,128)(2,1)S(1)}, f32[64,64,128]{2,1,0:T(8,128)S(1)}, f32[64,64,128]{2,1,0:T(8,128)S(1)}) custom-call(s32[46]{0:T(128)S(1)} %get-tuple-element.78.refs_0_, s32[3,64]{1,0:T(4,128)S(1)} %get-tuple-element.80.refs_1_, bf16[64,3,128,128]{3,2,1,0:T(8,128)(2,1)S(1)} %get-tuple-element.83.refs_2_, ...), custom_call_target="tpu_custom_call" | custom-call | flops 402653184 | bytes 6291456 | tf_op jit(solution)/shard_map/pallas_call | solution.py:390
  34.7 0.0 collective-permute-done.12.refs_3_.refs_4_
  34.7 0.0 collective-permute-done.11.refs_1_
  34.8 2.0 %collective-permute-start.15 = (f32[64,128]{1,0:T(8,128)S(1)}, f32[64,128]{1,0:T(8,128)S(1)}, u32[]{:S(2)}, u32[]{:S(2)}) collective-permute-start(f32[64,128]{1,0:T(8,128)S(1)} %get-tuple-element.127.refs_0_), channel_id=1, source_target_pairs={{0,8},{8,0},{1,9},{9,1},{2,10},{10,2},{3,11},{11,3},{4,12},{12,4},... | collective-permute-start | bytes 98312 | tf_op jit(solution)/shard_map/ppermute | solution.py:713
  36.8 0.1 collective-permute-start.14
  36.9 1.8 %shard_map.130 = (bf16[64,64,128]{2,1,0:T(8,128)(2,1)S(1)}, f32[64,64,128]{2,1,0:T(8,128)S(1)}, f32[64,64,128]{2,1,0:T(8,128)S(1)}, bf16[64,64,128]{2,1,0:T(8,12...) custom-call(s32[46]{0:T(128)S(1)} %get-tuple-element.78.refs_0_, ...), custom_call_target="tpu_custom_call", output_to_operand_aliasing={{0}: (8, {}), {1}: (9, {}), {2}: (10, {})} | custom-call | flops 402653184 | bytes 6291456 | tf_op jit(solution)/shard_map/pallas_call | solution.py:390
  38.6 0.3 collective-permute-done.15.refs_1_
  39.0 2.0 %collective-permute-start.17 = (f32[64,128]{1,0:T(8,128)S(1)}, f32[64,128]{1,0:T(8,128)S(1)}, u32[]{:S(2)}, u32[]{:S(2)}) collective-permute-start(f32[64,128]{1,0:T(8,128)S(1)} %get-tuple-element.137.refs_0_), channel_id=1, source_target_pairs={{0,4},{4,0},{1,5},{5,1},{2,6},{6,2},{3,7},{7,3},{8,12},{12,8},{9,1... | collective-permute-start | bytes 98312 | tf_op jit(solution)/shard_map/ppermute | solution.py:713
  41.0 0.1 collective-permute-start.16
  41.1 2.1 %shard_map.132 = (bf16[64,256]{1,0:T(8,128)(2,1)S(1)}, bf16[64,256]{1,0:T(8,128)(2,1)S(1)}, bf16[8,32,8,128]{3,2,1,0:T(8,128)(2,1)S(1)}, bf16[8,32,8,128]{3,2,1,...) custom-call(bf16[64,64,128]{2,1,0:T(8,128)(2,1)S(1)} %get-tuple-element.81.refs_3_.refs_6_.refs_0_.ref, ...), custom_call_target="tpu_custom_call" | custom-call | flops 536870912 | bytes 6291456 | tf_op jit(solution)/shard_map/pallas_call | solution.py:548
  43.2 0.0 collective-permute-done.17.refs_1_
  43.2 1.5 %collective-permute-start.19 = (f32[64,128]{1,0:T(8,128)S(1)}, f32[64,128]{1,0:T(8,128)S(1)}, u32[]{:S(2)}, u32[]{:S(2)}) collective-permute-start(f32[64,128]{1,0:T(8,128)S(1)} %get-tuple-element.147.refs_0_), channel_id=1, source_target_pairs={{0,2},{2,0},{1,3},{3,1},{4,6},{6,4},{5,7},{7,5},{8,10},{10,8},{9,1... | collective-permute-start | bytes 98312 | tf_op jit(solution)/shard_map/ppermute | solution.py:713
  44.7 0.6 %collective-permute-start.18 = (bf16[256,128]{1,0:T(8,128)(2,1)S(1)}, bf16[256,128]{1,0:T(8,128)(2,1)S(1)}, u32[]{:S(2)}, u32[]{:S(2)}) collective-permute-start(bf16[256,128]{1,0:T(8,128)(2,1)S(1)} %get-tuple-element.144), channel_id=1, source_target_pairs={{0,2},{2,0},{1,3},{3,1},{4,6},{6,4},{5,7},{7,5},{8,10},{10,8},{9,1... | collective-permute-start | bytes 196616 | tf_op jit(solution)/shard_map/ppermute | solution.py:713
  45.3 0.0 collective-permute-done.16.refs_7_.refs_3_
  45.3 1.0 %shard_map.134 = (f32[10,64,128]{2,1,0:T(8,128)S(1)}, f32[10,64,128]{2,1,0:T(8,128)S(1)}, bf16[10,8,8,128]{3,2,1,0:T(8,128)(2,1)S(1)}, bf16[10,8,8,128]{3,2,1,0:...) custom-call(s32[46]{0:T(128)S(1)} %get-tuple-element.78.refs_0_, ...), custom_call_target="tpu_custom_call", output_to_operand_aliasing={{4}: (19, {}), {5}: (20, {})} | custom-call | flops 83886080 | bytes 4194304 | tf_op jit(solution)/shard_map/pallas_call | solution.py:610
  46.3 0.9 %collective-permute-done.19.refs_1_ = f32[64,128]{1,0:T(8,128)S(1)} collective-permute-done((f32[64,128]{1,0:T(8,128)S(1)}, f32[64,128]{1,0:T(8,128)S(1)}, u32[]{:S(2)}, u32[]{:S(2)}) %collective-permute-start.19) | collective-permute-done | bytes 32800 | tf_op jit(solution)/shard_map/ppermute | solution.py:713
  47.2 1.2 %collective-permute-done.20.refs_16_ = f32[64,128]{1,0:T(8,128)S(1)} collective-permute-done((f32[64,128]{1,0:T(8,128)S(1)}, f32[64,128]{1,0:T(8,128)S(1)}, u32[]{:S(2)}, u32[]{:S(2)}) %collective-permute-start.20) | collective-permute-done | bytes 32800 | tf_op jit(solution)/shard_map/ppermute | solution.py:713
  48.4 0.5 %collective-permute-done.18.refs_4_ = bf16[256,128]{1,0:T(8,128)(2,1)S(1)} collective-permute-done((bf16[256,128]{1,0:T(8,128)(2,1)S(1)}, bf16[256,128]{1,0:T(8,128)(2,1)S(1)}, u32[]{:S(2)}, u32[]{:S(2)}) %collective-permute-start.18) | collective-permute-done | bytes 65568 | tf_op jit(solution)/shard_map/ppermute | solution.py:713
  48.9 1.6 %shard_map.136 = (bf16[8,64,8,128]{3,2,1,0:T(8,128)(2,1)}, bf16[8,64,8,128]{3,2,1,0:T(8,128)(2,1)}, f32[4,64,64]{2,1,0:T(8,128)}) custom-call(s32[46]{0:T(128)S(1)} %get-tuple-element.78.refs_0_, bf16[10,128,128]{2,1,0:T(8,128)(2,1)S(1)} %get-tuple-element.79.refs_4_.refs_1_, ...), custom_call_target="tpu_custom_call", output_to_operand_aliasing={{0}: (17, {}), {1}: (18, {})} | custom-call | flops 16777216 | bytes 2097152 | tf_op jit(solution)/shard_map/pallas_call | solution.py:661
  (12 shorter events, 0.1 us)
Async XLA Ops:
  4.1 13.3 %collective-permute-start = (bf16[256,128]{1,0:T(8,128)(2,1)S(1)}, bf16[256,128]{1,0:T(8,128)(2,1)S(1)}, u32[]{:S(2)}, u32[]{:S(2)}) collective-permute-start(bf16[256,128]{1,0:T(8,128)(2,1)S(1)} %get-tuple-element.90), channel_id=1, source_target_pairs={{0,1},{1,0},{2,3},{3,2},{4,5},{5,4},{6,7},{7,6},{8,9},{9,8},{10,11... | collective-permute-start | bytes 196616 | tf_op jit(solution)/shard_map/ppermute | solution.py:713
  4.9 12.5 %collective-permute-start.1 = (bf16[256,128]{1,0:T(8,128)(2,1)S(1)}, bf16[256,128]{1,0:T(8,128)(2,1)S(1)}, u32[]{:S(2)}, u32[]{:S(2)}) collective-permute-start(bf16[256,128]{1,0:T(8,128)(2,1)S(1)} %get-tuple-element.91), channel_id=1, source_target_pairs={{0,2},{2,0},{1,3},{3,1},{4,6},{6,4},{5,7},{7,5},{8,10},{10,8},{9,1... | collective-permute-start | bytes 196616 | tf_op jit(solution)/shard_map/ppermute | solution.py:713
  7.2 10.2 %collective-permute-start.2 = (bf16[256,128]{1,0:T(8,128)(2,1)S(1)}, bf16[256,128]{1,0:T(8,128)(2,1)S(1)}, u32[]{:S(2)}, u32[]{:S(2)}) collective-permute-start(bf16[256,128]{1,0:T(8,128)(2,1)S(1)} %get-tuple-element.92), channel_id=1, source_target_pairs={{0,4},{4,0},{1,5},{5,1},{2,6},{6,2},{3,7},{7,3},{8,12},{12,8},{9,1... | collective-permute-start | bytes 196616 | tf_op jit(solution)/shard_map/ppermute | solution.py:713
  8.9 8.5 %collective-permute-start.3 = (bf16[256,128]{1,0:T(8,128)(2,1)S(1)}, bf16[256,128]{1,0:T(8,128)(2,1)S(1)}, u32[]{:S(2)}, u32[]{:S(2)}) collective-permute-start(bf16[256,128]{1,0:T(8,128)(2,1)S(1)} %get-tuple-element.93), channel_id=1, source_target_pairs={{0,8},{8,0},{1,9},{9,1},{2,10},{10,2},{3,11},{11,3},{4,12},{12,4},... | collective-permute-start | bytes 196616 | tf_op jit(solution)/shard_map/ppermute | solution.py:713
  10.1 7.2 %collective-permute-start.4 = (bf16[256,128]{1,0:T(8,128)(2,1)S(1)}, bf16[256,128]{1,0:T(8,128)(2,1)S(1)}, u32[]{:S(2)}, u32[]{:S(2)}) collective-permute-start(bf16[256,128]{1,0:T(8,128)(2,1)S(1)} %get-tuple-element.94), channel_id=1, source_target_pairs={{0,16},{16,0},{1,17},{17,1},{2,18},{18,2},{3,19},{19,3},{4,20},{20... | collective-permute-start | bytes 196616 | tf_op jit(solution)/shard_map/ppermute | solution.py:713
  18.3 7.2 %collective-permute-start.5 = (bf16[256,128]{1,0:T(8,128)(2,1)S(1)}, bf16[256,128]{1,0:T(8,128)(2,1)S(1)}, u32[]{:S(2)}, u32[]{:S(2)}) collective-permute-start(bf16[256,128]{1,0:T(8,128)(2,1)S(1)} %get-tuple-element.103), channel_id=1, source_target_pairs={{0,1},{1,0},{2,3},{3,2},{4,5},{5,4},{6,7},{7,6},{8,9},{9,8},{10,11... | collective-permute-start | bytes 196616 | tf_op jit(solution)/shard_map/ppermute | solution.py:713
  18.4 7.1 %collective-permute-start.6 = (bf16[256,128]{1,0:T(8,128)(2,1)S(1)}, bf16[256,128]{1,0:T(8,128)(2,1)S(1)}, u32[]{:S(2)}, u32[]{:S(2)}) collective-permute-start(bf16[256,128]{1,0:T(8,128)(2,1)S(1)} %get-tuple-element.104), channel_id=1, source_target_pairs={{0,2},{2,0},{1,3},{3,1},{4,6},{6,4},{5,7},{7,5},{8,10},{10,8},{9,1... | collective-permute-start | bytes 196616 | tf_op jit(solution)/shard_map/ppermute | solution.py:713
  19.1 6.4 %collective-permute-start.7 = (bf16[256,128]{1,0:T(8,128)(2,1)S(1)}, bf16[256,128]{1,0:T(8,128)(2,1)S(1)}, u32[]{:S(2)}, u32[]{:S(2)}) collective-permute-start(bf16[256,128]{1,0:T(8,128)(2,1)S(1)} %get-tuple-element.105), channel_id=1, source_target_pairs={{0,4},{4,0},{1,5},{5,1},{2,6},{6,2},{3,7},{7,3},{8,12},{12,8},{9,1... | collective-permute-start | bytes 196616 | tf_op jit(solution)/shard_map/ppermute | solution.py:713
  20.3 5.2 %collective-permute-start.8 = (bf16[256,128]{1,0:T(8,128)(2,1)S(1)}, bf16[256,128]{1,0:T(8,128)(2,1)S(1)}, u32[]{:S(2)}, u32[]{:S(2)}) collective-permute-start(bf16[256,128]{1,0:T(8,128)(2,1)S(1)} %get-tuple-element.106), channel_id=1, source_target_pairs={{0,8},{8,0},{1,9},{9,1},{2,10},{10,2},{3,11},{11,3},{4,12},{12,4},... | collective-permute-start | bytes 196616 | tf_op jit(solution)/shard_map/ppermute | solution.py:713
  20.8 6.4 %collective-permute-start.9 = (bf16[256,128]{1,0:T(8,128)(2,1)S(1)}, bf16[256,128]{1,0:T(8,128)(2,1)S(1)}, u32[]{:S(2)}, u32[]{:S(2)}) collective-permute-start(bf16[256,128]{1,0:T(8,128)(2,1)S(1)} %get-tuple-element.107), channel_id=1, source_target_pairs={{0,16},{16,0},{1,17},{17,1},{2,18},{18,2},{3,19},{19,3},{4,20},{20... | collective-permute-start | bytes 196616 | tf_op jit(solution)/shard_map/ppermute | solution.py:713
  28.1 1.4 %collective-permute-start.10 = (f32[64,128]{1,0:T(8,128)S(1)}, f32[64,128]{1,0:T(8,128)S(1)}, u32[]{:S(2)}, u32[]{:S(2)}) collective-permute-start(f32[64,128]{1,0:T(8,128)S(1)} %get-tuple-element.113), channel_id=1, source_target_pairs={{0,1},{1,0},{2,3},{3,2},{4,5},{5,4},{6,7},{7,6},{8,9},{9,8},{10,11... | collective-permute-start | bytes 98312 | tf_op jit(solution)/shard_map/ppermute | solution.py:713
  29.0 5.7 %collective-permute-start.12 = (bf16[256,128]{1,0:T(8,128)(2,1)S(1)}, bf16[256,128]{1,0:T(8,128)(2,1)S(1)}, u32[]{:S(2)}, u32[]{:S(2)}) collective-permute-start(bf16[256,128]{1,0:T(8,128)(2,1)S(1)} %get-tuple-element.121), channel_id=1, source_target_pairs={{0,1},{1,0},{2,3},{3,2},{4,5},{5,4},{6,7},{7,6},{8,9},{9,8},{10,11... | collective-permute-start | bytes 196616 | tf_op jit(solution)/shard_map/ppermute | solution.py:713
  29.6 5.2 %collective-permute-start.11 = (f32[64,128]{1,0:T(8,128)S(1)}, f32[64,128]{1,0:T(8,128)S(1)}, u32[]{:S(2)}, u32[]{:S(2)}) collective-permute-start(f32[64,128]{1,0:T(8,128)S(1)} %get-tuple-element.119.refs_0_), channel_id=1, source_target_pairs={{0,16},{16,0},{1,17},{17,1},{2,18},{18,2},{3,19},{19,3},{4,20},{20... | collective-permute-start | bytes 98312 | tf_op jit(solution)/shard_map/ppermute | solution.py:713
  31.8 7.1 %collective-permute-start.13 = (bf16[256,128]{1,0:T(8,128)(2,1)S(1)}, bf16[256,128]{1,0:T(8,128)(2,1)S(1)}, u32[]{:S(2)}, u32[]{:S(2)}) collective-permute-start(bf16[256,128]{1,0:T(8,128)(2,1)S(1)} %get-tuple-element.125), channel_id=1, source_target_pairs={{0,16},{16,0},{1,17},{17,1},{2,18},{18,2},{3,19},{19,3},{4,20},{20... | collective-permute-start | bytes 196616 | tf_op jit(solution)/shard_map/ppermute | solution.py:713
  34.8 4.2 %collective-permute-start.15 = (f32[64,128]{1,0:T(8,128)S(1)}, f32[64,128]{1,0:T(8,128)S(1)}, u32[]{:S(2)}, u32[]{:S(2)}) collective-permute-start(f32[64,128]{1,0:T(8,128)S(1)} %get-tuple-element.127.refs_0_), channel_id=1, source_target_pairs={{0,8},{8,0},{1,9},{9,1},{2,10},{10,2},{3,11},{11,3},{4,12},{12,4},... | collective-permute-start | bytes 98312 | tf_op jit(solution)/shard_map/ppermute | solution.py:713
  36.8 6.4 %collective-permute-start.14 = (bf16[256,128]{1,0:T(8,128)(2,1)S(1)}, bf16[256,128]{1,0:T(8,128)(2,1)S(1)}, u32[]{:S(2)}, u32[]{:S(2)}) collective-permute-start(bf16[256,128]{1,0:T(8,128)(2,1)S(1)} %get-tuple-element.126), channel_id=1, source_target_pairs={{0,8},{8,0},{1,9},{9,1},{2,10},{10,2},{3,11},{11,3},{4,12},{12,4},... | collective-permute-start | bytes 196616 | tf_op jit(solution)/shard_map/ppermute | solution.py:713
  36.9 4.2 %copy-start = (bf16[4,64,64]{2,1,0:T(8,128)(2,1)S(1)}, bf16[4,64,64]{2,1,0:T(8,128)(2,1)}, u32[]{:S(2)}) copy-start(bf16[4,64,64]{2,1,0:T(8,128)(2,1)} %refs_8_.1) | copy-start | bytes 98308
  39.0 4.2 %collective-permute-start.17 = (f32[64,128]{1,0:T(8,128)S(1)}, f32[64,128]{1,0:T(8,128)S(1)}, u32[]{:S(2)}, u32[]{:S(2)}) collective-permute-start(f32[64,128]{1,0:T(8,128)S(1)} %get-tuple-element.137.refs_0_), channel_id=1, source_target_pairs={{0,4},{4,0},{1,5},{5,1},{2,6},{6,2},{3,7},{7,3},{8,12},{12,8},{9,1... | collective-permute-start | bytes 98312 | tf_op jit(solution)/shard_map/ppermute | solution.py:713
  41.0 4.3 %collective-permute-start.16 = (bf16[256,128]{1,0:T(8,128)(2,1)S(1)}, bf16[256,128]{1,0:T(8,128)(2,1)S(1)}, u32[]{:S(2)}, u32[]{:S(2)}) collective-permute-start(bf16[256,128]{1,0:T(8,128)(2,1)S(1)} %get-tuple-element.129), channel_id=1, source_target_pairs={{0,4},{4,0},{1,5},{5,1},{2,6},{6,2},{3,7},{7,3},{8,12},{12,8},{9,1... | collective-permute-start | bytes 196616 | tf_op jit(solution)/shard_map/ppermute | solution.py:713
  43.2 4.0 %collective-permute-start.19 = (f32[64,128]{1,0:T(8,128)S(1)}, f32[64,128]{1,0:T(8,128)S(1)}, u32[]{:S(2)}, u32[]{:S(2)}) collective-permute-start(f32[64,128]{1,0:T(8,128)S(1)} %get-tuple-element.147.refs_0_), channel_id=1, source_target_pairs={{0,2},{2,0},{1,3},{3,1},{4,6},{6,4},{5,7},{7,5},{8,10},{10,8},{9,1... | collective-permute-start | bytes 98312 | tf_op jit(solution)/shard_map/ppermute | solution.py:713
  44.7 4.3 %collective-permute-start.18 = (bf16[256,128]{1,0:T(8,128)(2,1)S(1)}, bf16[256,128]{1,0:T(8,128)(2,1)S(1)}, u32[]{:S(2)}, u32[]{:S(2)}) collective-permute-start(bf16[256,128]{1,0:T(8,128)(2,1)S(1)} %get-tuple-element.144), channel_id=1, source_target_pairs={{0,2},{2,0},{1,3},{3,1},{4,6},{6,4},{5,7},{7,5},{8,10},{10,8},{9,1... | collective-permute-start | bytes 196616 | tf_op jit(solution)/shard_map/ppermute | solution.py:713
  47.2 1.2 %collective-permute-start.20 = (f32[64,128]{1,0:T(8,128)S(1)}, f32[64,128]{1,0:T(8,128)S(1)}, u32[]{:S(2)}, u32[]{:S(2)}) collective-permute-start(f32[64,128]{1,0:T(8,128)S(1)} %shard_map.135.refs_15_), channel_id=1, source_target_pairs={{0,1},{1,0},{2,3},{3,2},{4,5},{5,4},{6,7},{7,6},{8,9},{9,8},{10,11... | collective-permute-start | bytes 98312 | tf_op jit(solution)/shard_map/ppermute | solution.py:713

commit v8 on v7

--- a/solution.py
+++ b/solution.py
@@ -13,7 +13,8 @@
 SUB = 8
 LANES = 128
 ROWS_FIRST = 8
-ROWS = 16
+ROWS_PART = 16
+ROWS = 32
 
 VMEM = pl.BlockSpec(memory_space=pltpu.VMEM)
 SMEM = pl.BlockSpec(memory_space=pltpu.SMEM)
@@ -165,6 +166,10 @@
     return (count + ROWS - 1) // ROWS
 
 
+def part_steps(count):
+    return (count + ROWS_PART - 1) // ROWS_PART
+
+
 def table_scratch(sz, col):
     return [pltpu.SMEM((sz.meta,), jnp.int32), pltpu.SMEM(col.shape, jnp.int32)]
 
@@ -277,7 +282,7 @@
     )(meta, col, keep(tiles), t0, s0)
 
 
-def row_products(sz, col, low, high, arrays, tnew, held, summed):
+def row_products(sz, col, low, high, rows, arrays, tnew, held, summed):
     tiles, turned, tcur, scur, tprev = arrays
 
     def block_row(i):
@@ -290,8 +295,8 @@
         scatter_terms(sz, summed, cols, nn(scur[i], wide))
 
     def step(g, carry):
-        for u in range(ROWS):
-            block_row(g * ROWS + u)
+        for u in range(rows):
+            block_row(g * rows + u)
         return carry
 
     lax.fori_loop(low, high, step, 0)
@@ -316,7 +321,7 @@
         copy.wait()
     steps = big_steps(meta[sz.live])
     arrays = (tiles, turned, tcur, scur, tprev)
-    row_products(sz, col, 0, steps, arrays, tnew, held, summed)
+    row_products(sz, col, 0, steps, ROWS, arrays, tnew, held, summed)
 
     def adjoint(i):
         return 2.0 * summed[i] - sprev[i].astype(F32)
@@ -357,9 +362,9 @@
     clear_sums(sz, summed)
     for copy in small:
         copy.wait()
-    cut = (3 * big_steps(meta[sz.live])) // 4
+    cut = (3 * part_steps(meta[sz.live])) // 4
     arrays = (tiles, turned, tcur, scur, tprev)
-    row_products(sz, col, 0, cut, arrays, tnew, held, summed)
+    row_products(sz, col, 0, cut, ROWS_PART, arrays, tnew, held, summed)
 
 
 def late_rows_kernel(sz, *refs):
@@ -367,9 +372,9 @@
     tnew, held, summed, snew, psel, qsel, meta, col, sem = refs[12:]
     for copy in start_table(meta_in, col_in, meta, col, sem):
         copy.wait()
-    steps = big_steps(meta[sz.live])
+    steps = part_steps(meta[sz.live])
     arrays = (tiles, turned, tcur, scur, tprev)
-    row_products(sz, col, (3 * steps) // 4, steps, arrays, tnew, held, summed)
+    row_products(sz, col, (3 * steps) // 4, steps, ROWS_PART, arrays, tnew, held, summed)
 
     def adjoint(i):
         return 2.0 * summed[i] - sprev[i].astype(F32)
@@ -791,22 +796,6 @@
         if at < len(windows):
             token = windows[at](token)
         last = at + 1 == len(bits)
-        if last:
-            *picked, left, right, out4, grad4 = early_outputs(
-                sz,
-                middle,
-                meta,
-                across,
-                state["picked"],
-                got,
-                early,
-                state["weights"],
-                history,
-                state["high"],
-                token,
-                state["outs"],
-            )
-            token = picked[0]
         gated = not last and bits[at + 1] < sz.rounds
         after = ([] if token is None else [token]) + held
         held = [got[bit]] if bit < sz.rounds else []
@@ -815,6 +804,20 @@
         else:
             mine, token, *rest = add(mine, theirs, pays[bits[at + 1]] if gated else None, after)
     theirs = from_partner(mine, 0)
+    *picked, left, right, out4, grad4 = early_outputs(
+        sz,
+        middle,
+        meta,
+        across,
+        state["picked"],
+        got,
+        early,
+        state["weights"],
+        history,
+        state["high"],
+        mine,
+        state["outs"],
+    )
     out4, grad4, grad_w = fix_outputs(
         sz,
         "dom",

time: 50.6 us -> 50.4 us (level)
  Pallas kernels: 23.1 us -> 24.7 us
  waiting for transfers between devices: 4.63 us -> 3.62 us
  starting transfers between devices: 21.2 us -> 20.4 us
    ppermute x21, waiting for transfers between devices: 4.63 us -> 3.62 us  [from_partner(): return lax.ppermute(values, 'dom', route)]
    pallas_call x1, Pallas kernels: 4.59 us -> 5.46 us  [first_products(): call(functools.partial(first_kernel, sz), [VMEM, VMEM, HBM, VMEM, VMEM],...]
    ppermute x21, starting transfers between devices: 21.2 us -> 20.4 us  [from_partner(): return lax.ppermute(values, 'dom', route)]
    pallas_call x1, Pallas kernels: 4.5 us -> 5.06 us  [local_products(): call(functools.partial(local_kernel, sz), [VMEM] * 8, [VMEM] * 5, [sz.fie...]
  transfers between devices with their start and end apart: 21 -> 21, of which waited for: 5 -> 6; matrix products, arithmetic and copies ran while one was open for 0% -> 0% of each run, Pallas kernels for 34% -> 37%
where the time goes in v8:
time: 50.4 us; the launch traced here: 50.2 us
  Pallas kernels  24.7 us (49%)
  starting transfers between devices  20.4 us (40%)
  waiting for transfers between devices  3.62 us (7%)
  between operations  1.52 us (3%)
    ppermute x21, starting transfers between devices, from_partner(): return lax.ppermute(values, 'dom', route)  20.4 us
    pallas_call x1, Pallas kernels, first_products(): call(functools.partial(first_kernel, sz), [VMEM, VMEM, HBM, VMEM, VMEM],...  5.46 us
    pallas_call x1, Pallas kernels, local_products(): call(functools.partial(local_kernel, sz), [VMEM] * 8, [VMEM] * 5, [sz.fie...  5.06 us
    pallas_call x2, Pallas kernels, part_products(): call(functools.partial(early_rows_kernel if before is None else late_rows...  3.97 us
    ppermute x21, waiting for transfers between devices, from_partner(): return lax.ppermute(values, 'dom', route)  3.62 us
    pallas_call x1, Pallas kernels, pack(): call(functools.partial(pack_kernel, sz), [HBM] * 6 + [SMEM, HBM], [VMEM]...  2.8 us
    pallas_call x1, Pallas kernels, base_outputs(): call(functools.partial(output_kernel, sz, middle), [VMEM] * len(args), [V...  2.14 us
    pallas_call x2, Pallas kernels, join(): call(functools.partial(start_kernel if first else join_kernel, sz), [VMEM...  1.7 us
  transfers between devices with their start and end apart: 21, of which 6 were waited for; matrix products, arithmetic and copies ran while one was open for 0% of the time, Pallas kernels for 37%

profile of v8, /device:TPU:0, one launch (start us, length us, event | category | flops | bytes accessed | tf_op | source)
XLA Modules:
  0.0 50.2 jit_solution(3543851070039148527)
XLA Ops:
  1.3 2.8 %shard_map.121 = (bf16[64,64,128]{2,1,0:T(8,128)(2,1)S(1)}, bf16[64,64,128]{2,1,0:T(8,128)(2,1)S(1)}, bf16[10,128,128]{2,1,0:T(8,128)(2,1)S(1)}, bf16[10,128,128...) custom-call(bf16[8,64,8,128]{3,2,1,0:T(8,128)(2,1)} %bitcast.18, ...), custom_call_target="tpu_custom_call" | custom-call | flops 1000 | bytes 4194304 | tf_op jit(solution)/shard_map/pallas_call | solution.py:144
  4.1 0.8 %collective-permute-start = (bf16[256,128]{1,0:T(8,128)(2,1)S(1)}, bf16[256,128]{1,0:T(8,128)(2,1)S(1)}, u32[]{:S(2)}, u32[]{:S(2)}) collective-permute-start(bf16[256,128]{1,0:T(8,128)(2,1)S(1)} %get-tuple-element.90), channel_id=1, source_target_pairs={{0,1},{1,0},{2,3},{3,2},{4,5},{5,4},{6,7},{7,6},{8,9},{9,8},{10,11... | collective-permute-start | bytes 196616 | tf_op jit(solution)/shard_map/ppermute | solution.py:718
  4.9 2.3 %collective-permute-start.1 = (bf16[256,128]{1,0:T(8,128)(2,1)S(1)}, bf16[256,128]{1,0:T(8,128)(2,1)S(1)}, u32[]{:S(2)}, u32[]{:S(2)}) collective-permute-start(bf16[256,128]{1,0:T(8,128)(2,1)S(1)} %get-tuple-element.91), channel_id=1, source_target_pairs={{0,2},{2,0},{1,3},{3,1},{4,6},{6,4},{5,7},{7,5},{8,10},{10,8},{9,1... | collective-permute-start | bytes 196616 | tf_op jit(solution)/shard_map/ppermute | solution.py:718
  7.2 1.7 %collective-permute-start.2 = (bf16[256,128]{1,0:T(8,128)(2,1)S(1)}, bf16[256,128]{1,0:T(8,128)(2,1)S(1)}, u32[]{:S(2)}, u32[]{:S(2)}) collective-permute-start(bf16[256,128]{1,0:T(8,128)(2,1)S(1)} %get-tuple-element.92), channel_id=1, source_target_pairs={{0,4},{4,0},{1,5},{5,1},{2,6},{6,2},{3,7},{7,3},{8,12},{12,8},{9,1... | collective-permute-start | bytes 196616 | tf_op jit(solution)/shard_map/ppermute | solution.py:718
  8.9 1.3 %collective-permute-start.3 = (bf16[256,128]{1,0:T(8,128)(2,1)S(1)}, bf16[256,128]{1,0:T(8,128)(2,1)S(1)}, u32[]{:S(2)}, u32[]{:S(2)}) collective-permute-start(bf16[256,128]{1,0:T(8,128)(2,1)S(1)} %get-tuple-element.93), channel_id=1, source_target_pairs={{0,8},{8,0},{1,9},{9,1},{2,10},{10,2},{3,11},{11,3},{4,12},{12,4},... | collective-permute-start | bytes 196616 | tf_op jit(solution)/shard_map/ppermute | solution.py:718
  10.1 2.6 %collective-permute-start.4 = (bf16[256,128]{1,0:T(8,128)(2,1)S(1)}, bf16[256,128]{1,0:T(8,128)(2,1)S(1)}, u32[]{:S(2)}, u32[]{:S(2)}) collective-permute-start(bf16[256,128]{1,0:T(8,128)(2,1)S(1)} %get-tuple-element.94), channel_id=1, source_target_pairs={{0,16},{16,0},{1,17},{17,1},{2,18},{18,2},{3,19},{19,3},{4,20},{20... | collective-permute-start | bytes 196616 | tf_op jit(solution)/shard_map/ppermute | solution.py:718
  12.7 5.5 %shard_map.122 = (bf16[64,64,128]{2,1,0:T(8,128)(2,1)S(1)}, bf16[64,64,128]{2,1,0:T(8,128)(2,1)S(1)}, f32[10,64,128]{2,1,0:T(8,128)S(1)}, f32[10,64,128]{2,1,0:T...) custom-call(s32[46]{0:T(128)S(1)} %get-tuple-element.78.refs_0_, ...), custom_call_target="tpu_custom_call" | custom-call | flops 805306368 | bytes 12582912 | tf_op jit(solution)/shard_map/pallas_call | solution.py:270
  18.2 0.0 collective-permute-done.refs_7_
  18.2 0.0 collective-permute-done.1.refs_8_
  18.2 0.0 collective-permute-done.2.refs_9_
  18.2 0.0 collective-permute-done.4.refs_11_
  18.3 0.9 %shard_map.123 = (bf16[64,64,128]{2,1,0:T(8,128)(2,1)S(1)}, bf16[64,64,128]{2,1,0:T(8,128)(2,1)S(1)}, bf16[256,128]{1,0:T(8,128)(2,1)S(1)}, bf16[256,128]{1,0:T(...) custom-call(s32[46]{0:T(128)S(1)} %get-tuple-element.78.refs_0_, ...), custom_call_target="tpu_custom_call", output_to_operand_aliasing={{0}: (2, {}), {1}: (3, {})} | custom-call | flops 20971520 | bytes 5242880 | tf_op jit(solution)/shard_map/pallas_call | solution.py:490
  19.2 0.1 collective-permute-start.5
  19.2 0.7 %collective-permute-start.6 = (bf16[256,128]{1,0:T(8,128)(2,1)S(1)}, bf16[256,128]{1,0:T(8,128)(2,1)S(1)}, u32[]{:S(2)}, u32[]{:S(2)}) collective-permute-start(bf16[256,128]{1,0:T(8,128)(2,1)S(1)} %get-tuple-element.104), channel_id=1, source_target_pairs={{0,2},{2,0},{1,3},{3,1},{4,6},{6,4},{5,7},{7,5},{8,10},{10,8},{9,1... | collective-permute-start | bytes 196616 | tf_op jit(solution)/shard_map/ppermute | solution.py:718
  20.0 0.3 collective-permute-start.7
  20.2 0.4 collective-permute-start.8
  20.7 0.3 collective-permute-start.9
  20.9 5.1 %shard_map.124 = (bf16[64,64,128]{2,1,0:T(8,128)(2,1)S(1)}, bf16[64,64,128]{2,1,0:T(8,128)(2,1)S(1)}, f32[10,64,128]{2,1,0:T(8,128)S(1)}, f32[10,64,128]{2,1,0:T(8,128)S(1)}, f32[128,128]{1,0:T(8,128)S(1)}) custom-call(s32[46]{0:T(128)S(1)} %get-tuple-element.78.refs_0_, s32[3,64]{1,0:T(4,128)S(1)} %get-tuple-element.80.refs_1_, ...), custom_call_target="tpu_custom_call" | custom-call | flops 805306368 | bytes 12582912 | tf_op jit(solution)/shard_map/pallas_call | solution.py:344
  26.0 0.0 collective-permute-done.6.refs_8_
  26.0 0.0 collective-permute-done.7.refs_9_
  26.0 1.0 %collective-permute-done.9.refs_11_ = bf16[256,128]{1,0:T(8,128)(2,1)S(1)} collective-permute-done((bf16[256,128]{1,0:T(8,128)(2,1)S(1)}, bf16[256,128]{1,0:T(8,128)(2,1)S(1)}, u32[]{:S(2)}, u32[]{:S(2)}) %collective-permute-start.9) | collective-permute-done | bytes 65568 | tf_op jit(solution)/shard_map/ppermute | solution.py:718
  27.1 0.9 %shard_map.125 = (f32[10,64,128]{2,1,0:T(8,128)S(1)}, f32[10,64,128]{2,1,0:T(8,128)S(1)}, f32[64,128]{1,0:T(8,128)S(1)}, f32[64,128]{1,0:T(8,128)S(1)}) custom-call(s32[46]{0:T(128)S(1)} %get-tuple-element.78.refs_0_, bf16[10,128,128]{2,1,0:T(8,128)(2,1)S(1)} %get-tuple-element.79.refs_4_.refs_1_, f32[10,64,128]{2,1,0:T(8,128)S(1)} %get-tuple-element.99.refs_2_, ...), custom_call_target="tpu_custom_call" | custom-call | flops 41943040 | bytes 3145728 | tf_op jit(solution)/shard_map/pallas_call | solution.py:453
  28.0 0.1 collective-permute-start.10
  28.1 0.8 %shard_map.126 = (bf16[64,64,128]{2,1,0:T(8,128)(2,1)S(1)}, bf16[64,64,128]{2,1,0:T(8,128)(2,1)S(1)}, bf16[256,128]{1,0:T(8,128)(2,1)S(1)}, bf16[256,128]{1,0:T(...) custom-call(s32[46]{0:T(128)S(1)} %get-tuple-element.78.refs_0_, ...), custom_call_target="tpu_custom_call", output_to_operand_aliasing={{0}: (2, {}), {1}: (3, {})} | custom-call | flops 20971520 | bytes 5242880 | tf_op jit(solution)/shard_map/pallas_call | solution.py:490
  28.9 0.6 %collective-permute-start.12 = (bf16[256,128]{1,0:T(8,128)(2,1)S(1)}, bf16[256,128]{1,0:T(8,128)(2,1)S(1)}, u32[]{:S(2)}, u32[]{:S(2)}) collective-permute-start(bf16[256,128]{1,0:T(8,128)(2,1)S(1)} %get-tuple-element.121), channel_id=1, source_target_pairs={{0,1},{1,0},{2,3},{3,2},{4,5},{5,4},{6,7},{7,6},{8,9},{9,8},{10,11... | collective-permute-start | bytes 196616 | tf_op jit(solution)/shard_map/ppermute | solution.py:718
  29.5 0.0 collective-permute-done.10.refs_1_
  29.5 1.6 %collective-permute-start.11 = (f32[64,128]{1,0:T(8,128)S(1)}, f32[64,128]{1,0:T(8,128)S(1)}, u32[]{:S(2)}, u32[]{:S(2)}) collective-permute-start(f32[64,128]{1,0:T(8,128)S(1)} %get-tuple-element.119.refs_0_), channel_id=1, source_target_pairs={{0,16},{16,0},{1,17},{17,1},{2,18},{18,2},{3,19},{19,3},{4,20},{20... | collective-permute-start | bytes 98312 | tf_op jit(solution)/shard_map/ppermute | solution.py:718
  31.0 1.4 %collective-permute-start.13 = (bf16[256,128]{1,0:T(8,128)(2,1)S(1)}, bf16[256,128]{1,0:T(8,128)(2,1)S(1)}, u32[]{:S(2)}, u32[]{:S(2)}) collective-permute-start(bf16[256,128]{1,0:T(8,128)(2,1)S(1)} %get-tuple-element.125), channel_id=1, source_target_pairs={{0,16},{16,0},{1,17},{17,1},{2,18},{18,2},{3,19},{19,3},{4,20},{20... | collective-permute-start | bytes 196616 | tf_op jit(solution)/shard_map/ppermute | solution.py:718
  32.5 2.1 %shard_map.128 = (bf16[64,64,128]{2,1,0:T(8,128)(2,1)S(1)}, f32[64,64,128]{2,1,0:T(8,128)S(1)}, f32[64,64,128]{2,1,0:T(8,128)S(1)}) custom-call(s32[46]{0:T(128)S(1)} %get-tuple-element.78.refs_0_, s32[3,64]{1,0:T(4,128)S(1)} %get-tuple-element.80.refs_1_, bf16[64,3,128,128]{3,2,1,0:T(8,128)(2,1)S(1)} %get-tuple-element.83.refs_2_, ...), custom_call_target="tpu_custom_call" | custom-call | flops 402653184 | bytes 6291456 | tf_op jit(solution)/shard_map/pallas_call | solution.py:395
  34.6 0.0 collective-permute-done.12.refs_3_.refs_4_
  34.6 0.4 collective-permute-done.11.refs_1_
  35.0 1.1 %collective-permute-start.15 = (f32[64,128]{1,0:T(8,128)S(1)}, f32[64,128]{1,0:T(8,128)S(1)}, u32[]{:S(2)}, u32[]{:S(2)}) collective-permute-start(f32[64,128]{1,0:T(8,128)S(1)} %get-tuple-element.127.refs_0_), channel_id=1, source_target_pairs={{0,8},{8,0},{1,9},{9,1},{2,10},{10,2},{3,11},{11,3},{4,12},{12,4},... | collective-permute-start | bytes 98312 | tf_op jit(solution)/shard_map/ppermute | solution.py:718
  36.1 1.0 %collective-permute-start.14 = (bf16[256,128]{1,0:T(8,128)(2,1)S(1)}, bf16[256,128]{1,0:T(8,128)(2,1)S(1)}, u32[]{:S(2)}, u32[]{:S(2)}) collective-permute-start(bf16[256,128]{1,0:T(8,128)(2,1)S(1)} %get-tuple-element.126), channel_id=1, source_target_pairs={{0,8},{8,0},{1,9},{9,1},{2,10},{10,2},{3,11},{11,3},{4,12},{12,4},... | collective-permute-start | bytes 196616 | tf_op jit(solution)/shard_map/ppermute | solution.py:718
  37.1 1.8 %shard_map.130 = (bf16[64,64,128]{2,1,0:T(8,128)(2,1)S(1)}, f32[64,64,128]{2,1,0:T(8,128)S(1)}, f32[64,64,128]{2,1,0:T(8,128)S(1)}, bf16[64,64,128]{2,1,0:T(8,12...) custom-call(s32[46]{0:T(128)S(1)} %get-tuple-element.78.refs_0_, ...), custom_call_target="tpu_custom_call", output_to_operand_aliasing={{0}: (8, {}), {1}: (9, {}), {2}: (10, {})} | custom-call | flops 402653184 | bytes 6291456 | tf_op jit(solution)/shard_map/pallas_call | solution.py:395
  38.9 0.1 collective-permute-done.15.refs_1_
  39.0 0.0 collective-permute-done.13.refs_4_.refs_5_
  39.0 1.7 %collective-permute-start.17 = (f32[64,128]{1,0:T(8,128)S(1)}, f32[64,128]{1,0:T(8,128)S(1)}, u32[]{:S(2)}, u32[]{:S(2)}) collective-permute-start(f32[64,128]{1,0:T(8,128)S(1)} %get-tuple-element.137.refs_0_), channel_id=1, source_target_pairs={{0,4},{4,0},{1,5},{5,1},{2,6},{6,2},{3,7},{7,3},{8,12},{12,8},{9,1... | collective-permute-start | bytes 98312 | tf_op jit(solution)/shard_map/ppermute | solution.py:718
  40.7 0.4 collective-permute-start.16
  41.1 2.1 %shard_map.132 = (bf16[64,256]{1,0:T(8,128)(2,1)S(1)}, bf16[64,256]{1,0:T(8,128)(2,1)S(1)}, bf16[8,32,8,128]{3,2,1,0:T(8,128)(2,1)S(1)}, bf16[8,32,8,128]{3,2,1,...) custom-call(bf16[64,64,128]{2,1,0:T(8,128)(2,1)S(1)} %get-tuple-element.81.refs_3_.refs_6_.refs_0_.ref, ...), custom_call_target="tpu_custom_call" | custom-call | flops 536870912 | bytes 6291456 | tf_op jit(solution)/shard_map/pallas_call | solution.py:553
  43.3 0.0 collective-permute-done.14.refs_4_.refs_6_
  43.3 1.1 %collective-permute-start.18 = (f32[64,128]{1,0:T(8,128)S(1)}, f32[64,128]{1,0:T(8,128)S(1)}, u32[]{:S(2)}, u32[]{:S(2)}) collective-permute-start(f32[64,128]{1,0:T(8,128)S(1)} %get-tuple-element.139.refs_0_), channel_id=1, source_target_pairs={{0,2},{2,0},{1,3},{3,1},{4,6},{6,4},{5,7},{7,5},{8,10},{10,8},{9,1... | collective-permute-start | bytes 98312 | tf_op jit(solution)/shard_map/ppermute | solution.py:718
  44.4 1.0 %collective-permute-start.19 = (bf16[256,128]{1,0:T(8,128)(2,1)S(1)}, bf16[256,128]{1,0:T(8,128)(2,1)S(1)}, u32[]{:S(2)}, u32[]{:S(2)}) collective-permute-start(bf16[256,128]{1,0:T(8,128)(2,1)S(1)} %get-tuple-element.145), channel_id=1, source_target_pairs={{0,2},{2,0},{1,3},{3,1},{4,6},{6,4},{5,7},{7,5},{8,10},{10,8},{9,1... | collective-permute-start | bytes 196616 | tf_op jit(solution)/shard_map/ppermute | solution.py:718
  45.4 1.9 %collective-permute-done.18.refs_1_ = f32[64,128]{1,0:T(8,128)S(1)} collective-permute-done((f32[64,128]{1,0:T(8,128)S(1)}, f32[64,128]{1,0:T(8,128)S(1)}, u32[]{:S(2)}, u32[]{:S(2)}) %collective-permute-start.18) | collective-permute-done | bytes 32800 | tf_op jit(solution)/shard_map/ppermute | solution.py:718
  47.3 0.1 collective-permute-start.20
  47.4 1.0 %shard_map.135 = (f32[10,64,128]{2,1,0:T(8,128)S(1)}, f32[10,64,128]{2,1,0:T(8,128)S(1)}, bf16[10,8,8,128]{3,2,1,0:T(8,128)(2,1)S(1)}, bf16[10,8,8,128]{3,2,1,0:...) custom-call(s32[46]{0:T(128)S(1)} %get-tuple-element.78.refs_0_, ...), custom_call_target="tpu_custom_call", output_to_operand_aliasing={{4}: (19, {}), {5}: (20, {})} | custom-call | flops 83886080 | bytes 4194304 | tf_op jit(solution)/shard_map/pallas_call | solution.py:615
  48.4 0.1 collective-permute-done.20.refs_16_
  48.6 0.1 collective-permute-done.19.refs_4_
  48.7 1.6 %shard_map.136 = (bf16[8,64,8,128]{3,2,1,0:T(8,128)(2,1)}, bf16[8,64,8,128]{3,2,1,0:T(8,128)(2,1)}, f32[4,64,64]{2,1,0:T(8,128)}) custom-call(s32[46]{0:T(128)S(1)} %get-tuple-element.78.refs_0_, bf16[10,128,128]{2,1,0:T(8,128)(2,1)S(1)} %get-tuple-element.79.refs_4_.refs_1_, ...), custom_call_target="tpu_custom_call", output_to_operand_aliasing={{0}: (17, {}), {1}: (18, {})} | custom-call | flops 16777216 | bytes 2097152 | tf_op jit(solution)/shard_map/pallas_call | solution.py:666
  (12 shorter events, 0.1 us)
Async XLA Ops:
  4.1 14.1 %collective-permute-start = (bf16[256,128]{1,0:T(8,128)(2,1)S(1)}, bf16[256,128]{1,0:T(8,128)(2,1)S(1)}, u32[]{:S(2)}, u32[]{:S(2)}) collective-permute-start(bf16[256,128]{1,0:T(8,128)(2,1)S(1)} %get-tuple-element.90), channel_id=1, source_target_pairs={{0,1},{1,0},{2,3},{3,2},{4,5},{5,4},{6,7},{7,6},{8,9},{9,8},{10,11... | collective-permute-start | bytes 196616 | tf_op jit(solution)/shard_map/ppermute | solution.py:718
  4.9 13.4 %collective-permute-start.1 = (bf16[256,128]{1,0:T(8,128)(2,1)S(1)}, bf16[256,128]{1,0:T(8,128)(2,1)S(1)}, u32[]{:S(2)}, u32[]{:S(2)}) collective-permute-start(bf16[256,128]{1,0:T(8,128)(2,1)S(1)} %get-tuple-element.91), channel_id=1, source_target_pairs={{0,2},{2,0},{1,3},{3,1},{4,6},{6,4},{5,7},{7,5},{8,10},{10,8},{9,1... | collective-permute-start | bytes 196616 | tf_op jit(solution)/shard_map/ppermute | solution.py:718
  7.2 11.0 %collective-permute-start.2 = (bf16[256,128]{1,0:T(8,128)(2,1)S(1)}, bf16[256,128]{1,0:T(8,128)(2,1)S(1)}, u32[]{:S(2)}, u32[]{:S(2)}) collective-permute-start(bf16[256,128]{1,0:T(8,128)(2,1)S(1)} %get-tuple-element.92), channel_id=1, source_target_pairs={{0,4},{4,0},{1,5},{5,1},{2,6},{6,2},{3,7},{7,3},{8,12},{12,8},{9,1... | collective-permute-start | bytes 196616 | tf_op jit(solution)/shard_map/ppermute | solution.py:718
  8.9 9.4 %collective-permute-start.3 = (bf16[256,128]{1,0:T(8,128)(2,1)S(1)}, bf16[256,128]{1,0:T(8,128)(2,1)S(1)}, u32[]{:S(2)}, u32[]{:S(2)}) collective-permute-start(bf16[256,128]{1,0:T(8,128)(2,1)S(1)} %get-tuple-element.93), channel_id=1, source_target_pairs={{0,8},{8,0},{1,9},{9,1},{2,10},{10,2},{3,11},{11,3},{4,12},{12,4},... | collective-permute-start | bytes 196616 | tf_op jit(solution)/shard_map/ppermute | solution.py:718
  10.1 8.1 %collective-permute-start.4 = (bf16[256,128]{1,0:T(8,128)(2,1)S(1)}, bf16[256,128]{1,0:T(8,128)(2,1)S(1)}, u32[]{:S(2)}, u32[]{:S(2)}) collective-permute-start(bf16[256,128]{1,0:T(8,128)(2,1)S(1)} %get-tuple-element.94), channel_id=1, source_target_pairs={{0,16},{16,0},{1,17},{17,1},{2,18},{18,2},{3,19},{19,3},{4,20},{20... | collective-permute-start | bytes 196616 | tf_op jit(solution)/shard_map/ppermute | solution.py:718
  19.2 6.8 %collective-permute-start.5 = (bf16[256,128]{1,0:T(8,128)(2,1)S(1)}, bf16[256,128]{1,0:T(8,128)(2,1)S(1)}, u32[]{:S(2)}, u32[]{:S(2)}) collective-permute-start(bf16[256,128]{1,0:T(8,128)(2,1)S(1)} %get-tuple-element.103), channel_id=1, source_target_pairs={{0,1},{1,0},{2,3},{3,2},{4,5},{5,4},{6,7},{7,6},{8,9},{9,8},{10,11... | collective-permute-start | bytes 196616 | tf_op jit(solution)/shard_map/ppermute | solution.py:718
  19.2 6.8 %collective-permute-start.6 = (bf16[256,128]{1,0:T(8,128)(2,1)S(1)}, bf16[256,128]{1,0:T(8,128)(2,1)S(1)}, u32[]{:S(2)}, u32[]{:S(2)}) collective-permute-start(bf16[256,128]{1,0:T(8,128)(2,1)S(1)} %get-tuple-element.104), channel_id=1, source_target_pairs={{0,2},{2,0},{1,3},{3,1},{4,6},{6,4},{5,7},{7,5},{8,10},{10,8},{9,1... | collective-permute-start | bytes 196616 | tf_op jit(solution)/shard_map/ppermute | solution.py:718
  20.0 6.1 %collective-permute-start.7 = (bf16[256,128]{1,0:T(8,128)(2,1)S(1)}, bf16[256,128]{1,0:T(8,128)(2,1)S(1)}, u32[]{:S(2)}, u32[]{:S(2)}) collective-permute-start(bf16[256,128]{1,0:T(8,128)(2,1)S(1)} %get-tuple-element.105), channel_id=1, source_target_pairs={{0,4},{4,0},{1,5},{5,1},{2,6},{6,2},{3,7},{7,3},{8,12},{12,8},{9,1... | collective-permute-start | bytes 196616 | tf_op jit(solution)/shard_map/ppermute | solution.py:718
  20.2 5.8 %collective-permute-start.8 = (bf16[256,128]{1,0:T(8,128)(2,1)S(1)}, bf16[256,128]{1,0:T(8,128)(2,1)S(1)}, u32[]{:S(2)}, u32[]{:S(2)}) collective-permute-start(bf16[256,128]{1,0:T(8,128)(2,1)S(1)} %get-tuple-element.106), channel_id=1, source_target_pairs={{0,8},{8,0},{1,9},{9,1},{2,10},{10,2},{3,11},{11,3},{4,12},{12,4},... | collective-permute-start | bytes 196616 | tf_op jit(solution)/shard_map/ppermute | solution.py:718
  20.7 6.4 %collective-permute-start.9 = (bf16[256,128]{1,0:T(8,128)(2,1)S(1)}, bf16[256,128]{1,0:T(8,128)(2,1)S(1)}, u32[]{:S(2)}, u32[]{:S(2)}) collective-permute-start(bf16[256,128]{1,0:T(8,128)(2,1)S(1)} %get-tuple-element.107), channel_id=1, source_target_pairs={{0,16},{16,0},{1,17},{17,1},{2,18},{18,2},{3,19},{19,3},{4,20},{20... | collective-permute-start | bytes 196616 | tf_op jit(solution)/shard_map/ppermute | solution.py:718
  28.0 1.4 %collective-permute-start.10 = (f32[64,128]{1,0:T(8,128)S(1)}, f32[64,128]{1,0:T(8,128)S(1)}, u32[]{:S(2)}, u32[]{:S(2)}) collective-permute-start(f32[64,128]{1,0:T(8,128)S(1)} %get-tuple-element.113), channel_id=1, source_target_pairs={{0,1},{1,0},{2,3},{3,2},{4,5},{5,4},{6,7},{7,6},{8,9},{9,8},{10,11... | collective-permute-start | bytes 98312 | tf_op jit(solution)/shard_map/ppermute | solution.py:718
  28.9 5.7 %collective-permute-start.12 = (bf16[256,128]{1,0:T(8,128)(2,1)S(1)}, bf16[256,128]{1,0:T(8,128)(2,1)S(1)}, u32[]{:S(2)}, u32[]{:S(2)}) collective-permute-start(bf16[256,128]{1,0:T(8,128)(2,1)S(1)} %get-tuple-element.121), channel_id=1, source_target_pairs={{0,1},{1,0},{2,3},{3,2},{4,5},{5,4},{6,7},{7,6},{8,9},{9,8},{10,11... | collective-permute-start | bytes 196616 | tf_op jit(solution)/shard_map/ppermute | solution.py:718
  29.5 5.5 %collective-permute-start.11 = (f32[64,128]{1,0:T(8,128)S(1)}, f32[64,128]{1,0:T(8,128)S(1)}, u32[]{:S(2)}, u32[]{:S(2)}) collective-permute-start(f32[64,128]{1,0:T(8,128)S(1)} %get-tuple-element.119.refs_0_), channel_id=1, source_target_pairs={{0,16},{16,0},{1,17},{17,1},{2,18},{18,2},{3,19},{19,3},{4,20},{20... | collective-permute-start | bytes 98312 | tf_op jit(solution)/shard_map/ppermute | solution.py:718
  31.0 8.0 %collective-permute-start.13 = (bf16[256,128]{1,0:T(8,128)(2,1)S(1)}, bf16[256,128]{1,0:T(8,128)(2,1)S(1)}, u32[]{:S(2)}, u32[]{:S(2)}) collective-permute-start(bf16[256,128]{1,0:T(8,128)(2,1)S(1)} %get-tuple-element.125), channel_id=1, source_target_pairs={{0,16},{16,0},{1,17},{17,1},{2,18},{18,2},{3,19},{19,3},{4,20},{20... | collective-permute-start | bytes 196616 | tf_op jit(solution)/shard_map/ppermute | solution.py:718
  35.0 4.0 %collective-permute-start.15 = (f32[64,128]{1,0:T(8,128)S(1)}, f32[64,128]{1,0:T(8,128)S(1)}, u32[]{:S(2)}, u32[]{:S(2)}) collective-permute-start(f32[64,128]{1,0:T(8,128)S(1)} %get-tuple-element.127.refs_0_), channel_id=1, source_target_pairs={{0,8},{8,0},{1,9},{9,1},{2,10},{10,2},{3,11},{11,3},{4,12},{12,4},... | collective-permute-start | bytes 98312 | tf_op jit(solution)/shard_map/ppermute | solution.py:718
  36.1 7.2 %collective-permute-start.14 = (bf16[256,128]{1,0:T(8,128)(2,1)S(1)}, bf16[256,128]{1,0:T(8,128)(2,1)S(1)}, u32[]{:S(2)}, u32[]{:S(2)}) collective-permute-start(bf16[256,128]{1,0:T(8,128)(2,1)S(1)} %get-tuple-element.126), channel_id=1, source_target_pairs={{0,8},{8,0},{1,9},{9,1},{2,10},{10,2},{3,11},{11,3},{4,12},{12,4},... | collective-permute-start | bytes 196616 | tf_op jit(solution)/shard_map/ppermute | solution.py:718
  37.1 4.0 %copy-start = (bf16[4,64,64]{2,1,0:T(8,128)(2,1)S(1)}, bf16[4,64,64]{2,1,0:T(8,128)(2,1)}, u32[]{:S(2)}) copy-start(bf16[4,64,64]{2,1,0:T(8,128)(2,1)} %refs_8_.1) | copy-start | bytes 98308
  39.0 4.2 %collective-permute-start.17 = (f32[64,128]{1,0:T(8,128)S(1)}, f32[64,128]{1,0:T(8,128)S(1)}, u32[]{:S(2)}, u32[]{:S(2)}) collective-permute-start(f32[64,128]{1,0:T(8,128)S(1)} %get-tuple-element.137.refs_0_), channel_id=1, source_target_pairs={{0,4},{4,0},{1,5},{5,1},{2,6},{6,2},{3,7},{7,3},{8,12},{12,8},{9,1... | collective-permute-start | bytes 98312 | tf_op jit(solution)/shard_map/ppermute | solution.py:718
  40.7 6.6 %collective-permute-start.16 = (bf16[256,128]{1,0:T(8,128)(2,1)S(1)}, bf16[256,128]{1,0:T(8,128)(2,1)S(1)}, u32[]{:S(2)}, u32[]{:S(2)}) collective-permute-start(bf16[256,128]{1,0:T(8,128)(2,1)S(1)} %get-tuple-element.129), channel_id=1, source_target_pairs={{0,4},{4,0},{1,5},{5,1},{2,6},{6,2},{3,7},{7,3},{8,12},{12,8},{9,1... | collective-permute-start | bytes 196616 | tf_op jit(solution)/shard_map/ppermute | solution.py:718
  43.3 4.0 %collective-permute-start.18 = (f32[64,128]{1,0:T(8,128)S(1)}, f32[64,128]{1,0:T(8,128)S(1)}, u32[]{:S(2)}, u32[]{:S(2)}) collective-permute-start(f32[64,128]{1,0:T(8,128)S(1)} %get-tuple-element.139.refs_0_), channel_id=1, source_target_pairs={{0,2},{2,0},{1,3},{3,1},{4,6},{6,4},{5,7},{7,5},{8,10},{10,8},{9,1... | collective-permute-start | bytes 98312 | tf_op jit(solution)/shard_map/ppermute | solution.py:718
  44.4 4.3 %collective-permute-start.19 = (bf16[256,128]{1,0:T(8,128)(2,1)S(1)}, bf16[256,128]{1,0:T(8,128)(2,1)S(1)}, u32[]{:S(2)}, u32[]{:S(2)}) collective-permute-start(bf16[256,128]{1,0:T(8,128)(2,1)S(1)} %get-tuple-element.145), channel_id=1, source_target_pairs={{0,2},{2,0},{1,3},{3,1},{4,6},{6,4},{5,7},{7,5},{8,10},{10,8},{9,1... | collective-permute-start | bytes 196616 | tf_op jit(solution)/shard_map/ppermute | solution.py:718
  47.3 1.3 %collective-permute-start.20 = (f32[64,128]{1,0:T(8,128)S(1)}, f32[64,128]{1,0:T(8,128)S(1)}, u32[]{:S(2)}, u32[]{:S(2)}) collective-permute-start(f32[64,128]{1,0:T(8,128)S(1)} %shard_map.134.refs_18_.refs_15_), channel_id=1, source_target_pairs={{0,1},{1,0},{2,3},{3,2},{4,5},{5,4},{6,7},{7,6},{8,9},{9,8},{10,11... | collective-permute-start | bytes 98312 | tf_op jit(solution)/shard_map/ppermute | solution.py:718

commit v9 on v8

--- a/solution.py
+++ b/solution.py
@@ -140,12 +140,12 @@
     _, _, _, send, row, pair, _, col = args
     groups = sz.chan // SUB
     cross = shape((sz.pairs, sz.blk, sz.blk), BF16)
-    table = shape((sz.meta,), jnp.int32)
+    table = pltpu.SMEM((sz.meta,), jnp.int32)
     return call(
         functools.partial(pack_kernel, sz),
         [HBM] * 6 + [SMEM, HBM],
-        [VMEM] * 4 + [SMEM, VMEM] + [VMEM] * sz.rounds,
-        [sz.field, sz.field, cross, cross, table, shape(col.shape, jnp.int32)]
+        [VMEM] * 4 + [SMEM, SMEM] + [VMEM] * sz.rounds,
+        [sz.field, sz.field, cross, cross, table, pltpu.SMEM(col.shape, jnp.int32)]
         + [sz.pay] * sz.rounds,
         [
             pltpu.SMEM(send.shape, jnp.int32),
@@ -170,10 +170,6 @@
     return (count + ROWS_PART - 1) // ROWS_PART
 
 
-def table_scratch(sz, col):
-    return [pltpu.SMEM((sz.meta,), jnp.int32), pltpu.SMEM(col.shape, jnp.int32)]
-
-
 def clear_sums(sz, summed):
     def clear(i, carry):
         summed[i] = jnp.zeros(summed.shape[1:], F32)
@@ -210,16 +206,8 @@
 
 
 def first_kernel(sz, *refs):
-    meta_in, col_in, tiles_hbm, t0, s0 = refs[:5]
-    tnew, snew, psel, qsel, tiles, turned, gram, held, summed, meta, col, sem, sem_i = refs[5:]
-    small = [
-        pltpu.make_async_copy(meta_in, meta, sem_i.at[0]),
-        pltpu.make_async_copy(col_in, col, sem_i.at[1]),
-    ]
-    for copy in small:
-        copy.start()
-    for copy in small:
-        copy.wait()
+    meta, col, tiles_hbm, t0, s0 = refs[:5]
+    tnew, snew, psel, qsel, tiles, turned, gram, held, summed, sem = refs[5:]
     count = meta[sz.live]
     steps = big_steps(count)
     loads = steps * (ROWS // ROWS_FIRST)
@@ -254,14 +242,19 @@
         tnew[i] = forward.astype(BF16)
         scatter_terms(sz, summed, cols, nn(s0[i], jnp.concatenate(parts, axis=1)))
 
-    def step(g, carry):
-        for part in range(ROWS // ROWS_FIRST):
-            fetch(g * (ROWS // ROWS_FIRST) + part).wait()
-        for u in range(ROWS):
-            block_row(g * ROWS + u)
-        return carry
-
-    lax.fori_loop(0, steps, step, 0)
+    def stepper(rows):
+        def step(g, carry):
+            for part in range(rows // ROWS_FIRST):
+                fetch(g * (rows // ROWS_FIRST) + part).wait()
+            for u in range(rows):
+                block_row(g * rows + u)
+            return carry
+
+        return step
+
+    short = ROWS // ROWS_PART
+    lax.fori_loop(0, short, stepper(ROWS_PART), 0)
+    lax.fori_loop(1, steps, stepper(ROWS), 0)
     finish_local(sz, meta, held, lambda i: summed[i], tnew, snew, psel, qsel)
 
 
@@ -269,13 +262,12 @@
     turned = shape((sz.blocks, sz.nz * sz.blk, sz.blk), BF16)
     return call(
         functools.partial(first_kernel, sz),
-        [VMEM, VMEM, HBM, VMEM, VMEM],
+        [SMEM, SMEM, HBM, VMEM, VMEM],
         [VMEM] * 7,
         [sz.field, sz.field, sz.picked, sz.picked, shape(tiles.shape, BF16), turned]
         + [shape((sz.chan, sz.chan), F32)],
         [pltpu.VMEM((sz.blocks, sz.chan, sz.blk), F32)] * 2
-        + table_scratch(sz, col)
-        + [pltpu.SemaphoreType.DMA((sz.blocks // ROWS_FIRST,)), pltpu.SemaphoreType.DMA((2,))],
+        + [pltpu.SemaphoreType.DMA((sz.blocks // ROWS_FIRST,))],
         4 * sz.blocks * sz.nz * sz.chan * sz.blk * sz.blk,
         12 << 20,
         24,
@@ -302,23 +294,10 @@
     lax.fori_loop(low, high, step, 0)
 
 
-def start_table(meta_in, col_in, meta, col, sem):
-    small = [
-        pltpu.make_async_copy(meta_in, meta, sem.at[0]),
-        pltpu.make_async_copy(col_in, col, sem.at[1]),
-    ]
-    for copy in small:
-        copy.start()
-    return small
-
-
 def local_kernel(sz, *refs):
-    meta_in, col_in, tiles, turned, tcur, scur, tprev, sprev = refs[:8]
-    tnew, snew, psel, qsel, gram, held, summed, meta, col, sem = refs[8:]
-    small = start_table(meta_in, col_in, meta, col, sem)
+    meta, col, tiles, turned, tcur, scur, tprev, sprev = refs[:8]
+    tnew, snew, psel, qsel, gram, held, summed = refs[8:]
     clear_sums(sz, summed)
-    for copy in small:
-        copy.wait()
     steps = big_steps(meta[sz.live])
     arrays = (tiles, turned, tcur, scur, tprev)
     row_products(sz, col, 0, steps, ROWS, arrays, tnew, held, summed)
@@ -343,12 +322,10 @@
     gram = shape((2 * sz.chan, 2 * sz.chan), F32)
     return call(
         functools.partial(local_kernel, sz),
-        [VMEM] * 8,
+        [SMEM] * 2 + [VMEM] * 6,
         [VMEM] * 5,
         [sz.field, sz.field, sz.picked, sz.picked, gram],
-        [pltpu.VMEM((sz.blocks, sz.chan, sz.blk), F32)] * 2
-        + table_scratch(sz, col)
-        + [pltpu.SemaphoreType.DMA((2,))],
+        [pltpu.VMEM((sz.blocks, sz.chan, sz.blk), F32)] * 2,
         4 * sz.blocks * sz.nz * sz.chan * sz.blk * sz.blk,
         12 << 20,
         24,
@@ -356,22 +333,17 @@
 
 
 def early_rows_kernel(sz, *refs):
-    meta_in, col_in, tiles, turned, tcur, scur, tprev, _ = refs[:8]
-    tnew, held, summed, meta, col, sem = refs[8:]
-    small = start_table(meta_in, col_in, meta, col, sem)
+    meta, col, tiles, turned, tcur, scur, tprev, _ = refs[:8]
+    tnew, held, summed = refs[8:]
     clear_sums(sz, summed)
-    for copy in small:
-        copy.wait()
     cut = (3 * part_steps(meta[sz.live])) // 4
     arrays = (tiles, turned, tcur, scur, tprev)
     row_products(sz, col, 0, cut, ROWS_PART, arrays, tnew, held, summed)
 
 
 def late_rows_kernel(sz, *refs):
-    meta_in, col_in, tiles, turned, tcur, scur, tprev, sprev = refs[:8]
-    tnew, held, summed, snew, psel, qsel, meta, col, sem = refs[12:]
-    for copy in start_table(meta_in, col_in, meta, col, sem):
-        copy.wait()
+    meta, col, tiles, turned, tcur, scur, tprev, sprev = refs[:8]
+    tnew, held, summed, snew, psel, qsel = refs[12:]
     steps = part_steps(meta[sz.live])
     arrays = (tiles, turned, tcur, scur, tprev)
     row_products(sz, col, (3 * steps) // 4, steps, ROWS_PART, arrays, tnew, held, summed)
@@ -394,10 +366,10 @@
         outs += [sz.field, sz.picked, sz.picked]
     return call(
         functools.partial(early_rows_kernel if before is None else late_rows_kernel, sz),
-        [VMEM] * len(args),
+        [SMEM] * 2 + [VMEM] * (len(args) - 2),
         [VMEM] * len(outs),
         outs,
-        table_scratch(sz, col) + [pltpu.SemaphoreType.DMA((2,))],
+        [],
         2 * sz.blocks * sz.nz * sz.chan * sz.blk * sz.blk,
         6 << 20,
         8,
@@ -405,16 +377,12 @@
     )(*args)
 
 
-def add_coupled(sz, scale, table, got, across, psel, qsel, pacc, qacc, which):
-    meta_in, meta, sem = table
-    copy = pltpu.make_async_copy(meta_in, meta, sem)
-    copy.start()
+def add_coupled(sz, scale, meta, got, across, psel, qsel, pacc, qacc, which):
     for j in range(sz.pairs):
         pacc[j] = psel[j]
         qacc[j] = qsel[j]
     some = [(r, h, j) for r, h, j in sz.couplings() if r in which]
     terms = {j: nn(got[r][sz.forward_part(h), :], across[j]) for r, h, j in some}
-    copy.wait()
     for r, h, j in some:
         terms[j] = (scale * meta[sz.flags + r].astype(F32)) * terms[j]
         spot = meta[sz.first_row + j]
@@ -424,16 +392,12 @@
     return terms
 
 
-def table_copy(sz):
-    return [pltpu.SMEM((sz.meta,), jnp.int32), pltpu.SemaphoreType.DMA]
-
-
 def correct_kernel(sz, axis, *refs):
-    meta_in, across, psel, qsel, gram0, gram, sold = refs[:7]
+    meta, across, psel, qsel, gram0, gram, sold = refs[:7]
     got, refs = refs[7 : 7 + sz.rounds], refs[7 + sz.rounds :]
-    pacc, qacc, keep_half, give_half, whole, meta, sem = refs
-    which, table = range(sz.rounds), (meta_in, meta, sem)
-    terms = add_coupled(sz, 2.0, table, got, across, psel, qsel, pacc, qacc, which)
+    pacc, qacc, keep_half, give_half, whole = refs
+    which = range(sz.rounds)
+    terms = add_coupled(sz, 2.0, meta, got, across, psel, qsel, pacc, qacc, which)
     left = jnp.concatenate([terms[j].astype(BF16) for j in range(sz.pairs)], axis=1)
     right = [sold[meta[sz.rows + j]].T for j in range(sz.pairs)]
     extra = nn(left, jnp.concatenate(right, axis=0))
@@ -452,10 +416,10 @@
     half = shape((sz.chan, 2 * sz.chan), F32)
     return call(
         functools.partial(correct_kernel, sz, axis),
-        [VMEM] * len(args),
+        [SMEM] + [VMEM] * (len(args) - 1),
         [VMEM] * 4,
         [sz.picked, sz.picked, half, half],
-        [pltpu.VMEM((2 * sz.chan, 2 * sz.chan), F32)] + table_copy(sz),
+        [pltpu.VMEM((2 * sz.chan, 2 * sz.chan), F32)],
         4 * sz.pairs * sz.chan * sz.blk * sz.blk,
         3 << 20,
         8,
@@ -470,13 +434,12 @@
 
 
 def start_kernel(sz, *refs):
-    meta_in, cross, _, _, across, psel, qsel = refs[:7]
+    meta, cross, _, _, across, psel, qsel = refs[:7]
     got, refs = refs[7 : 7 + sz.rounds], refs[7 + sz.rounds :]
     tnew, snew = refs[:2]
-    pacc, qacc, meta, sem = refs[-4:]
-    table = (meta_in, meta, sem)
-    add_coupled(sz, 1.0, table, got, across, psel, qsel, pacc, qacc, range(sz.rounds))
-    patch(sz, meta, cross, tnew, snew, pacc, qacc, refs[2:-4])
+    pacc, qacc = refs[-2:]
+    add_coupled(sz, 1.0, meta, got, across, psel, qsel, pacc, qacc, range(sz.rounds))
+    patch(sz, meta, cross, tnew, snew, pacc, qacc, refs[2:-2])
 
 
 def join_kernel(sz, *refs):
@@ -489,10 +452,10 @@
     outs = [sz.field, sz.field] + [sz.pay] * sz.rounds
     outs = call(
         functools.partial(start_kernel if first else join_kernel, sz),
-        [VMEM if first else SMEM] + [VMEM] * (len(args) - 1),
+        [SMEM] + [VMEM] * (len(args) - 1),
         [VMEM] * len(outs),
         outs,
-        [pltpu.VMEM(sz.picked.shape, F32)] * 2 + table_copy(sz) if first else [],
+        [pltpu.VMEM(sz.picked.shape, F32)] * 2 if first else [],
         2 * sz.pairs * sz.chan * sz.blk * sz.blk,
         5 << 20,
         8,
@@ -591,10 +554,10 @@
 
 
 def early_kernel(sz, which, low, *refs):
-    meta_in, across, psel, qsel = refs[:4]
+    meta, across, psel, qsel = refs[:4]
     got, refs = dict(zip(which, refs[4 : 4 + len(which)])), refs[4 + len(which) :]
     weights, fields, high = refs[:2], refs[2:8], refs[8:10]
-    pacc, qacc, held_out, held_grad, out4, grad4, meta, sem, sem_base = refs[13:]
+    pacc, qacc, held_out, held_grad, out4, grad4, sem_base = refs[13:]
     part = pl.ds(low, high[0].shape[1])
     base = [
         pltpu.make_async_copy(high[0], out4.at[:, part], sem_base.at[0]),
@@ -602,7 +565,7 @@
     ]
     for copy in base:
         copy.start()
-    add_coupled(sz, 2.0, (meta_in, meta, sem), got, across, psel, qsel, pacc, qacc, which)
+    add_coupled(sz, 2.0, meta, got, across, psel, qsel, pacc, qacc, which)
     fixed_blocks(sz, meta, which, weights, fields, (pacc, qacc), (held_out, held_grad))
     for copy in base:
         copy.wait()
@@ -614,10 +577,10 @@
     held = shape((sz.pairs, sz.chan // SUB, SUB, sz.blk), BF16)
     return call(
         functools.partial(early_kernel, sz, which, low),
-        [VMEM] * len(args) + [HBM] * 2,
+        [SMEM] + [VMEM] * (len(args) - 1) + [HBM] * 2,
         [VMEM] * 4 + [HBM] * 2,
         [sz.picked, sz.picked, held, held] + whole,
-        table_copy(sz) + [pltpu.SemaphoreType.DMA((2,))],
+        [pltpu.SemaphoreType.DMA((2,))],
         8 * sz.pairs * sz.chan * sz.blk * sz.blk,
         4 << 20,
         8,
@@ -626,11 +589,11 @@
 
 
 def fix_kernel(sz, axis, early, late, *refs):
-    meta_in, across, psel, qsel = refs[:4]
+    meta, across, psel, qsel = refs[:4]
     got, refs = dict(zip(late, refs[4 : 4 + len(late)])), refs[4 + len(late) :]
     weights, fields, fixed = refs[:2], refs[2:8], refs[8:10]
     mine, theirs = refs[10:12]
-    out4, grad4, grad_w, pacc, qacc, held_out, held_grad, total, meta, sem, sem_out, sem_w = refs[14:]
+    out4, grad4, grad_w, pacc, qacc, held_out, held_grad, total, sem_out, sem_w = refs[14:]
     held, outs = (held_out, held_grad), (out4, grad4)
     odd = lax.rem(lax.axis_index(axis), 2) == 1
     top = jnp.where(odd, theirs[...], mine[...])
@@ -642,7 +605,7 @@
     total[3] = 2.0 * top[:, sz.chan :] - first
     weight_copy = pltpu.make_async_copy(total, grad_w, sem_w)
     weight_copy.start()
-    add_coupled(sz, 2.0, (meta_in, meta, sem), got, across, psel, qsel, pacc, qacc, late)
+    add_coupled(sz, 2.0, meta, got, across, psel, qsel, pacc, qacc, late)
     copies = fixed_copies(sz, meta, early, late, fixed, outs, sem_out)
     for fresh, copy in copies:
         pl.when(fresh)(copy.start)
@@ -665,12 +628,11 @@
     total = (4, sz.chan, sz.chan)
     return call(
         functools.partial(fix_kernel, sz, axis, early, late),
-        [VMEM] * len(args) + [HBM] * 2,
+        [SMEM] + [VMEM] * (len(args) - 1) + [HBM] * 2,
         [HBM] * 3,
         whole + [shape(total, F32)],
         [pltpu.VMEM(sz.picked.shape, F32)] * 2
         + [held, held, pltpu.VMEM(total, F32)]
-        + table_copy(sz)
         + [pltpu.SemaphoreType.DMA((2, sz.pairs)), pltpu.SemaphoreType.DMA],
         8 * len(late) * sz.hb * sz.chan * sz.blk * sz.blk,
         2 << 20,

time: 50.4 us -> 48.2 us (0.956)
  Pallas kernels: 24.7 us -> 20 us
  waiting for transfers between devices: 3.62 us -> 5.23 us
  starting transfers between devices: 20.4 us -> 21.3 us
    pallas_call x7, Pallas kernels: 15.7 us -> 12.6 us  [the longest x1 4.56 us: first_products(): call(functools.partial(first_kernel, sz), [SMEM, SMEM, HBM, VMEM, VMEM],...]
    ppermute x21, waiting for transfers between devices: 3.62 us -> 5.23 us  [from_partner(): return lax.ppermute(values, 'dom', route)]
    pallas_call x2, Pallas kernels: 3.97 us -> 2.94 us  [part_products(): call(functools.partial(early_rows_kernel if before is None else late_rows...]
    ppermute x21, starting transfers between devices: 20.4 us -> 21.3 us  [from_partner(): return lax.ppermute(values, 'dom', route)]
  transfers between devices with their start and end apart: 21 -> 21, of which waited for: 6 -> 6; matrix products, arithmetic and copies ran while one was open for 0% -> 0% of each run, Pallas kernels for 37% -> 33%
where the time goes in v9:
time: 48.2 us; the launch traced here: 48 us
  starting transfers between devices  21.3 us (44%)
  Pallas kernels  20 us (41%)
  waiting for transfers between devices  5.23 us (11%)
  between operations  1.5 us (3%)
    ppermute x21, starting transfers between devices, from_partner(): return lax.ppermute(values, 'dom', route)  21.3 us
    ppermute x21, waiting for transfers between devices, from_partner(): return lax.ppermute(values, 'dom', route)  5.23 us
    pallas_call x1, Pallas kernels, first_products(): call(functools.partial(first_kernel, sz), [SMEM, SMEM, HBM, VMEM, VMEM],...  4.56 us
    pallas_call x1, Pallas kernels, local_products(): call(functools.partial(local_kernel, sz), [SMEM] * 2 + [VMEM] * 6, [VMEM]...  4.49 us
    pallas_call x2, Pallas kernels, part_products(): call(functools.partial(early_rows_kernel if before is None else late_rows...  2.94 us
    pallas_call x1, Pallas kernels, pack(): call(functools.partial(pack_kernel, sz), [HBM] * 6 + [SMEM, HBM], [VMEM]...  2.37 us
    pallas_call x1, Pallas kernels, base_outputs(): call(functools.partial(output_kernel, sz, middle), [VMEM] * len(args), [V...  2.1 us
    pallas_call x1, Pallas kernels, early_outputs(): call(functools.partial(early_kernel, sz, which, low), [SMEM] + [VMEM] * (...  1.31 us
  transfers between devices with their start and end apart: 21, of which 6 were waited for; matrix products, arithmetic and copies ran while one was open for 0% of the time, Pallas kernels for 33%

profile of v9, /device:TPU:0, one launch (start us, length us, event | category | flops | bytes accessed | tf_op | source)
XLA Modules:
  0.0 48.0 jit_solution(17678420829919199578)
XLA Ops:
  1.3 2.4 %shard_map.121 = (bf16[64,64,128]{2,1,0:T(8,128)(2,1)S(1)}, bf16[64,64,128]{2,1,0:T(8,128)(2,1)S(1)}, bf16[10,128,128]{2,1,0:T(8,128)(2,1)S(1)}, bf16[10,128,128...) custom-call(bf16[8,64,8,128]{3,2,1,0:T(8,128)(2,1)} %bitcast.18, ...), custom_call_target="tpu_custom_call" | custom-call | flops 1000 | bytes 4194304 | tf_op jit(solution)/shard_map/pallas_call | solution.py:144
  3.7 0.8 %collective-permute-start = (bf16[256,128]{1,0:T(8,128)(2,1)S(1)}, bf16[256,128]{1,0:T(8,128)(2,1)S(1)}, u32[]{:S(2)}, u32[]{:S(2)}) collective-permute-start(bf16[256,128]{1,0:T(8,128)(2,1)S(1)} %get-tuple-element.90), channel_id=1, source_target_pairs={{0,1},{1,0},{2,3},{3,2},{4,5},{5,4},{6,7},{7,6},{8,9},{9,8},{10,11... | collective-permute-start | bytes 196616 | tf_op jit(solution)/shard_map/ppermute | solution.py:680
  4.4 2.3 %collective-permute-start.1 = (bf16[256,128]{1,0:T(8,128)(2,1)S(1)}, bf16[256,128]{1,0:T(8,128)(2,1)S(1)}, u32[]{:S(2)}, u32[]{:S(2)}) collective-permute-start(bf16[256,128]{1,0:T(8,128)(2,1)S(1)} %get-tuple-element.91), channel_id=1, source_target_pairs={{0,2},{2,0},{1,3},{3,1},{4,6},{6,4},{5,7},{7,5},{8,10},{10,8},{9,1... | collective-permute-start | bytes 196616 | tf_op jit(solution)/shard_map/ppermute | solution.py:680
  6.8 1.7 %collective-permute-start.2 = (bf16[256,128]{1,0:T(8,128)(2,1)S(1)}, bf16[256,128]{1,0:T(8,128)(2,1)S(1)}, u32[]{:S(2)}, u32[]{:S(2)}) collective-permute-start(bf16[256,128]{1,0:T(8,128)(2,1)S(1)} %get-tuple-element.92), channel_id=1, source_target_pairs={{0,4},{4,0},{1,5},{5,1},{2,6},{6,2},{3,7},{7,3},{8,12},{12,8},{9,1... | collective-permute-start | bytes 196616 | tf_op jit(solution)/shard_map/ppermute | solution.py:680
  8.5 1.3 %collective-permute-start.3 = (bf16[256,128]{1,0:T(8,128)(2,1)S(1)}, bf16[256,128]{1,0:T(8,128)(2,1)S(1)}, u32[]{:S(2)}, u32[]{:S(2)}) collective-permute-start(bf16[256,128]{1,0:T(8,128)(2,1)S(1)} %get-tuple-element.93), channel_id=1, source_target_pairs={{0,8},{8,0},{1,9},{9,1},{2,10},{10,2},{3,11},{11,3},{4,12},{12,4},... | collective-permute-start | bytes 196616 | tf_op jit(solution)/shard_map/ppermute | solution.py:680
  9.7 2.6 %collective-permute-start.4 = (bf16[256,128]{1,0:T(8,128)(2,1)S(1)}, bf16[256,128]{1,0:T(8,128)(2,1)S(1)}, u32[]{:S(2)}, u32[]{:S(2)}) collective-permute-start(bf16[256,128]{1,0:T(8,128)(2,1)S(1)} %get-tuple-element.94), channel_id=1, source_target_pairs={{0,16},{16,0},{1,17},{17,1},{2,18},{18,2},{3,19},{19,3},{4,20},{20... | collective-permute-start | bytes 196616 | tf_op jit(solution)/shard_map/ppermute | solution.py:680
  12.3 4.6 %shard_map.122 = (bf16[64,64,128]{2,1,0:T(8,128)(2,1)S(1)}, bf16[64,64,128]{2,1,0:T(8,128)(2,1)S(1)}, f32[10,64,128]{2,1,0:T(8,128)S(1)}, f32[10,64,128]{2,1,0:T...) custom-call(s32[46]{0:T(128)S(4)} %get-tuple-element.78.refs_0_, ...), custom_call_target="tpu_custom_call" | custom-call | flops 805306368 | bytes 12582912 | tf_op jit(solution)/shard_map/pallas_call | solution.py:263
  16.9 0.0 collective-permute-done.refs_7_
  16.9 0.0 collective-permute-done.1.refs_8_
  16.9 0.0 collective-permute-done.2.refs_9_
  16.9 0.0 collective-permute-done.3.refs_10_
  16.9 0.3 shard_map.123
  17.3 0.1 collective-permute-start.5
  17.4 0.7 %collective-permute-start.6 = (bf16[256,128]{1,0:T(8,128)(2,1)S(1)}, bf16[256,128]{1,0:T(8,128)(2,1)S(1)}, u32[]{:S(2)}, u32[]{:S(2)}) collective-permute-start(bf16[256,128]{1,0:T(8,128)(2,1)S(1)} %get-tuple-element.104), channel_id=1, source_target_pairs={{0,2},{2,0},{1,3},{3,1},{4,6},{6,4},{5,7},{7,5},{8,10},{10,8},{9,1... | collective-permute-start | bytes 196616 | tf_op jit(solution)/shard_map/ppermute | solution.py:680
  18.1 0.3 collective-permute-start.7
  18.3 0.4 collective-permute-start.8
  18.8 1.2 %collective-permute-start.9 = (bf16[256,128]{1,0:T(8,128)(2,1)S(1)}, bf16[256,128]{1,0:T(8,128)(2,1)S(1)}, u32[]{:S(2)}, u32[]{:S(2)}) collective-permute-start(bf16[256,128]{1,0:T(8,128)(2,1)S(1)} %get-tuple-element.107), channel_id=1, source_target_pairs={{0,16},{16,0},{1,17},{17,1},{2,18},{18,2},{3,19},{19,3},{4,20},{20... | collective-permute-start | bytes 196616 | tf_op jit(solution)/shard_map/ppermute | solution.py:680
  19.9 4.5 %shard_map.124 = (bf16[64,64,128]{2,1,0:T(8,128)(2,1)S(1)}, bf16[64,64,128]{2,1,0:T(8,128)(2,1)S(1)}, f32[10,64,128]{2,1,0:T(8,128)S(1)}, f32[10,64,128]{2,1,0:T(8,128)S(1)}, f32[128,128]{1,0:T(8,128)S(1)}) custom-call(s32[46]{0:T(128)S(4)} %get-tuple-element.78.refs_0_, s32[3,64]{1,0:T(4,128)S(4)} %get-tuple-element.80.refs_1_, ...), custom_call_target="tpu_custom_call" | custom-call | flops 805306368 | bytes 12582912 | tf_op jit(solution)/shard_map/pallas_call | solution.py:323
  24.4 0.0 collective-permute-done.5.refs_7_
  24.5 0.0 collective-permute-done.8.refs_10_
  24.5 0.7 %collective-permute-done.9.refs_11_ = bf16[256,128]{1,0:T(8,128)(2,1)S(1)} collective-permute-done((bf16[256,128]{1,0:T(8,128)(2,1)S(1)}, bf16[256,128]{1,0:T(8,128)(2,1)S(1)}, u32[]{:S(2)}, u32[]{:S(2)}) %collective-permute-start.9) | collective-permute-done | bytes 65568 | tf_op jit(solution)/shard_map/ppermute | solution.py:680
  25.2 0.5 shard_map.125
  25.6 0.1 collective-permute-start.10
  25.7 0.3 shard_map.126
  26.0 0.6 %collective-permute-start.12 = (bf16[256,128]{1,0:T(8,128)(2,1)S(1)}, bf16[256,128]{1,0:T(8,128)(2,1)S(1)}, u32[]{:S(2)}, u32[]{:S(2)}) collective-permute-start(bf16[256,128]{1,0:T(8,128)(2,1)S(1)} %get-tuple-element.121), channel_id=1, source_target_pairs={{0,1},{1,0},{2,3},{3,2},{4,5},{5,4},{6,7},{7,6},{8,9},{9,8},{10,11... | collective-permute-start | bytes 196616 | tf_op jit(solution)/shard_map/ppermute | solution.py:680
  26.5 0.4 collective-permute-done.10.refs_1_
  26.9 1.0 %collective-permute-start.11 = (f32[64,128]{1,0:T(8,128)S(1)}, f32[64,128]{1,0:T(8,128)S(1)}, u32[]{:S(2)}, u32[]{:S(2)}) collective-permute-start(f32[64,128]{1,0:T(8,128)S(1)} %get-tuple-element.119.refs_0_), channel_id=1, source_target_pairs={{0,16},{16,0},{1,17},{17,1},{2,18},{18,2},{3,19},{19,3},{4,20},{20... | collective-permute-start | bytes 98312 | tf_op jit(solution)/shard_map/ppermute | solution.py:680
  27.9 2.0 %collective-permute-start.13 = (bf16[256,128]{1,0:T(8,128)(2,1)S(1)}, bf16[256,128]{1,0:T(8,128)(2,1)S(1)}, u32[]{:S(2)}, u32[]{:S(2)}) collective-permute-start(bf16[256,128]{1,0:T(8,128)(2,1)S(1)} %get-tuple-element.125), channel_id=1, source_target_pairs={{0,16},{16,0},{1,17},{17,1},{2,18},{18,2},{3,19},{19,3},{4,20},{20... | collective-permute-start | bytes 196616 | tf_op jit(solution)/shard_map/ppermute | solution.py:680
  29.9 1.7 %shard_map.128 = (bf16[64,64,128]{2,1,0:T(8,128)(2,1)S(1)}, f32[64,64,128]{2,1,0:T(8,128)S(1)}, f32[64,64,128]{2,1,0:T(8,128)S(1)}) custom-call(s32[46]{0:T(128)S(4)} %get-tuple-element.78.refs_0_, s32[3,64]{1,0:T(4,128)S(4)} %get-tuple-element.80.refs_1_, bf16[64,3,128,128]{3,2,1,0:T(8,128)(2,1)S(1)} %get-tuple-element.83.refs_2_, ...), custom_call_target="tpu_custom_call" | custom-call | flops 402653184 | bytes 6291456 | tf_op jit(solution)/shard_map/pallas_call | solution.py:367
  31.6 0.0 collective-permute-done.12.refs_3_.refs_4_
  31.7 0.7 %collective-permute-done.11.refs_1_ = f32[64,128]{1,0:T(8,128)S(1)} collective-permute-done((f32[64,128]{1,0:T(8,128)S(1)}, f32[64,128]{1,0:T(8,128)S(1)}, u32[]{:S(2)}, u32[]{:S(2)}) %collective-permute-start.11) | collective-permute-done | bytes 32800 | tf_op jit(solution)/shard_map/ppermute | solution.py:680
  32.4 0.6 %collective-permute-start.15 = (f32[64,128]{1,0:T(8,128)S(1)}, f32[64,128]{1,0:T(8,128)S(1)}, u32[]{:S(2)}, u32[]{:S(2)}) collective-permute-start(f32[64,128]{1,0:T(8,128)S(1)} %get-tuple-element.127.refs_0_), channel_id=1, source_target_pairs={{0,8},{8,0},{1,9},{9,1},{2,10},{10,2},{3,11},{11,3},{4,12},{12,4},... | collective-permute-start | bytes 98312 | tf_op jit(solution)/shard_map/ppermute | solution.py:680
  32.9 1.5 %collective-permute-start.14 = (bf16[256,128]{1,0:T(8,128)(2,1)S(1)}, bf16[256,128]{1,0:T(8,128)(2,1)S(1)}, u32[]{:S(2)}, u32[]{:S(2)}) collective-permute-start(bf16[256,128]{1,0:T(8,128)(2,1)S(1)} %get-tuple-element.126), channel_id=1, source_target_pairs={{0,8},{8,0},{1,9},{9,1},{2,10},{10,2},{3,11},{11,3},{4,12},{12,4},... | collective-permute-start | bytes 196616 | tf_op jit(solution)/shard_map/ppermute | solution.py:680
  34.5 1.2 %shard_map.130 = (bf16[64,64,128]{2,1,0:T(8,128)(2,1)S(1)}, f32[64,64,128]{2,1,0:T(8,128)S(1)}, f32[64,64,128]{2,1,0:T(8,128)S(1)}, bf16[64,64,128]{2,1,0:T(8,12...) custom-call(s32[46]{0:T(128)S(4)} %get-tuple-element.78.refs_0_, ...), custom_call_target="tpu_custom_call", output_to_operand_aliasing={{0}: (8, {}), {1}: (9, {}), {2}: (10, {})} | custom-call | flops 402653184 | bytes 6291456 | tf_op jit(solution)/shard_map/pallas_call | solution.py:367
  35.7 0.6 %collective-permute-done.15.refs_1_ = f32[64,128]{1,0:T(8,128)S(1)} collective-permute-done((f32[64,128]{1,0:T(8,128)S(1)}, f32[64,128]{1,0:T(8,128)S(1)}, u32[]{:S(2)}, u32[]{:S(2)}) %collective-permute-start.15) | collective-permute-done | bytes 32800 | tf_op jit(solution)/shard_map/ppermute | solution.py:680
  36.4 0.0 collective-permute-done.13.refs_4_.refs_5_
  36.4 1.3 %collective-permute-start.17 = (f32[64,128]{1,0:T(8,128)S(1)}, f32[64,128]{1,0:T(8,128)S(1)}, u32[]{:S(2)}, u32[]{:S(2)}) collective-permute-start(f32[64,128]{1,0:T(8,128)S(1)} %get-tuple-element.137.refs_0_), channel_id=1, source_target_pairs={{0,4},{4,0},{1,5},{5,1},{2,6},{6,2},{3,7},{7,3},{8,12},{12,8},{9,1... | collective-permute-start | bytes 98312 | tf_op jit(solution)/shard_map/ppermute | solution.py:680
  37.7 0.8 %collective-permute-start.16 = (bf16[256,128]{1,0:T(8,128)(2,1)S(1)}, bf16[256,128]{1,0:T(8,128)(2,1)S(1)}, u32[]{:S(2)}, u32[]{:S(2)}) collective-permute-start(bf16[256,128]{1,0:T(8,128)(2,1)S(1)} %get-tuple-element.129), channel_id=1, source_target_pairs={{0,4},{4,0},{1,5},{5,1},{2,6},{6,2},{3,7},{7,3},{8,12},{12,8},{9,1... | collective-permute-start | bytes 196616 | tf_op jit(solution)/shard_map/ppermute | solution.py:680
  38.5 2.1 %shard_map.132 = (bf16[64,256]{1,0:T(8,128)(2,1)S(1)}, bf16[64,256]{1,0:T(8,128)(2,1)S(1)}, bf16[8,32,8,128]{3,2,1,0:T(8,128)(2,1)S(1)}, bf16[8,32,8,128]{3,2,1,...) custom-call(bf16[64,64,128]{2,1,0:T(8,128)(2,1)S(1)} %get-tuple-element.81.refs_3_.refs_6_.refs_0_.ref, ...), custom_call_target="tpu_custom_call" | custom-call | flops 536870912 | bytes 6291456 | tf_op jit(solution)/shard_map/pallas_call | solution.py:516
  40.6 0.0 collective-permute-done.14.refs_4_.refs_6_
  40.6 2.0 %collective-permute-start.18 = (f32[64,128]{1,0:T(8,128)S(1)}, f32[64,128]{1,0:T(8,128)S(1)}, u32[]{:S(2)}, u32[]{:S(2)}) collective-permute-start(f32[64,128]{1,0:T(8,128)S(1)} %get-tuple-element.139.refs_0_), channel_id=1, source_target_pairs={{0,2},{2,0},{1,3},{3,1},{4,6},{6,4},{5,7},{7,5},{8,10},{10,8},{9,1... | collective-permute-start | bytes 98312 | tf_op jit(solution)/shard_map/ppermute | solution.py:680
  42.6 0.1 collective-permute-start.19
  42.7 1.9 %collective-permute-done.18.refs_1_ = f32[64,128]{1,0:T(8,128)S(1)} collective-permute-done((f32[64,128]{1,0:T(8,128)S(1)}, f32[64,128]{1,0:T(8,128)S(1)}, u32[]{:S(2)}, u32[]{:S(2)}) %collective-permute-start.18) | collective-permute-done | bytes 32800 | tf_op jit(solution)/shard_map/ppermute | solution.py:680
  44.6 0.1 collective-permute-start.20
  44.7 1.3 %shard_map.135 = (f32[10,64,128]{2,1,0:T(8,128)S(1)}, f32[10,64,128]{2,1,0:T(8,128)S(1)}, bf16[10,8,8,128]{3,2,1,0:T(8,128)(2,1)S(1)}, bf16[10,8,8,128]{3,2,1,0:...) custom-call(s32[46]{0:T(128)S(4)} %get-tuple-element.78.refs_0_, ...), custom_call_target="tpu_custom_call", output_to_operand_aliasing={{4}: (19, {}), {5}: (20, {})} | custom-call | flops 83886080 | bytes 4194304 | tf_op jit(solution)/shard_map/pallas_call | solution.py:578
  46.0 0.0 collective-permute-done.20.refs_16_
  46.0 0.9 %collective-permute-done.19.refs_4_ = bf16[256,128]{1,0:T(8,128)(2,1)S(1)} collective-permute-done((bf16[256,128]{1,0:T(8,128)(2,1)S(1)}, bf16[256,128]{1,0:T(8,128)(2,1)S(1)}, u32[]{:S(2)}, u32[]{:S(2)}) %collective-permute-start.19) | collective-permute-done | bytes 65568 | tf_op jit(solution)/shard_map/ppermute | solution.py:680
  46.9 1.1 %shard_map.136 = (bf16[8,64,8,128]{3,2,1,0:T(8,128)(2,1)}, bf16[8,64,8,128]{3,2,1,0:T(8,128)(2,1)}, f32[4,64,64]{2,1,0:T(8,128)}) custom-call(s32[46]{0:T(128)S(4)} %get-tuple-element.78.refs_0_, bf16[10,128,128]{2,1,0:T(8,128)(2,1)S(1)} %get-tuple-element.79.refs_4_.refs_1_, ...), custom_call_target="tpu_custom_call", output_to_operand_aliasing={{0}: (17, {}), {1}: (18, {})} | custom-call | flops 16777216 | bytes 2097152 | tf_op jit(solution)/shard_map/pallas_call | solution.py:629
  (12 shorter events, 0.1 us)
Async XLA Ops:
  3.7 13.2 %collective-permute-start = (bf16[256,128]{1,0:T(8,128)(2,1)S(1)}, bf16[256,128]{1,0:T(8,128)(2,1)S(1)}, u32[]{:S(2)}, u32[]{:S(2)}) collective-permute-start(bf16[256,128]{1,0:T(8,128)(2,1)S(1)} %get-tuple-element.90), channel_id=1, source_target_pairs={{0,1},{1,0},{2,3},{3,2},{4,5},{5,4},{6,7},{7,6},{8,9},{9,8},{10,11... | collective-permute-start | bytes 196616 | tf_op jit(solution)/shard_map/ppermute | solution.py:680
  4.4 12.5 %collective-permute-start.1 = (bf16[256,128]{1,0:T(8,128)(2,1)S(1)}, bf16[256,128]{1,0:T(8,128)(2,1)S(1)}, u32[]{:S(2)}, u32[]{:S(2)}) collective-permute-start(bf16[256,128]{1,0:T(8,128)(2,1)S(1)} %get-tuple-element.91), channel_id=1, source_target_pairs={{0,2},{2,0},{1,3},{3,1},{4,6},{6,4},{5,7},{7,5},{8,10},{10,8},{9,1... | collective-permute-start | bytes 196616 | tf_op jit(solution)/shard_map/ppermute | solution.py:680
  6.8 10.1 %collective-permute-start.2 = (bf16[256,128]{1,0:T(8,128)(2,1)S(1)}, bf16[256,128]{1,0:T(8,128)(2,1)S(1)}, u32[]{:S(2)}, u32[]{:S(2)}) collective-permute-start(bf16[256,128]{1,0:T(8,128)(2,1)S(1)} %get-tuple-element.92), channel_id=1, source_target_pairs={{0,4},{4,0},{1,5},{5,1},{2,6},{6,2},{3,7},{7,3},{8,12},{12,8},{9,1... | collective-permute-start | bytes 196616 | tf_op jit(solution)/shard_map/ppermute | solution.py:680
  8.5 8.5 %collective-permute-start.3 = (bf16[256,128]{1,0:T(8,128)(2,1)S(1)}, bf16[256,128]{1,0:T(8,128)(2,1)S(1)}, u32[]{:S(2)}, u32[]{:S(2)}) collective-permute-start(bf16[256,128]{1,0:T(8,128)(2,1)S(1)} %get-tuple-element.93), channel_id=1, source_target_pairs={{0,8},{8,0},{1,9},{9,1},{2,10},{10,2},{3,11},{11,3},{4,12},{12,4},... | collective-permute-start | bytes 196616 | tf_op jit(solution)/shard_map/ppermute | solution.py:680
  9.7 7.2 %collective-permute-start.4 = (bf16[256,128]{1,0:T(8,128)(2,1)S(1)}, bf16[256,128]{1,0:T(8,128)(2,1)S(1)}, u32[]{:S(2)}, u32[]{:S(2)}) collective-permute-start(bf16[256,128]{1,0:T(8,128)(2,1)S(1)} %get-tuple-element.94), channel_id=1, source_target_pairs={{0,16},{16,0},{1,17},{17,1},{2,18},{18,2},{3,19},{19,3},{4,20},{20... | collective-permute-start | bytes 196616 | tf_op jit(solution)/shard_map/ppermute | solution.py:680
  17.3 7.2 %collective-permute-start.5 = (bf16[256,128]{1,0:T(8,128)(2,1)S(1)}, bf16[256,128]{1,0:T(8,128)(2,1)S(1)}, u32[]{:S(2)}, u32[]{:S(2)}) collective-permute-start(bf16[256,128]{1,0:T(8,128)(2,1)S(1)} %get-tuple-element.103), channel_id=1, source_target_pairs={{0,1},{1,0},{2,3},{3,2},{4,5},{5,4},{6,7},{7,6},{8,9},{9,8},{10,11... | collective-permute-start | bytes 196616 | tf_op jit(solution)/shard_map/ppermute | solution.py:680
  17.4 7.1 %collective-permute-start.6 = (bf16[256,128]{1,0:T(8,128)(2,1)S(1)}, bf16[256,128]{1,0:T(8,128)(2,1)S(1)}, u32[]{:S(2)}, u32[]{:S(2)}) collective-permute-start(bf16[256,128]{1,0:T(8,128)(2,1)S(1)} %get-tuple-element.104), channel_id=1, source_target_pairs={{0,2},{2,0},{1,3},{3,1},{4,6},{6,4},{5,7},{7,5},{8,10},{10,8},{9,1... | collective-permute-start | bytes 196616 | tf_op jit(solution)/shard_map/ppermute | solution.py:680
  18.1 6.4 %collective-permute-start.7 = (bf16[256,128]{1,0:T(8,128)(2,1)S(1)}, bf16[256,128]{1,0:T(8,128)(2,1)S(1)}, u32[]{:S(2)}, u32[]{:S(2)}) collective-permute-start(bf16[256,128]{1,0:T(8,128)(2,1)S(1)} %get-tuple-element.105), channel_id=1, source_target_pairs={{0,4},{4,0},{1,5},{5,1},{2,6},{6,2},{3,7},{7,3},{8,12},{12,8},{9,1... | collective-permute-start | bytes 196616 | tf_op jit(solution)/shard_map/ppermute | solution.py:680
  18.3 6.1 %collective-permute-start.8 = (bf16[256,128]{1,0:T(8,128)(2,1)S(1)}, bf16[256,128]{1,0:T(8,128)(2,1)S(1)}, u32[]{:S(2)}, u32[]{:S(2)}) collective-permute-start(bf16[256,128]{1,0:T(8,128)(2,1)S(1)} %get-tuple-element.106), channel_id=1, source_target_pairs={{0,8},{8,0},{1,9},{9,1},{2,10},{10,2},{3,11},{11,3},{4,12},{12,4},... | collective-permute-start | bytes 196616 | tf_op jit(solution)/shard_map/ppermute | solution.py:680
  18.8 6.4 %collective-permute-start.9 = (bf16[256,128]{1,0:T(8,128)(2,1)S(1)}, bf16[256,128]{1,0:T(8,128)(2,1)S(1)}, u32[]{:S(2)}, u32[]{:S(2)}) collective-permute-start(bf16[256,128]{1,0:T(8,128)(2,1)S(1)} %get-tuple-element.107), channel_id=1, source_target_pairs={{0,16},{16,0},{1,17},{17,1},{2,18},{18,2},{3,19},{19,3},{4,20},{20... | collective-permute-start | bytes 196616 | tf_op jit(solution)/shard_map/ppermute | solution.py:680
  25.6 1.3 %collective-permute-start.10 = (f32[64,128]{1,0:T(8,128)S(1)}, f32[64,128]{1,0:T(8,128)S(1)}, u32[]{:S(2)}, u32[]{:S(2)}) collective-permute-start(f32[64,128]{1,0:T(8,128)S(1)} %get-tuple-element.113), channel_id=1, source_target_pairs={{0,1},{1,0},{2,3},{3,2},{4,5},{5,4},{6,7},{7,6},{8,9},{9,8},{10,11... | collective-permute-start | bytes 98312 | tf_op jit(solution)/shard_map/ppermute | solution.py:680
  26.0 5.7 %collective-permute-start.12 = (bf16[256,128]{1,0:T(8,128)(2,1)S(1)}, bf16[256,128]{1,0:T(8,128)(2,1)S(1)}, u32[]{:S(2)}, u32[]{:S(2)}) collective-permute-start(bf16[256,128]{1,0:T(8,128)(2,1)S(1)} %get-tuple-element.121), channel_id=1, source_target_pairs={{0,1},{1,0},{2,3},{3,2},{4,5},{5,4},{6,7},{7,6},{8,9},{9,8},{10,11... | collective-permute-start | bytes 196616 | tf_op jit(solution)/shard_map/ppermute | solution.py:680
  26.9 5.4 %collective-permute-start.11 = (f32[64,128]{1,0:T(8,128)S(1)}, f32[64,128]{1,0:T(8,128)S(1)}, u32[]{:S(2)}, u32[]{:S(2)}) collective-permute-start(f32[64,128]{1,0:T(8,128)S(1)} %get-tuple-element.119.refs_0_), channel_id=1, source_target_pairs={{0,16},{16,0},{1,17},{17,1},{2,18},{18,2},{3,19},{19,3},{4,20},{20... | collective-permute-start | bytes 98312 | tf_op jit(solution)/shard_map/ppermute | solution.py:680
  27.9 8.4 %collective-permute-start.13 = (bf16[256,128]{1,0:T(8,128)(2,1)S(1)}, bf16[256,128]{1,0:T(8,128)(2,1)S(1)}, u32[]{:S(2)}, u32[]{:S(2)}) collective-permute-start(bf16[256,128]{1,0:T(8,128)(2,1)S(1)} %get-tuple-element.125), channel_id=1, source_target_pairs={{0,16},{16,0},{1,17},{17,1},{2,18},{18,2},{3,19},{19,3},{4,20},{20... | collective-permute-start | bytes 196616 | tf_op jit(solution)/shard_map/ppermute | solution.py:680
  32.4 4.0 %collective-permute-start.15 = (f32[64,128]{1,0:T(8,128)S(1)}, f32[64,128]{1,0:T(8,128)S(1)}, u32[]{:S(2)}, u32[]{:S(2)}) collective-permute-start(f32[64,128]{1,0:T(8,128)S(1)} %get-tuple-element.127.refs_0_), channel_id=1, source_target_pairs={{0,8},{8,0},{1,9},{9,1},{2,10},{10,2},{3,11},{11,3},{4,12},{12,4},... | collective-permute-start | bytes 98312 | tf_op jit(solution)/shard_map/ppermute | solution.py:680
  32.9 7.6 %collective-permute-start.14 = (bf16[256,128]{1,0:T(8,128)(2,1)S(1)}, bf16[256,128]{1,0:T(8,128)(2,1)S(1)}, u32[]{:S(2)}, u32[]{:S(2)}) collective-permute-start(bf16[256,128]{1,0:T(8,128)(2,1)S(1)} %get-tuple-element.126), channel_id=1, source_target_pairs={{0,8},{8,0},{1,9},{9,1},{2,10},{10,2},{3,11},{11,3},{4,12},{12,4},... | collective-permute-start | bytes 196616 | tf_op jit(solution)/shard_map/ppermute | solution.py:680
  34.5 4.0 %copy-start = (bf16[4,64,64]{2,1,0:T(8,128)(2,1)S(1)}, bf16[4,64,64]{2,1,0:T(8,128)(2,1)}, u32[]{:S(2)}) copy-start(bf16[4,64,64]{2,1,0:T(8,128)(2,1)} %refs_8_.1) | copy-start | bytes 98308
  36.4 4.2 %collective-permute-start.17 = (f32[64,128]{1,0:T(8,128)S(1)}, f32[64,128]{1,0:T(8,128)S(1)}, u32[]{:S(2)}, u32[]{:S(2)}) collective-permute-start(f32[64,128]{1,0:T(8,128)S(1)} %get-tuple-element.137.refs_0_), channel_id=1, source_target_pairs={{0,4},{4,0},{1,5},{5,1},{2,6},{6,2},{3,7},{7,3},{8,12},{12,8},{9,1... | collective-permute-start | bytes 98312 | tf_op jit(solution)/shard_map/ppermute | solution.py:680
  37.7 6.9 %collective-permute-start.16 = (bf16[256,128]{1,0:T(8,128)(2,1)S(1)}, bf16[256,128]{1,0:T(8,128)(2,1)S(1)}, u32[]{:S(2)}, u32[]{:S(2)}) collective-permute-start(bf16[256,128]{1,0:T(8,128)(2,1)S(1)} %get-tuple-element.129), channel_id=1, source_target_pairs={{0,4},{4,0},{1,5},{5,1},{2,6},{6,2},{3,7},{7,3},{8,12},{12,8},{9,1... | collective-permute-start | bytes 196616 | tf_op jit(solution)/shard_map/ppermute | solution.py:680
  40.6 4.0 %collective-permute-start.18 = (f32[64,128]{1,0:T(8,128)S(1)}, f32[64,128]{1,0:T(8,128)S(1)}, u32[]{:S(2)}, u32[]{:S(2)}) collective-permute-start(f32[64,128]{1,0:T(8,128)S(1)} %get-tuple-element.139.refs_0_), channel_id=1, source_target_pairs={{0,2},{2,0},{1,3},{3,1},{4,6},{6,4},{5,7},{7,5},{8,10},{10,8},{9,1... | collective-permute-start | bytes 98312 | tf_op jit(solution)/shard_map/ppermute | solution.py:680
  42.6 4.3 %collective-permute-start.19 = (bf16[256,128]{1,0:T(8,128)(2,1)S(1)}, bf16[256,128]{1,0:T(8,128)(2,1)S(1)}, u32[]{:S(2)}, u32[]{:S(2)}) collective-permute-start(bf16[256,128]{1,0:T(8,128)(2,1)S(1)} %get-tuple-element.145), channel_id=1, source_target_pairs={{0,2},{2,0},{1,3},{3,1},{4,6},{6,4},{5,7},{7,5},{8,10},{10,8},{9,1... | collective-permute-start | bytes 196616 | tf_op jit(solution)/shard_map/ppermute | solution.py:680
  44.6 1.4 %collective-permute-start.20 = (f32[64,128]{1,0:T(8,128)S(1)}, f32[64,128]{1,0:T(8,128)S(1)}, u32[]{:S(2)}, u32[]{:S(2)}) collective-permute-start(f32[64,128]{1,0:T(8,128)S(1)} %shard_map.134.refs_18_.refs_15_), channel_id=1, source_target_pairs={{0,1},{1,0},{2,3},{3,2},{4,5},{5,4},{6,7},{7,6},{8,9},{9,8},{10,11... | collective-permute-start | bytes 98312 | tf_op jit(solution)/shard_map/ppermute | solution.py:680
